TPU v7x, 32 devices: a whole 2x2x4 slice. The times are simulated.
32 devices in a mesh: rep: 8 (over y, x, core), shard: 4 (over z).
Axes of the slice: x: 2, y: 2, z: 4, core: 2. Of those that a mesh axis runs over, the one named last changes fastest.
Arguments:
- tokens: bfloat16 [32, 512, 1024], P(('rep', 'shard')), may hold values from -6 to 6
- segments: int32 [32, 512], P(('rep', 'shard')), may hold values from 0 to 25, as said below
- lengths: int32 [32], P(('rep', 'shard')), may hold values from 449 to 512, as said below
- cotangent: bfloat16 [32, 512, 1024], P(('rep', 'shard')), may hold values from -6 to 6
- w_qkv: bfloat16 [1024, 3072], P('shard'), may hold values from -0.1875 to 0.1875
- b_qv: bfloat16 [2048], P('shard'), may hold values from -4 to 4
- w_out: bfloat16 [1024, 1024], P('shard'), may hold values from -0.5 to 0.5
- b_out: bfloat16 [1024], P('shard'), may hold values from -4 to 4
- gain_one: bfloat16 [1024], P('shard'), may hold values from 0.5 to 1.5
- shift_one: bfloat16 [1024], P('shard'), may hold values from -4 to 4
- w_in: bfloat16 [1024, 4096], P('shard'), may hold values from -0.1875 to 0.1875
- b_in: bfloat16 [4096], P('shard'), may hold values from -4 to 4
- w_down: bfloat16 [4096, 1024], P('shard'), may hold values from -0.09375 to 0.09375
- b_down: bfloat16 [1024], P('shard'), may hold values from -4 to 4
- gain_two: bfloat16 [1024], P('shard'), may hold values from 0.5 to 1.5
- shift_two: bfloat16 [1024], P('shard'), may hold values from -4 to 4
Outputs:
- layer_out: bfloat16 [32, 512, 1024], P(('rep', 'shard'))
- grad_tokens: float32 [32, 512, 1024], P(('rep', 'shard'))
- grad_w_qkv: float32 [1024, 3072], P('shard')
- grad_b_qv: float32 [2048], P('shard')
- grad_w_out: float32 [1024, 1024], P('shard')
- grad_b_out: float32 [1024], P('shard')
- grad_gain_one: float32 [1024], P('shard')
- grad_shift_one: float32 [1024], P('shard')
- grad_w_in: float32 [1024, 4096], P('shard')
- grad_b_in: float32 [4096], P('shard')
- grad_w_down: float32 [4096, 1024], P('shard')
- grad_b_down: float32 [1024], P('shard')
- grad_gain_two: float32 [1024], P('shard')
- grad_shift_two: float32 [1024], P('shard')
Inputs may be any that keep to these rules, and one draw needn't show every extreme that they name: `segments`: within a sequence the document numbers start at 0 and never fall; every document spans 20 to 200 positions unless the sequence's end cuts it; the first sequence is made of documents of 20 positions. `lengths`: positions from a sequence's length on are padding; the first sequence has none, the second has the most.
All inputs are finite; a program needn't handle non-finite values.
Results may differ from a plain program's by a relative error of at most 0.019.
Values may be sent and summed in bfloat16 or wider, within the bound.
No kernel may reach another device: no remote copies, remote signals or barrier semaphores. Data moves between devices by JAX's collectives and lax.ppermute only.
A program may use at most 192 MiB of HBM per device.

v0:
```python
from functools import partial

import jax
import jax.numpy as jnp
from jax import lax
from jax.sharding import PartitionSpec as P

HEAD_DIM = 64


def layer_norm(hidden, norm_gain, norm_shift):
    average = jnp.mean(hidden, axis=-1, keepdims=True)
    centred = hidden - average
    variance = jnp.mean(centred * centred, axis=-1, keepdims=True)
    return centred * lax.rsqrt(variance + 1e-06) * norm_gain + norm_shift


def matmul(left, right):
    return jnp.dot(left, right, preferred_element_type=jnp.float32)


def project_back(left, right):
    return lax.dot_general(
        left, right, (((1,), (1,)), ((), ())), preferred_element_type=jnp.float32
    )


def outer_sum(left, right):
    return lax.dot_general(
        left, right, (((0,), (0,)), ((), ())), preferred_element_type=jnp.float32
    )


def column_sum(values):
    return jnp.sum(values.astype(jnp.float32), axis=0)


def allowed_pairs(doc_ids, length):
    positions = jnp.arange(doc_ids.shape[0])
    is_valid = positions < length
    return (doc_ids[:, None] == doc_ids[None, :]) & (is_valid[:, None] == is_valid[None, :])


def attend(items):
    query_heads, key_heads, value_heads, doc_ids, length = items
    scale = query_heads.shape[2] ** (-0.5)
    allowed = allowed_pairs(doc_ids, length)
    scores = (
        jnp.einsum("qhd,khd->hqk", query_heads, key_heads, preferred_element_type=jnp.float32)
        * scale
    )
    scores = jnp.where(allowed[None], scores, -1e30)
    maxima = jnp.max(scores, axis=2, keepdims=True)
    expo = jnp.exp(scores - maxima)
    totals = jnp.sum(expo, axis=2, keepdims=True)
    attn_probs = (expo / totals).astype(jnp.bfloat16)
    context = jnp.einsum(
        "hqk,khd->qhd", attn_probs, value_heads, preferred_element_type=jnp.float32
    )
    return (context.astype(jnp.bfloat16), maxima + jnp.log(totals))


def attend_back(items):
    query_heads, key_heads, value_heads, grad_context, doc_ids, length, log_totals = items
    scale = query_heads.shape[2] ** (-0.5)
    allowed = allowed_pairs(doc_ids, length)
    scores = (
        jnp.einsum("qhd,khd->hqk", query_heads, key_heads, preferred_element_type=jnp.float32)
        * scale
    )
    scores = jnp.where(allowed[None], scores, -1e30)
    attn_probs = jnp.exp(scores - log_totals)
    grad_probs = jnp.einsum(
        "qhd,khd->hqk", grad_context, value_heads, preferred_element_type=jnp.float32
    )
    grad_scores = attn_probs * (
        grad_probs - jnp.sum(attn_probs * grad_probs, axis=2, keepdims=True)
    )
    grad_low = grad_scores.astype(jnp.bfloat16)
    grad_query = (
        jnp.einsum("hqk,khd->qhd", grad_low, key_heads, preferred_element_type=jnp.float32) * scale
    )
    grad_key = (
        jnp.einsum("hqk,qhd->khd", grad_low, query_heads, preferred_element_type=jnp.float32)
        * scale
    )
    grad_value = jnp.einsum(
        "hqk,qhd->khd",
        attn_probs.astype(jnp.bfloat16),
        grad_context,
        preferred_element_type=jnp.float32,
    )
    return (
        grad_query.astype(jnp.bfloat16),
        grad_key.astype(jnp.bfloat16),
        grad_value.astype(jnp.bfloat16),
    )


def local(
    tokens,
    segments,
    lengths,
    cotangent,
    w_qkv,
    b_qv,
    w_out,
    b_out,
    gain_one,
    shift_one,
    w_in,
    b_in,
    w_down,
    b_down,
    gain_two,
    shift_two,
):
    gathered = (
        lax.all_gather(w_qkv, "shard", axis=0, tiled=True),
        lax.all_gather(b_qv, "shard", axis=0, tiled=True),
        lax.all_gather(w_out, "shard", axis=0, tiled=True),
        lax.all_gather(b_out, "shard", axis=0, tiled=True),
        lax.all_gather(gain_one, "shard", axis=0, tiled=True),
        lax.all_gather(shift_one, "shard", axis=0, tiled=True),
        lax.all_gather(w_in, "shard", axis=0, tiled=True),
        lax.all_gather(b_in, "shard", axis=0, tiled=True),
        lax.all_gather(w_down, "shard", axis=0, tiled=True),
        lax.all_gather(b_down, "shard", axis=0, tiled=True),
        lax.all_gather(gain_two, "shard", axis=0, tiled=True),
        lax.all_gather(shift_two, "shard", axis=0, tiled=True),
    )
    (
        full_qkv,
        full_bqv,
        full_out,
        full_bout,
        full_gone,
        full_sone,
        full_in,
        full_bin,
        full_down,
        full_bdown,
        full_gtwo,
        full_stwo,
    ) = gathered
    bias_qv = full_bqv.astype(jnp.float32)
    bias_out = full_bout.astype(jnp.float32)
    norm_gone = full_gone.astype(jnp.float32)
    norm_sone = full_sone.astype(jnp.float32)
    bias_in = full_bin.astype(jnp.float32)
    bias_down = full_bdown.astype(jnp.float32)
    norm_gtwo = full_gtwo.astype(jnp.float32)
    norm_stwo = full_stwo.astype(jnp.float32)
    seq_count, seq_len, model_width = tokens.shape
    num_heads = model_width // HEAD_DIM
    split_shape = (seq_count, seq_len, num_heads, HEAD_DIM)
    flat_in = tokens.reshape(seq_count * seq_len, model_width)
    projected = matmul(flat_in, full_qkv)
    queries = (projected[:, :model_width] + bias_qv[:model_width]).astype(jnp.bfloat16)
    key_rows = projected[:, model_width : 2 * model_width].astype(jnp.bfloat16)
    value_rows = (projected[:, 2 * model_width :] + bias_qv[model_width:]).astype(jnp.bfloat16)
    query_heads = queries.reshape(split_shape)
    key_heads = key_rows.reshape(split_shape)
    value_heads = value_rows.reshape(split_shape)
    context, log_totals = lax.map(attend, (query_heads, key_heads, value_heads, segments, lengths))
    context_flat = context.reshape(-1, model_width)
    attn_out = matmul(context_flat, full_out) + bias_out
    first_sum = flat_in.astype(jnp.float32) + attn_out
    normed_one = layer_norm(first_sum, norm_gone, norm_sone)
    normed_low = normed_one.astype(jnp.bfloat16)
    inner = matmul(normed_low, full_in) + bias_in
    activated = jax.nn.gelu(inner, approximate=False)
    act_low = activated.astype(jnp.bfloat16)
    branch = matmul(act_low, full_down) + bias_down
    second_sum = normed_one + branch
    output_rows = layer_norm(second_sum, norm_gtwo, norm_stwo)
    mat_qkv, mat_out, mat_in, mat_down = (
        lax.all_gather(w_qkv, "shard", axis=0, tiled=True),
        lax.all_gather(w_out, "shard", axis=0, tiled=True),
        lax.all_gather(w_in, "shard", axis=0, tiled=True),
        lax.all_gather(w_down, "shard", axis=0, tiled=True),
    )
    grad_rows = cotangent.reshape(-1, model_width).astype(jnp.float32)
    _, norm_two_back = jax.vjp(layer_norm, second_sum, norm_gtwo, norm_stwo)
    grad_second, grad_gtwo, grad_stwo = norm_two_back(grad_rows)
    grad_branch = grad_second.astype(jnp.bfloat16)
    grad_wdown = outer_sum(act_low, grad_branch)
    grad_bdown = column_sum(grad_branch)
    grad_act = project_back(grad_branch, mat_down)
    _, gelu_back = jax.vjp(partial(jax.nn.gelu, approximate=False), inner)
    grad_inner = gelu_back(grad_act)[0].astype(jnp.bfloat16)
    grad_win = outer_sum(normed_low, grad_inner)
    grad_bin = column_sum(grad_inner)
    grad_normed = grad_second + project_back(grad_inner, mat_in)
    _, norm_one_back = jax.vjp(layer_norm, first_sum, norm_gone, norm_sone)
    grad_first, grad_gone, grad_sone = norm_one_back(grad_normed)
    grad_attn = grad_first.astype(jnp.bfloat16)
    grad_wout = outer_sum(context_flat, grad_attn)
    grad_bout = column_sum(grad_attn)
    grad_context = project_back(grad_attn, mat_out).astype(jnp.bfloat16).reshape(split_shape)
    grad_query, grad_key, grad_value = lax.map(
        attend_back,
        (query_heads, key_heads, value_heads, grad_context, segments, lengths, log_totals),
    )
    grad_query = grad_query.reshape(-1, model_width)
    grad_key = grad_key.reshape(-1, model_width)
    grad_value = grad_value.reshape(-1, model_width)
    grad_proj = jnp.concatenate([grad_query, grad_key, grad_value], axis=1)
    grad_wqkv = outer_sum(flat_in, grad_proj)
    grad_bqv = jnp.concatenate([column_sum(grad_query), column_sum(grad_value)], axis=0)
    grad_input = grad_first + project_back(grad_proj, mat_qkv)
    shares = (
        lax.psum_scatter(
            grad_wqkv.astype(jnp.bfloat16), "shard", scatter_dimension=0, tiled=True
        ).astype(jnp.float32),
        lax.psum_scatter(
            grad_bqv.astype(jnp.bfloat16), "shard", scatter_dimension=0, tiled=True
        ).astype(jnp.float32),
        lax.psum_scatter(
            grad_wout.astype(jnp.bfloat16), "shard", scatter_dimension=0, tiled=True
        ).astype(jnp.float32),
        lax.psum_scatter(
            grad_bout.astype(jnp.bfloat16), "shard", scatter_dimension=0, tiled=True
        ).astype(jnp.float32),
        lax.psum_scatter(
            grad_gone.astype(jnp.bfloat16), "shard", scatter_dimension=0, tiled=True
        ).astype(jnp.float32),
        lax.psum_scatter(
            grad_sone.astype(jnp.bfloat16), "shard", scatter_dimension=0, tiled=True
        ).astype(jnp.float32),
        lax.psum_scatter(
            grad_win.astype(jnp.bfloat16), "shard", scatter_dimension=0, tiled=True
        ).astype(jnp.float32),
        lax.psum_scatter(
            grad_bin.astype(jnp.bfloat16), "shard", scatter_dimension=0, tiled=True
        ).astype(jnp.float32),
        lax.psum_scatter(
            grad_wdown.astype(jnp.bfloat16), "shard", scatter_dimension=0, tiled=True
        ).astype(jnp.float32),
        lax.psum_scatter(
            grad_bdown.astype(jnp.bfloat16), "shard", scatter_dimension=0, tiled=True
        ).astype(jnp.float32),
        lax.psum_scatter(
            grad_gtwo.astype(jnp.bfloat16), "shard", scatter_dimension=0, tiled=True
        ).astype(jnp.float32),
        lax.psum_scatter(
            grad_stwo.astype(jnp.bfloat16), "shard", scatter_dimension=0, tiled=True
        ).astype(jnp.float32),
    )
    summed = (
        lax.psum(shares[0].astype(jnp.bfloat16), "rep").astype(jnp.float32),
        lax.psum(shares[1].astype(jnp.bfloat16), "rep").astype(jnp.float32),
        lax.psum(shares[2].astype(jnp.bfloat16), "rep").astype(jnp.float32),
        lax.psum(shares[3].astype(jnp.bfloat16), "rep").astype(jnp.float32),
        lax.psum(shares[4].astype(jnp.bfloat16), "rep").astype(jnp.float32),
        lax.psum(shares[5].astype(jnp.bfloat16), "rep").astype(jnp.float32),
        lax.psum(shares[6].astype(jnp.bfloat16), "rep").astype(jnp.float32),
        lax.psum(shares[7].astype(jnp.bfloat16), "rep").astype(jnp.float32),
        lax.psum(shares[8].astype(jnp.bfloat16), "rep").astype(jnp.float32),
        lax.psum(shares[9].astype(jnp.bfloat16), "rep").astype(jnp.float32),
        lax.psum(shares[10].astype(jnp.bfloat16), "rep").astype(jnp.float32),
        lax.psum(shares[11].astype(jnp.bfloat16), "rep").astype(jnp.float32),
    )
    layer_result = output_rows.astype(jnp.bfloat16).reshape(tokens.shape)
    grad_tokens = grad_input.reshape(tokens.shape)
    return (
        layer_result,
        grad_tokens,
        summed[0],
        summed[1],
        summed[2],
        summed[3],
        summed[4],
        summed[5],
        summed[6],
        summed[7],
        summed[8],
        summed[9],
        summed[10],
        summed[11],
    )


def solution(mesh):
    in_specs = (
        P(("rep", "shard"), None, None),
        P(("rep", "shard"), None),
        P(("rep", "shard")),
        P(("rep", "shard"), None, None),
        P("shard", None),
        P("shard"),
        P("shard", None),
        P("shard"),
        P("shard"),
        P("shard"),
        P("shard", None),
        P("shard"),
        P("shard", None),
        P("shard"),
        P("shard"),
        P("shard"),
    )
    out_specs = (
        P(("rep", "shard"), None, None),
        P(("rep", "shard"), None, None),
        P("shard", None),
        P("shard"),
        P("shard", None),
        P("shard"),
        P("shard"),
        P("shard"),
        P("shard", None),
        P("shard"),
        P("shard", None),
        P("shard"),
        P("shard"),
        P("shard"),
    )
    return jax.shard_map(local, mesh=mesh, in_specs=in_specs, out_specs=out_specs, check_vma=False)
```

profile of v0, /device:TPU:9, one launch (start us, length us, event | category | flops | bytes accessed | tf_op | source)
XLA Modules:
  0.0 1106.1 jit_solution(8435936859858021904)
XLA Ops:
  10.9 6.2 all-gather.6
  17.2 9.4 all-gather.5
  26.5 6.1 all-gather.4
  32.6 10.6 all-gather.3
  49.2 11.1 %all-gather.1 = bf16[4,1,256]{2,1,0:T(2,128)(2,1)S(1)} all-gather(bf16[1,1,256]{2,1,0:T(2,128)(2,1)S(1)} %reshape.227), channel_id=1, replica_groups=mesh['rep'=8,'shard'=4] {'shard'}, dimensions={0}, use_global_device_ids=true | all-gather | bytes 2560 | tf_op jit(solution)/shard_map/all_gather | solution.py:122
  60.3 9.9 all-gather
  70.3 14.7 %all_gather.47 = bf16[4096]{0:T(1024)(128)(2,1)S(1)} all-gather(bf16[1024]{0:T(1024)(128)(2,1)S(1)} %copy-done.35), channel_id=1, replica_groups=mesh['rep'=8,'shard'=4] {'shard'}, dimensions={0}, use_global_device_ids=true | all-gather | bytes 10240 | tf_op jit(solution)/shard_map/all_gather | solution.py:126
  85.3 38.7 %all-gather.12.cloned.1.call-done = bf16[1024,3072]{1,0:T(8,128)(2,1)} async-done(((bf16[256,3072]{1,0:T(8,128)(2,1)}), bf16[1024,3072]{1,0:T(8,128)(2,1)}) %all-gather.12.cloned.1.call-update) | async-done | bytes 6291472 | tf_op jit(solution)/shard_map/all_gather | solution.py:119
  134.2 7.4 fusion.41
  141.7 8.4 fusion
  150.1 8.6 fusion.19
  158.6 12.1 %all-gather.14.cloned.1.call-done = bf16[1024,1024]{1,0:T(8,128)(2,1)} async-done(((bf16[256,1024]{1,0:T(8,128)(2,1)}), bf16[1024,1024]{1,0:T(8,128)(2,1)}) %all-gather.14.cloned.1.call-update) | async-done | bytes 2097168 | tf_op jit(solution)/shard_map/all_gather | solution.py:121
  175.6 144.1 %all-gather.16.cloned.1.call-done = bf16[1024,4096]{1,0:T(8,128)(2,1)} async-done(((bf16[256,4096]{1,0:T(8,128)(2,1)}), bf16[1024,4096]{1,0:T(8,128)(2,1)}) %all-gather.16.cloned.1.call-update) | async-done | bytes 8388624 | tf_op jit(solution)/shard_map/all_gather | solution.py:125
  319.7 28.0 %multiply_convert_fusion.1 = (bf16[512,4096]{1,0:T(8,128)(2,1)}, f32[512,4096]{1,0:T(8,128)}, f32[512,4096]{1,0:T(8,128)}) fusion(f32[4096]{0:T(1024)S(1)} %convert_element_type.212, bf16[1024,4096]{1,0:T(8,128)(2,1)} %all-gather.16.cloned.1.call-done, f32[512,1024]{1,0:T(8,128)S(1)} %get-tuple-element.158, f32[1024]{0:T(1024)S(1)} %bitcast.106, ...), kind=kOutput, calls=%fused_computation.13 | convolution fusion | flops 4436000768 | bytes 31485952 | tf_op jit(solution)/shard_map/dot_general | solution.py:19
  347.7 121.4 %all-gather.18.cloned.1.call-done = bf16[4096,1024]{1,0:T(8,128)(2,1)} async-done(((bf16[1024,1024]{1,0:T(8,128)(2,1)}), bf16[4096,1024]{1,0:T(8,128)(2,1)}) %all-gather.18.cloned.1.call-update) | async-done | bytes 8388624 | tf_op jit(solution)/shard_map/all_gather | solution.py:127
  469.0 8.5 fusion.43
  481.5 14.3 %fusion.35 = (bf16[4096]{0:T(1024)(128)(2,1)}, bf16[512,4096]{1,0:T(8,128)(2,1)S(1)}) fusion(f32[512,4096]{1,0:T(8,128)} %get-tuple-element.149, f32[512,4096]{1,0:T(8,128)} %get-tuple-element.159, f32[4096]{0:T(1024)S(1)} %convert_element_type.212, bf16[512,1024]{1,0:T(8,128)(2,1)S(1)} %get-tuple-element.139, ...), kind=kOutput, calls=%fused_computation.88 | convolution fusion | flops 4328517632 | bytes 30433280 | tf_op jit(solution)/shard_map/dot_general | solution.py:23
  495.8 9.7 multiply_reduce_fusion.1
  514.9 15.0 %multiply_reduce_fusion = (f32[16,512]{1,0:T(8,128)}, f32[16,512,512]{1,2,0:T(8,128)}) fusion(f32[16,512,512]{1,2,0:T(8,128)} %get-tuple-element.156, f32[16,512]{1,0:T(8,128)} %log_add_fusion, bf16[512,16,64]{0,2,1:T(8,128)(2,1)S(1)} %bitcast.82, bf16[512,16,64]{0,2,1:T(8,128)(2,1)} %bitcast.85), kind=kOutput, calls=%fused_computation.1 | convolution fusion | flops 549445632 | bytes 35717120 | tf_op jit(solution)/shard_map/while/body/eval_jaxpr/qhd,khd->hqk/dot_general | solution.py:73
  532.0 10.7 multiply_convert_fusion
  542.7 6.2 multiply_convert_fusion.2
  550.6 9.1 bitcast_reduce_fusion
  560.7 9.1 convert_bitcast_fusion
  571.4 9.4 convolution_convert_fusion.1
  582.1 9.0 convolution_convert_fusion
  591.2 90.9 %reduce-scatter.5.cloned.1.call-done = bf16[256,3072]{0,1:T(8,128)(2,1)} async-done(((bf16[1024,3072]{0,1:T(8,128)(2,1)}), bf16[256,3072]{0,1:T(8,128)(2,1)}) %reduce-scatter.5.cloned.1.call-update) | async-done | bytes 1572880 | tf_op jit(solution)/shard_map/reduce_scatter | solution.py:213
  682.1 147.2 %reduce-scatter.9.cloned.1.call-done = bf16[256,4096]{1,0:T(8,128)(2,1)} async-done(((bf16[1024,4096]{1,0:T(8,128)(2,1)}), bf16[256,4096]{1,0:T(8,128)(2,1)}) %reduce-scatter.9.cloned.1.call-update) | async-done | bytes 2097168 | tf_op jit(solution)/shard_map/reduce_scatter | solution.py:231
  829.3 147.7 %reduce-scatter.11.cloned.1.call-done = bf16[1024,1024]{1,0:T(8,128)(2,1)} async-done(((bf16[4096,1024]{1,0:T(8,128)(2,1)}), bf16[1024,1024]{1,0:T(8,128)(2,1)}) %reduce-scatter.11.cloned.1.call-update) | async-done | bytes 2097168 | tf_op jit(solution)/shard_map/reduce_scatter | solution.py:237
  980.0 12.4 %all-reduce.10 = (bf16[2048]{0:T(1024)(128)(2,1)S(1)}, bf16[1024]{0:T(1024)(128)(2,1)S(1)}, bf16[1024]{0:T(1024)(128)(2,1)S(1)}, bf16[1024]{0:T(1024)(128)(2,1)S...) all-reduce(bf16[2048]{0:T(1024)(128)(2,1)S(1)} %pad_maximum_fusion., ...), channel_id=3, replica_groups=mesh['rep'=8,'shard'=4] {'shard'}, use_global_device_ids=true, to_apply=%region_15.16.clone | all-reduce | flops 12288 | bytes 49152
  992.9 16.1 %all-reduce.8 = (bf16[512]{0:T(512)(128)(2,1)S(1)}, bf16[256]{0:T(256)(128)(2,1)S(1)}, bf16[256]{0:T(256)(128)(2,1)S(1)}, bf16[256]{0:T(256)(128)(2,1)S(1)}, bf1...) all-reduce(bf16[512]{0:T(512)(128)(2,1)S(1)} %dynamic-slice.2, ...), channel_id=1, replica_groups=mesh['rep'=8,'shard'=4] {'rep'}, use_global_device_ids=true, to_apply=%region_16.17 | all-reduce | flops 3072 | bytes 12288 | tf_op jit(solution)/shard_map/psum | solution.py:252
  1013.5 8.8 add_bitcast_fusion
  1022.4 64.8 %all-reduce.13.cloned.1.call-done = (bf16[256,3072]{0,1:T(8,128)(2,1)}, bf16[256,1024]{1,0:T(8,128)(2,1)}, bf16[256,4096]{1,0:T(8,128)(2,1)}, bf16[1024,1024]{1,0:T(8,128)(2,1)}) async-done(((bf16[256,3072]{0,1:T(8,128)(2,1)}, bf16[256,1024]{1,0:T(8,128)(2,1)}, bf16[256,4096]{1,0:T(8,128)(2,1)}, bf16[1024,1024]{1,0:T(8,128)(2,1)}), (bf16[256,3072]{0,1:T(8,128)(2,1)}, bf16[256,1024]{1,0:T(8,128)(2,1)}, ...) | async-done | bytes 6291472 | tf_op jit(solution)/shard_map/psum | solution.py:251
  (192 shorter events, 63.0 us)
Async XLA Ops:
  7.3 63.0 %copy-start.35 = (bf16[1024]{0:T(1024)(128)(2,1)S(1)}, bf16[1024]{0:T(1024)(128)(2,1)}, u32[]{:S(2)}) copy-start(bf16[1024]{0:T(1024)(128)(2,1)} %param.27) | copy-start | bytes 6148
  7.3 77.7 %copy-start.25 = (s32[1,512]{1,0:T(1,128)S(1)}, s32[1,512]{1,0:T(1,128)}, u32[]{:S(2)}) copy-start(s32[1,512]{1,0:T(1,128)} %param.17) | copy-start | bytes 6148
  7.3 116.7 %copy-start.20 = (bf16[1,512,1024]{2,1,0:T(8,128)(2,1)S(1)}, bf16[1,512,1024]{2,1,0:T(8,128)(2,1)}, u32[]{:S(2)}) copy-start(bf16[1,512,1024]{2,1,0:T(8,128)(2,1)} %param.16) | copy-start | bytes 3145732
  7.3 116.7 %all-gather.12.cloned.1.call-start = ((), (), s32[]{:S(2)}) async-start(), calls=%async_computation.4 | async-start | bytes 7864320 | tf_op jit(solution)/shard_map/all_gather | solution.py:119
  8.0 162.7 %all-gather.14.cloned.1.call-start = ((), (), s32[]{:S(2)}) async-start(), calls=%async_computation.5 | async-start | bytes 2621440 | tf_op jit(solution)/shard_map/all_gather | solution.py:121
  8.8 310.9 %all-gather.16.cloned.1.call-start = ((), (), s32[]{:S(2)}) async-start(), calls=%async_computation.6 | async-start | bytes 10485760 | tf_op jit(solution)/shard_map/all_gather | solution.py:125
  9.5 459.5 %all-gather.18.cloned.1.call-start = ((), (), s32[]{:S(2)}) async-start(), calls=%async_computation.7 | async-start | bytes 10485760 | tf_op jit(solution)/shard_map/all_gather | solution.py:127
  10.1 581.1 %reduce-scatter.7.cloned.1.call-start = ((), (), s32[]{:S(2)}) async-start(), calls=%async_computation.9 | async-start | bytes 2621440 | tf_op jit(solution)/shard_map/reduce_scatter | solution.py:219
  43.3 425.7 %copy-start.33 = (f32[4,1,256]{2,1,0:T(1,128)}, f32[4,1,256]{2,1,0:T(1,128)S(1)}, u32[]{:S(2)}) copy-start(f32[4,1,256]{2,1,0:T(1,128)S(1)} %convert_element_type.258) | copy-start | bytes 12292
  134.2 24.4 %copy-start.13 = (bf16[512,1024]{0,1:T(8,128)(2,1)}, bf16[512,1024]{0,1:T(8,128)(2,1)S(1)}, u32[]{:S(2)}) copy-start(bf16[512,1024]{0,1:T(8,128)(2,1)S(1)} %copy.52) | copy-start | bytes 3145732
  174.2 331.3 %copy-start.1 = (f32[512,1024]{1,0:T(8,128)}, f32[512,1024]{1,0:T(8,128)S(1)}, u32[]{:S(2)}) copy-start(f32[512,1024]{1,0:T(8,128)S(1)} %get-tuple-element.158) | copy-start | bytes 6291460
  174.6 330.9 %copy-start.30 = (f32[512]{0:T(512)}, f32[512]{0:T(512)S(1)}, u32[]{:S(2)}) copy-start(f32[512]{0:T(512)S(1)} %fusion.27) | copy-start | bytes 6148
  481.5 14.3 %copy-start.18 = (bf16[512,1024]{1,0:T(8,128)(2,1)}, bf16[512,1024]{1,0:T(8,128)(2,1)S(1)}, u32[]{:S(2)}) copy-start(bf16[512,1024]{1,0:T(8,128)(2,1)S(1)} %get-tuple-element.139) | copy-start | bytes 3145732
  514.7 15.1 %copy-start.9 = (bf16[512,1024]{0,1:T(8,128)(2,1)}, bf16[512,1024]{0,1:T(8,128)(2,1)S(1)}, u32[]{:S(2)}) copy-start(bf16[512,1024]{0,1:T(8,128)(2,1)S(1)} %copy.56) | copy-start | bytes 3145732
  514.8 167.3 %reduce-scatter.5.cloned.1.call-start = ((), (), s32[]{:S(2)}) async-start(), calls=%async_computation.8 | async-start | bytes 7864320 | tf_op jit(solution)/shard_map/reduce_scatter | solution.py:213
  514.8 15.0 %slice-start = ((s8[16777216]{0:T(1024)(128)(4,1)}), s8[4194304]{0:T(1024)(128)(4,1)S(1)}, s32[]{:S(2)}) async-start(s8[16777216]{0:T(1024)(128)(4,1)} %bitcast.76), calls=%async_computation.13 | async-start | bytes 8388608
  514.8 15.0 %slice-start.1 = ((s8[16777216]{0:T(1024)(128)(4,1)}), s8[4194304]{0:T(1024)(128)(4,1)S(1)}, s32[]{:S(2)}) async-start(s8[16777216]{0:T(1024)(128)(4,1)} %bitcast.76), calls=%async_computation.14 | async-start | bytes 8388608
  514.8 15.9 %slice-start.2 = ((s8[16777216]{0:T(1024)(128)(4,1)}), s8[4194304]{0:T(1024)(128)(4,1)S(1)}, s32[]{:S(2)}) async-start(s8[16777216]{0:T(1024)(128)(4,1)} %bitcast.76), calls=%async_computation.15 | async-start | bytes 8388608
  514.9 17.1 %slice-start.3 = ((s8[16777216]{0:T(1024)(128)(4,1)}), s8[4194304]{0:T(1024)(128)(4,1)S(1)}, s32[]{:S(2)}) async-start(s8[16777216]{0:T(1024)(128)(4,1)} %bitcast.76), calls=%async_computation.16 | async-start | bytes 8388608
  549.0 10.7 copy-start.17
  569.8 259.4 %reduce-scatter.9.cloned.1.call-start = ((), (), s32[]{:S(2)}) async-start(), calls=%async_computation.10 | async-start | bytes 10485760 | tf_op jit(solution)/shard_map/reduce_scatter | solution.py:231
  580.9 396.1 %reduce-scatter.11.cloned.1.call-start = ((), (), s32[]{:S(2)}) async-start(), calls=%async_computation.11 | async-start | bytes 10485760 | tf_op jit(solution)/shard_map/reduce_scatter | solution.py:237
  591.1 385.9 %copy-start.45 = (u32[32]{0:T(128)S(1)}, u32[32]{0:T(128)}, u32[]{:S(2)}) copy-start(u32[32]{0:T(128)} %constant.139) | copy-start | bytes 388
  591.1 388.5 %copy-start.8 = (bf16[1,512,1024]{2,1,0:T(8,128)(2,1)S(1)}, bf16[1,512,1024]{2,1,0:T(8,128)(2,1)}, u32[]{:S(2)}) copy-start(bf16[1,512,1024]{2,1,0:T(8,128)(2,1)} %param.19) | copy-start | bytes 3145732
  591.1 388.9 %copy-start.26 = (bf16[1024]{0:T(1024)(128)(2,1)S(1)}, bf16[1024]{0:T(1024)(128)(2,1)}, u32[]{:S(2)}) copy-start(bf16[1024]{0:T(1024)(128)(2,1)} %get-tuple-element.138) | copy-start | bytes 6148
  591.1 388.9 %copy-start.27 = (bf16[1024]{0:T(1024)(128)(2,1)S(1)}, bf16[1024]{0:T(1024)(128)(2,1)}, u32[]{:S(2)}) copy-start(bf16[1024]{0:T(1024)(128)(2,1)} %get-tuple-element.142) | copy-start | bytes 6148
  591.1 388.9 %copy-start.32 = (bf16[4096]{0:T(1024)(128)(2,1)S(1)}, bf16[4096]{0:T(1024)(128)(2,1)}, u32[]{:S(2)}) copy-start(bf16[4096]{0:T(1024)(128)(2,1)} %get-tuple-element.140) | copy-start | bytes 24580
  591.1 388.9 %copy-start.36 = (bf16[1024]{0:T(1024)(128)(2,1)S(1)}, bf16[1024]{0:T(1024)(128)(2,1)}, u32[]{:S(2)}) copy-start(bf16[1024]{0:T(1024)(128)(2,1)} %get-tuple-element.113) | copy-start | bytes 6148
  591.1 388.9 %copy-start.37 = (bf16[1024]{0:T(1024)(128)(2,1)S(1)}, bf16[1024]{0:T(1024)(128)(2,1)}, u32[]{:S(2)}) copy-start(bf16[1024]{0:T(1024)(128)(2,1)} %get-tuple-element.117) | copy-start | bytes 6148
  591.1 422.4 %copy-start.12 = (f32[512,1024]{1,0:T(8,128)S(1)}, f32[512,1024]{1,0:T(8,128)}, u32[]{:S(2)}) copy-start(f32[512,1024]{1,0:T(8,128)} %copy-done.11) | copy-start | bytes 6291460
  591.1 422.4 %copy-start.29 = (f32[512]{0:T(512)S(1)}, f32[512]{0:T(512)}, u32[]{:S(2)}) copy-start(f32[512]{0:T(512)} %copy-done.28) | copy-start | bytes 6148
  591.1 496.0 %all-reduce.13.cloned.1.call-start = ((), (), s32[]{:S(2)}) async-start(), calls=%async_computation.12 | async-start | bytes 12582912 | tf_op jit(solution)/shard_map/psum | solution.py:251
  (28 other events, 139.1 us)
Sparse Core Ops, SparseCore 0:
  9.7 114.2 all-gather.11
  125.5 45.0 all-gather.13
  172.3 147.3 all-gather.15
  321.1 147.8 all-gather.17
  514.9 42.5 reduce-scatter.6
  570.0 112.0 reduce-scatter.4
  684.5 144.6 reduce-scatter.8
  831.7 145.1 reduce-scatter.10
  981.0 106.1 all-reduce.12
where the time goes:
time: 1120 us; the launch traced here: 1110 us
  waiting for transfers between devices  769 us (69%)
  matrix products  158 us (14%)
  blocking collectives  102 us (9%)
  other arithmetic  41.4 us (4%)
  between operations  17.5 us (2%)
  local copies, waits for them, and re-layouts  16.3 us (1%)
    reduce_scatter x1, waiting for transfers between devices, local(): lax.psum_scatter(grad_wdown.astype(jnp.bfloat16), 'shard', scatter_dimens...  148 us
    reduce_scatter x1, waiting for transfers between devices, local(): lax.psum_scatter(grad_win.astype(jnp.bfloat16), 'shard', scatter_dimensio...  147 us
    all_gather x1, waiting for transfers between devices, local(): lax.all_gather(w_in, 'shard', axis=0, tiled=True)  144 us
    all_gather x1, waiting for transfers between devices, local(): lax.all_gather(w_down, 'shard', axis=0, tiled=True)  121 us
    reduce_scatter x1, waiting for transfers between devices, local(): lax.psum_scatter(grad_wqkv.astype(jnp.bfloat16), 'shard', scatter_dimensi...  90.9 us
    psum x1, waiting for transfers between devices, local(): lax.psum(shares[0].astype(jnp.bfloat16), 'rep').astype(jnp.float32)  64.8 us
    dot_general x4, matrix products, matmul(): return jnp.dot(left, right, preferred_element_type=jnp.float32)  45.5 us
    all_gather x1, waiting for transfers between devices, local(): lax.all_gather(w_qkv, 'shard', axis=0, tiled=True)  38.7 us
  transfers between devices with their start and end apart: 9, of which 8 were waited for; matrix products, arithmetic and copies ran while one was open for 14% of the time, Pallas kernels for 0%

commit v1 on v0

v1 whole, which is shorter than its diff:
```python
from functools import partial

import jax
import jax.numpy as jnp
from jax import lax
from jax.sharding import Mesh
from jax.sharding import PartitionSpec as P

HEAD_DIM = 64
REP = ("chip", "core")
ALL = ("chip", "core", "shard")


def layer_norm(hidden, norm_gain, norm_shift):
    average = jnp.mean(hidden, axis=-1, keepdims=True)
    centred = hidden - average
    variance = jnp.mean(centred * centred, axis=-1, keepdims=True)
    return centred * lax.rsqrt(variance + 1e-06) * norm_gain + norm_shift


def matmul(left, right):
    return jnp.dot(left, right, preferred_element_type=jnp.float32)


def project_back(left, right):
    return lax.dot_general(
        left, right, (((1,), (1,)), ((), ())), preferred_element_type=jnp.float32
    )


def outer_sum(left, right):
    return lax.dot_general(
        left, right, (((0,), (0,)), ((), ())), preferred_element_type=jnp.float32
    )


def column_sum(values):
    return jnp.sum(values.astype(jnp.float32), axis=0)


def allowed_pairs(doc_ids, length):
    positions = jnp.arange(doc_ids.shape[0])
    is_valid = positions < length
    return (doc_ids[:, None] == doc_ids[None, :]) & (is_valid[:, None] == is_valid[None, :])


def attend(query_heads, key_heads, value_heads, allowed):
    scale = HEAD_DIM ** (-0.5)
    scores = (
        jnp.einsum("qhd,khd->hqk", query_heads, key_heads, preferred_element_type=jnp.float32)
        * scale
    )
    scores = jnp.where(allowed[None], scores, -1e30)
    maxima = jnp.max(scores, axis=2, keepdims=True)
    expo = jnp.exp(scores - maxima)
    totals = jnp.sum(expo, axis=2, keepdims=True)
    attn_probs = (expo / totals).astype(jnp.bfloat16)
    context = jnp.einsum(
        "hqk,khd->qhd", attn_probs, value_heads, preferred_element_type=jnp.float32
    )
    return (context.astype(jnp.bfloat16), maxima + jnp.log(totals))


def attend_back(query_heads, key_heads, value_heads, grad_context, allowed, log_totals):
    scale = HEAD_DIM ** (-0.5)
    scores = (
        jnp.einsum("qhd,khd->hqk", query_heads, key_heads, preferred_element_type=jnp.float32)
        * scale
    )
    scores = jnp.where(allowed[None], scores, -1e30)
    attn_probs = jnp.exp(scores - log_totals)
    grad_probs = jnp.einsum(
        "qhd,khd->hqk", grad_context, value_heads, preferred_element_type=jnp.float32
    )
    grad_scores = attn_probs * (
        grad_probs - jnp.sum(attn_probs * grad_probs, axis=2, keepdims=True)
    )
    grad_low = grad_scores.astype(jnp.bfloat16)
    grad_query = (
        jnp.einsum("hqk,khd->qhd", grad_low, key_heads, preferred_element_type=jnp.float32) * scale
    )
    grad_key = (
        jnp.einsum("hqk,qhd->khd", grad_low, query_heads, preferred_element_type=jnp.float32)
        * scale
    )
    grad_value = jnp.einsum(
        "hqk,qhd->khd",
        attn_probs.astype(jnp.bfloat16),
        grad_context,
        preferred_element_type=jnp.float32,
    )
    return (
        grad_query.astype(jnp.bfloat16),
        grad_key.astype(jnp.bfloat16),
        grad_value.astype(jnp.bfloat16),
    )


def local(
    chips,
    group,
    tokens,
    segments,
    lengths,
    cotangent,
    w_qkv,
    b_qv,
    w_out,
    b_out,
    gain_one,
    shift_one,
    w_in,
    b_in,
    w_down,
    b_down,
    gain_two,
    shift_two,
):
    reps = 2 * chips
    core = lax.axis_index("core")
    rank = lax.axis_index("chip") * 2 + core
    own = lax.axis_index("shard")
    _, seq_len, model_width = tokens.shape
    num_heads = model_width // HEAD_DIM
    split_shape = (seq_len, num_heads, HEAD_DIM)
    ff_rows = w_down.shape[0]
    ff_width = w_in.shape[1]
    qkv_width = w_qkv.shape[1]

    def from_shard(value, step):
        return lax.ppermute(value, "shard", [(i, (i - step) % group) for i in range(group)])

    def to_shard(value, step):
        return lax.ppermute(value, "shard", [(i, (i + step) % group) for i in range(group)])

    def sibling(value):
        return lax.ppermute(value, "core", [(0, 1), (1, 0)])

    def roll_left(value, width):
        twice = jnp.concatenate([value, value], axis=1)
        return lax.dynamic_slice_in_dim(twice, own * width, value.shape[1], axis=1)

    def roll_right(value, width):
        twice = jnp.concatenate([value, value], axis=1)
        start = ((group - own) % group) * width
        return lax.dynamic_slice_in_dim(twice, start, value.shape[1], axis=1)

    vectors = (b_qv, b_out, gain_one, shift_one, b_in, b_down, gain_two, shift_two)
    sizes = [v.shape[0] for v in vectors]
    w_one = jnp.concatenate([w_qkv, w_out], axis=1)
    part = w_one.shape[1] // reps
    rows = w_one.shape[0]
    packed = jnp.concatenate(vectors)
    extra = -(-packed.shape[0] // (16 * part)) * 16
    packed = jnp.pad(packed, (0, extra * part - packed.shape[0])).reshape(extra, part)
    piece_one = jnp.concatenate(
        [lax.dynamic_slice_in_dim(w_one, rank * part, part, axis=1), packed], axis=0
    )
    part_in = ff_width // reps
    piece_in = lax.dynamic_slice_in_dim(w_in, rank * part_in, part_in, axis=1)
    part_down = ff_rows // reps
    piece_down = lax.dynamic_slice_in_dim(w_down, rank * part_down, part_down, axis=0)

    got_one = [from_shard(piece_one, s) for s in range(1, group)]
    got_in = [from_shard(piece_in, s) for s in range(1, group)]
    got_down = [from_shard(piece_down, s) for s in range(1, group)]
    rest_one = lax.all_gather(
        jnp.concatenate([g[:rows] for g in got_one], axis=0), REP, axis=1, tiled=True
    )
    rest_in = lax.all_gather(jnp.concatenate(got_in, axis=0), REP, axis=1, tiled=True)
    rest_down = lax.all_gather(jnp.stack(got_down), REP, axis=1, tiled=True)
    rest_down = rest_down.reshape(-1, model_width)

    relative = jnp.stack([packed.reshape(-1)] + [g[rows:].reshape(-1) for g in got_one])
    natural = jnp.concatenate([relative, relative], axis=0)
    natural = lax.dynamic_slice_in_dim(natural, (group - own) % group, group, axis=0)
    full, start = [], 0
    for size in sizes:
        full.append(natural[:, start : start + size].reshape(-1).astype(jnp.float32))
        start += size
    bias_qv, bias_out, norm_gone, norm_sone, bias_in, bias_down, norm_gtwo, norm_stwo = full

    own_qkv, own_out = w_qkv, w_out
    rest_qkv, rest_out = rest_one[:, :qkv_width], rest_one[:, qkv_width:]

    flat_in = tokens[0]
    in_rel = roll_left(flat_in, rows)
    projected = matmul(in_rel[:, :rows], own_qkv) + matmul(in_rel[:, rows:], rest_qkv)
    queries = (projected[:, :model_width] + bias_qv[:model_width]).astype(jnp.bfloat16)
    key_rows = projected[:, model_width : 2 * model_width].astype(jnp.bfloat16)
    value_rows = (projected[:, 2 * model_width :] + bias_qv[model_width:]).astype(jnp.bfloat16)
    query_heads = queries.reshape(split_shape)
    key_heads = key_rows.reshape(split_shape)
    value_heads = value_rows.reshape(split_shape)
    allowed = allowed_pairs(segments[0], lengths[0])
    context, log_totals = attend(query_heads, key_heads, value_heads, allowed)
    context_rel = roll_left(context.reshape(-1, model_width), rows)
    attn_out = (
        matmul(context_rel[:, :rows], own_out)
        + matmul(context_rel[:, rows:], rest_out)
        + bias_out
    )
    first_sum = flat_in.astype(jnp.float32) + attn_out
    normed_one = layer_norm(first_sum, norm_gone, norm_sone)
    normed_rel = roll_left(normed_one.astype(jnp.bfloat16), rows)
    inner = matmul(normed_rel[:, :rows], w_in) + matmul(normed_rel[:, rows:], rest_in) + bias_in
    activated = jax.nn.gelu(inner, approximate=False)
    act_rel = roll_left(activated.astype(jnp.bfloat16), ff_rows)
    branch = (
        matmul(act_rel[:, :ff_rows], w_down) + matmul(act_rel[:, ff_rows:], rest_down) + bias_down
    )
    second_sum = normed_one + branch
    output_rows = layer_norm(second_sum, norm_gtwo, norm_stwo)

    def half(value, width, which):
        split = value.reshape(seq_len, -1, 2, width)
        return lax.dynamic_index_in_dim(split, which, axis=2, keepdims=False).reshape(seq_len, -1)

    def pair(value, width):
        return half(value, width, core), sibling(half(value, width, 1 - core))

    def both(left, right):
        return outer_sum(left[0], right[0]) + outer_sum(left[1], right[1])

    in_pair = (in_rel, sibling(in_rel))
    context_pair = (context_rel, sibling(context_rel))
    normed_pair = (normed_rel, sibling(normed_rel))
    act_pair = pair(act_rel, part_down)

    def own_sum(parts):
        total = parts[0].astype(jnp.float32)
        for s in range(1, group):
            total = total + to_shard(parts[s], s).astype(jnp.float32)
        return total.astype(jnp.bfloat16)

    def scatter_columns(grad):
        share = lax.psum_scatter(
            grad.astype(jnp.bfloat16), "chip", scatter_dimension=1, tiled=True
        )
        share = own_sum(share.reshape(group, rows, -1))
        return lax.all_gather(share, REP, axis=1, tiled=True).astype(jnp.float32)

    grad_rows = cotangent[0].astype(jnp.float32)
    _, norm_two_back = jax.vjp(layer_norm, second_sum, norm_gtwo, norm_stwo)
    grad_second, grad_gtwo, grad_stwo = norm_two_back(grad_rows)
    grad_branch = grad_second.astype(jnp.bfloat16)
    branch_pair = (grad_branch, sibling(grad_branch))
    grad_bdown = column_sum(grad_branch)
    grad_down = both(act_pair, branch_pair).astype(jnp.bfloat16)
    grad_down = lax.psum_scatter(
        grad_down.reshape(group, chips * part_down, model_width),
        "chip",
        scatter_dimension=1,
        tiled=True,
    )
    grad_wdown = lax.all_gather(own_sum(grad_down), REP, axis=0, tiled=True).astype(jnp.float32)

    grad_act = jnp.concatenate(
        [project_back(grad_branch, w_down), project_back(grad_branch, rest_down)], axis=1
    )
    grad_act = roll_right(grad_act, ff_rows)
    _, gelu_back = jax.vjp(partial(jax.nn.gelu, approximate=False), inner)
    grad_inner = gelu_back(grad_act)[0].astype(jnp.bfloat16)
    grad_win = scatter_columns(both(normed_pair, pair(grad_inner, part_in)))
    grad_bin = column_sum(grad_inner)
    back_in = jnp.concatenate(
        [project_back(grad_inner, w_in), project_back(grad_inner, rest_in)], axis=1
    )
    grad_normed = grad_second + roll_right(back_in, rows)
    _, norm_one_back = jax.vjp(layer_norm, first_sum, norm_gone, norm_sone)
    grad_first, grad_gone, grad_sone = norm_one_back(grad_normed)
    grad_attn = grad_first.astype(jnp.bfloat16)
    half_out = both(context_pair, pair(grad_attn, part))
    grad_bout = column_sum(grad_attn)
    grad_context = jnp.concatenate(
        [project_back(grad_attn, own_out), project_back(grad_attn, rest_out)], axis=1
    ).astype(jnp.bfloat16)
    grad_context = roll_right(grad_context, rows).reshape(split_shape)
    grad_query, grad_key, grad_value = attend_back(
        query_heads, key_heads, value_heads, grad_context, allowed, log_totals
    )
    grad_query = grad_query.reshape(-1, model_width)
    grad_key = grad_key.reshape(-1, model_width)
    grad_value = grad_value.reshape(-1, model_width)
    grad_proj = jnp.concatenate([grad_query, grad_key, grad_value], axis=1)
    half_qkv = both(in_pair, pair(grad_proj, part))
    grad_one = scatter_columns(jnp.concatenate([half_qkv, half_out], axis=1))
    back_proj = jnp.concatenate(
        [project_back(grad_proj, own_qkv), project_back(grad_proj, rest_qkv)], axis=1
    )
    grad_input = grad_first + roll_right(back_proj, rows)

    small = (
        jnp.concatenate([column_sum(grad_query), column_sum(grad_value)]),
        grad_bout,
        grad_gone,
        grad_sone,
        grad_bin,
        grad_bdown,
        grad_gtwo,
        grad_stwo,
    )
    small = jnp.concatenate([v.reshape(group, -1) for v in small], axis=1)
    small = lax.psum(small, ALL)
    small = lax.dynamic_index_in_dim(small, own, axis=0, keepdims=False)
    vecs, start = [], 0
    for size in sizes:
        vecs.append(small[start : start + size])
        start += size

    return (
        output_rows.astype(jnp.bfloat16).reshape(tokens.shape),
        grad_input.reshape(tokens.shape),
        grad_one[:, :qkv_width],
        vecs[0],
        grad_one[:, qkv_width:],
        vecs[1],
        vecs[2],
        vecs[3],
        grad_win,
        vecs[4],
        grad_wdown,
        vecs[5],
        vecs[6],
        vecs[7],
    )


def solution(mesh):
    reps, group = mesh.devices.shape
    fine = Mesh(mesh.devices.reshape(reps // 2, 2, group), ALL)
    rows = P(ALL, None, None)
    matrix = P("shard", None)
    vector = P("shard")
    in_specs = (
        rows,
        P(ALL, None),
        P(ALL),
        rows,
        matrix,
        vector,
        matrix,
        vector,
        vector,
        vector,
        matrix,
        vector,
        matrix,
        vector,
        vector,
        vector,
    )
    out_specs = (
        rows,
        rows,
        matrix,
        vector,
        matrix,
        vector,
        vector,
        vector,
        matrix,
        vector,
        matrix,
        vector,
        vector,
        vector,
    )
    return jax.shard_map(
        partial(local, reps // 2, group),
        mesh=fine,
        in_specs=in_specs,
        out_specs=out_specs,
        check_vma=False,
    )
```

time: 1120 us -> 580 us (0.52)
  waiting for transfers between devices: 769 us -> 173 us
  local copies, waits for them, and re-layouts: 16.3 us -> 89.4 us
  blocking collectives: 102 us -> 39.1 us
  other arithmetic: 41.4 us -> 84.6 us
  starting transfers between devices: 0.36 us -> 24.7 us
    reduce_scatter x4 -> x3, waiting for transfers between devices: 386 us -> 40.4 us  [the longest x1 28.5 us: local(): lax.psum_scatter(grad_down.reshape(group, chips * part_down, model_width)...]
    all_gather x4 -> x6, waiting for transfers between devices: 316 us -> 4.46 us  [the longest x1 4.45 us: local(): lax.all_gather(own_sum(grad_down), REP, axis=0, tiled=True)]
    ppermute x0 -> x26, waiting for transfers between devices: none -> 128 us  [the longest x9 65.7 us: from_shard(): lax.ppermute(value, 'shard', [(i, (i - step) % group) for i in range(grou...]
    all_gather x8 -> x0, blocking collectives: 74 us -> none  [the longest x1 14.7 us: local(): lax.all_gather(b_in, 'shard', axis=0, tiled=True)]
    psum x1 -> x0, waiting for transfers between devices: 64.8 us -> none  [local(): lax.psum(shares[0].astype(jnp.bfloat16), 'rep').astype(jnp.float32)]
    dynamic_slice x0 -> x8, local copies, waits for them, and re-layouts: none -> 27 us  [the longest x4 18.1 us: half(): lax.dynamic_index_in_dim(split, which, axis=2, keepdims=False)]
    ppermute x0 -> x26, starting transfers between devices: none -> 24.2 us  [the longest x9 13.3 us: to_shard(): lax.ppermute(value, 'shard', [(i, (i + step) % group) for i in range(grou...]
    psum x1, blocking collectives: 16.1 us -> 39.1 us  [local(): small = lax.psum(small, ALL)]
  transfers between devices with their start and end apart: 9 -> 35, of which waited for: 8 -> 22; matrix products, arithmetic and copies ran while one was open for 14% -> 35% of each run, Pallas kernels for 0% -> 0%
where the time goes in v1:
time: 580 us; the launch traced here: 574 us
  waiting for transfers between devices  173 us (30%)
  matrix products  147 us (25%)
  local copies, waits for them, and re-layouts  89.4 us (15%)
  other arithmetic  84.6 us (15%)
  blocking collectives  39.1 us (7%)
  starting transfers between devices  24.7 us (4%)
  between operations  15.8 us (3%)
    ppermute x9, waiting for transfers between devices, from_shard(): lax.ppermute(value, 'shard', [(i, (i - step) % group) for i in range(grou...  65.7 us
    ppermute x9, waiting for transfers between devices, to_shard(): lax.ppermute(value, 'shard', [(i, (i + step) % group) for i in range(grou...  59.9 us
    dot_general x8, matrix products, matmul(): return jnp.dot(left, right, preferred_element_type=jnp.float32)  51.8 us
    psum x1, blocking collectives, local(): small = lax.psum(small, ALL)  39.1 us
    unnamed x118, local copies, waits for them, and re-layouts  34.4 us
    reduce_scatter x1, waiting for transfers between devices, local(): lax.psum_scatter(grad_down.reshape(group, chips * part_down, model_width)...  28.5 us
    dot_general x8, matrix products, outer_sum(): lax.dot_general(left, right, (((0,), (0,)), ((), ())), preferred_element_...  28.1 us
    dot_general x8, matrix products, project_back(): lax.dot_general(left, right, (((1,), (1,)), ((), ())), preferred_element_...  25.8 us
  transfers between devices with their start and end apart: 35, of which 22 were waited for; matrix products, arithmetic and copies ran while one was open for 35% of the time, Pallas kernels for 0%

profile of v1, /device:TPU:9, one launch (start us, length us, event | category | flops | bytes accessed | tf_op | source)
XLA Modules:
  0.0 573.8 jit_solution(13355373292585005239)
XLA Ops:
  22.9 17.0 %collective-permute-done.1 = bf16[272,512]{1,0:T(8,128)(2,1)S(1)} collective-permute-done((bf16[272,512]{1,0:T(8,128)(2,1)S(1)}, bf16[272,512]{1,0:T(8,128)(2,1)S(1)}, u32[]{:S(2)}, u32[]{:S(2)}) %collective-permute-start.1) | collective-permute-done | bytes 278560 | tf_op jit(solution)/shard_map/ppermute | solution.py:131
  46.9 5.0 collective-permute-done.5
  51.9 15.0 %collective-permute-done.4 = bf16[256,512]{1,0:T(8,128)(2,1)S(1)} collective-permute-done((bf16[256,512]{1,0:T(8,128)(2,1)S(1)}, bf16[256,512]{1,0:T(8,128)(2,1)S(1)}, u32[]{:S(2)}, u32[]{:S(2)}) %collective-permute-start.4) | collective-permute-done | bytes 262176 | tf_op jit(solution)/shard_map/ppermute | solution.py:131
  79.6 15.0 %collective-permute-done.7 = bf16[128,1024]{1,0:T(8,128)(2,1)} collective-permute-done((bf16[128,1024]{1,0:T(8,128)(2,1)}, bf16[128,1024]{1,0:T(8,128)(2,1)}, u32[]{:S(2)}, u32[]{:S(2)}) %collective-permute-start.7) | collective-permute-done | bytes 262176 | tf_op jit(solution)/shard_map/ppermute | solution.py:131
  103.1 4.9 fusion.18
  117.8 8.9 %fusion.82 = (f32[16,512]{1,0:T(8,128)S(1)}, f32[16,512,512]{1,2,0:T(8,128)}) fusion(bf16[512,16,64]{0,2,1:T(8,128)(2,1)} %bitcast.174, bf16[512,16,64]{0,2,1:T(8,128)(2,1)S(1)} %bitcast.172, pred[512,512]{0,1:T(8,128)(4,1)S(1)} %compare_and_fusion), kind=kOutput, calls=%fused_computation.211 | convolution fusion | flops 549445632 | bytes 19169280 | tf_op jit(solution)/shard_map/qhd,khd->hqk/dot_general | solution.py:50
  126.7 8.5 %fusion = f32[16,512]{1,0:T(8,128)S(1)} fusion(f32[16,512,512]{1,2,0:T(8,128)} %get-tuple-element.65, f32[16,512]{1,0:T(8,128)S(1)} %get-tuple-element.64), kind=kLoop, calls=%fused_computation.10 | loop fusion | flops 8380416 | bytes 16842752 | tf_op jit(solution)/shard_map/reduce_sum | solution.py:56
  135.2 8.1 %fusion.42 = bf16[16,64,512]{2,1,0:T(8,128)(2,1)S(1)} fusion(bf16[512,16,64]{0,2,1:T(8,128)(2,1)S(1)} %bitcast.184, f32[16,512,512]{1,2,0:T(8,128)} %get-tuple-element.65, f32[16,512]{1,0:T(8,128)S(1)} %fusion, f32[16,512]{1,0:T(8,128)S(1)} %get-tuple-element.64), kind=kOutput, calls=%fused_computation.115 | convolution fusion | flops 549978112 | bytes 18939904 | tf_op jit(solution)/shard_map/hqk,khd->qhd/dot_general | solution.py:58
  157.5 24.7 %multiply_convert_fusion.1 = (bf16[512,4096]{1,0:T(8,128)(2,1)S(1)}, f32[512,4096]{1,0:T(8,128)}) fusion(f32[4096]{0:T(1024)S(1)} %bitcast.218, f32[512,4096]{1,0:T(8,128)} %fusion.67, bf16[768,4096]{1,0:T(8,128)(2,1)} %all-gather.9.cloned.1.call-done, bf16[512,1024]{1,0:T(8,128)(2,1)S(1)} %fusion.54), kind=kOutput, calls=%fused_computation.25 | convolution fusion | flops 3361734656 | bytes 28065792 | tf_op jit(solution)/shard_map/dot_general | solution.py:22
  189.5 8.7 %fusion.84 = (f32[512]{0:T(512)S(1)}, f32[512,1024]{1,0:T(8,128)S(1)}) fusion(f32[1024]{0:T(1024)S(1)} %bitcast.220, f32[512,1024]{1,0:T(8,128)} %fusion.57, bf16[3072,1024]{1,0:T(8,128)(2,1)} %bitcast.229, bf16[512,4096]{1,0:T(8,128)(2,1)} %copy-done.6, f32[1024]{0:T(1024)S(1)} %bitcast.214, f32[1024]{0:T(1024)S(1)} %bitcast.207, f32[512]{0:T(512)S(1)} %fusion.72, ...), kind=kOutput, calls=%fused_computation.213 | convolution fusion | flops 3225419264 | bytes 15747072 | tf_op jit(solution)/shard_map/dot_general | solution.py:22
  201.7 6.1 %fusion.86 = f32[512,3072]{1,0:T(8,128)S(1)} fusion(bf16[512,1024]{1,0:T(8,128)(2,1)S(1)} %get-tuple-element.20, bf16[3072,1024]{1,0:T(8,128)(2,1)} %bitcast.230), kind=kOutput, calls=%fused_computation.215 | convolution fusion | flops 3221225472 | bytes 13631488 | tf_op jit(solution)/shard_map/dot_general | solution.py:26
  209.1 22.9 %convert_reduce_fusion = (f32[4096]{0:T(1024)S(1)}, bf16[512,4096]{1,0:T(8,128)(2,1)S(1)}) fusion(f32[512,4096]{1,0:T(8,128)S(1)} %bitcast.179, s32[]{:T(128)S(6)} %select_n.73, f32[512,3072]{1,0:T(8,128)S(1)} %fusion.86, f32[512,1024]{1,0:T(8,128)S(1)} %fusion.85), kind=kLoop, calls=%fused_computation.22 | loop fusion | flops 161476608 | bytes 20987908 | tf_op jit(solution)/shard_map/reduce_sum | solution.py:38
  233.5 5.9 %fusion.88 = f32[512,768]{1,0:T(8,128)S(1)} fusion(bf16[512,4096]{1,0:T(8,128)(2,1)S(1)} %get-tuple-element.22, bf16[768,4096]{1,0:T(8,128)(2,1)} %all-gather.9.cloned.1.call-done), kind=kOutput, calls=%fused_computation.217 | convolution fusion | flops 3221225472 | bytes 12058624 | tf_op jit(solution)/shard_map/dot_general | solution.py:26
  247.9 8.6 %convert_reduce_fusion.4 = (f32[16,64]{1,0:T(8,128)S(1)}, bf16[16,64,512]{2,1,0:T(8,128)(2,1)S(1)}) fusion(bf16[512,16,64]{0,2,1:T(8,128)(2,1)S(1)} %bitcast.176, f32[16,512,512]{1,2,0:T(8,128)} %get-tuple-element.65, f32[16,512]{1,0:T(8,128)S(1)} %log_add_fusion), kind=kOutput, calls=%fused_computation.100 | convolution fusion | flops 546831360 | bytes 18911232 | tf_op jit(solution)/shard_map/hqk,qhd->khd/dot_general | solution.py:86
  256.6 11.4 %multiply_reduce_fusion = (f32[16,512]{1,0:T(8,128)S(1)}, f32[16,512,512]{1,2,0:T(8,128)}) fusion(f32[16,512,512]{1,2,0:T(8,128)} %get-tuple-element.65, f32[16,512]{1,0:T(8,128)S(1)} %log_add_fusion, bf16[512,16,64]{0,2,1:T(8,128)(2,1)S(1)} %bitcast.177, bf16[512,16,64]{0,2,1:T(8,128)(2,1)S(1)} %bitcast.185), kind=kOutput, calls=%fused_computation.5 | convolution fusion | flops 549445632 | bytes 35717120 | tf_op jit(solution)/shard_map/qhd,khd->hqk/dot_general | solution.py:72
  268.0 12.0 %multiply_convert_fusion = bf16[16,512,512]{1,2,0:T(8,128)(2,1)S(1)} fusion(f32[16,512,512]{1,2,0:T(8,128)} %get-tuple-element.73, f32[16,512,512]{1,2,0:T(8,128)} %get-tuple-element.65, f32[16,512]{1,0:T(8,128)S(1)} %get-tuple-element.72, f32[16,512]{1,0:T(8,128)S(1)} %log_add_fusion), kind=kLoop, calls=%fused_computation.4 | loop fusion | flops 16777216 | bytes 42008576 | tf_op jit(solution)/shard_map/convert_element_type | solution.py:78
  305.2 8.3 %reshape.403 = bf16[512,4,2,512]{3,2,1,0:T(2,128)(2,1)} reshape(bf16[512,4096]{1,0:T(8,128)(2,1)} %copy-done.7) | data formatting | bytes 8388608 | tf_op jit(solution)/shard_map/reshape | solution.py:216
  313.5 11.3 %constant_dynamic-slice_fusion.3 = (bf16[512,4,1,512]{3,2,1,0:T(2,128)(2,1)}, bf16[512,4,1,512]{3,2,1,0:T(2,128)(2,1)}) fusion(bf16[512,4,2,512]{3,2,1,0:T(2,128)(2,1)} %reshape.403, s32[]{:T(128)S(6)} %select_n.76, s32[]{:T(128)S(6)} %select_n.75), kind=kLoop, calls=%fused_computation.175 | loop fusion | bytes 8388616 | tf_op jit(solution)/shard_map/jit(dynamic_index_in_dim)/dynamic_slice | solution.py:217
  324.8 9.0 %copy.100 = bf16[512,4,1,512]{0,3,1,2:T(8,128)(2,1)S(1)} copy(bf16[512,4,1,512]{3,2,1,0:T(2,128)(2,1)} %get-tuple-element.34) | data formatting | bytes 4194304
  334.4 10.6 %copy.99 = bf16[512,4,1,512]{0,3,1,2:T(8,128)(2,1)} copy(bf16[512,4,1,512]{3,2,1,0:T(2,128)(2,1)} %get-tuple-element.35) | data formatting | bytes 4194304
  349.3 6.3 %add_convert_fusion.1 = bf16[1024,2048]{1,0:T(8,128)(2,1)} fusion(f32[1024,2048]{1,0:T(8,128)S(1)} %fusion.90, bf16[512,1024]{1,0:T(8,128)(2,1)} %collective-permute-done.16, bf16[512,2048]{0,1:T(8,128)(2,1)} %collective-permute-done.17), kind=kOutput, calls=%fused_computation.21 | convolution fusion | flops 2151677952 | bytes 15728640 | tf_op jit(solution)/shard_map/dot_general | solution.py:32
  355.7 6.5 %copy.88 = bf16[512,4096]{0,1:T(8,128)(2,1)} copy(bf16[512,4096]{1,0:T(8,128)(2,1)} %copy-done.6) | data formatting | bytes 8388608 | tf_op jit(solution)/shard_map/dynamic_slice | solution.py:141
  384.1 10.6 %collective-permute-done.14 = bf16[256,512]{1,0:T(8,128)(2,1)S(1)} collective-permute-done((bf16[256,512]{1,0:T(8,128)(2,1)S(1)}, bf16[256,512]{1,0:T(8,128)(2,1)S(1)}, u32[]{:S(2)}, u32[]{:S(2)}) %collective-permute-start.14) | collective-permute-done | bytes 262176 | tf_op jit(solution)/shard_map/ppermute | solution.py:134
  394.7 5.6 collective-permute-done.13
  402.2 11.9 %reduce-scatter.6.cloned.1.call-done = bf16[1024,512]{1,0:T(8,128)(2,1)} async-done(((bf16[1024,2048]{1,0:T(8,128)(2,1)}), bf16[1024,512]{1,0:T(8,128)(2,1)}) %reduce-scatter.6.cloned.1.call-update) | async-done | bytes 1048592 | tf_op jit(solution)/shard_map/reduce_scatter | solution.py:237
  422.4 11.8 %collective-permute-done.19 = bf16[256,512]{1,0:T(8,128)(2,1)S(1)} collective-permute-done((bf16[256,512]{1,0:T(8,128)(2,1)S(1)}, bf16[256,512]{1,0:T(8,128)(2,1)S(1)}, u32[]{:S(2)}, u32[]{:S(2)}) %collective-permute-start.19) | collective-permute-done | bytes 262176 | tf_op jit(solution)/shard_map/ppermute | solution.py:134
  434.2 5.6 collective-permute-done.18
  441.7 28.5 %reduce-scatter.8.cloned.1.call-done = bf16[4,128,1024]{2,1,0:T(8,128)(2,1)} async-done(((bf16[4,512,1024]{2,1,0:T(8,128)(2,1)}), bf16[4,128,1024]{2,1,0:T(8,128)(2,1)}) %reduce-scatter.8.cloned.1.call-update) | async-done | bytes 1048592 | tf_op jit(solution)/shard_map/reduce_scatter | solution.py:250
  478.6 11.8 %collective-permute-done.24 = bf16[128,1024]{1,0:T(8,128)(2,1)S(1)} collective-permute-done((bf16[128,1024]{1,0:T(8,128)(2,1)S(1)}, bf16[128,1024]{1,0:T(8,128)(2,1)S(1)}, u32[]{:S(2)}, u32[]{:S(2)}) %collective-permute-start.24) | collective-permute-done | bytes 262176 | tf_op jit(solution)/shard_map/ppermute | solution.py:134
  490.4 5.6 collective-permute-done.23
  498.4 39.1 %psum.7 = f32[4,3072]{1,0:T(4,128)S(1)} all-reduce(f32[4,3072]{1,0:T(4,128)S(1)} %constant_dynamic-update-slice_fusion), channel_id=1, replica_groups=mesh['chip'=4,'core'=2,'shard'=4] {'chip','core','shard'}, use_global_device_ids=true, to_apply=%region_21.22 | all-reduce | flops 12288 | bytes 98304 | tf_op jit(solution)/shard_map/psum | solution.py:304
  542.4 5.2 fusion.16
  (286 shorter events, 187.7 us)
Async XLA Ops:
  7.2 95.9 %all-gather.7.cloned.1.call-start = ((), (), s32[]{:S(2)}) async-start(), calls=%async_computation.3 | async-start | bytes 7077888 | tf_op jit(solution)/shard_map/all_gather | solution.py:167
  15.2 7.6 %collective-permute-start.2 = (bf16[272,512]{1,0:T(8,128)(2,1)S(1)}, bf16[272,512]{1,0:T(8,128)(2,1)S(1)}, u32[]{:S(2)}, u32[]{:S(2)}) collective-permute-start(bf16[272,512]{1,0:T(8,128)(2,1)S(1)} %pad_maximum_fusion.8), channel_id=1, source_target_pairs={{0,1},{1,2},{2,3},{3,0},{4,5},{5,6},{6,7},{7,4},{8,9},{9,10},{10,1... | collective-permute-start | bytes 835592 | tf_op jit(solution)/shard_map/ppermute | solution.py:131
  16.6 23.2 %collective-permute-start.1 = (bf16[272,512]{1,0:T(8,128)(2,1)S(1)}, bf16[272,512]{1,0:T(8,128)(2,1)S(1)}, u32[]{:S(2)}, u32[]{:S(2)}) collective-permute-start(bf16[272,512]{1,0:T(8,128)(2,1)S(1)} %pad_maximum_fusion.8), channel_id=1, source_target_pairs={{0,2},{1,3},{2,0},{3,1},{4,6},{5,7},{6,4},{7,5},{8,10},{9,11},{10,... | collective-permute-start | bytes 835592 | tf_op jit(solution)/shard_map/ppermute | solution.py:131
  17.7 25.0 %collective-permute-start = (bf16[272,512]{1,0:T(8,128)(2,1)S(1)}, bf16[272,512]{1,0:T(8,128)(2,1)S(1)}, u32[]{:S(2)}, u32[]{:S(2)}) collective-permute-start(bf16[272,512]{1,0:T(8,128)(2,1)S(1)} %pad_maximum_fusion.8), channel_id=1, source_target_pairs={{0,3},{1,0},{2,1},{3,2},{4,7},{5,4},{6,5},{7,6},{8,11},{9,8},{10,9... | collective-permute-start | bytes 835592 | tf_op jit(solution)/shard_map/ppermute | solution.py:131
  44.4 113.1 %all-gather.9.cloned.1.call-start = ((), (), s32[]{:S(2)}) async-start(), calls=%async_computation.4 | async-start | bytes 7077888 | tf_op jit(solution)/shard_map/all_gather | solution.py:170
  44.5 7.4 %collective-permute-start.5 = (bf16[256,512]{1,0:T(8,128)(2,1)S(1)}, bf16[256,512]{1,0:T(8,128)(2,1)S(1)}, u32[]{:S(2)}, u32[]{:S(2)}) collective-permute-start(bf16[256,512]{1,0:T(8,128)(2,1)S(1)} %constant_dynamic-slice_fusion.11), channel_id=1, source_target_pairs={{0,1},{1,2},{2,3},{3,0},{4,5},{5,6},{6,7},{7,4},{8,9},{9,10},{10,1... | collective-permute-start | bytes 786440 | tf_op jit(solution)/shard_map/ppermute | solution.py:131
  44.5 22.3 %collective-permute-start.4 = (bf16[256,512]{1,0:T(8,128)(2,1)S(1)}, bf16[256,512]{1,0:T(8,128)(2,1)S(1)}, u32[]{:S(2)}, u32[]{:S(2)}) collective-permute-start(bf16[256,512]{1,0:T(8,128)(2,1)S(1)} %constant_dynamic-slice_fusion.11), channel_id=1, source_target_pairs={{0,2},{1,3},{2,0},{3,1},{4,6},{5,7},{6,4},{7,5},{8,10},{9,11},{10,... | collective-permute-start | bytes 786440 | tf_op jit(solution)/shard_map/ppermute | solution.py:131
  45.6 23.6 %collective-permute-start.3 = (bf16[256,512]{1,0:T(8,128)(2,1)S(1)}, bf16[256,512]{1,0:T(8,128)(2,1)S(1)}, u32[]{:S(2)}, u32[]{:S(2)}) collective-permute-start(bf16[256,512]{1,0:T(8,128)(2,1)S(1)} %constant_dynamic-slice_fusion.11), channel_id=1, source_target_pairs={{0,3},{1,0},{2,1},{3,2},{4,7},{5,4},{6,5},{7,6},{8,11},{9,8},{10,9... | collective-permute-start | bytes 786440 | tf_op jit(solution)/shard_map/ppermute | solution.py:131
  70.1 119.4 %all-gather.11.cloned.1.call-start = ((), (), s32[]{:S(2)}) async-start(), calls=%async_computation.5 | async-start | bytes 7077888 | tf_op jit(solution)/shard_map/all_gather | solution.py:171
  71.9 7.7 %collective-permute-start.8 = (bf16[128,1024]{1,0:T(8,128)(2,1)}, bf16[128,1024]{1,0:T(8,128)(2,1)}, u32[]{:S(2)}, u32[]{:S(2)}) collective-permute-start(bf16[128,1024]{1,0:T(8,128)(2,1)} %constant_dynamic-slice_fusion.10), channel_id=1, source_target_pairs={{0,1},{1,2},{2,3},{3,0},{4,5},{5,6},{6,7},{7,4},{8,9},{9,10},{10,1... | collective-permute-start | bytes 786440 | tf_op jit(solution)/shard_map/ppermute | solution.py:131
  71.9 22.7 %collective-permute-start.7 = (bf16[128,1024]{1,0:T(8,128)(2,1)}, bf16[128,1024]{1,0:T(8,128)(2,1)}, u32[]{:S(2)}, u32[]{:S(2)}) collective-permute-start(bf16[128,1024]{1,0:T(8,128)(2,1)} %constant_dynamic-slice_fusion.10), channel_id=1, source_target_pairs={{0,2},{1,3},{2,0},{3,1},{4,6},{5,7},{6,4},{7,5},{8,10},{9,11},{10,... | collective-permute-start | bytes 786440 | tf_op jit(solution)/shard_map/ppermute | solution.py:131
  72.7 24.0 %collective-permute-start.6 = (bf16[128,1024]{1,0:T(8,128)(2,1)}, bf16[128,1024]{1,0:T(8,128)(2,1)}, u32[]{:S(2)}, u32[]{:S(2)}) collective-permute-start(bf16[128,1024]{1,0:T(8,128)(2,1)} %constant_dynamic-slice_fusion.10), channel_id=1, source_target_pairs={{0,3},{1,0},{2,1},{3,2},{4,7},{5,4},{6,5},{7,6},{8,11},{9,8},{10,9... | collective-permute-start | bytes 786440 | tf_op jit(solution)/shard_map/ppermute | solution.py:131
  98.8 276.5 %reduce-scatter.4.cloned.1.call-start = ((), (), s32[]{:S(2)}) async-start(), calls=%async_computation.6 | async-start | bytes 5242880 | tf_op jit(solution)/shard_map/reduce_scatter | solution.py:237
  286.6 12.2 %collective-permute-start.10 = (bf16[512,1536]{0,1:T(8,128)(2,1)}, bf16[512,1536]{0,1:T(8,128)(2,1)}, u32[]{:S(2)}, u32[]{:S(2)}) collective-permute-start(bf16[512,1536]{0,1:T(8,128)(2,1)} %bitcast.26), channel_id=1, source_target_pairs={{0,4},{4,0},{1,5},{5,1},{2,6},{6,2},{3,7},{7,3},{8,12},{12,8},{9,1... | collective-permute-start | bytes 4718600 | tf_op jit(solution)/shard_map/ppermute | solution.py:137
  287.1 9.8 %collective-permute-start.11 = (bf16[512,1024]{0,1:T(8,128)(2,1)}, bf16[512,1024]{0,1:T(8,128)(2,1)}, u32[]{:S(2)}, u32[]{:S(2)}) collective-permute-start(bf16[512,1024]{0,1:T(8,128)(2,1)} %fusion.55), channel_id=1, source_target_pairs={{0,4},{4,0},{1,5},{5,1},{2,6},{6,2},{3,7},{7,3},{8,12},{12,8},{9,1... | collective-permute-start | bytes 3145736 | tf_op jit(solution)/shard_map/ppermute | solution.py:137
  287.1 11.7 %collective-permute-start.9 = (bf16[512,1024]{1,0:T(8,128)(2,1)}, bf16[512,1024]{1,0:T(8,128)(2,1)}, u32[]{:S(2)}, u32[]{:S(2)}) collective-permute-start(bf16[512,1024]{1,0:T(8,128)(2,1)} %fusion.56), channel_id=1, source_target_pairs={{0,4},{4,0},{1,5},{5,1},{2,6},{6,2},{3,7},{7,3},{8,12},{12,8},{9,1... | collective-permute-start | bytes 3145736 | tf_op jit(solution)/shard_map/ppermute | solution.py:137
  305.2 108.9 %reduce-scatter.6.cloned.1.call-start = ((), (), s32[]{:S(2)}) async-start(), calls=%async_computation.8 | async-start | bytes 5242880 | tf_op jit(solution)/shard_map/reduce_scatter | solution.py:237
  333.8 15.5 %collective-permute-start.17 = (bf16[512,2048]{0,1:T(8,128)(2,1)S(1)}, bf16[512,2048]{0,1:T(8,128)(2,1)}, u32[]{:S(2)}, u32[]{:S(2)}) collective-permute-start(bf16[512,2048]{0,1:T(8,128)(2,1)S(1)} %bitcast.193), channel_id=1, source_target_pairs={{0,4},{4,0},{1,5},{5,1},{2,6},{6,2},{3,7},{7,3},{8,12},{12,8},{9,1... | collective-permute-start | bytes 6291464 | tf_op jit(solution)/shard_map/ppermute | solution.py:137
  334.4 15.0 %collective-permute-start.16 = (bf16[512,1024]{1,0:T(8,128)(2,1)}, bf16[512,1024]{1,0:T(8,128)(2,1)}, u32[]{:S(2)}, u32[]{:S(2)}) collective-permute-start(bf16[512,1024]{1,0:T(8,128)(2,1)} %copy-done.29), channel_id=1, source_target_pairs={{0,4},{4,0},{1,5},{5,1},{2,6},{6,2},{3,7},{7,3},{8,12},{12,8},{9,1... | collective-permute-start | bytes 3145736 | tf_op jit(solution)/shard_map/ppermute | solution.py:137
  355.7 114.5 %reduce-scatter.8.cloned.1.call-start = ((), (), s32[]{:S(2)}) async-start(), calls=%async_computation.10 | async-start | bytes 5242880 | tf_op jit(solution)/shard_map/reduce_scatter | solution.py:250
  375.2 174.4 %all-gather.13.cloned.1.call-start = ((), (), s32[]{:S(2)}) async-start(), calls=%async_computation.7 | async-start | bytes 2359296 | tf_op jit(solution)/shard_map/all_gather | solution.py:241
  376.5 7.7 %collective-permute-start.15 = (bf16[256,512]{1,0:T(8,128)(2,1)S(1)}, bf16[256,512]{1,0:T(8,128)(2,1)S(1)}, u32[]{:S(2)}, u32[]{:S(2)}) collective-permute-start(bf16[256,512]{1,0:T(8,128)(2,1)S(1)} %get-tuple-element.46), channel_id=1, source_target_pairs={{0,3},{1,0},{2,1},{3,2},{4,7},{5,4},{6,5},{7,6},{8,11},{9,8},{10,9... | collective-permute-start | bytes 786440 | tf_op jit(solution)/shard_map/ppermute | solution.py:134
  376.5 18.2 %collective-permute-start.14 = (bf16[256,512]{1,0:T(8,128)(2,1)S(1)}, bf16[256,512]{1,0:T(8,128)(2,1)S(1)}, u32[]{:S(2)}, u32[]{:S(2)}) collective-permute-start(bf16[256,512]{1,0:T(8,128)(2,1)S(1)} %get-tuple-element.47), channel_id=1, source_target_pairs={{0,2},{1,3},{2,0},{3,1},{4,6},{5,7},{6,4},{7,5},{8,10},{9,11},{10,... | collective-permute-start | bytes 786440 | tf_op jit(solution)/shard_map/ppermute | solution.py:134
  378.2 22.1 %collective-permute-start.13 = (bf16[256,512]{1,0:T(8,128)(2,1)S(1)}, bf16[256,512]{1,0:T(8,128)(2,1)S(1)}, u32[]{:S(2)}, u32[]{:S(2)}) collective-permute-start(bf16[256,512]{1,0:T(8,128)(2,1)S(1)} %get-tuple-element.45), channel_id=1, source_target_pairs={{0,1},{1,2},{2,3},{3,0},{4,5},{5,6},{6,7},{7,4},{8,9},{9,10},{10,1... | collective-permute-start | bytes 786440 | tf_op jit(solution)/shard_map/ppermute | solution.py:134
  402.1 152.2 %all-gather.15.cloned.1.call-start = ((), (), s32[]{:S(2)}) async-start(), calls=%async_computation.9 | async-start | bytes 2359296 | tf_op jit(solution)/shard_map/all_gather | solution.py:241
  415.2 7.2 %collective-permute-start.20 = (bf16[256,512]{1,0:T(8,128)(2,1)S(1)}, bf16[256,512]{1,0:T(8,128)(2,1)S(1)}, u32[]{:S(2)}, u32[]{:S(2)}) collective-permute-start(bf16[256,512]{1,0:T(8,128)(2,1)S(1)} %get-tuple-element.43), channel_id=1, source_target_pairs={{0,3},{1,0},{2,1},{3,2},{4,7},{5,4},{6,5},{7,6},{8,11},{9,8},{10,9... | collective-permute-start | bytes 786440 | tf_op jit(solution)/shard_map/ppermute | solution.py:134
  415.5 18.7 %collective-permute-start.19 = (bf16[256,512]{1,0:T(8,128)(2,1)S(1)}, bf16[256,512]{1,0:T(8,128)(2,1)S(1)}, u32[]{:S(2)}, u32[]{:S(2)}) collective-permute-start(bf16[256,512]{1,0:T(8,128)(2,1)S(1)} %get-tuple-element.44), channel_id=1, source_target_pairs={{0,2},{1,3},{2,0},{3,1},{4,6},{5,7},{6,4},{7,5},{8,10},{9,11},{10,... | collective-permute-start | bytes 786440 | tf_op jit(solution)/shard_map/ppermute | solution.py:134
  417.7 22.2 %collective-permute-start.18 = (bf16[256,512]{1,0:T(8,128)(2,1)S(1)}, bf16[256,512]{1,0:T(8,128)(2,1)S(1)}, u32[]{:S(2)}, u32[]{:S(2)}) collective-permute-start(bf16[256,512]{1,0:T(8,128)(2,1)S(1)} %get-tuple-element.42), channel_id=1, source_target_pairs={{0,1},{1,2},{2,3},{3,0},{4,5},{5,6},{6,7},{7,4},{8,9},{9,10},{10,1... | collective-permute-start | bytes 786440 | tf_op jit(solution)/shard_map/ppermute | solution.py:134
  441.7 121.3 %all-gather.17.cloned.1.call-start = ((), (), s32[]{:S(2)}) async-start(), calls=%async_computation.11 | async-start | bytes 2359296 | tf_op jit(solution)/shard_map/all_gather | solution.py:256
  471.4 7.2 %collective-permute-start.25 = (bf16[128,1024]{1,0:T(8,128)(2,1)S(1)}, bf16[128,1024]{1,0:T(8,128)(2,1)S(1)}, u32[]{:S(2)}, u32[]{:S(2)}) collective-permute-start(bf16[128,1024]{1,0:T(8,128)(2,1)S(1)} %get-tuple-element.40), channel_id=1, source_target_pairs={{0,3},{1,0},{2,1},{3,2},{4,7},{5,4},{6,5},{7,6},{8,11},{9,8},{10,9... | collective-permute-start | bytes 786440 | tf_op jit(solution)/shard_map/ppermute | solution.py:134
  471.6 18.8 %collective-permute-start.24 = (bf16[128,1024]{1,0:T(8,128)(2,1)S(1)}, bf16[128,1024]{1,0:T(8,128)(2,1)S(1)}, u32[]{:S(2)}, u32[]{:S(2)}) collective-permute-start(bf16[128,1024]{1,0:T(8,128)(2,1)S(1)} %get-tuple-element.41), channel_id=1, source_target_pairs={{0,2},{1,3},{2,0},{3,1},{4,6},{5,7},{6,4},{7,5},{8,10},{9,11},{10,... | collective-permute-start | bytes 786440 | tf_op jit(solution)/shard_map/ppermute | solution.py:134
  473.8 22.2 %collective-permute-start.23 = (bf16[128,1024]{1,0:T(8,128)(2,1)S(1)}, bf16[128,1024]{1,0:T(8,128)(2,1)S(1)}, u32[]{:S(2)}, u32[]{:S(2)}) collective-permute-start(bf16[128,1024]{1,0:T(8,128)(2,1)S(1)} %get-tuple-element.39), channel_id=1, source_target_pairs={{0,1},{1,2},{2,3},{3,0},{4,5},{5,6},{6,7},{7,4},{8,9},{9,10},{10,1... | collective-permute-start | bytes 786440 | tf_op jit(solution)/shard_map/ppermute | solution.py:134
  (46 other events, 644.9 us)
Sparse Core Ops, SparseCore 0:
  44.5 47.7 all-gather.6
  94.7 46.6 all-gather.8
  143.4 45.5 all-gather.10
  305.3 52.9 reduce-scatter.3
  361.4 52.6 reduce-scatter.5
  417.4 52.6 reduce-scatter.7
  472.8 28.5 all-gather.12
  504.0 28.3 all-gather.14
  535.1 27.8 all-gather.16

commit v2 on v1

v2 whole, which is shorter than its diff:
```python
from functools import partial

import jax
import jax.numpy as jnp
from jax import lax
from jax.experimental import pallas as pl
from jax.experimental.pallas import tpu as pltpu
from jax.sharding import Mesh
from jax.sharding import PartitionSpec as P

HEAD_DIM = 64
REP = ("chip", "core")
ALL = ("chip", "core", "shard")
F32 = jnp.float32
BF16 = jnp.bfloat16
VMEM_LIMIT = 60 * 1024 * 1024


def dot(left, right):
    return jnp.dot(left, right, preferred_element_type=F32)


def dot_t(left, right):
    return lax.dot_general(left, right, (((1,), (1,)), ((), ())), preferred_element_type=F32)


def t_dot(left, right):
    return lax.dot_general(left, right, (((0,), (0,)), ((), ())), preferred_element_type=F32)


def call(body, grid, ins, outs, out_shape, scratch=(), flops=0, moved=0):
    return pl.pallas_call(
        body,
        grid_spec=pltpu.PrefetchScalarGridSpec(
            num_scalar_prefetch=1,
            grid=grid,
            in_specs=ins,
            out_specs=outs,
            scratch_shapes=list(scratch),
        ),
        out_shape=out_shape,
        compiler_params=pltpu.CompilerParams(
            dimension_semantics=("arbitrary",) * len(grid), vmem_limit_bytes=VMEM_LIMIT
        ),
        cost_estimate=pl.CostEstimate(flops=flops, bytes_accessed=moved, transcendentals=0),
    )


def spec(shape, index):
    return pl.BlockSpec(shape, index)


def fixed(shape):
    zeros = (0,) * len(shape)
    return pl.BlockSpec(shape, lambda *_: zeros)


def struct(shape, dtype):
    return jax.ShapeDtypeStruct(shape, dtype)


def natural(where, step, group):
    return lax.rem(where[0] + step, group)


def normalise(hidden):
    average = jnp.mean(hidden, axis=-1, keepdims=True)
    centred = hidden - average
    variance = jnp.mean(centred * centred, axis=-1, keepdims=True)
    inverse = lax.rsqrt(variance + 1e-06)
    return centred * inverse, inverse


def normalise_back(grad, unit, inverse, gain):
    scaled = grad * gain
    first = jnp.mean(scaled, axis=-1, keepdims=True)
    second = jnp.mean(scaled * unit, axis=-1, keepdims=True)
    return inverse * (scaled - first - unit * second)


def rows_sum(value):
    return jnp.sum(value, axis=0, keepdims=True)


def qkv_kernel(group, where, x, own, rest, bias, out, rolled):
    rows = own.shape[0]

    @pl.when(pl.program_id(0) == 0)
    def _():
        for s in range(group):
            start = pl.multiple_of(natural(where, s, group) * rows, 128)
            rolled[:, s * rows : (s + 1) * rows] = x[:, pl.ds(start, rows)]

    total = dot(rolled[:, :rows], own[...]) + dot(rolled[:, rows:], rest[...])
    out[...] = (total + bias[...]).astype(BF16)


def qkv(where, x, w_qkv, rest_one, bias, group):
    seq, width = x.shape
    rows, columns = w_qkv.shape
    block = 512
    return call(
        partial(qkv_kernel, group),
        (columns // block,),
        [
            fixed((seq, width)),
            spec((rows, block), lambda j, w: (0, j)),
            spec((width - rows, block), lambda j, w: (0, j)),
            spec((1, block), lambda j, w: (0, j)),
        ],
        spec((seq, block), lambda j, w: (0, j)),
        struct((seq, columns), BF16),
        [pltpu.VMEM((seq, width), BF16)],
        flops=2 * seq * width * columns,
        moved=2 * (width * columns + seq * columns),
    )(where, x, w_qkv, rest_one, bias)


def attend_kernel(where, q, k, v, column, row, out, log_totals, bias):
    step = pl.program_id(0)
    seq = q.shape[0]

    @pl.when(step == 0)
    def _():
        bias[...] = jnp.where(column[...] == row[...], 0.0, -1e30)
        log_totals[...] = jnp.zeros_like(log_totals)

    lanes = lax.broadcasted_iota(jnp.int32, (1, 128), 1)
    heads = q.shape[1] // HEAD_DIM
    for h in range(heads):
        part = slice(h * HEAD_DIM, (h + 1) * HEAD_DIM)
        scores = dot_t(q[:, part] * BF16(HEAD_DIM**-0.5), k[:, part]) + bias[...]
        maxima = jnp.max(scores, axis=1, keepdims=True)
        expo = jnp.exp(scores - maxima)
        totals = jnp.sum(expo, axis=1, keepdims=True)
        probs = (expo * (1.0 / totals)).astype(BF16)
        out[:, part] = dot(probs, v[:, part]).astype(BF16)
        log_totals[...] = jnp.where(
            lanes == step * heads + h, maxima + jnp.log(totals), log_totals[...]
        )


def attention(where, projected, column, row, width):
    seq = projected.shape[0]
    block = 2 * HEAD_DIM
    count = width // block
    return call(
        attend_kernel,
        (count,),
        [
            spec((seq, block), lambda h, w: (0, h)),
            spec((seq, block), lambda h, w: (0, count + h)),
            spec((seq, block), lambda h, w: (0, 2 * count + h)),
            fixed((seq, 1)),
            fixed((1, seq)),
        ],
        [spec((seq, block), lambda h, w: (0, h)), fixed((seq, 128))],
        [struct((seq, width), BF16), struct((seq, 128), F32)],
        [pltpu.VMEM((seq, seq), F32)],
        flops=4 * seq * seq * width,
        moved=8 * seq * width,
    )(where, projected, projected, projected, column, row)


def attend_back_kernel(where, q, k, v, grad, log_totals, column, row, out, sums, bias):
    step = pl.program_id(0)

    @pl.when(step == 0)
    def _():
        bias[...] = jnp.where(column[...] == row[...], 0.0, -1e30)

    lanes = lax.broadcasted_iota(jnp.int32, (1, 128), 1)
    heads = q.shape[1] // HEAD_DIM
    for h in range(heads):
        part = slice(h * HEAD_DIM, (h + 1) * HEAD_DIM)
        picked = jnp.where(lanes == step * heads + h, log_totals[...], 0.0)
        logs = jnp.sum(picked, axis=1, keepdims=True)
        query = q[:, part] * BF16(HEAD_DIM**-0.5)
        scores = dot_t(query, k[:, part]) + bias[...]
        probs = jnp.exp(scores - logs)
        grad_probs = dot_t(grad[:, part], v[:, part])
        weighted = probs * grad_probs
        low = (weighted - probs * jnp.sum(weighted, axis=1, keepdims=True)).astype(BF16)
        grad_q = (dot(low, k[:, part]) * (HEAD_DIM**-0.5)).astype(BF16)
        grad_k = t_dot(low, query).astype(BF16)
        grad_v = t_dot(probs.astype(BF16), grad[:, part]).astype(BF16)
        out[0, :, part] = grad_q
        out[1, :, part] = grad_k
        out[2, :, part] = grad_v
        sums[0, :, part] = rows_sum(grad_q.astype(F32))
        sums[1, :, part] = rows_sum(grad_k.astype(F32))
        sums[2, :, part] = rows_sum(grad_v.astype(F32))


def attention_back(where, projected, grad, log_totals, column, row):
    seq, width = grad.shape
    block = 2 * HEAD_DIM
    count = width // block
    return call(
        attend_back_kernel,
        (count,),
        [
            spec((seq, block), lambda h, w: (0, h)),
            spec((seq, block), lambda h, w: (0, count + h)),
            spec((seq, block), lambda h, w: (0, 2 * count + h)),
            spec((seq, block), lambda h, w: (0, h)),
            fixed((seq, 128)),
            fixed((seq, 1)),
            fixed((1, seq)),
        ],
        [
            spec((3, seq, block), lambda h, w: (0, 0, h)),
            spec((3, 1, block), lambda h, w: (0, 0, h)),
        ],
        [struct((3, seq, width), BF16), struct((3, 1, width), F32)],
        [pltpu.VMEM((seq, seq), F32)],
        flops=10 * seq * seq * width,
        moved=14 * seq * width,
    )(where, projected, projected, projected, grad, log_totals, column, row)


def out_kernel(group, where, context, x, own, rest, bias, gain, shift, hidden, low):
    rows = own.shape[0]
    total = bias[...] + x[...].astype(F32)
    for s in range(group):
        start = pl.multiple_of(natural(where, s, group) * rows, 128)
        weight = own[...] if s == 0 else rest[(s - 1) * rows : s * rows, :]
        total = total + dot(context[:, pl.ds(start, rows)], weight)
    hidden[...] = total
    unit, _ = normalise(total)
    low[...] = (unit * gain[...] + shift[...]).astype(BF16)


def out_norm(where, context, x, w_out, rest_one, bias, gain, shift, group):
    seq, width = x.shape
    rows = w_out.shape[0]
    last = rest_one.shape[1] // width - 1
    block = seq // 2
    vector = fixed((1, width))
    return call(
        partial(out_kernel, group),
        (seq // block,),
        [
            spec((block, width), lambda i, w: (i, 0)),
            spec((block, width), lambda i, w: (i, 0)),
            fixed((rows, width)),
            spec((width - rows, width), lambda i, w: (0, last)),
            vector,
            vector,
            vector,
        ],
        [spec((block, width), lambda i, w: (i, 0))] * 2,
        [struct((seq, width), F32), struct((seq, width), BF16)],
        flops=2 * seq * width * width,
        moved=2 * width * width + 10 * seq * width,
    )(where, context, x, w_out, rest_one, bias, gain, shift)


def inner_kernel(group, where, x, own, rest, bias, act, slope, rolled):
    rows = own.shape[0]

    @pl.when(pl.program_id(0) == 0)
    def _():
        for s in range(group):
            start = pl.multiple_of(natural(where, s, group) * rows, 128)
            rolled[:, s * rows : (s + 1) * rows] = x[:, pl.ds(start, rows)]

    total = dot(rolled[:, :rows], own[...]) + dot(rolled[:, rows:], rest[...])
    total = total + bias[...]
    below = 0.5 + 0.5 * lax.erf(total * (0.5**0.5))
    act[...] = (total * below).astype(BF16)
    density = jnp.exp(-0.5 * total * total) * ((2.0 * jnp.pi) ** -0.5)
    slope[...] = (below + total * density).astype(BF16)


def inner(where, x, w_in, rest_in, bias, group):
    seq, width = x.shape
    rows, columns = w_in.shape
    block = 512
    return call(
        partial(inner_kernel, group),
        (columns // block,),
        [
            fixed((seq, width)),
            spec((rows, block), lambda j, w: (0, j)),
            spec((width - rows, block), lambda j, w: (0, j)),
            spec((1, block), lambda j, w: (0, j)),
        ],
        [spec((seq, block), lambda j, w: (0, j))] * 2,
        [struct((seq, columns), BF16)] * 2,
        [pltpu.VMEM((seq, width), BF16)],
        flops=2 * seq * width * columns,
        moved=2 * (width * columns + 2 * seq * columns),
    )(where, x, w_in, rest_in, bias)


def outer_kernel(
    group,
    where,
    act,
    own,
    rest,
    hidden,
    cotangent,
    gain_one,
    shift_one,
    bias,
    gain_two,
    shift_two,
    out,
    grad,
    low,
    sums,
    total,
):
    step = pl.program_id(0)

    @pl.when(step == 0)
    def _():
        total[...] = dot(act[...], own[...])

    @pl.when(step > 0)
    def _():
        total[...] += dot(act[...], rest[...])

    @pl.when(step == group - 1)
    def _():
        unit_one, _ = normalise(hidden[...])
        second = unit_one * gain_one[...] + shift_one[...] + total[...] + bias[...]
        unit, inverse = normalise(second)
        out[...] = (unit * gain_two[...] + shift_two[...]).astype(BF16)
        given = cotangent[...].astype(F32)
        back = normalise_back(given, unit, inverse, gain_two[...])
        grad[...] = back
        rounded = back.astype(BF16)
        low[...] = rounded
        sums[0:1, :] = rows_sum(given * unit)
        sums[1:2, :] = rows_sum(given)
        sums[2:3, :] = rows_sum(rounded.astype(F32))


def outer(where, act, w_down, rest_down, hidden, cotangent, vectors, group):
    seq, width = hidden.shape
    rows = w_down.shape[0]
    full = fixed((seq, width))
    vector = fixed((1, width))
    return call(
        partial(outer_kernel, group),
        (group,),
        [
            spec((seq, rows), lambda s, w: (0, natural(w, s, group))),
            fixed((rows, width)),
            spec((rows, width), lambda s, w: (jnp.maximum(s - 1, 0), 0)),
            full,
            full,
        ]
        + [vector] * 5,
        [full, full, full, fixed((8, width))],
        [
            struct((seq, width), BF16),
            struct((seq, width), F32),
            struct((seq, width), BF16),
            struct((8, width), F32),
        ],
        [pltpu.VMEM((seq, width), F32)],
        flops=2 * seq * width * rows * group,
        moved=2 * width * rows * group + 14 * seq * width,
    )(where, act, w_down, rest_down, hidden, cotangent, *vectors)


def inner_back_kernel(
    group,
    where,
    low,
    own_down,
    rest_down,
    slope,
    own_in,
    rest_in,
    grad_two,
    hidden,
    gain,
    own_out,
    rest_out,
    grad_inner,
    bias_sums,
    grad_one,
    low_one,
    grad_context,
    sums,
    total,
):
    step = pl.program_id(0)
    rows = own_in.shape[0]

    def place(s):
        return pl.ds(pl.multiple_of(natural(where, s, group) * rows, 128), rows)

    def finish(back):
        value = (back * slope[...].astype(F32)).astype(BF16)
        grad_inner[...] = value
        bias_sums[...] = rows_sum(value.astype(F32))

    @pl.when(step == 0)
    def _():
        finish(dot_t(low[...], own_down[...]))
        total[...] = grad_two[...]

    @pl.when(step > 0)
    def _():
        finish(dot_t(low[...], rest_down[...]))

    value = grad_inner[...]
    total[:, place(0)] += dot_t(value, own_in[...])
    for s in range(1, group):
        total[:, place(s)] += dot_t(value, rest_in[(s - 1) * rows : s * rows, :])

    @pl.when(step == group - 1)
    def _():
        unit, inverse = normalise(hidden[...])
        given = total[...]
        back = normalise_back(given, unit, inverse, gain[...])
        grad_one[...] = back
        rounded = back.astype(BF16)
        low_one[...] = rounded
        sums[0:1, :] = rows_sum(given * unit)
        sums[1:2, :] = rows_sum(given)
        sums[2:3, :] = rows_sum(rounded.astype(F32))
        grad_context[:, place(0)] = dot_t(rounded, own_out[...]).astype(BF16)
        for s in range(1, group):
            weight = rest_out[(s - 1) * rows : s * rows, :]
            grad_context[:, place(s)] = dot_t(rounded, weight).astype(BF16)


def inner_back(
    where, low, w_down, rest_down, slope, w_in, rest_in, grad_two, hidden, gain, w_out, rest_one, group
):
    seq, width = hidden.shape
    ff_rows = w_down.shape[0]
    rows, columns = w_in.shape
    last = rest_one.shape[1] // width - 1
    full = fixed((seq, width))

    def block(rows_of):
        return spec((rows_of, ff_rows), lambda s, w: (0, natural(w, s, group)))

    return call(
        partial(inner_back_kernel, group),
        (group,),
        [
            full,
            fixed((ff_rows, width)),
            spec((ff_rows, width), lambda s, w: (jnp.maximum(s - 1, 0), 0)),
            block(seq),
            block(rows),
            block(width - rows),
            full,
            full,
            fixed((1, width)),
            fixed((rows, width)),
            spec((width - rows, width), lambda s, w: (0, last)),
        ],
        [block(seq), block(1), full, full, full, fixed((8, width))],
        [
            struct((seq, columns), BF16),
            struct((1, columns), F32),
            struct((seq, width), F32),
            struct((seq, width), BF16),
            struct((seq, width), BF16),
            struct((8, width), F32),
        ],
        [pltpu.VMEM((seq, width), F32)],
        flops=4 * seq * width * columns + 2 * seq * width * width,
        moved=4 * width * columns + 4 * seq * columns + 18 * seq * width,
    )(where, low, w_down, rest_down, slope, w_in, rest_in, grad_two, hidden, gain, w_out, rest_one)


def input_back_kernel(where, grad, first, own, rest, out):
    def result(weight):
        width = grad.shape[2]
        total = first[...]
        for m in range(3):
            total = total + dot_t(grad[m], weight[:, m * width : (m + 1) * width])
        out[...] = total

    @pl.when(pl.program_id(0) == 0)
    def _():
        result(own)

    @pl.when(pl.program_id(0) > 0)
    def _():
        result(rest)


def input_back(where, grad, first, w_qkv, rest_one, group):
    _, seq, width = grad.shape
    rows, columns = w_qkv.shape
    block = spec((seq, rows), lambda s, w: (0, natural(w, s, group)))
    return call(
        input_back_kernel,
        (group,),
        [
            fixed((3, seq, width)),
            block,
            fixed((rows, columns)),
            spec((rows, columns), lambda s, w: (jnp.maximum(s - 1, 0), 0)),
        ],
        block,
        struct((seq, width), F32),
        flops=2 * seq * width * columns,
        moved=2 * (width * columns + seq * columns) + 8 * seq * width,
    )(where, grad, first, w_qkv, rest_one)


def down_grad_kernel(where, act, act_other, low, low_other, out):
    out[...] = (t_dot(act[...], low[...]) + t_dot(act_other[...], low_other[...])).astype(BF16)


def down_grad(where, act, act_other, low, low_other, rows, group):
    seq, columns = act.shape
    half = low.shape[1] // 2
    left = spec((seq, rows), lambda s, w: (0, natural(w, s, group)))
    right = spec((seq, half), lambda s, w: (0, w[1]))
    return call(
        down_grad_kernel,
        (group,),
        [left, left, right, right],
        spec((rows, half), lambda s, w: (s, 0)),
        struct((columns, half), BF16),
        flops=4 * seq * columns * half,
        moved=2 * (2 * seq * columns + columns * half),
    )(where, act, act_other, low, low_other)


def in_grad_kernel(group, where, x, x_other, grad, grad_other, out):
    width = x.shape[1]
    rows = width // group
    for s in range(group):
        place = pl.ds(pl.multiple_of(natural(where, s, group) * rows, 128), rows)
        value = t_dot(x[:, place], grad[...]) + t_dot(x_other[:, place], grad_other[...])
        out[0, s * rows : (s + 1) * rows, :] = value.astype(BF16)


def in_grad(where, x, x_other, grad, grad_other, chips, group):
    seq, width = x.shape
    part = grad.shape[1] // (2 * chips)
    full = fixed((seq, width))
    right = spec((seq, part), lambda p, w: (0, 2 * p + w[1]))
    return call(
        partial(in_grad_kernel, group),
        (chips,),
        [full, full, right, right],
        spec((1, width, part), lambda p, w: (p, 0, 0)),
        struct((chips, width, part), BF16),
        flops=4 * seq * width * part * chips,
        moved=2 * (4 * seq * width + width * part * chips),
    )(where, x, x_other, grad, grad_other)


def first_grad_kernel(group, split, where, x, x_other, c, c_other, g, g_other, a, a_other, out):
    width = x.shape[1]
    rows = width // group

    def result(left, left_other, right, right_other):
        for s in range(group):
            place = pl.ds(pl.multiple_of(natural(where, s, group) * rows, 128), rows)
            value = t_dot(left[:, place], right) + t_dot(left_other[:, place], right_other)
            out[0, s * rows : (s + 1) * rows, :] = value.astype(BF16)

    @pl.when(pl.program_id(0) < split)
    def _():
        result(x, x_other, g[0], g_other[0])

    @pl.when(pl.program_id(0) >= split)
    def _():
        result(c, c_other, a[...], a_other[...])


def first_grad(where, x, x_other, c, c_other, g, g_other, a, a_other, chips, group):
    seq, width = x.shape
    part = 4 * width // (2 * chips)
    each = width // part
    split = 3 * chips // 4
    full = fixed((seq, width))

    def proj_block(p, w):
        block = jnp.minimum(2 * p + w[1], 3 * each - 1)
        return (block // each, 0, lax.rem(block, each))

    def attn_block(p, w):
        return (0, jnp.maximum(2 * p + w[1] - 3 * each, 0))

    proj = spec((1, seq, part), proj_block)
    attn = spec((seq, part), attn_block)
    return call(
        partial(first_grad_kernel, group, split),
        (chips,),
        [full, full, full, full, proj, proj, attn, attn],
        spec((1, width, part), lambda p, w: (p, 0, 0)),
        struct((chips, width, part), BF16),
        flops=4 * seq * width * part * chips,
        moved=2 * (8 * seq * width + width * part * chips),
    )(where, x, x_other, c, c_other, g, g_other, a, a_other)


def local(
    chips,
    group,
    tokens,
    segments,
    lengths,
    cotangent,
    w_qkv,
    b_qv,
    w_out,
    b_out,
    gain_one,
    shift_one,
    w_in,
    b_in,
    w_down,
    b_down,
    gain_two,
    shift_two,
):
    reps = 2 * chips
    core = lax.axis_index("core")
    rank = lax.axis_index("chip") * 2 + core
    own = lax.axis_index("shard")
    _, seq_len, model_width = tokens.shape
    ff_rows = w_down.shape[0]
    ff_width = w_in.shape[1]
    qkv_width = w_qkv.shape[1]

    def from_shard(value, step):
        return lax.ppermute(value, "shard", [(i, (i - step) % group) for i in range(group)])

    def to_shard(value, step):
        return lax.ppermute(value, "shard", [(i, (i + step) % group) for i in range(group)])

    def sibling(value):
        return lax.ppermute(value, "core", [(0, 1), (1, 0)])

    vectors = (b_qv, b_out, gain_one, shift_one, b_in, b_down, gain_two, shift_two)
    sizes = [v.shape[0] for v in vectors]
    w_one = jnp.concatenate([w_qkv, w_out], axis=1)
    part = w_one.shape[1] // reps
    rows = w_one.shape[0]
    packed = jnp.concatenate(vectors)
    extra = -(-packed.shape[0] // (16 * part)) * 16
    packed = jnp.pad(packed, (0, extra * part - packed.shape[0])).reshape(extra, part)
    piece_one = jnp.concatenate(
        [lax.dynamic_slice_in_dim(w_one, rank * part, part, axis=1), packed], axis=0
    )
    part_in = ff_width // reps
    piece_in = lax.dynamic_slice_in_dim(w_in, rank * part_in, part_in, axis=1)
    part_down = ff_rows // reps
    piece_down = lax.dynamic_slice_in_dim(w_down, rank * part_down, part_down, axis=0)

    got_one = [from_shard(piece_one, s) for s in range(1, group)]
    got_in = [from_shard(piece_in, s) for s in range(1, group)]
    got_down = [from_shard(piece_down, s) for s in range(1, group)]
    rest_one = lax.all_gather(
        jnp.concatenate([g[:rows] for g in got_one], axis=0), REP, axis=1, tiled=True
    )
    rest_in = lax.all_gather(jnp.concatenate(got_in, axis=0), REP, axis=1, tiled=True)
    rest_down = lax.all_gather(jnp.stack(got_down), REP, axis=1, tiled=True)
    rest_down = rest_down.reshape(-1, model_width)

    relative = jnp.stack([packed.reshape(-1)] + [g[rows:].reshape(-1) for g in got_one])
    ordered = jnp.concatenate([relative, relative], axis=0)
    ordered = lax.dynamic_slice_in_dim(ordered, (group - own) % group, group, axis=0)
    full, start = [], 0
    for size in sizes:
        full.append(ordered[:, start : start + size].reshape(1, -1).astype(F32))
        start += size
    bias_qv, bias_out, norm_gone, norm_sone, bias_in, bias_down, norm_gtwo, norm_stwo = full

    where = jnp.stack([own, core]).astype(jnp.int32)
    none = jnp.zeros((1, model_width), F32)
    bias_qkv = jnp.concatenate([bias_qv[:, :model_width], none, bias_qv[:, model_width:]], axis=1)
    kind = segments[0] * 2 + (jnp.arange(seq_len) < lengths[0]).astype(jnp.int32)
    column, row = kind[:, None], kind[None, :]

    flat_in = tokens[0]
    projected = qkv(where, flat_in, w_qkv, rest_one, bias_qkv, group)
    context, log_totals = attention(where, projected, column, row, model_width)
    hidden, normed = out_norm(
        where, context, flat_in, w_out, rest_one, bias_out, norm_gone, norm_sone, group
    )
    act, slope = inner(where, normed, w_in, rest_in, bias_in, group)
    in_other, context_other = sibling(flat_in), sibling(context)
    normed_other, act_other = sibling(normed), sibling(act)
    output_rows, grad_second, grad_branch, sums_two = outer(
        where,
        act,
        w_down,
        rest_down,
        hidden,
        cotangent[0],
        (norm_gone, norm_sone, bias_down, norm_gtwo, norm_stwo),
        group,
    )

    def own_sum(parts):
        total = parts[0].astype(F32)
        for s in range(1, group):
            total = total + to_shard(parts[s], s).astype(F32)
        return total.astype(BF16)

    def scatter_columns(grad):
        flat = grad.reshape(-1, grad.shape[2])
        share = lax.psum_scatter(flat, "chip", scatter_dimension=0, tiled=True)
        share = own_sum(share.reshape(group, rows, -1))
        return lax.all_gather(share, REP, axis=1, tiled=True).astype(F32)

    grad_down = down_grad(
        where, act, act_other, grad_branch, sibling(grad_branch), ff_rows, group
    )
    half = model_width // 2
    grad_down = lax.psum_scatter(
        grad_down.reshape(group, ff_rows, half), "chip", scatter_dimension=1, tiled=True
    )
    grad_down = lax.all_gather(own_sum(grad_down), REP, axis=0, tiled=False)
    grad_down = grad_down.reshape(chips, 2, ff_rows // chips, half).transpose(0, 2, 1, 3)
    grad_wdown = grad_down.reshape(ff_rows, model_width).astype(F32)

    grad_inner, sums_in, grad_first, grad_attn, grad_context, sums_one = inner_back(
        where,
        grad_branch,
        w_down,
        rest_down,
        slope,
        w_in,
        rest_in,
        grad_second,
        hidden,
        norm_gone,
        w_out,
        rest_one,
        group,
    )
    grad_win = scatter_columns(
        in_grad(where, normed, normed_other, grad_inner, sibling(grad_inner), chips, group)
    )
    grad_proj, sums_proj = attention_back(
        where, projected, grad_context, log_totals, column, row
    )
    grad_one = scatter_columns(
        first_grad(
            where,
            flat_in,
            in_other,
            context,
            context_other,
            grad_proj,
            sibling(grad_proj),
            grad_attn,
            sibling(grad_attn),
            chips,
            group,
        )
    )
    grad_input = input_back(where, grad_proj, grad_first, w_qkv, rest_one, group)

    small = (
        jnp.concatenate([sums_proj[0, 0], sums_proj[2, 0]]),
        sums_one[2],
        sums_one[0],
        sums_one[1],
        sums_in[0],
        sums_two[2],
        sums_two[0],
        sums_two[1],
    )
    small = jnp.concatenate([v.reshape(group, -1) for v in small], axis=1)
    small = lax.psum(small, ALL)
    small = lax.dynamic_index_in_dim(small, own, axis=0, keepdims=False)
    vecs, start = [], 0
    for size in sizes:
        vecs.append(small[start : start + size])
        start += size

    return (
        output_rows.reshape(tokens.shape),
        grad_input.reshape(tokens.shape),
        grad_one[:, :qkv_width],
        vecs[0],
        grad_one[:, qkv_width:],
        vecs[1],
        vecs[2],
        vecs[3],
        grad_win,
        vecs[4],
        grad_wdown,
        vecs[5],
        vecs[6],
        vecs[7],
    )


def solution(mesh):
    reps, group = mesh.devices.shape
    fine = Mesh(mesh.devices.reshape(reps // 2, 2, group), ALL)
    rows = P(ALL, None, None)
    matrix = P("shard", None)
    vector = P("shard")
    in_specs = (
        rows,
        P(ALL, None),
        P(ALL),
        rows,
        matrix,
        vector,
        matrix,
        vector,
        vector,
        vector,
        matrix,
        vector,
        matrix,
        vector,
        vector,
        vector,
    )
    out_specs = (
        rows,
        rows,
        matrix,
        vector,
        matrix,
        vector,
        vector,
        vector,
        matrix,
        vector,
        matrix,
        vector,
        vector,
        vector,
    )
    return jax.shard_map(
        partial(local, reps // 2, group),
        mesh=fine,
        in_specs=in_specs,
        out_specs=out_specs,
        check_vma=False,
    )
```

time: 580 us -> 543 us (0.936)
  matrix products: 147 us -> 0 us
  Pallas kernels: 0 us -> 145 us
  waiting for transfers between devices: 173 us -> 259 us
  other arithmetic: 84.6 us -> 16.9 us
  local copies, waits for them, and re-layouts: 89.4 us -> 37.1 us
    dot_general x30 -> x0, matrix products: 147 us -> none  [the longest x8 51.8 us: matmul(): return jnp.dot(left, right, preferred_element_type=jnp.float32)]
    pallas_call x0 -> x11, Pallas kernels: none -> 145 us  [the longest x1 23.6 us: inner_back(): call(partial(inner_back_kernel, group), (group,), [full, fixed((ff_rows,...]
    reduce_sum x11 -> x0, other arithmetic: 38 us -> none  [the longest x3 23.4 us: column_sum(): return jnp.sum(values.astype(jnp.float32), axis=0)]
    all_gather x1, waiting for transfers between devices: 0.01 us -> 33.4 us  [local(): rest_down = lax.all_gather(jnp.stack(got_down), REP, axis=1, tiled=True)]
    reduce_scatter x3, waiting for transfers between devices: 40.4 us -> 70.4 us  [the longest x2 42.2 us: scatter_columns(): share = lax.psum_scatter(flat, 'chip', scatter_dimension=0, tiled=True)]
    dynamic_slice x6 -> x0, local copies, waits for them, and re-layouts: 25.2 us -> none  [the longest x4 18.1 us: half(): lax.dynamic_index_in_dim(split, which, axis=2, keepdims=False)]
    ppermute x8, waiting for transfers between devices: 2.77 us -> 23.9 us  [sibling(): return lax.ppermute(value, 'core', [(0, 1), (1, 0)])]
    convert_element_type x9 -> x4, other arithmetic: 27.7 us -> 9.47 us  [the longest x3 5.37 us: own_sum(): return total.astype(BF16)]
  transfers between devices with their start and end apart: 35 -> 35, of which waited for: 22 -> 28; matrix products, arithmetic and copies ran while one was open for 35% -> 7% of each run, Pallas kernels for 0% -> 14%
where the time goes in v2:
time: 543 us; the launch traced here: 537 us
  waiting for transfers between devices  259 us (48%)
  Pallas kernels  145 us (27%)
  blocking collectives  39.1 us (7%)
  local copies, waits for them, and re-layouts  37.1 us (7%)
  starting transfers between devices  25.6 us (5%)
  other arithmetic  16.9 us (3%)
  between operations  14.9 us (3%)
    ppermute x9, waiting for transfers between devices, from_shard(): lax.ppermute(value, 'shard', [(i, (i - step) % group) for i in range(grou...  67.9 us
    ppermute x9, waiting for transfers between devices, to_shard(): lax.ppermute(value, 'shard', [(i, (i + step) % group) for i in range(grou...  60.4 us
    reduce_scatter x2, waiting for transfers between devices, scatter_columns(): share = lax.psum_scatter(flat, 'chip', scatter_dimension=0, tiled=True)  42.2 us
    psum x1, blocking collectives, local(): small = lax.psum(small, ALL)  39.1 us
    all_gather x1, waiting for transfers between devices, local(): rest_down = lax.all_gather(jnp.stack(got_down), REP, axis=1, tiled=True)  33.4 us
    reduce_scatter x1, waiting for transfers between devices, local(): lax.psum_scatter(grad_down.reshape(group, ff_rows, half), 'chip', scatter...  28.2 us
    ppermute x8, waiting for transfers between devices, sibling(): return lax.ppermute(value, 'core', [(0, 1), (1, 0)])  23.9 us
    pallas_call x1, Pallas kernels, inner_back(): call(partial(inner_back_kernel, group), (group,), [full, fixed((ff_rows,...  23.6 us
  transfers between devices with their start and end apart: 35, of which 28 were waited for; matrix products, arithmetic and copies ran while one was open for 7% of the time, Pallas kernels for 14%

profile of v2, /device:TPU:9, one launch (start us, length us, event | category | flops | bytes accessed | tf_op | source)
XLA Modules:
  0.0 537.4 jit_solution(9677000173511615328)
XLA Ops:
  18.9 3.7 collective-permute-done.2
  22.7 17.0 %collective-permute-done.1 = bf16[272,512]{1,0:T(8,128)(2,1)S(1)} collective-permute-done((bf16[272,512]{1,0:T(8,128)(2,1)S(1)}, bf16[272,512]{1,0:T(8,128)(2,1)S(1)}, u32[]{:S(2)}, u32[]{:S(2)}) %collective-permute-start.1) | collective-permute-done | bytes 278560 | tf_op jit(solution)/shard_map/ppermute | solution.py:636
  46.3 5.6 %collective-permute-done.5 = bf16[256,512]{1,0:T(8,128)(2,1)S(1)} collective-permute-done((bf16[256,512]{1,0:T(8,128)(2,1)S(1)}, bf16[256,512]{1,0:T(8,128)(2,1)S(1)}, u32[]{:S(2)}, u32[]{:S(2)}) %collective-permute-start.5) | collective-permute-done | bytes 262176 | tf_op jit(solution)/shard_map/ppermute | solution.py:636
  52.0 15.0 %collective-permute-done.4 = bf16[256,512]{1,0:T(8,128)(2,1)S(1)} collective-permute-done((bf16[256,512]{1,0:T(8,128)(2,1)S(1)}, bf16[256,512]{1,0:T(8,128)(2,1)S(1)}, u32[]{:S(2)}, u32[]{:S(2)}) %collective-permute-start.4) | collective-permute-done | bytes 262176 | tf_op jit(solution)/shard_map/ppermute | solution.py:636
  73.6 4.5 collective-permute-done.8
  78.1 14.9 %collective-permute-done.7 = bf16[128,1024]{1,0:T(8,128)(2,1)S(1)} collective-permute-done((bf16[128,1024]{1,0:T(8,128)(2,1)S(1)}, bf16[128,1024]{1,0:T(8,128)(2,1)S(1)}, u32[]{:S(2)}, u32[]{:S(2)}) %collective-permute-start.7) | collective-permute-done | bytes 262176 | tf_op jit(solution)/shard_map/ppermute | solution.py:636
  105.4 9.2 %shard_map.263.q.k.v = bf16[512,3072]{1,0:T(8,128)(2,1)} custom-call(s32[2]{0:T(128)} %pad_add_fusion.where, bf16[512,1024]{1,0:T(8,128)(2,1)} %bitcast.90, bf16[256,3072]{1,0:T(8,128)(2,1)} %own.9, bf16[768,4096]{1,0:T(8,128)(2,1)} %all-gather.8.cloned.1.call-done.rest.rest_out, f32[1,3072]{1,0:T(1,128)} %pad_maximum_fusion.4.bias), custom_call_target="tpu_custom_call" | custom-call | flops 3221225472 | bytes 9437184 | tf_op jit(solution)/shard_map/pallas_call | solution.py:102
  114.7 17.0 %shard_map.264 = (bf16[512,1024]{1,0:T(8,128)(2,1)}, f32[512,128]{1,0:T(8,128)}) custom-call(s32[2]{0:T(128)} %pad_add_fusion.where, bf16[512,3072]{1,0:T(8,128)(2,1)} %shard_map.263.q.k.v, bf16[512,3072]{1,0:T(8,128)(2,1)} %shard_map.263.q.k.v, bf16[512,3072]{1,0:T(8,128)(2,1)} %shard_map.263.q.k.v, s32[512,1]{1,0:T(8,128)} %convert_add_fusion.1.column, ...), custom_call_target="tpu_custom_call" | custom-call | flops 1073741824 | bytes 4194304 | tf_op jit(solution)/shard_map/pallas_call | solution.py:147
  131.6 5.4 %shard_map.265 = (f32[512,1024]{1,0:T(8,128)}, bf16[512,1024]{1,0:T(8,128)(2,1)}) custom-call(s32[2]{0:T(128)} %pad_add_fusion.where, bf16[512,1024]{1,0:T(8,128)(2,1)} %get-tuple-element.32.context.c, bf16[512,1024]{1,0:T(8,128)(2,1)} %bitcast.91, bf16[256,1024]{1,0:T(8,128)(2,1)} %own_out.1, bf16[768,4096]{1,0:T(8,128)(2,1)} %all-gather.8.cloned.1.call-done.rest.rest_out, ...), custom_call_target="tpu_custom_call" | custom-call | flops 1073741824 | bytes 7340032 | tf_op jit(solution)/shard_map/pallas_call | solution.py:240
  139.9 14.0 %shard_map.266 = (bf16[512,4096]{1,0:T(8,128)(2,1)}, bf16[512,4096]{1,0:T(8,128)(2,1)}) custom-call(s32[2]{0:T(128)} %pad_add_fusion.where, bf16[512,1024]{1,0:T(8,128)(2,1)} %get-tuple-element.33.x, bf16[256,4096]{1,0:T(8,128)(2,1)} %own_in.1, bf16[768,4096]{1,0:T(8,128)(2,1)} %all-gather.10.cloned.1.call-done.rest.rest_in, f32[1,4096]{1,0:T(1,128)} %bitcast.116), custom_call_target="tpu_custom_call" | custom-call | flops 4294967296 | bytes 16777216 | tf_op jit(solution)/shard_map/pallas_call | solution.py:280
  154.0 33.4 %all-gather.12.cloned.1.call-done = bf16[3,1024,1024]{2,1,0:T(8,128)(2,1)} async-done(((bf16[3,128,1024]{2,1,0:T(8,128)(2,1)}), bf16[3,1024,1024]{2,1,0:T(8,128)(2,1)}) %all-gather.12.cloned.1.call-update) | async-done | bytes 6291472 | tf_op jit(solution)/shard_map/all_gather | solution.py:667
  187.4 14.7 %shard_map.267 = (bf16[512,1024]{1,0:T(8,128)(2,1)}, f32[512,1024]{1,0:T(8,128)}, bf16[512,1024]{1,0:T(8,128)(2,1)}, f32[8,1024]{1,0:T(8,128)}) custom-call(s32[2]{0:T(128)} %pad_add_fusion.where, bf16[512,4096]{1,0:T(8,128)(2,1)} %get-tuple-element.34.act, bf16[1024,1024]{1,0:T(8,128)(2,1)} %own_down.1, bf16[3072,1024]{1,0:T(8,128)(2,1)} %bitcast.128, ...), custom_call_target="tpu_custom_call" | custom-call | flops 4294967296 | bytes 15728640 | tf_op jit(solution)/shard_map/pallas_call | solution.py:347
  202.1 23.6 %shard_map.268 = (bf16[512,4096]{1,0:T(8,128)(2,1)}, f32[1,4096]{1,0:T(1,128)}, f32[512,1024]{1,0:T(8,128)}, bf16[512,1024]{1,0:T(8,128)(2,1)}, bf16[512,1024]{1,0:T(8,128)(2,1)}, /*index=5*/f32[8,1024]{1,0:T(8,128)}) custom-call(s32[2]{0:T(128)} %pad_add_fusion.where, bf16[512,1024]{1,0:T(8,128)(2,1)} %get-tuple-element.37.low, ...), custom_call_target="tpu_custom_call" | custom-call | flops 9663676416 | bytes 34603008 | tf_op jit(solution)/shard_map/pallas_call | solution.py:447
  225.7 22.4 %shard_map.269 = (bf16[3,512,1024]{2,1,0:T(8,128)(2,1)}, f32[3,1,1024]{2,1,0:T(1,128)}) custom-call(s32[2]{0:T(128)} %pad_add_fusion.where, bf16[512,3072]{1,0:T(8,128)(2,1)} %shard_map.263.q.k.v, bf16[512,3072]{1,0:T(8,128)(2,1)} %shard_map.263.q.k.v, bf16[512,3072]{1,0:T(8,128)(2,1)} %shard_map.263.q.k.v, bf16[512,1024]{1,0:T(8,128)(2,1)} %get-tuple-element.40.grad, ...), custom_call_target="tpu_custom_call" | custom-call | flops 2684354560 | bytes 7340032 | tf_op jit(solution)/shard_map/pallas_call | solution.py:199
  249.0 5.7 %collective-permute-done.9.x_other = bf16[512,1024]{1,0:T(8,128)(2,1)S(1)} collective-permute-done((bf16[512,1024]{1,0:T(8,128)(2,1)S(1)}, bf16[512,1024]{1,0:T(8,128)(2,1)S(1)}, u32[]{:S(2)}, u32[]{:S(2)}) %collective-permute-start.9) | collective-permute-done | bytes 1048608 | tf_op jit(solution)/shard_map/ppermute | solution.py:642
  259.2 10.3 %shard_map.271 = bf16[4,1024,512]{2,1,0:T(8,128)(2,1)} custom-call(s32[2]{0:T(128)} %pad_add_fusion.where, bf16[512,1024]{1,0:T(8,128)(2,1)} %bitcast.92, bf16[512,1024]{1,0:T(8,128)(2,1)} %copy-done.4, bf16[512,1024]{1,0:T(8,128)(2,1)} %get-tuple-element.32.context.c, bf16[512,1024]{1,0:T(8,128)(2,1)} %copy-done.5, ...), custom_call_target="tpu_custom_call" | custom-call | flops 4294967296 | bytes 12582912 | tf_op jit(solution)/shard_map/pallas_call | solution.py:595
  271.0 7.3 %collective-permute-done.22.low_other = bf16[512,1024]{1,0:T(8,128)(2,1)S(1)} collective-permute-done((bf16[512,1024]{1,0:T(8,128)(2,1)S(1)}, bf16[512,1024]{1,0:T(8,128)(2,1)S(1)}, u32[]{:S(2)}, u32[]{:S(2)}) %collective-permute-start.22) | collective-permute-done | bytes 1048608 | tf_op jit(solution)/shard_map/ppermute | solution.py:642
  279.3 9.5 %shard_map.273 = bf16[4096,512]{1,0:T(8,128)(2,1)} custom-call(s32[2]{0:T(128)} %pad_add_fusion.where, bf16[512,4096]{1,0:T(8,128)(2,1)} %get-tuple-element.34.act, bf16[512,4096]{1,0:T(8,128)(2,1)} %collective-permute-done.21.act_other, bf16[512,1024]{1,0:T(8,128)(2,1)} %get-tuple-element.37.low, bf16[512,1024]{1,0:T(8,128)(2,1)} %copy-done.12), custom_call_target="tpu_custom_call" | custom-call | flops 4294967296 | bytes 12582912 | tf_op jit(solution)/shard_map/pallas_call | solution.py:524
  290.5 7.5 %collective-permute-done.16.x_other = bf16[512,1024]{1,0:T(8,128)(2,1)S(1)} collective-permute-done((bf16[512,1024]{1,0:T(8,128)(2,1)S(1)}, bf16[512,1024]{1,0:T(8,128)(2,1)S(1)}, u32[]{:S(2)}, u32[]{:S(2)}) %collective-permute-start.16) | collective-permute-done | bytes 1048608 | tf_op jit(solution)/shard_map/ppermute | solution.py:642
  298.9 9.2 %shard_map.272 = bf16[4,1024,512]{2,1,0:T(8,128)(2,1)} custom-call(s32[2]{0:T(128)} %pad_add_fusion.where, bf16[512,1024]{1,0:T(8,128)(2,1)} %get-tuple-element.33.x, bf16[512,1024]{1,0:T(8,128)(2,1)} %copy-done.13, bf16[512,4096]{1,0:T(8,128)(2,1)} %get-tuple-element.49.grad, bf16[512,4096]{1,0:T(8,128)(2,1)} %collective-permute-done.17.grad_other), custom_call_target="tpu_custom_call" | custom-call | flops 4294967296 | bytes 8388608 | tf_op jit(solution)/shard_map/pallas_call | solution.py:549
  308.1 13.8 %reduce-scatter.4.cloned.1.call-done = bf16[1024,512]{1,0:T(8,128)(2,1)} async-done(((bf16[4096,512]{1,0:T(8,128)(2,1)}), bf16[1024,512]{1,0:T(8,128)(2,1)}) %reduce-scatter.4.cloned.1.call-update) | async-done | bytes 1048592 | tf_op jit(solution)/shard_map/reduce_scatter | solution.py:713
  330.3 11.8 %collective-permute-done.14 = bf16[256,512]{1,0:T(8,128)(2,1)S(1)} collective-permute-done((bf16[256,512]{1,0:T(8,128)(2,1)S(1)}, bf16[256,512]{1,0:T(8,128)(2,1)S(1)}, u32[]{:S(2)}, u32[]{:S(2)}) %collective-permute-start.14) | collective-permute-done | bytes 262176 | tf_op jit(solution)/shard_map/ppermute | solution.py:639
  342.1 5.6 %collective-permute-done.13 = bf16[256,512]{1,0:T(8,128)(2,1)S(1)} collective-permute-done((bf16[256,512]{1,0:T(8,128)(2,1)S(1)}, bf16[256,512]{1,0:T(8,128)(2,1)S(1)}, u32[]{:S(2)}, u32[]{:S(2)}) %collective-permute-start.13) | collective-permute-done | bytes 262176 | tf_op jit(solution)/shard_map/ppermute | solution.py:639
  349.6 28.2 %reduce-scatter.8.cloned.1.call-done = bf16[4,256,512]{2,1,0:T(8,128)(2,1)} async-done(((bf16[4,1024,512]{2,1,0:T(8,128)(2,1)}), bf16[4,256,512]{2,1,0:T(8,128)(2,1)}) %reduce-scatter.8.cloned.1.call-update) | async-done | bytes 1048592 | tf_op jit(solution)/shard_map/reduce_scatter | solution.py:721
  386.2 11.8 %collective-permute-done.24 = bf16[256,512]{1,0:T(8,128)(2,1)S(1)} collective-permute-done((bf16[256,512]{1,0:T(8,128)(2,1)S(1)}, bf16[256,512]{1,0:T(8,128)(2,1)S(1)}, u32[]{:S(2)}, u32[]{:S(2)}) %collective-permute-start.24) | collective-permute-done | bytes 262176 | tf_op jit(solution)/shard_map/ppermute | solution.py:639
  398.0 5.6 %collective-permute-done.23 = bf16[256,512]{1,0:T(8,128)(2,1)S(1)} collective-permute-done((bf16[256,512]{1,0:T(8,128)(2,1)S(1)}, bf16[256,512]{1,0:T(8,128)(2,1)S(1)}, u32[]{:S(2)}, u32[]{:S(2)}) %collective-permute-start.23) | collective-permute-done | bytes 262176 | tf_op jit(solution)/shard_map/ppermute | solution.py:639
  405.5 28.4 %reduce-scatter.6.cloned.1.call-done = bf16[1024,512]{1,0:T(8,128)(2,1)} async-done(((bf16[4096,512]{1,0:T(8,128)(2,1)}), bf16[1024,512]{1,0:T(8,128)(2,1)}) %reduce-scatter.6.cloned.1.call-update) | async-done | bytes 1048592 | tf_op jit(solution)/shard_map/reduce_scatter | solution.py:713
  442.2 11.9 %collective-permute-done.19 = bf16[256,512]{1,0:T(8,128)(2,1)S(1)} collective-permute-done((bf16[256,512]{1,0:T(8,128)(2,1)S(1)}, bf16[256,512]{1,0:T(8,128)(2,1)S(1)}, u32[]{:S(2)}, u32[]{:S(2)}) %collective-permute-start.19) | collective-permute-done | bytes 262176 | tf_op jit(solution)/shard_map/ppermute | solution.py:639
  454.1 5.6 %collective-permute-done.18 = bf16[256,512]{1,0:T(8,128)(2,1)S(1)} collective-permute-done((bf16[256,512]{1,0:T(8,128)(2,1)S(1)}, bf16[256,512]{1,0:T(8,128)(2,1)S(1)}, u32[]{:S(2)}, u32[]{:S(2)}) %collective-permute-start.18) | collective-permute-done | bytes 262176 | tf_op jit(solution)/shard_map/ppermute | solution.py:639
  464.8 39.1 %psum.7 = f32[4,3072]{1,0:T(4,128)S(1)} all-reduce(f32[4,3072]{1,0:T(4,128)S(1)} %constant_dynamic-update-slice_fusion), channel_id=1, replica_groups=mesh['chip'=4,'core'=2,'shard'=4] {'chip','core','shard'}, use_global_device_ids=true, to_apply=%region_1.2 | all-reduce | flops 12288 | bytes 98304 | tf_op jit(solution)/shard_map/psum | solution.py:777
  505.8 9.5 %shard_map.270 = f32[512,1024]{1,0:T(8,128)} custom-call(s32[2]{0:T(128)} %pad_add_fusion.where, bf16[3,512,1024]{2,1,0:T(8,128)(2,1)} %get-tuple-element.42.grad.g, f32[512,1024]{1,0:T(8,128)} %get-tuple-element.43.first, bf16[256,3072]{1,0:T(8,128)(2,1)} %own.9, bf16[768,4096]{1,0:T(8,128)(2,1)} %all-gather.8.cloned.1.call-done.rest.rest_out), custom_call_target="tpu_custom_call" | custom-call | flops 3221225472 | bytes 13631488 | tf_op jit(solution)/shard_map/pallas_call | solution.py:499
  526.8 4.1 convert_element_type.165
  (171 shorter events, 97.2 us)
Async XLA Ops:
  7.2 98.2 %all-gather.8.cloned.1.call-start = ((), (), s32[]{:S(2)}) async-start(), calls=%async_computation.3 | async-start | bytes 7077888 | tf_op jit(solution)/shard_map/all_gather | solution.py:663
  15.1 7.6 %collective-permute-start.2 = (bf16[272,512]{1,0:T(8,128)(2,1)S(1)}, bf16[272,512]{1,0:T(8,128)(2,1)S(1)}, u32[]{:S(2)}, u32[]{:S(2)}) collective-permute-start(bf16[272,512]{1,0:T(8,128)(2,1)S(1)} %pad_maximum_fusion.3), channel_id=1, source_target_pairs={{0,1},{1,2},{2,3},{3,0},{4,5},{5,6},{6,7},{7,4},{8,9},{9,10},{10,1... | collective-permute-start | bytes 835592 | tf_op jit(solution)/shard_map/ppermute | solution.py:636
  16.4 23.2 %collective-permute-start.1 = (bf16[272,512]{1,0:T(8,128)(2,1)S(1)}, bf16[272,512]{1,0:T(8,128)(2,1)S(1)}, u32[]{:S(2)}, u32[]{:S(2)}) collective-permute-start(bf16[272,512]{1,0:T(8,128)(2,1)S(1)} %pad_maximum_fusion.3), channel_id=1, source_target_pairs={{0,2},{1,3},{2,0},{3,1},{4,6},{5,7},{6,4},{7,5},{8,10},{9,11},{10,... | collective-permute-start | bytes 835592 | tf_op jit(solution)/shard_map/ppermute | solution.py:636
  17.5 25.0 %collective-permute-start = (bf16[272,512]{1,0:T(8,128)(2,1)S(1)}, bf16[272,512]{1,0:T(8,128)(2,1)S(1)}, u32[]{:S(2)}, u32[]{:S(2)}) collective-permute-start(bf16[272,512]{1,0:T(8,128)(2,1)S(1)} %pad_maximum_fusion.3), channel_id=1, source_target_pairs={{0,3},{1,0},{2,1},{3,2},{4,7},{5,4},{6,5},{7,6},{8,11},{9,8},{10,9... | collective-permute-start | bytes 835592 | tf_op jit(solution)/shard_map/ppermute | solution.py:636
  43.5 96.4 %all-gather.10.cloned.1.call-start = ((), (), s32[]{:S(2)}) async-start(), calls=%async_computation.4 | async-start | bytes 7077888 | tf_op jit(solution)/shard_map/all_gather | solution.py:666
  44.5 7.4 %collective-permute-start.5 = (bf16[256,512]{1,0:T(8,128)(2,1)S(1)}, bf16[256,512]{1,0:T(8,128)(2,1)S(1)}, u32[]{:S(2)}, u32[]{:S(2)}) collective-permute-start(bf16[256,512]{1,0:T(8,128)(2,1)S(1)} %constant_dynamic-slice_fusion.2), channel_id=1, source_target_pairs={{0,1},{1,2},{2,3},{3,0},{4,5},{5,6},{6,7},{7,4},{8,9},{9,10},{10,1... | collective-permute-start | bytes 786440 | tf_op jit(solution)/shard_map/ppermute | solution.py:636
  44.6 22.3 %collective-permute-start.4 = (bf16[256,512]{1,0:T(8,128)(2,1)S(1)}, bf16[256,512]{1,0:T(8,128)(2,1)S(1)}, u32[]{:S(2)}, u32[]{:S(2)}) collective-permute-start(bf16[256,512]{1,0:T(8,128)(2,1)S(1)} %constant_dynamic-slice_fusion.2), channel_id=1, source_target_pairs={{0,2},{1,3},{2,0},{3,1},{4,6},{5,7},{6,4},{7,5},{8,10},{9,11},{10,... | collective-permute-start | bytes 786440 | tf_op jit(solution)/shard_map/ppermute | solution.py:636
  44.9 23.6 %collective-permute-start.3 = (bf16[256,512]{1,0:T(8,128)(2,1)S(1)}, bf16[256,512]{1,0:T(8,128)(2,1)S(1)}, u32[]{:S(2)}, u32[]{:S(2)}) collective-permute-start(bf16[256,512]{1,0:T(8,128)(2,1)S(1)} %constant_dynamic-slice_fusion.2), channel_id=1, source_target_pairs={{0,3},{1,0},{2,1},{3,2},{4,7},{5,4},{6,5},{7,6},{8,11},{9,8},{10,9... | collective-permute-start | bytes 786440 | tf_op jit(solution)/shard_map/ppermute | solution.py:636
  69.5 117.9 %all-gather.12.cloned.1.call-start = ((), (), s32[]{:S(2)}) async-start(), calls=%async_computation.5 | async-start | bytes 7077888 | tf_op jit(solution)/shard_map/all_gather | solution.py:667
  70.5 7.5 %collective-permute-start.8 = (bf16[128,1024]{1,0:T(8,128)(2,1)S(1)}, bf16[128,1024]{1,0:T(8,128)(2,1)S(1)}, u32[]{:S(2)}, u32[]{:S(2)}) collective-permute-start(bf16[128,1024]{1,0:T(8,128)(2,1)S(1)} %constant_dynamic-slice_fusion.1), channel_id=1, source_target_pairs={{0,1},{1,2},{2,3},{3,0},{4,5},{5,6},{6,7},{7,4},{8,9},{9,10},{10,1... | collective-permute-start | bytes 786440 | tf_op jit(solution)/shard_map/ppermute | solution.py:636
  70.6 22.3 %collective-permute-start.7 = (bf16[128,1024]{1,0:T(8,128)(2,1)S(1)}, bf16[128,1024]{1,0:T(8,128)(2,1)S(1)}, u32[]{:S(2)}, u32[]{:S(2)}) collective-permute-start(bf16[128,1024]{1,0:T(8,128)(2,1)S(1)} %constant_dynamic-slice_fusion.1), channel_id=1, source_target_pairs={{0,2},{1,3},{2,0},{3,1},{4,6},{5,7},{6,4},{7,5},{8,10},{9,11},{10,... | collective-permute-start | bytes 786440 | tf_op jit(solution)/shard_map/ppermute | solution.py:636
  72.2 23.6 %collective-permute-start.6 = (bf16[128,1024]{1,0:T(8,128)(2,1)S(1)}, bf16[128,1024]{1,0:T(8,128)(2,1)S(1)}, u32[]{:S(2)}, u32[]{:S(2)}) collective-permute-start(bf16[128,1024]{1,0:T(8,128)(2,1)S(1)} %constant_dynamic-slice_fusion.1), channel_id=1, source_target_pairs={{0,3},{1,0},{2,1},{3,2},{4,7},{5,4},{6,5},{7,6},{8,11},{9,8},{10,9... | collective-permute-start | bytes 786440 | tf_op jit(solution)/shard_map/ppermute | solution.py:636
  96.8 225.2 %reduce-scatter.4.cloned.1.call-start = ((), (), s32[]{:S(2)}) async-start(), calls=%async_computation.6 | async-start | bytes 5242880 | tf_op jit(solution)/shard_map/reduce_scatter | solution.py:713
  248.0 11.2 %collective-permute-start.11 = (bf16[3,512,1024]{2,1,0:T(8,128)(2,1)}, bf16[3,512,1024]{2,1,0:T(8,128)(2,1)}, u32[]{:S(2)}, u32[]{:S(2)}) collective-permute-start(bf16[3,512,1024]{2,1,0:T(8,128)(2,1)} %get-tuple-element.42.grad.g), channel_id=1, source_target_pairs={{0,4},{4,0},{1,5},{5,1},{2,6},{6,2},{3,7},{7,3},{8,12},{12,8},{9,1... | collective-permute-start | bytes 9437192 | tf_op jit(solution)/shard_map/ppermute | solution.py:642
  248.5 8.1 %collective-permute-start.10 = (bf16[512,1024]{1,0:T(8,128)(2,1)S(1)}, bf16[512,1024]{1,0:T(8,128)(2,1)S(1)}, u32[]{:S(2)}, u32[]{:S(2)}) collective-permute-start(bf16[512,1024]{1,0:T(8,128)(2,1)S(1)} %copy-done.2), channel_id=1, source_target_pairs={{0,4},{4,0},{1,5},{5,1},{2,6},{6,2},{3,7},{7,3},{8,12},{12,8},{9,1... | collective-permute-start | bytes 3145736 | tf_op jit(solution)/shard_map/ppermute | solution.py:642
  248.8 9.4 %collective-permute-start.12 = (bf16[512,1024]{1,0:T(8,128)(2,1)S(1)}, bf16[512,1024]{1,0:T(8,128)(2,1)S(1)}, u32[]{:S(2)}, u32[]{:S(2)}) collective-permute-start(bf16[512,1024]{1,0:T(8,128)(2,1)S(1)} %copy-done.3), channel_id=1, source_target_pairs={{0,4},{4,0},{1,5},{5,1},{2,6},{6,2},{3,7},{7,3},{8,12},{12,8},{9,1... | collective-permute-start | bytes 3145736 | tf_op jit(solution)/shard_map/ppermute | solution.py:642
  269.5 108.2 %reduce-scatter.8.cloned.1.call-start = ((), (), s32[]{:S(2)}) async-start(), calls=%async_computation.10 | async-start | bytes 5242880 | tf_op jit(solution)/shard_map/reduce_scatter | solution.py:721
  269.6 8.7 %collective-permute-start.21 = (bf16[512,4096]{1,0:T(8,128)(2,1)}, bf16[512,4096]{1,0:T(8,128)(2,1)}, u32[]{:S(2)}, u32[]{:S(2)}) collective-permute-start(bf16[512,4096]{1,0:T(8,128)(2,1)} %get-tuple-element.34.act), channel_id=1, source_target_pairs={{0,4},{4,0},{1,5},{5,1},{2,6},{6,2},{3,7},{7,3},{8,12},{12,8},{9,1... | collective-permute-start | bytes 12582920 | tf_op jit(solution)/shard_map/ppermute | solution.py:642
  270.7 7.6 %collective-permute-start.22 = (bf16[512,1024]{1,0:T(8,128)(2,1)S(1)}, bf16[512,1024]{1,0:T(8,128)(2,1)S(1)}, u32[]{:S(2)}, u32[]{:S(2)}) collective-permute-start(bf16[512,1024]{1,0:T(8,128)(2,1)S(1)} %copy-done.11), channel_id=1, source_target_pairs={{0,4},{4,0},{1,5},{5,1},{2,6},{6,2},{3,7},{7,3},{8,12},{12,8},{9,1... | collective-permute-start | bytes 3145736 | tf_op jit(solution)/shard_map/ppermute | solution.py:642
  288.8 145.1 %reduce-scatter.6.cloned.1.call-start = ((), (), s32[]{:S(2)}) async-start(), calls=%async_computation.8 | async-start | bytes 5242880 | tf_op jit(solution)/shard_map/reduce_scatter | solution.py:713
  289.1 8.8 %collective-permute-start.17 = (bf16[512,4096]{1,0:T(8,128)(2,1)}, bf16[512,4096]{1,0:T(8,128)(2,1)}, u32[]{:S(2)}, u32[]{:S(2)}) collective-permute-start(bf16[512,4096]{1,0:T(8,128)(2,1)} %get-tuple-element.49.grad), channel_id=1, source_target_pairs={{0,4},{4,0},{1,5},{5,1},{2,6},{6,2},{3,7},{7,3},{8,12},{12,8},{9,1... | collective-permute-start | bytes 12582920 | tf_op jit(solution)/shard_map/ppermute | solution.py:642
  290.0 7.9 %collective-permute-start.16 = (bf16[512,1024]{1,0:T(8,128)(2,1)S(1)}, bf16[512,1024]{1,0:T(8,128)(2,1)S(1)}, u32[]{:S(2)}, u32[]{:S(2)}) collective-permute-start(bf16[512,1024]{1,0:T(8,128)(2,1)S(1)} %copy-done.10), channel_id=1, source_target_pairs={{0,4},{4,0},{1,5},{5,1},{2,6},{6,2},{3,7},{7,3},{8,12},{12,8},{9,1... | collective-permute-start | bytes 3145736 | tf_op jit(solution)/shard_map/ppermute | solution.py:642
  308.1 207.3 %all-gather.14.cloned.1.call-start = ((), (), s32[]{:S(2)}) async-start(), calls=%async_computation.7 | async-start | bytes 2359296 | tf_op jit(solution)/shard_map/all_gather | solution.py:715
  323.1 7.2 %collective-permute-start.15 = (bf16[256,512]{1,0:T(8,128)(2,1)S(1)}, bf16[256,512]{1,0:T(8,128)(2,1)S(1)}, u32[]{:S(2)}, u32[]{:S(2)}) collective-permute-start(bf16[256,512]{1,0:T(8,128)(2,1)S(1)} %get-tuple-element.65), channel_id=1, source_target_pairs={{0,3},{1,0},{2,1},{3,2},{4,7},{5,4},{6,5},{7,6},{8,11},{9,8},{10,9... | collective-permute-start | bytes 786440 | tf_op jit(solution)/shard_map/ppermute | solution.py:639
  323.4 18.7 %collective-permute-start.14 = (bf16[256,512]{1,0:T(8,128)(2,1)S(1)}, bf16[256,512]{1,0:T(8,128)(2,1)S(1)}, u32[]{:S(2)}, u32[]{:S(2)}) collective-permute-start(bf16[256,512]{1,0:T(8,128)(2,1)S(1)} %get-tuple-element.66), channel_id=1, source_target_pairs={{0,2},{1,3},{2,0},{3,1},{4,6},{5,7},{6,4},{7,5},{8,10},{9,11},{10,... | collective-permute-start | bytes 786440 | tf_op jit(solution)/shard_map/ppermute | solution.py:639
  325.5 22.2 %collective-permute-start.13 = (bf16[256,512]{1,0:T(8,128)(2,1)S(1)}, bf16[256,512]{1,0:T(8,128)(2,1)S(1)}, u32[]{:S(2)}, u32[]{:S(2)}) collective-permute-start(bf16[256,512]{1,0:T(8,128)(2,1)S(1)} %get-tuple-element.64), channel_id=1, source_target_pairs={{0,1},{1,2},{2,3},{3,0},{4,5},{5,6},{6,7},{7,4},{8,9},{9,10},{10,1... | collective-permute-start | bytes 786440 | tf_op jit(solution)/shard_map/ppermute | solution.py:639
  349.6 170.5 %all-gather.18.cloned.1.call-start = ((), (), s32[]{:S(2)}) async-start(), calls=%async_computation.11 | async-start | bytes 2359296 | tf_op jit(solution)/shard_map/all_gather | solution.py:724
  379.3 18.8 %collective-permute-start.24 = (bf16[256,512]{1,0:T(8,128)(2,1)S(1)}, bf16[256,512]{1,0:T(8,128)(2,1)S(1)}, u32[]{:S(2)}, u32[]{:S(2)}) collective-permute-start(bf16[256,512]{1,0:T(8,128)(2,1)S(1)} %get-tuple-element.60), channel_id=1, source_target_pairs={{0,2},{1,3},{2,0},{3,1},{4,6},{5,7},{6,4},{7,5},{8,10},{9,11},{10,... | collective-permute-start | bytes 786440 | tf_op jit(solution)/shard_map/ppermute | solution.py:639
  381.4 22.2 %collective-permute-start.23 = (bf16[256,512]{1,0:T(8,128)(2,1)S(1)}, bf16[256,512]{1,0:T(8,128)(2,1)S(1)}, u32[]{:S(2)}, u32[]{:S(2)}) collective-permute-start(bf16[256,512]{1,0:T(8,128)(2,1)S(1)} %get-tuple-element.58), channel_id=1, source_target_pairs={{0,1},{1,2},{2,3},{3,0},{4,5},{5,6},{6,7},{7,4},{8,9},{9,10},{10,1... | collective-permute-start | bytes 786440 | tf_op jit(solution)/shard_map/ppermute | solution.py:639
  405.4 121.4 %all-gather.16.cloned.1.call-start = ((), (), s32[]{:S(2)}) async-start(), calls=%async_computation.9 | async-start | bytes 2359296 | tf_op jit(solution)/shard_map/all_gather | solution.py:715
  435.4 18.8 %collective-permute-start.19 = (bf16[256,512]{1,0:T(8,128)(2,1)S(1)}, bf16[256,512]{1,0:T(8,128)(2,1)S(1)}, u32[]{:S(2)}, u32[]{:S(2)}) collective-permute-start(bf16[256,512]{1,0:T(8,128)(2,1)S(1)} %get-tuple-element.63), channel_id=1, source_target_pairs={{0,2},{1,3},{2,0},{3,1},{4,6},{5,7},{6,4},{7,5},{8,10},{9,11},{10,... | collective-permute-start | bytes 786440 | tf_op jit(solution)/shard_map/ppermute | solution.py:639
  437.5 22.2 %collective-permute-start.18 = (bf16[256,512]{1,0:T(8,128)(2,1)S(1)}, bf16[256,512]{1,0:T(8,128)(2,1)S(1)}, u32[]{:S(2)}, u32[]{:S(2)}) collective-permute-start(bf16[256,512]{1,0:T(8,128)(2,1)S(1)} %get-tuple-element.61), channel_id=1, source_target_pairs={{0,1},{1,2},{2,3},{3,0},{4,5},{5,6},{6,7},{7,4},{8,9},{9,10},{10,1... | collective-permute-start | bytes 786440 | tf_op jit(solution)/shard_map/ppermute | solution.py:639
  (17 other events, 293.5 us)
Sparse Core Ops, SparseCore 0:
  43.6 47.0 all-gather.7
  93.2 46.6 all-gather.9
  141.8 45.5 all-gather.11
  269.7 52.2 reduce-scatter.3
  325.0 52.6 reduce-scatter.7
  381.2 52.6 reduce-scatter.5
  436.5 28.6 all-gather.13
  467.2 28.0 all-gather.17
  497.9 28.1 all-gather.15

commit v3 on v2

v3 whole, which is shorter than its diff:
```python
from functools import partial

import jax
import jax.numpy as jnp
from jax import lax
from jax.experimental import pallas as pl
from jax.experimental.pallas import tpu as pltpu
from jax.sharding import Mesh
from jax.sharding import PartitionSpec as P

HEAD_DIM = 64
REP = ("chip", "core")
ALL = ("chip", "core", "shard")
F32 = jnp.float32
BF16 = jnp.bfloat16
MIB = 1024 * 1024
HINT = 3690000


def dot(left, right):
    return jnp.dot(left, right, preferred_element_type=F32)


def dot_t(left, right):
    return lax.dot_general(left, right, (((1,), (1,)), ((), ())), preferred_element_type=F32)


def t_dot(left, right):
    return lax.dot_general(left, right, (((0,), (0,)), ((), ())), preferred_element_type=F32)


def call(body, grid, ins, outs, out_shape, scratch=(), micros=1, limit=63, aliases=None):
    return pl.pallas_call(
        body,
        grid_spec=pltpu.PrefetchScalarGridSpec(
            num_scalar_prefetch=1,
            grid=grid,
            in_specs=ins,
            out_specs=outs,
            scratch_shapes=list(scratch),
        ),
        out_shape=out_shape,
        compiler_params=pltpu.CompilerParams(
            dimension_semantics=("arbitrary",) * len(grid), vmem_limit_bytes=limit * MIB
        ),
        input_output_aliases=aliases or {},
        cost_estimate=pl.CostEstimate(
            flops=0, bytes_accessed=int(micros * HINT), transcendentals=0
        ),
    )


def spec(shape, index):
    return pl.BlockSpec(shape, index)


def fixed(shape):
    zeros = (0,) * len(shape)
    return pl.BlockSpec(shape, lambda *_: zeros)


def struct(shape, dtype):
    return jax.ShapeDtypeStruct(shape, dtype)


def natural(where, step, group):
    return lax.rem(where[0] + step, group)


def block_of(where, unit, chips):
    return 2 * where[2 + unit] + jnp.where(unit < chips, where[1], 1 - where[1])


def part_specs(parts, first=0):
    half, steps, rows, columns = parts[0].shape

    def given(index):
        return spec(
            (1, steps, rows, columns),
            lambda u, w: (jnp.clip(u - first - index * half, 0, half - 1), 0, 0, 0),
        )

    return [given(index) for index in range(4)]


def load_weight(unit, half, own, parts, weight):
    rows = own.shape[0]
    weight[:rows, :] = own[...]
    for index, part in enumerate(parts):

        @pl.when(unit // half == index)
        def _(part=part):
            weight[rows:, :] = part[0].reshape(-1, part.shape[3])


def normalise(hidden):
    average = jnp.mean(hidden, axis=-1, keepdims=True)
    centred = hidden - average
    variance = jnp.mean(centred * centred, axis=-1, keepdims=True)
    inverse = lax.rsqrt(variance + 1e-06)
    return centred * inverse, inverse


def normalise_back(grad, unit, inverse, gain):
    scaled = grad * gain
    first = jnp.mean(scaled, axis=-1, keepdims=True)
    second = jnp.mean(scaled * unit, axis=-1, keepdims=True)
    return inverse * (scaled - first - unit * second)


def rows_sum(value):
    return jnp.sum(value, axis=0, keepdims=True)


def roll_into(rolled, x, where, rows, group):
    for s in range(group):
        start = pl.multiple_of(natural(where, s, group) * rows, 128)
        rolled[:, s * rows : (s + 1) * rows] = x[:, pl.ds(start, rows)]


def qkv_kernel(dims, where, x, own, a, b, c, d, bias, out, rest_out, rolled, weight):
    group, half, qkv_width = dims
    unit = pl.program_id(0)
    rows, columns = own.shape

    @pl.when(unit == 0)
    def _():
        roll_into(rolled, x, where, rows, group)

    load_weight(unit, half, own, (a, b, c, d), weight)
    start = block_of(where, unit, 2 * half) * columns

    @pl.when(start < qkv_width)
    def _():
        out[...] = (dot(rolled[...], weight[...]) + bias[...]).astype(BF16)

    @pl.when(start >= qkv_width)
    def _():
        place = pl.ds(pl.multiple_of(start - qkv_width, 128), columns)
        rest_out[:, place] = weight[rows:, :]


def qkv(where, x, w_qkv, parts, bias, group):
    seq, width = x.shape
    rows, qkv_width = w_qkv.shape
    half, _, _, block = parts[0].shape
    chips = 2 * half
    total = 2 * chips * block
    top = qkv_width // block - 1
    return call(
        partial(qkv_kernel, (group, half, qkv_width)),
        (2 * chips,),
        [
            fixed((seq, width)),
            spec((rows, block), lambda u, w: (0, jnp.minimum(block_of(w, u, chips), top))),
        ]
        + part_specs(parts)
        + [spec((1, block), lambda u, w: (0, block_of(w, u, chips)))],
        [
            spec((seq, block), lambda u, w: (0, block_of(w, u, chips))),
            fixed((width - rows, total - qkv_width)),
        ],
        [struct((seq, total), BF16), struct((width - rows, total - qkv_width), BF16)],
        [pltpu.VMEM((seq, width), BF16), pltpu.VMEM((width, block), BF16)],
        micros=12,
    )(where, x, w_qkv, *parts, bias)


def attend_kernel(first, where, q, k, v, x, column, row, *refs):
    out, turned, log_totals, bias = refs[-4:]
    step = pl.program_id(0)
    turned[0] = x[...].T

    @pl.when(step == 0)
    def _():
        bias[...] = jnp.where(column[...] == row[...], 0.0, -1e30)
        log_totals[...] = jnp.zeros_like(log_totals)

    lanes = lax.broadcasted_iota(jnp.int32, (1, 128), 1)
    heads = q.shape[1] // HEAD_DIM
    for h in range(heads):
        part = slice(h * HEAD_DIM, (h + 1) * HEAD_DIM)
        scores = dot_t(q[:, part] * BF16(HEAD_DIM**-0.5), k[:, part]) + bias[...]
        maxima = jnp.max(scores, axis=1, keepdims=True)
        expo = jnp.exp(scores - maxima)
        totals = jnp.sum(expo, axis=1, keepdims=True)
        probs = (expo * (1.0 / totals)).astype(BF16)
        out[:, part] = dot(probs, v[:, part]).astype(BF16)
        log_totals[...] = jnp.where(
            lanes == (first + step) * heads + h, maxima + jnp.log(totals), log_totals[...]
        )
    turned[1] = out[...].T


def attention(where, projected, x, column, row, first, count, before=()):
    seq, width = x.shape
    block = 2 * HEAD_DIM
    each = width // block
    anywhere = pl.BlockSpec(memory_space=pl.ANY)
    return call(
        partial(attend_kernel, first),
        (count,),
        [
            spec((seq, block), lambda h, w: (0, first + h)),
            spec((seq, block), lambda h, w: (0, each + first + h)),
            spec((seq, block), lambda h, w: (0, 2 * each + first + h)),
            spec((seq, block), lambda h, w: (0, first + h)),
            fixed((seq, 1)),
            fixed((1, seq)),
        ]
        + [anywhere] * len(before),
        [
            spec((seq, block), lambda h, w: (0, first + h)),
            spec((2, block, seq), lambda h, w: (0, first + h, 0)),
            fixed((seq, 128)),
        ],
        [
            struct((seq, width), BF16),
            struct((2, width, seq), BF16),
            struct((seq, 128), F32),
        ],
        [pltpu.VMEM((seq, seq), F32)],
        micros=11,
        aliases={7: 0, 8: 1} if before else None,
    )(where, projected, projected, projected, x, column, row, *before)


def attend_back_kernel(dims, where, q, k, v, grad, logs_a, logs_b, attn, column, row, *refs):
    out, sums, bias = refs
    mine, per = dims
    step = pl.program_id(0)
    pair = pair_of(where, step, mine, per)
    out[3] = attn[...]

    @pl.when(step == 0)
    def _():
        bias[...] = jnp.where(column[...] == row[...], 0.0, -1e30)

    lanes = lax.broadcasted_iota(jnp.int32, (1, 128), 1)
    heads = q.shape[1] // HEAD_DIM
    for h in range(heads):
        part = slice(h * HEAD_DIM, (h + 1) * HEAD_DIM)
        picked = jnp.where(lanes == pair * heads + h, logs_a[...] + logs_b[...], 0.0)
        logs = jnp.sum(picked, axis=1, keepdims=True)
        query = q[:, part] * BF16(HEAD_DIM**-0.5)
        scores = dot_t(query, k[:, part]) + bias[...]
        probs = jnp.exp(scores - logs)
        grad_probs = dot_t(grad[:, part], v[:, part])
        weighted = probs * grad_probs
        low = (weighted - probs * jnp.sum(weighted, axis=1, keepdims=True)).astype(BF16)
        grad_q = (dot(low, k[:, part]) * (HEAD_DIM**-0.5)).astype(BF16)
        grad_k = t_dot(low, query).astype(BF16)
        grad_v = t_dot(probs.astype(BF16), grad[:, part]).astype(BF16)
        for m, value in enumerate((grad_q, grad_k, grad_v)):
            out[m, :, part] = value
            sums[m, :, part] = rows_sum(value.astype(F32))


def pair_of(where, step, mine, per):
    parity = where[1] if mine else 1 - where[1]
    return (2 * (step // per) + parity) * per + lax.rem(step, per)


def attention_back(where, projected, grad, logs, attn, column, row, mine, part):
    seq, width = grad.shape
    block = 2 * HEAD_DIM
    each = width // block
    per = part // block

    def pairs(first):
        return spec((seq, block), lambda h, w: (0, first + pair_of(w, h, mine, per)))

    return call(
        partial(attend_back_kernel, (mine, per)),
        (each // 2,),
        [
            pairs(0),
            pairs(each),
            pairs(2 * each),
            pairs(0),
            fixed((seq, 128)),
            fixed((seq, 128)),
            pairs(0),
            fixed((seq, 1)),
            fixed((1, seq)),
        ],
        [
            spec((4, seq, block), lambda h, w: (0, 0, h)),
            spec((3, 1, block), lambda h, w: (0, 0, h)),
        ],
        [struct((4, seq, width // 2), BF16), struct((3, 1, width // 2), F32)],
        [pltpu.VMEM((seq, seq), F32)],
        micros=13,
    )(where, projected, projected, projected, grad, *logs, attn, column, row)


def out_kernel(group, where, context, x, own, rest, bias, gain, shift, hidden, low, turned):
    rows = own.shape[0]
    total = bias[...] + x[...].astype(F32)
    for s in range(group):
        start = pl.multiple_of(natural(where, s, group) * rows, 128)
        weight = own[...] if s == 0 else rest[(s - 1) * rows : s * rows, :]
        total = total + dot(context[:, pl.ds(start, rows)], weight)
    hidden[...] = total
    unit, _ = normalise(total)
    value = (unit * gain[...] + shift[...]).astype(BF16)
    low[...] = value
    turned[...] = value.T


def out_norm(where, context, x, w_out, rest_out, bias, gain, shift, group):
    seq, width = x.shape
    rows = w_out.shape[0]
    block = seq // 2
    vector = fixed((1, width))
    return call(
        partial(out_kernel, group),
        (seq // block,),
        [
            spec((block, width), lambda i, w: (i, 0)),
            spec((block, width), lambda i, w: (i, 0)),
            fixed((rows, width)),
            fixed((width - rows, width)),
            vector,
            vector,
            vector,
        ],
        [spec((block, width), lambda i, w: (i, 0))] * 2
        + [spec((width, block), lambda i, w: (0, i))],
        [
            struct((seq, width), F32),
            struct((seq, width), BF16),
            struct((width, seq), BF16),
        ],
        micros=6,
    )(where, context, x, w_out, rest_out, bias, gain, shift)


def inner_kernel(dims, where, x, own, a, b, c, d, bias, act, turned, slope, rolled, weight):
    group, half = dims
    unit = pl.program_id(0)

    @pl.when(unit == 0)
    def _():
        roll_into(rolled, x, where, own.shape[0], group)

    load_weight(unit, half, own, (a, b, c, d), weight)
    total = dot(rolled[...], weight[...]) + bias[...]
    below = 0.5 + 0.5 * lax.erf(total * (0.5**0.5))
    value = (total * below).astype(BF16)
    act[...] = value
    turned[...] = value.T
    density = jnp.exp(-0.5 * total * total) * ((2.0 * jnp.pi) ** -0.5)
    slope[...] = (below + total * density).astype(BF16)


def inner(where, x, w_in, parts, bias, group):
    seq, width = x.shape
    rows, columns = w_in.shape
    half, _, _, block = parts[0].shape
    chips = 2 * half

    def columns_at(height):
        return spec((height, block), lambda u, w: (0, block_of(w, u, chips)))

    return call(
        partial(inner_kernel, (group, half)),
        (2 * chips,),
        [fixed((seq, width)), columns_at(rows)] + part_specs(parts) + [columns_at(1)],
        [
            columns_at(seq),
            spec((block, seq), lambda u, w: (block_of(w, u, chips), 0)),
            columns_at(seq),
        ],
        [
            struct((seq, columns), BF16),
            struct((columns, seq), BF16),
            struct((seq, columns), BF16),
        ],
        [pltpu.VMEM((seq, width), BF16), pltpu.VMEM((width, block), BF16)],
        micros=16,
    )(where, x, w_in, *parts, bias)


def outer_kernel(
    dims,
    where,
    act,
    own,
    a,
    b,
    c,
    d,
    hidden,
    cotangent,
    gain_one,
    shift_one,
    bias,
    gain_two,
    shift_two,
    out,
    grad,
    low,
    low_other,
    sums,
    total,
    picked,
):
    group, half = dims
    step = pl.program_id(0)
    ff_rows = own.shape[0]
    rows = a.shape[2]

    @pl.when(step == 0)
    def _():
        start = pl.multiple_of(where[0] * ff_rows, 128)
        total[...] = dot(act[:, pl.ds(start, ff_rows)], own[...])

    for index, part in enumerate((a, b, c, d)):

        @pl.when(step == index + 1)
        def _(index=index, part=part):
            at = 0
            for i in range(half):
                block = block_of(where, index * half + i, 2 * half)
                for s in range(1, group):
                    start = natural(where, s, group) * ff_rows + block * rows
                    picked[:, at : at + rows] = act[:, pl.ds(pl.multiple_of(start, rows), rows)]
                    at += rows
            total[...] += dot(picked[...], part[...].reshape(-1, part.shape[3]))

    @pl.when(step == 4)
    def _():
        unit_one, _ = normalise(hidden[...])
        second = unit_one * gain_one[...] + shift_one[...] + total[...] + bias[...]
        unit, inverse = normalise(second)
        out[...] = (unit * gain_two[...] + shift_two[...]).astype(BF16)
        given = cotangent[...].astype(F32)
        back = normalise_back(given, unit, inverse, gain_two[...])
        grad[...] = back
        rounded = back.astype(BF16)
        low[...] = rounded
        size = low_other.shape[1]
        start = pl.multiple_of((1 - where[1]) * size, 128)
        low_other[...] = low[:, pl.ds(start, size)]
        sums[0:1, :] = rows_sum(given * unit)
        sums[1:2, :] = rows_sum(given)
        sums[2:3, :] = rows_sum(rounded.astype(F32))


def outer(where, act, w_down, parts, hidden, cotangent, vectors, group):
    seq, width = hidden.shape
    rows = w_down.shape[0]
    half, steps, size, _ = parts[0].shape
    full = fixed((seq, width))
    vector = fixed((1, width))
    return call(
        partial(outer_kernel, (group, half)),
        (5,),
        [fixed(act.shape), fixed((rows, width))]
        + [fixed(parts[0].shape)] * 4
        + [full, full]
        + [vector] * 5,
        [full, full, full, fixed((seq, width // 2)), fixed((8, width))],
        [
            struct((seq, width), BF16),
            struct((seq, width), F32),
            struct((seq, width), BF16),
            struct((seq, width // 2), BF16),
            struct((8, width), F32),
        ],
        [pltpu.VMEM((seq, width), F32), pltpu.VMEM((seq, half * steps * size), BF16)],
        micros=60,
    )(where, act, w_down, *parts, hidden, cotangent, *vectors)


def slope_kernel(dims, where, low, own, a, b, c, d, slope, grad, grad_other, sums):
    group, half, width = dims
    step = pl.program_id(0)
    ff_rows = own.shape[0]
    rows = a.shape[2]

    def finish(back, start, size):
        place = pl.ds(pl.multiple_of(start, size), size)
        value = (back * slope[:, place].astype(F32)).astype(BF16)
        grad[:, place] = value
        sums[:, place] = rows_sum(value.astype(F32))
        piece = min(size, width)
        for at in range(0, size, piece):
            block = (start + at) // width
            inside = start + at - block * width

            @pl.when(lax.rem(block, 2) != where[1])
            def _(at=at, block=block, inside=inside):
                there = pl.multiple_of((block // 2) * width + inside, piece)
                grad_other[:, pl.ds(there, piece)] = value[:, at : at + piece]

    @pl.when(step == 0)
    def _():
        finish(dot_t(low[...], own[...]), where[0] * ff_rows, ff_rows)

    for index, part in enumerate((a, b, c, d)):

        @pl.when(step == index + 1)
        def _(index=index, part=part):
            back = dot_t(low[...], part[...].reshape(-1, part.shape[3]))
            at = 0
            for i in range(half):
                block = block_of(where, index * half + i, 2 * half)
                for s in range(1, group):
                    start = natural(where, s, group) * ff_rows + block * rows
                    finish(back[:, at : at + rows], start, rows)
                    at += rows


def slope_back(where, low, w_down, parts, slope, part, group):
    seq, width = low.shape
    rows = w_down.shape[0]
    half = parts[0].shape[0]
    columns = slope.shape[1]
    return call(
        partial(slope_kernel, (group, half, part)),
        (5,),
        [fixed((seq, width)), fixed((rows, width))]
        + [fixed(parts[0].shape)] * 4
        + [fixed((seq, columns))],
        [fixed((seq, columns)), fixed((seq, columns // 2)), fixed((1, columns))],
        [
            struct((seq, columns), BF16),
            struct((seq, columns // 2), BF16),
            struct((1, columns), F32),
        ],
        micros=14,
    )(where, low, w_down, *parts, slope)


def inner_back_kernel(
    dims,
    where,
    grad_inner,
    own,
    a,
    b,
    c,
    d,
    grad_two,
    hidden,
    gain,
    own_out,
    rest_out,
    grad_one,
    low_one,
    grad_context,
    sums,
    total,
    weight,
):
    group, half = dims
    unit = pl.program_id(0)
    rows = own.shape[0]

    def place(s):
        return pl.ds(pl.multiple_of(natural(where, s, group) * rows, 128), rows)

    load_weight(unit, half, own, (a, b, c, d), weight)
    value = dot_t(grad_inner[...], weight[...])

    @pl.when(unit == 0)
    def _():
        total[...] = value

    @pl.when(unit > 0)
    def _():
        total[...] += value

    @pl.when(unit == 4 * half - 1)
    def _():
        unit_one, inverse = normalise(hidden[...])
        for s in range(group):
            grad_one[:, place(s)] = total[:, s * rows : (s + 1) * rows]
        given = grad_one[...] + grad_two[...]
        back = normalise_back(given, unit_one, inverse, gain[...])
        grad_one[...] = back
        rounded = back.astype(BF16)
        low_one[...] = rounded
        sums[0:1, :] = rows_sum(given * unit_one)
        sums[1:2, :] = rows_sum(given)
        sums[2:3, :] = rows_sum(rounded.astype(F32))
        grad_context[:, place(0)] = dot_t(rounded, own_out[...]).astype(BF16)
        for s in range(1, group):
            piece = rest_out[(s - 1) * rows : s * rows, :]
            grad_context[:, place(s)] = dot_t(rounded, piece).astype(BF16)


def inner_back(where, grad_inner, w_in, parts, grad_two, hidden, gain, w_out, rest_out, group):
    seq, width = hidden.shape
    rows, columns = w_in.shape
    half, _, _, block = parts[0].shape
    chips = 2 * half
    full = fixed((seq, width))

    def columns_at(height):
        return spec((height, block), lambda u, w: (0, block_of(w, u, chips)))

    return call(
        partial(inner_back_kernel, (group, half)),
        (2 * chips,),
        [columns_at(seq), columns_at(rows)]
        + part_specs(parts)
        + [full, full, fixed((1, width)), fixed((rows, width)), fixed((width - rows, width))],
        [full, full, full, fixed((8, width))],
        [
            struct((seq, width), F32),
            struct((seq, width), BF16),
            struct((seq, width), BF16),
            struct((8, width), F32),
        ],
        [pltpu.VMEM((seq, width), F32), pltpu.VMEM((width, block), BF16)],
        micros=19,
    )(where, grad_inner, w_in, *parts, grad_two, hidden, gain, w_out, rest_out)


def input_back_kernel(dims, where, mine, others, own, a, b, c, d, first, out, total, weight):
    group, half, qkv_width = dims
    unit = pl.program_id(0)
    rows, columns = own.shape

    @pl.when(unit == 0)
    def _():
        total[...] = jnp.zeros_like(total)

    block = block_of(where, unit, 2 * half)
    inside = block * columns < qkv_width
    same = lax.rem(block, 2) == where[1]

    @pl.when(inside)
    def _():
        load_weight(unit, half, own, (a, b, c, d), weight)

    @pl.when(inside & same)
    def _():
        total[...] += dot_t(mine[0], weight[...])

    @pl.when(inside & ~same)
    def _():
        total[...] += dot_t(others[0], weight[...])

    @pl.when(unit == 4 * half - 1)
    def _():
        for s in range(group):
            place = pl.ds(pl.multiple_of(natural(where, s, group) * rows, 128), rows)
            out[:, place] = first[:, place] + total[:, s * rows : (s + 1) * rows]


def input_back(where, mine, others, first, w_qkv, parts, group):
    seq, width = first.shape
    rows, qkv_width = w_qkv.shape
    half, _, _, block = parts[0].shape
    chips = 2 * half
    each = width // block
    top = qkv_width // block - 1

    def plane(u, w):
        n = jnp.minimum(block_of(w, u, chips), top)
        return (n // each, 0, lax.rem(n, each) // 2)

    return call(
        partial(input_back_kernel, (group, half, qkv_width)),
        (2 * chips,),
        [
            spec((1, seq, block), plane),
            spec((1, seq, block), plane),
            spec((rows, block), lambda u, w: (0, jnp.minimum(block_of(w, u, chips), top))),
        ]
        + part_specs(parts)
        + [fixed((seq, width))],
        fixed((seq, width)),
        struct((seq, width), F32),
        [pltpu.VMEM((seq, width), F32), pltpu.VMEM((width, block), BF16)],
        micros=12,
    )(where, mine, others, w_qkv, *parts, first)


def widen_kernel(dims, where, *refs):
    parts, outs = refs[:4], refs[4:]
    phases, by_rows = dims
    chips = 1 << phases
    half = chips // 2
    for side in range(2):
        core = where[1] if side == 0 else 1 - where[1]
        for order in range(chips):
            value = parts[2 * side + order // half][order % half].astype(F32)
            rows, columns = value.shape
            chip = where[2 + side * chips + order]
            if by_rows:
                outs[0][
                    pl.ds(pl.multiple_of(chip * rows, 8), rows),
                    pl.ds(pl.multiple_of(core * columns, 128), columns),
                ] = value
                continue
            start = (2 * chip + core) * columns
            base = 0
            for out in outs:
                size = out.shape[1]
                inside = (start >= base) & (start < base + size)

                @pl.when(inside)
                def _(out=out, start=start, base=base, value=value):
                    out[:, pl.ds(pl.multiple_of(start - base, 128), columns)] = value

                base += size


def widen(where, parts, phases, by_rows, shapes):
    return call(
        partial(widen_kernel, (phases, by_rows)),
        (1,),
        [fixed(part.shape) for part in parts],
        [fixed(shape) for shape in shapes],
        [struct(shape, F32) for shape in shapes],
        micros=4,
    )(where, *parts)


def grads_kernel(dims, where, *refs):
    orders, adds, last, group = dims
    units = len(orders)
    step = pl.program_id(0)
    at = 0
    outs = refs[units * (4 + adds) :]
    for u in range(units):
        left, left_other, right, right_other = refs[at : at + 4]
        value = dot(left[0], right[0]) + dot(left_other[0], right_other[0])
        for add in refs[at + 4 : at + 4 + adds]:
            value = value + add[0].astype(F32)
        at += 4 + adds
        value = value.astype(BF16)
        if not last:
            outs[0][u] = value
            continue
        for s in range(group):

            @pl.when(step == s)
            def _(s=s, value=value):
                outs[s][...] = value


def grads(where, left, right, maps, shape, units, received, group):
    rows, columns = shape
    seq = left[0].shape[2]
    left_map, right_map, other_map = maps
    last = units == [0]
    ins, args = [], []
    for order in units:
        lefts = spec((1, rows, seq), partial(left_map, order))
        rights = spec((1, seq, columns), partial(right_map, order))
        others = spec((1, seq, columns), partial(other_map, order))
        ins += [lefts, lefts, rights, others]
        args += [left[0], left[1], right[0], right[1]]
        for phase, value in enumerate(received):
            index = order >> (phase + 1)
            ins.append(spec((1, rows, columns), lambda s, w, index=index: (index, s, 0)))
            args.append(value)
    count = len(units)
    if last:
        outs = [fixed((rows, columns))] * group
        out_shape = [struct((rows, columns), BF16)] * group
    else:
        outs = [spec((count, rows, columns), lambda s, w: (0, s, 0))]
        out_shape = [struct((count, group * rows, columns), BF16)]
    return call(
        partial(grads_kernel, (units, len(received), last, group)),
        (group,),
        ins,
        outs,
        out_shape,
        micros=6,
    )(where, *args)


def after(value, *others):
    return lax.optimization_barrier((value, others))[0]


def local(
    chips,
    group,
    tokens,
    segments,
    lengths,
    cotangent,
    w_qkv,
    b_qv,
    w_out,
    b_out,
    gain_one,
    shift_one,
    w_in,
    b_in,
    w_down,
    b_down,
    gain_two,
    shift_two,
):
    reps = 2 * chips
    phases = chips.bit_length() - 1
    core = lax.axis_index("core")
    chip = lax.axis_index("chip")
    rank = chip * 2 + core
    own = lax.axis_index("shard")
    _, seq_len, model_width = tokens.shape
    ff_rows = w_down.shape[0]
    ff_width = w_in.shape[1]
    qkv_width = w_qkv.shape[1]

    def from_shard(value, step):
        return lax.ppermute(value, "shard", [(i, (i - step) % group) for i in range(group)])

    def to_shard(value, step):
        return lax.ppermute(value, "shard", [(i, (i + step) % group) for i in range(group)])

    def sibling(value):
        return lax.ppermute(value, "core", [(0, 1), (1, 0)])

    def bit(phase, which):
        return 1 << ((phase + which) % phases)

    def swap(value, phase):
        pairs = [
            (q * 2 + c, (q ^ bit(phase, c)) * 2 + c) for q in range(chips) for c in range(2)
        ]
        return lax.ppermute(value, REP, pairs)

    def table(which):
        orders = []
        for order in range(chips):
            mask = sum(bit(f, which) for f in range(phases) if order >> f & 1)
            orders.append(mask)
        return orders

    masks = jnp.where(core == 0, jnp.array(table(0)), jnp.array(table(1)))
    masks_other = jnp.where(core == 0, jnp.array(table(1)), jnp.array(table(0)))
    where = jnp.concatenate(
        [jnp.stack([own, core]), chip ^ masks, chip ^ masks_other]
    ).astype(jnp.int32)

    def gather(value, *gates):
        for phase in range(phases - 1):
            value = jnp.concatenate([value, swap(value, phase)], axis=0)
        rest = swap(value, phases - 1)
        return value, rest, sibling(after(value, gates)), sibling(rest)

    w_one = jnp.concatenate([w_qkv, w_out], axis=1)
    part = w_one.shape[1] // reps
    rows = w_one.shape[0]
    piece_one = lax.dynamic_slice_in_dim(w_one, rank * part, part, axis=1)
    part_in = ff_width // reps
    piece_in = lax.dynamic_slice_in_dim(w_in, rank * part_in, part_in, axis=1)
    part_down = ff_rows // reps
    piece_down = lax.dynamic_slice_in_dim(w_down, rank * part_down, part_down, axis=0)

    class Gather:

        def __init__(self, value):
            self.value = value
            self.first = swap(value, 0)

        def step(self, *gates):
            other = self.first
            for phase in range(phases - 1):
                self.value = after(jnp.concatenate([self.value, other], axis=0), gates)
                other = swap(self.value, phase + 1)
            self.rest = other
            self.side = sibling(self.value)

        def finish(self, *gates):
            self.parts = (self.value, self.rest, self.side, sibling(after(self.rest, gates)))

    got_one = [from_shard(piece_one, s) for s in range(1, group)]
    got_in = [from_shard(piece_in, s) for s in range(1, group)]

    vectors = (b_qv, b_out, gain_one, shift_one, b_in, b_down, gain_two, shift_two)
    sizes = [v.shape[0] for v in vectors]
    packed = jnp.concatenate(after(vectors, piece_one))
    got_packed = [from_shard(packed, s) for s in range(1, group)]

    parts_one = gather(jnp.stack(got_one)[None], got_packed)
    parts_in = Gather(jnp.stack(got_in)[None])
    parts_in.step()
    got_down = [from_shard(after(piece_down, got_in), s) for s in range(1, group)]

    relative = jnp.stack([packed] + got_packed)
    ordered = jnp.concatenate([relative, relative], axis=0)
    ordered = lax.dynamic_slice_in_dim(ordered, (group - own) % group, group, axis=0)
    full, start = [], 0
    for size in sizes:
        full.append(ordered[:, start : start + size].reshape(1, -1).astype(F32))
        start += size
    bias_qv, bias_out, norm_gone, norm_sone, bias_in, bias_down, norm_gtwo, norm_stwo = full
    none = jnp.zeros((1, model_width), F32)
    bias_qkv = jnp.concatenate(
        [bias_qv[:, :model_width], none, bias_qv[:, model_width:], none], axis=1
    )
    kind = segments[0] * 2 + (jnp.arange(seq_len) < lengths[0]).astype(jnp.int32)
    column, row = kind[:, None], kind[None, :]

    flat_in = tokens[0]
    projected, rest_out = qkv(where, after(flat_in, parts_in.rest), w_qkv, parts_one, bias_qkv, group)
    parts_in.finish()
    count = model_width // (4 * HEAD_DIM)
    context, turned, logs_a = attention(where, projected, flat_in, column, row, 0, count)
    parts_down = Gather(jnp.stack(got_down)[None])
    context, turned, logs_b = attention(
        where,
        projected,
        flat_in,
        column,
        row,
        count,
        count,
        (context, turned),
    )
    first_left = (turned, sibling(turned))
    parts_down.step(logs_b)
    hidden, normed, normed_turned = out_norm(
        where,
        after(context, parts_down.value),
        flat_in,
        w_out,
        rest_out,
        bias_out,
        norm_gone,
        norm_sone,
        group,
    )
    parts_in = parts_in.parts
    in_left = (normed_turned[None], sibling(normed_turned)[None])
    act, act_turned, slope = inner(where, normed, w_in, parts_in, bias_in, group)
    parts_down.finish(act)
    parts_down = parts_down.parts
    down_left = (act_turned[None], sibling(act_turned)[None])
    where_down = where
    if part_down % 128:
        merged = jnp.zeros((group - 1, ff_rows, model_width), BF16)
        for unit in range(reps):
            piece = parts_down[2 * unit // chips][unit % (chips // 2)]
            at = block_of(where, unit, chips) * part_down
            merged = lax.dynamic_update_slice_in_dim(merged, piece, at, axis=1)
        fourth = ff_rows // 4
        parts_down = [
            merged[:, b * fourth : (b + 1) * fourth][None] for b in (0, 2, 1, 3)
        ]
        where_down = jnp.stack([own, 0, 0, 1, 0, 1]).astype(jnp.int32)
    output_rows, grad_second, grad_branch, branch_other, sums_two = outer(
        where_down,
        act,
        w_down,
        parts_down,
        hidden,
        cotangent[0],
        (norm_gone, norm_sone, bias_down, norm_gtwo, norm_stwo),
        group,
    )

    class Scatter:

        def __init__(self, left, right, maps, shape):
            self.fixed = (where, left, right, maps, shape)
            self.received = []

        def send(self, *gates):
            phase = len(self.received)
            units = list(range(1 << phase, chips, 2 << phase))
            received = after(self.received, gates) if phase else []
            sent = grads(*self.fixed, units, received, group)[0]
            self.received.append(swap(sent, phase))
            return sent

        def send_rest(self, *gates):
            while len(self.received) < phases:
                sent = self.send(*gates)
            return sent

        def finish(self, *gates):
            received = after(self.received, gates)
            parts = grads(*self.fixed, [0], received, group)
            self.own = parts[0]
            self.given = [to_shard(parts[s], s) for s in range(1, group)]
            return parts[0]

        def total(self):
            total = self.own.astype(F32)
            for value in self.given:
                total = total + value.astype(F32)
            return total.astype(BF16)

    half = model_width // 2
    part_rows = ff_rows // chips
    down_maps = (
        lambda o, s, w: (0, natural(w, s, group) * chips + w[2 + o], 0),
        lambda o, s, w: (0, 0, w[1]),
        lambda o, s, w: (0, 0, 0),
    )
    down_right = (grad_branch[None], sibling(branch_other)[None])
    down = Scatter(down_left, down_right, down_maps, (part_rows, half))
    sent = down.send()
    grad_inner, inner_other, sums_in = slope_back(
        where_down, after(grad_branch, sent), w_down, parts_down, slope, part_in, group
    )
    grad_first, grad_attn, grad_context, sums_one = inner_back(
        where,
        after(grad_inner, in_left),
        w_in,
        parts_in,
        grad_second,
        hidden,
        norm_gone,
        w_out,
        rest_out,
        group,
    )
    in_other = sibling(inner_other)
    sent = down.send_rest(grad_first, first_left)
    logs = (logs_a, logs_b)
    others, sums_others = attention_back(
        where, projected, after(grad_context, sent), logs, grad_attn, column, row, False, part
    )
    in_maps = (
        lambda o, s, w: (0, natural(w, s, group), 0),
        lambda o, s, w: (0, 0, 2 * w[2 + o] + w[1]),
        lambda o, s, w: (0, 0, w[2 + o]),
    )
    in_right = after((grad_inner[None], in_other[None]), down.received, others)
    inward = Scatter(in_left, in_right, in_maps, (rows, part_in))
    sent = inward.send()
    done = down.finish(sent)
    other_proj = sibling(others)
    mine, sums_mine = attention_back(
        where, projected, after(grad_context, done), logs, grad_attn, column, row, True, part
    )
    each = model_width // part

    def plane(order, w):
        return 2 * w[2 + order] + w[1]

    def compact(o, s, w):
        return (plane(o, w) // each, 0, lax.rem(plane(o, w), each) // 2)

    first_maps = (
        lambda o, s, w: (plane(o, w) // (3 * each), natural(w, s, group), 0),
        compact,
        compact,
    )
    first = Scatter(first_left, (mine, other_proj), first_maps, (rows, part))
    sent = first.send()
    sent = inward.send_rest(sent)
    share_down = down.total()[None]
    grad_input = input_back(
        where, after(mine, sent), others, grad_first, w_qkv, parts_one, group
    )
    done = inward.finish(grad_input)
    sent = first.send_rest(done)
    share_in = inward.total()[None]
    def blocks(core_parity):
        value = jnp.where(core == core_parity, sums_mine, sums_others)
        return value.reshape(3, -1, 1, part)

    sums_proj = jnp.concatenate([blocks(0), blocks(1)], axis=2).reshape(3, model_width)
    small = (
        jnp.concatenate([sums_proj[0], sums_proj[2]]),
        sums_one[2],
        sums_one[0],
        sums_one[1],
        sums_in[0],
        sums_two[2],
        sums_two[0],
        sums_two[1],
    )
    small = jnp.concatenate([v.reshape(group, -1) for v in small], axis=1)
    done = first.finish(sent, share_in)
    shares = jnp.stack([share_down.reshape(share_in.shape), share_in], axis=1)
    shares = after(shares, done)
    gathered = Gather(shares)
    share_one = after(first.total()[None], gathered.first)
    gathered.step(share_one)
    gathered.finish()
    final_parts = gather(share_one)
    small = after(small, done)
    small = small + sibling(small)
    for phase in range(phases):
        small = small + swap(small, phase)
    small = jnp.concatenate([small, small], axis=0)
    small = lax.dynamic_slice_in_dim(small, own, group, axis=0)
    small = after(small, final_parts)
    total = small[0]
    for s in range(1, group):
        total = total + to_shard(small[s], s)
    down_parts = [
        value[:, 0].reshape(-1, *share_down.shape[1:]) for value in gathered.parts
    ]
    in_parts = [value[:, 1] for value in gathered.parts]
    (grad_wdown,) = widen(where, down_parts, phases, True, [(ff_rows, model_width)])
    (grad_win,) = widen(where, in_parts, phases, False, [(rows, ff_width)])
    grad_wqkv, grad_wout = widen(
        where,
        final_parts,
        phases,
        False,
        [(rows, qkv_width), (rows, model_width)],
    )

    vecs, start = [], 0
    for size in sizes:
        vecs.append(total[start : start + size])
        start += size

    return (
        output_rows.reshape(tokens.shape),
        grad_input.reshape(tokens.shape),
        grad_wqkv,
        vecs[0],
        grad_wout,
        vecs[1],
        vecs[2],
        vecs[3],
        grad_win,
        vecs[4],
        grad_wdown,
        vecs[5],
        vecs[6],
        vecs[7],
    )


def solution(mesh):
    reps, group = mesh.devices.shape
    fine = Mesh(mesh.devices.reshape(reps // 2, 2, group), ALL)
    rows = P(ALL, None, None)
    matrix = P("shard", None)
    vector = P("shard")
    in_specs = (
        rows,
        P(ALL, None),
        P(ALL),
        rows,
        matrix,
        vector,
        matrix,
        vector,
        vector,
        vector,
        matrix,
        vector,
        matrix,
        vector,
        vector,
        vector,
    )
    out_specs = (
        rows,
        rows,
        matrix,
        vector,
        matrix,
        vector,
        vector,
        vector,
        matrix,
        vector,
        matrix,
        vector,
        vector,
        vector,
    )
    return jax.shard_map(
        partial(local, reps // 2, group),
        mesh=fine,
        in_specs=in_specs,
        out_specs=out_specs,
        check_vma=False,
    )
```

time: 543 us -> 477 us (0.88)
  waiting for transfers between devices: 259 us -> 151 us
  Pallas kernels: 145 us -> 218 us
  blocking collectives: 39.1 us -> 0 us
  starting transfers between devices: 25.6 us -> 63.4 us
  local copies, waits for them, and re-layouts: 37.1 us -> 22.9 us
  between operations: 14.9 us -> 2.09 us
    pallas_call x10 -> x22, Pallas kernels: 139 us -> 212 us  [the longest x9 56.9 us: grads(): call(partial(grads_kernel, (units, len(received), last, group)), (group,)...]
    reduce_scatter x3 -> x0, waiting for transfers between devices: 70.4 us -> none  [the longest x2 42.2 us: scatter_columns(): share = lax.psum_scatter(flat, 'chip', scatter_dimension=0, tiled=True)]
    ppermute x0 -> x18, waiting for transfers between devices: none -> 56.2 us  [swap(): return lax.ppermute(value, REP, pairs)]
    psum x1 -> x0, blocking collectives: 39.1 us -> none  [local(): small = lax.psum(small, ALL)]
    all_gather x6 -> x0, waiting for transfers between devices: 36.3 us -> none  [the longest x1 33.4 us: local(): rest_down = lax.all_gather(jnp.stack(got_down), REP, axis=1, tiled=True)]
    ppermute x8 -> x17, waiting for transfers between devices: 23.9 us -> 3.79 us  [sibling(): return lax.ppermute(value, 'core', [(0, 1), (1, 0)])]
    ppermute x9 -> x12, waiting for transfers between devices: 67.9 us -> 48.6 us  [from_shard(): lax.ppermute(value, 'shard', [(i, (i - step) % group) for i in range(grou...]
    ppermute x9 -> x12, waiting for transfers between devices: 60.4 us -> 42.8 us  [to_shard(): lax.ppermute(value, 'shard', [(i, (i + step) % group) for i in range(grou...]
  transfers between devices with their start and end apart: 35 -> 59, of which waited for: 28 -> 25; matrix products, arithmetic and copies ran while one was open for 7% -> 6% of each run, Pallas kernels for 14% -> 40%
where the time goes in v3:
time: 477 us; the launch traced here: 470 us
  Pallas kernels  218 us (46%)
  waiting for transfers between devices  151 us (32%)
  starting transfers between devices  63.4 us (13%)
  local copies, waits for them, and re-layouts  22.9 us (5%)
  other arithmetic  12.1 us (3%)
    pallas_call x9, Pallas kernels, grads(): call(partial(grads_kernel, (units, len(received), last, group)), (group,)...  56.9 us
    ppermute x18, waiting for transfers between devices, swap(): return lax.ppermute(value, REP, pairs)  56.2 us
    ppermute x12, waiting for transfers between devices, from_shard(): lax.ppermute(value, 'shard', [(i, (i - step) % group) for i in range(grou...  48.6 us
    ppermute x12, waiting for transfers between devices, to_shard(): lax.ppermute(value, 'shard', [(i, (i + step) % group) for i in range(grou...  42.8 us
    pallas_call x2, Pallas kernels, attention_back(): call(partial(attend_back_kernel, (mine, per)), (each // 2,), [pairs(0), p...  26.1 us
    pallas_call x2, Pallas kernels, attention(): call(partial(attend_kernel, first), (count,), [spec((seq, block), lambda...  21.7 us
    pallas_call x1, Pallas kernels, inner_back(): call(partial(inner_back_kernel, (group, half)), (2 * chips,), [columns_at...  18.8 us
    ppermute x18, starting transfers between devices, swap(): return lax.ppermute(value, REP, pairs)  17.3 us
  transfers between devices with their start and end apart: 59, of which 25 were waited for; matrix products, arithmetic and copies ran while one was open for 6% of the time, Pallas kernels for 40%

profile of v3, /device:TPU:9, one launch (start us, length us, event | category | flops | bytes accessed | tf_op | source)
XLA Modules:
  0.0 470.1 jit_solution(4113843553427175606)
XLA Ops:
  10.7 10.0 %collective-permute-done.1 = bf16[256,512]{1,0:T(8,128)(2,1)S(1)} collective-permute-done((bf16[256,512]{1,0:T(8,128)(2,1)S(1)}, bf16[256,512]{1,0:T(8,128)(2,1)S(1)}, u32[]{:S(2)}, u32[]{:S(2)}) %collective-permute-start.1) | collective-permute-done | bytes 262176 | tf_op jit(solution)/shard_map/ppermute | solution.py:817
  20.7 16.9 %collective-permute-done.2 = bf16[256,512]{1,0:T(8,128)(2,1)S(1)} collective-permute-done((bf16[256,512]{1,0:T(8,128)(2,1)S(1)}, bf16[256,512]{1,0:T(8,128)(2,1)S(1)}, u32[]{:S(2)}, u32[]{:S(2)}) %collective-permute-start.2) | collective-permute-done | bytes 262176 | tf_op jit(solution)/shard_map/ppermute | solution.py:817
  43.2 5.6 %collective-permute-done.7 = bf16[256,512]{1,0:T(8,128)(2,1)S(1)} collective-permute-done((bf16[256,512]{1,0:T(8,128)(2,1)S(1)}, bf16[256,512]{1,0:T(8,128)(2,1)S(1)}, u32[]{:S(2)}, u32[]{:S(2)}) %collective-permute-start.7) | collective-permute-done | bytes 262176 | tf_op jit(solution)/shard_map/ppermute | solution.py:817
  52.9 10.7 %collective-permute-done.8 = bf16[1,3,256,512]{3,2,1,0:T(8,128)(2,1)S(1)} collective-permute-done((bf16[1,3,256,512]{3,2,1,0:T(8,128)(2,1)S(1)}, bf16[1,3,256,512]{3,2,1,0:T(8,128)(2,1)S(1)}, u32[]{:S(2)}, u32[]{:S(2)}) %collective-permute-start.8) | collective-permute-done | bytes 786464 | tf_op jit(solution)/shard_map/ppermute | solution.py:832
  76.7 11.7 %collective-permute-done.12 = bf16[3072]{0:T(1024)(128)(2,1)S(1)} collective-permute-done((bf16[3072]{0:T(1024)(128)(2,1)S(1)}, bf16[3072]{0:T(1024)(128)(2,1)S(1)}, u32[]{:S(2)}, u32[]{:S(2)}) %collective-permute-start.12) | collective-permute-done | bytes 6176 | tf_op jit(solution)/shard_map/ppermute | solution.py:817
  102.5 6.5 %collective-permute-done.18 = bf16[1,3,128,1024]{3,2,1,0:T(8,128)(2,1)S(1)} collective-permute-done((bf16[1,3,128,1024]{3,2,1,0:T(8,128)(2,1)S(1)}, bf16[1,3,128,1024]{3,2,1,0:T(8,128)(2,1)S(1)}, u32[]{:S(2)}, u32[]{:S(2)}) %collective-permute-start.18) | collective-permute-done | bytes 786464 | tf_op jit(solution)/shard_map/ppermute | solution.py:832
  110.3 12.0 %shard_map.299 = (bf16[512,4096]{1,0:T(8,128)(2,1)}, bf16[768,1024]{1,0:T(8,128)(2,1)}) custom-call(s32[10]{0:T(128)} %pad_add_fusion.where, bf16[512,1024]{1,0:T(8,128)(2,1)} %bitcast.112, bf16[256,3072]{1,0:T(8,128)(2,1)} %own.13, bf16[2,3,256,512]{3,2,1,0:T(8,128)(2,1)} %copy-done, bf16[2,3,256,512]{3,2,1,0:T(8,128)(2,1)} %copy-done.2, ...), custom_call_target="tpu_custom_call" | custom-call | bytes 44280000 | tf_op jit(solution)/shard_map/pallas_call | solution.py:150
  122.3 10.9 %shard_map.300 = (bf16[512,1024]{1,0:T(8,128)(2,1)}, bf16[2,1024,512]{2,1,0:T(8,128)(2,1)}, f32[512,128]{1,0:T(8,128)}) custom-call(s32[10]{0:T(128)} %pad_add_fusion.where, bf16[512,4096]{1,0:T(8,128)(2,1)} %get-tuple-element.103.q.k.v, bf16[512,4096]{1,0:T(8,128)(2,1)} %get-tuple-element.103.q.k.v, bf16[512,4096]{1,0:T(8,128)(2,1)} %get-tuple-element.103.q.k.v, ...), custom_call_target="tpu_custom_call" | custom-call | bytes 40590000 | tf_op jit(solution)/shard_map/pallas_call | solution.py:200
  133.2 10.9 %shard_map.301 = (bf16[512,1024]{1,0:T(8,128)(2,1)}, bf16[2,1024,512]{2,1,0:T(8,128)(2,1)}, f32[512,128]{1,0:T(8,128)}) custom-call(s32[10]{0:T(128)} %pad_add_fusion.where, bf16[512,4096]{1,0:T(8,128)(2,1)} %get-tuple-element.103.q.k.v, bf16[512,4096]{1,0:T(8,128)(2,1)} %get-tuple-element.103.q.k.v, ...), custom_call_target="tpu_custom_call", output_to_operand_aliasing={{0}: (7, {}), {1}: (8, {})} | custom-call | bytes 40590000 | tf_op jit(solution)/shard_map/pallas_call | solution.py:200
  144.1 6.0 %shard_map.302 = (f32[512,1024]{1,0:T(8,128)}, bf16[512,1024]{1,0:T(8,128)(2,1)}, bf16[1024,512]{1,0:T(8,128)(2,1)}) custom-call(s32[10]{0:T(128)} %pad_add_fusion.where, bf16[512,1024]{1,0:T(8,128)(2,1)} %get-tuple-element.110.context, bf16[512,1024]{1,0:T(8,128)(2,1)} %bitcast.115, bf16[256,1024]{1,0:T(8,128)(2,1)} %own_out.1, ...), custom_call_target="tpu_custom_call" | custom-call | bytes 22140000 | tf_op jit(solution)/shard_map/pallas_call | solution.py:316
  150.1 15.9 %shard_map.303 = (bf16[512,4096]{1,0:T(8,128)(2,1)}, bf16[4096,512]{1,0:T(8,128)(2,1)}, bf16[512,4096]{1,0:T(8,128)(2,1)}) custom-call(s32[10]{0:T(128)} %pad_add_fusion.where, bf16[512,1024]{1,0:T(8,128)(2,1)} %get-tuple-element.112.x, bf16[256,4096]{1,0:T(8,128)(2,1)} %own.12, bf16[2,3,256,512]{3,2,1,0:T(8,128)(2,1)} %pad_maximum_fusion.a, ...), custom_call_target="tpu_custom_call" | custom-call | bytes 59040000 | tf_op jit(solution)/shard_map/pallas_call | solution.py:366
  172.0 17.5 %collective-permute-done.21.b = bf16[2,3,128,1024]{3,2,1,0:T(8,128)(2,1)S(1)} collective-permute-done((bf16[2,3,128,1024]{3,2,1,0:T(8,128)(2,1)}, bf16[2,3,128,1024]{3,2,1,0:T(8,128)(2,1)S(1)}, u32[]{:S(2)}, u32[]{:S(2)}) %collective-permute-start.21) | collective-permute-done | bytes 1572896 | tf_op jit(solution)/shard_map/ppermute | solution.py:832
  196.0 16.5 %shard_map.304 = (bf16[512,1024]{1,0:T(8,128)(2,1)}, f32[512,1024]{1,0:T(8,128)}, bf16[512,1024]{1,0:T(8,128)(2,1)}, bf16[512,512]{1,0:T(8,128)(2,1)}, f32[8,1024]{1,0:T(8,128)}) custom-call(s32[10]{0:T(128)} %pad_add_fusion.where, bf16[512,4096]{1,0:T(8,128)(2,1)} %get-tuple-element.113.act, bf16[1024,1024]{1,0:T(8,128)(2,1)} %own.11, ...), custom_call_target="tpu_custom_call" | custom-call | bytes 221400000 | tf_op jit(solution)/shard_map/pallas_call | solution.py:457
  215.4 7.3 %shard_map.305 = bf16[2,1024,512]{2,1,0:T(8,128)(2,1)} custom-call(s32[10]{0:T(128)} %pad_add_fusion.where, bf16[1,4096,512]{2,1,0:T(8,128)(2,1)} %bitcast.104, bf16[1,4096,512]{2,1,0:T(8,128)(2,1)} %bitcast.20.refs_1_.refs_5_, bf16[1,512,1024]{2,1,0:T(8,128)(2,1)} %bitcast.108, bf16[1,512,512]{2,1,0:T(8,128)(2,1)} %bitcast.120, ...), custom_call_target="tpu_custom_call" | custom-call | bytes 22140000 | tf_op jit(solution)/shard_map/pallas_call | solution.py:771
  224.7 17.1 %shard_map.306 = (bf16[512,4096]{1,0:T(8,128)(2,1)}, bf16[512,2048]{1,0:T(8,128)(2,1)}, f32[1,4096]{1,0:T(1,128)}) custom-call(s32[10]{0:T(128)} %pad_add_fusion.where, bf16[512,1024]{1,0:T(8,128)(2,1)} %get-tuple-element.120.low, bf16[1024,1024]{1,0:T(8,128)(2,1)} %own.11, bf16[2,3,128,1024]{3,2,1,0:T(8,128)(2,1)} %pad_maximum_fusion.2.a, ...), custom_call_target="tpu_custom_call" | custom-call | bytes 51660000 | tf_op jit(solution)/shard_map/pallas_call | solution.py:521
  242.0 18.8 %shard_map.307 = (f32[512,1024]{1,0:T(8,128)}, bf16[512,1024]{1,0:T(8,128)(2,1)}, bf16[512,1024]{1,0:T(8,128)(2,1)}, f32[8,1024]{1,0:T(8,128)}) custom-call(s32[10]{0:T(128)} %pad_add_fusion.where, bf16[512,4096]{1,0:T(8,128)(2,1)} %get-tuple-element.124.grad_inner, bf16[256,4096]{1,0:T(8,128)(2,1)} %own.12, bf16[2,3,256,512]{3,2,1,0:T(8,128)(2,1)} %pad_maximum_fusion.a, ...), custom_call_target="tpu_custom_call" | custom-call | bytes 70110000 | tf_op jit(solution)/shard_map/pallas_call | solution.py:605
  260.8 5.7 %shard_map.308 = bf16[1,1024,512]{2,1,0:T(8,128)(2,1)} custom-call(s32[10]{0:T(128)} %pad_add_fusion.where, bf16[1,4096,512]{2,1,0:T(8,128)(2,1)} %bitcast.106, bf16[1,4096,512]{2,1,0:T(8,128)(2,1)} %bitcast.20.refs_1_.refs_5_, bf16[1,512,1024]{2,1,0:T(8,128)(2,1)} %bitcast.110, bf16[1,512,512]{2,1,0:T(8,128)(2,1)} %bitcast.122, ...), custom_call_target="tpu_custom_call" | custom-call | bytes 22140000 | tf_op jit(solution)/shard_map/pallas_call | solution.py:771
  266.5 13.2 %shard_map.309 = (bf16[4,512,512]{2,1,0:T(8,128)(2,1)}, f32[3,1,512]{2,1,0:T(1,128)}) custom-call(s32[10]{0:T(128)} %pad_add_fusion.where, bf16[512,4096]{1,0:T(8,128)(2,1)} %get-tuple-element.103.q.k.v, bf16[512,4096]{1,0:T(8,128)(2,1)} %get-tuple-element.103.q.k.v, bf16[512,4096]{1,0:T(8,128)(2,1)} %get-tuple-element.103.q.k.v, ...), custom_call_target="tpu_custom_call" | custom-call | bytes 47970000 | tf_op jit(solution)/shard_map/pallas_call | solution.py:273
  280.7 7.1 %shard_map.310 = bf16[2,1024,512]{2,1,0:T(8,128)(2,1)} custom-call(s32[10]{0:T(128)} %pad_add_fusion.where, bf16[1,1024,512]{2,1,0:T(8,128)(2,1)} %bitcast.116, bf16[1,1024,512]{2,1,0:T(8,128)(2,1)} %bitcast.24.refs_1_.refs_5_, bf16[1,512,4096]{2,1,0:T(8,128)(2,1)} %bitcast.100, bf16[1,512,2048]{2,1,0:T(8,128)(2,1)} %bitcast.26.refs_3_.refs_7_, ...), custom_call_target="tpu_custom_call" | custom-call | bytes 22140000 | tf_op jit(solution)/shard_map/pallas_call | solution.py:771
  288.8 6.0 %shard_map.311 = (bf16[256,512]{1,0:T(8,128)(2,1)}, bf16[256,512]{1,0:T(8,128)(2,1)}, bf16[256,512]{1,0:T(8,128)(2,1)}, bf16[256,512]{1,0:T(8,128)(2,1)}) custom-call(s32[10]{0:T(128)} %pad_add_fusion.where, bf16[1,4096,512]{2,1,0:T(8,128)(2,1)} %bitcast.107, bf16[1,4096,512]{2,1,0:T(8,128)(2,1)} %bitcast.20.refs_1_.refs_5_, ...), custom_call_target="tpu_custom_call" | custom-call | bytes 22140000 | tf_op jit(solution)/shard_map/pallas_call | solution.py:771
  294.8 13.0 %shard_map.312 = (bf16[4,512,512]{2,1,0:T(8,128)(2,1)}, f32[3,1,512]{2,1,0:T(1,128)}) custom-call(s32[10]{0:T(128)} %pad_add_fusion.where, bf16[512,4096]{1,0:T(8,128)(2,1)} %get-tuple-element.103.q.k.v, bf16[512,4096]{1,0:T(8,128)(2,1)} %get-tuple-element.103.q.k.v, bf16[512,4096]{1,0:T(8,128)(2,1)} %get-tuple-element.103.q.k.v, ...), custom_call_target="tpu_custom_call" | custom-call | bytes 47970000 | tf_op jit(solution)/shard_map/pallas_call | solution.py:273
  307.8 7.2 %shard_map.313 = bf16[2,1024,512]{2,1,0:T(8,128)(2,1)} custom-call(s32[10]{0:T(128)} %pad_add_fusion.where, bf16[2,1024,512]{2,1,0:T(8,128)(2,1)} %get-tuple-element.128.refs_0_.refs_4_, bf16[2,1024,512]{2,1,0:T(8,128)(2,1)} %collective-permute-done.28.refs_1_.refs_5_, bf16[4,512,512]{2,1,0:T(8,128)(2,1)} %get-tuple-element.143.refs_2_.refs_6_.mine, ...), custom_call_target="tpu_custom_call" | custom-call | bytes 22140000 | tf_op jit(solution)/shard_map/pallas_call | solution.py:771
  315.7 5.7 %shard_map.314 = bf16[1,1024,512]{2,1,0:T(8,128)(2,1)} custom-call(s32[10]{0:T(128)} %pad_add_fusion.where, bf16[1,1024,512]{2,1,0:T(8,128)(2,1)} %bitcast.118, bf16[1,1024,512]{2,1,0:T(8,128)(2,1)} %bitcast.24.refs_1_.refs_5_, bf16[1,512,4096]{2,1,0:T(8,128)(2,1)} %bitcast.102, bf16[1,512,2048]{2,1,0:T(8,128)(2,1)} %bitcast.26.refs_3_.refs_7_, ...), custom_call_target="tpu_custom_call" | custom-call | bytes 22140000 | tf_op jit(solution)/shard_map/pallas_call | solution.py:771
  330.2 13.4 %shard_map.315 = f32[512,1024]{1,0:T(8,128)} custom-call(s32[10]{0:T(128)} %pad_add_fusion.where, bf16[4,512,512]{2,1,0:T(8,128)(2,1)} %get-tuple-element.143.refs_2_.refs_6_.mine, bf16[4,512,512]{2,1,0:T(8,128)(2,1)} %get-tuple-element.134.others, bf16[256,3072]{1,0:T(8,128)(2,1)} %own.13, bf16[2,3,256,512]{3,2,1,0:T(8,128)(2,1)} %copy-done, ...), custom_call_target="tpu_custom_call" | custom-call | bytes 44280000 | tf_op jit(solution)/shard_map/pallas_call | solution.py:667
  346.9 6.1 %shard_map.316 = (bf16[256,512]{1,0:T(8,128)(2,1)}, bf16[256,512]{1,0:T(8,128)(2,1)}, bf16[256,512]{1,0:T(8,128)(2,1)}, bf16[256,512]{1,0:T(8,128)(2,1)}) custom-call(s32[10]{0:T(128)} %pad_add_fusion.where, bf16[1,1024,512]{2,1,0:T(8,128)(2,1)} %bitcast.119, bf16[1,1024,512]{2,1,0:T(8,128)(2,1)} %bitcast.24.refs_1_.refs_5_, ...), custom_call_target="tpu_custom_call" | custom-call | bytes 22140000 | tf_op jit(solution)/shard_map/pallas_call | solution.py:771
  353.0 5.8 %shard_map.317 = bf16[1,1024,512]{2,1,0:T(8,128)(2,1)} custom-call(s32[10]{0:T(128)} %pad_add_fusion.where, bf16[2,1024,512]{2,1,0:T(8,128)(2,1)} %get-tuple-element.128.refs_0_.refs_4_, bf16[2,1024,512]{2,1,0:T(8,128)(2,1)} %collective-permute-done.28.refs_1_.refs_5_, bf16[4,512,512]{2,1,0:T(8,128)(2,1)} %get-tuple-element.143.refs_2_.refs_6_.mine, ...), custom_call_target="tpu_custom_call" | custom-call | bytes 22140000 | tf_op jit(solution)/shard_map/pallas_call | solution.py:771
  367.7 15.9 %collective-permute-done.43 = bf16[256,512]{1,0:T(8,128)(2,1)S(1)} collective-permute-done((bf16[256,512]{1,0:T(8,128)(2,1)}, bf16[256,512]{1,0:T(8,128)(2,1)S(1)}, u32[]{:S(2)}, u32[]{:S(2)}) %collective-permute-start.43) | collective-permute-done | bytes 262176 | tf_op jit(solution)/shard_map/ppermute | solution.py:820
  387.9 6.1 %shard_map.318 = (bf16[256,512]{1,0:T(8,128)(2,1)}, bf16[256,512]{1,0:T(8,128)(2,1)}, bf16[256,512]{1,0:T(8,128)(2,1)}, bf16[256,512]{1,0:T(8,128)(2,1)}) custom-call(s32[10]{0:T(128)} %pad_add_fusion.where, bf16[2,1024,512]{2,1,0:T(8,128)(2,1)} %get-tuple-element.128.refs_0_.refs_4_, bf16[2,1024,512]{2,1,0:T(8,128)(2,1)} %collective-permute-done.28.refs_1_.refs_5_, ...), custom_call_target="tpu_custom_call" | custom-call | bytes 22140000 | tf_op jit(solution)/shard_map/pallas_call | solution.py:771
  396.0 4.8 %collective-permute-done.36 = bf16[256,512]{1,0:T(8,128)(2,1)S(1)} collective-permute-done((bf16[256,512]{1,0:T(8,128)(2,1)}, bf16[256,512]{1,0:T(8,128)(2,1)S(1)}, u32[]{:S(2)}, u32[]{:S(2)}) %collective-permute-start.36) | collective-permute-done | bytes 262176 | tf_op jit(solution)/shard_map/ppermute | solution.py:820
  400.8 15.0 %collective-permute-done.37 = bf16[256,512]{1,0:T(8,128)(2,1)S(1)} collective-permute-done((bf16[256,512]{1,0:T(8,128)(2,1)}, bf16[256,512]{1,0:T(8,128)(2,1)S(1)}, u32[]{:S(2)}, u32[]{:S(2)}) %collective-permute-start.37) | collective-permute-done | bytes 262176 | tf_op jit(solution)/shard_map/ppermute | solution.py:820
  420.5 4.9 %collective-permute-done.46 = bf16[1,256,512]{2,1,0:T(8,128)(2,1)S(1)} collective-permute-done((bf16[1,256,512]{2,1,0:T(8,128)(2,1)S(1)}, bf16[1,256,512]{2,1,0:T(8,128)(2,1)S(1)}, u32[]{:S(2)}, u32[]{:S(2)}) %collective-permute-start.46) | collective-permute-done | bytes 262176 | tf_op jit(solution)/shard_map/ppermute | solution.py:832
  435.3 7.7 %collective-permute-done.52 = f32[4,3072]{1,0:T(4,128)S(1)} collective-permute-done((f32[4,3072]{1,0:T(4,128)S(1)}, f32[4,3072]{1,0:T(4,128)S(1)}, u32[]{:S(2)}, u32[]{:S(2)}) %collective-permute-start.52) | collective-permute-done | bytes 49184 | tf_op jit(solution)/shard_map/ppermute | solution.py:832
  (239 shorter events, 136.2 us)
Async XLA Ops:
  1.7 19.0 %collective-permute-start.1 = (bf16[256,512]{1,0:T(8,128)(2,1)S(1)}, bf16[256,512]{1,0:T(8,128)(2,1)S(1)}, u32[]{:S(2)}, u32[]{:S(2)}) collective-permute-start(bf16[256,512]{1,0:T(8,128)(2,1)S(1)} %constant_dynamic-slice_fusion.1), channel_id=1, source_target_pairs={{0,2},{1,3},{2,0},{3,1},{4,6},{5,7},{6,4},{7,5},{8,10},{9,11},{10,... | collective-permute-start | bytes 786440 | tf_op jit(solution)/shard_map/ppermute | solution.py:817
  4.2 33.4 %collective-permute-start.2 = (bf16[256,512]{1,0:T(8,128)(2,1)S(1)}, bf16[256,512]{1,0:T(8,128)(2,1)S(1)}, u32[]{:S(2)}, u32[]{:S(2)}) collective-permute-start(bf16[256,512]{1,0:T(8,128)(2,1)S(1)} %constant_dynamic-slice_fusion.1), channel_id=1, source_target_pairs={{0,1},{1,2},{2,3},{3,0},{4,5},{5,6},{6,7},{7,4},{8,9},{9,10},{10,1... | collective-permute-start | bytes 786440 | tf_op jit(solution)/shard_map/ppermute | solution.py:817
  7.4 35.2 %collective-permute-start.5 = (bf16[256,512]{1,0:T(8,128)(2,1)S(1)}, bf16[256,512]{1,0:T(8,128)(2,1)S(1)}, u32[]{:S(2)}, u32[]{:S(2)}) collective-permute-start(bf16[256,512]{1,0:T(8,128)(2,1)S(1)} %fusion), channel_id=1, source_target_pairs={{0,3},{1,0},{2,1},{3,2},{4,7},{5,4},{6,5},{7,6},{8,11},{9,8},{10,9... | collective-permute-start | bytes 786440 | tf_op jit(solution)/shard_map/ppermute | solution.py:817
  7.5 35.7 %collective-permute-start.6 = (bf16[256,512]{1,0:T(8,128)(2,1)S(1)}, bf16[256,512]{1,0:T(8,128)(2,1)S(1)}, u32[]{:S(2)}, u32[]{:S(2)}) collective-permute-start(bf16[256,512]{1,0:T(8,128)(2,1)S(1)} %fusion), channel_id=1, source_target_pairs={{0,2},{1,3},{2,0},{3,1},{4,6},{5,7},{6,4},{7,5},{8,10},{9,11},{10,... | collective-permute-start | bytes 786440 | tf_op jit(solution)/shard_map/ppermute | solution.py:817
  8.9 40.0 %collective-permute-start.7 = (bf16[256,512]{1,0:T(8,128)(2,1)S(1)}, bf16[256,512]{1,0:T(8,128)(2,1)S(1)}, u32[]{:S(2)}, u32[]{:S(2)}) collective-permute-start(bf16[256,512]{1,0:T(8,128)(2,1)S(1)} %fusion), channel_id=1, source_target_pairs={{0,1},{1,2},{2,3},{3,0},{4,5},{5,6},{6,7},{7,4},{8,9},{9,10},{10,1... | collective-permute-start | bytes 786440 | tf_op jit(solution)/shard_map/ppermute | solution.py:817
  51.6 39.3 %collective-permute-start.4 = (bf16[2,3,256,512]{3,2,1,0:T(8,128)(2,1)}, bf16[2,3,256,512]{3,2,1,0:T(8,128)(2,1)}, u32[]{:S(2)}, u32[]{:S(2)}) collective-permute-start(bf16[2,3,256,512]{3,2,1,0:T(8,128)(2,1)} %pad_maximum_fusion.a), channel_id=1, source_target_pairs={{0,16},{4,12},{8,24},{12,4},{16,0},{20,28},{24,8},{28,20},{1,17},{... | collective-permute-start | bytes 4718600 | tf_op jit(solution)/shard_map/ppermute | solution.py:832
  63.7 31.8 %collective-permute-start.9 = (bf16[2,3,256,512]{3,2,1,0:T(8,128)(2,1)S(1)}, bf16[2,3,256,512]{3,2,1,0:T(8,128)(2,1)S(1)}, u32[]{:S(2)}, u32[]{:S(2)}) collective-permute-start(bf16[2,3,256,512]{3,2,1,0:T(8,128)(2,1)S(1)} %pad_maximum_fusion.1.a), channel_id=1, source_target_pairs={{0,16},{4,12},{8,24},{12,4},{16,0},{20,28},{24,8},{28,20},{1,17},{... | collective-permute-start | bytes 4718600 | tf_op jit(solution)/shard_map/ppermute | solution.py:832
  72.4 21.4 %collective-permute-start.15 = (bf16[128,1024]{1,0:T(8,128)(2,1)}, bf16[128,1024]{1,0:T(8,128)(2,1)}, u32[]{:S(2)}, u32[]{:S(2)}) collective-permute-start(bf16[128,1024]{1,0:T(8,128)(2,1)} %constant_dynamic-slice_fusion), channel_id=1, source_target_pairs={{0,3},{1,0},{2,1},{3,2},{4,7},{5,4},{6,5},{7,6},{8,11},{9,8},{10,9... | collective-permute-start | bytes 786440 | tf_op jit(solution)/shard_map/ppermute | solution.py:817
  72.5 21.4 %collective-permute-start.16 = (bf16[128,1024]{1,0:T(8,128)(2,1)}, bf16[128,1024]{1,0:T(8,128)(2,1)}, u32[]{:S(2)}, u32[]{:S(2)}) collective-permute-start(bf16[128,1024]{1,0:T(8,128)(2,1)} %constant_dynamic-slice_fusion), channel_id=1, source_target_pairs={{0,2},{1,3},{2,0},{3,1},{4,6},{5,7},{6,4},{7,5},{8,10},{9,11},{10,... | collective-permute-start | bytes 786440 | tf_op jit(solution)/shard_map/ppermute | solution.py:817
  90.8 59.3 %collective-permute-start.19 = (bf16[2,3,256,512]{3,2,1,0:T(8,128)(2,1)}, bf16[2,3,256,512]{3,2,1,0:T(8,128)(2,1)}, u32[]{:S(2)}, u32[]{:S(2)}) collective-permute-start(bf16[2,3,256,512]{3,2,1,0:T(8,128)(2,1)} %pad_maximum_fusion.a), channel_id=1, source_target_pairs={{0,4},{4,0},{1,5},{5,1},{2,6},{6,2},{3,7},{7,3},{8,12},{12,8},{9,1... | collective-permute-start | bytes 4718600 | tf_op jit(solution)/shard_map/ppermute | solution.py:823
  93.9 56.2 %collective-permute-start.20 = (bf16[2,3,256,512]{3,2,1,0:T(8,128)(2,1)}, bf16[2,3,256,512]{3,2,1,0:T(8,128)(2,1)}, u32[]{:S(2)}, u32[]{:S(2)}) collective-permute-start(bf16[2,3,256,512]{3,2,1,0:T(8,128)(2,1)} %collective-permute-done.4.b), channel_id=1, source_target_pairs={{0,4},{4,0},{1,5},{5,1},{2,6},{6,2},{3,7},{7,3},{8,12},{12,8},{9,1... | collective-permute-start | bytes 4718600 | tf_op jit(solution)/shard_map/ppermute | solution.py:823
  166.1 48.5 %collective-permute-start.24 = (bf16[4096,512]{1,0:T(8,128)(2,1)}, bf16[4096,512]{1,0:T(8,128)(2,1)}, u32[]{:S(2)}, u32[]{:S(2)}) collective-permute-start(bf16[4096,512]{1,0:T(8,128)(2,1)} %get-tuple-element.118), channel_id=1, source_target_pairs={{0,4},{4,0},{1,5},{5,1},{2,6},{6,2},{3,7},{7,3},{8,12},{12,8},{9,1... | collective-permute-start | bytes 12582920 | tf_op jit(solution)/shard_map/ppermute | solution.py:823
  168.7 20.8 %collective-permute-start.21 = (bf16[2,3,128,1024]{3,2,1,0:T(8,128)(2,1)}, bf16[2,3,128,1024]{3,2,1,0:T(8,128)(2,1)S(1)}, u32[]{:S(2)}, u32[]{:S(2)}) collective-permute-start(bf16[2,3,128,1024]{3,2,1,0:T(8,128)(2,1)} %pad_maximum_fusion.2.a), channel_id=1, source_target_pairs={{0,16},{4,12},{8,24},{12,4},{16,0},{20,28},{24,8},{28,20},{1,17},{... | collective-permute-start | bytes 4718600 | tf_op jit(solution)/shard_map/ppermute | solution.py:832
  171.2 22.4 %collective-permute-start.22 = (bf16[2,3,128,1024]{3,2,1,0:T(8,128)(2,1)}, bf16[2,3,128,1024]{3,2,1,0:T(8,128)(2,1)S(1)}, u32[]{:S(2)}, u32[]{:S(2)}) collective-permute-start(bf16[2,3,128,1024]{3,2,1,0:T(8,128)(2,1)} %pad_maximum_fusion.2.a), channel_id=1, source_target_pairs={{0,4},{4,0},{1,5},{5,1},{2,6},{6,2},{3,7},{7,3},{8,12},{12,8},{9,1... | collective-permute-start | bytes 4718600 | tf_op jit(solution)/shard_map/ppermute | solution.py:823
  212.8 48.0 %collective-permute-start.28 = (bf16[2,1024,512]{2,1,0:T(8,128)(2,1)}, bf16[2,1024,512]{2,1,0:T(8,128)(2,1)}, u32[]{:S(2)}, u32[]{:S(2)}) collective-permute-start(bf16[2,1024,512]{2,1,0:T(8,128)(2,1)} %get-tuple-element.128.refs_0_.refs_4_), channel_id=1, source_target_pairs={{0,4},{4,0},{1,5},{5,1},{2,6},{6,2},{3,7},{7,3},{8,12},{12,8},{9,1... | collective-permute-start | bytes 6291464 | tf_op jit(solution)/shard_map/ppermute | solution.py:823
  222.7 38.1 %collective-permute-start.27 = (bf16[2,1024,512]{2,1,0:T(8,128)(2,1)}, bf16[2,1024,512]{2,1,0:T(8,128)(2,1)}, u32[]{:S(2)}, u32[]{:S(2)}) collective-permute-start(bf16[2,1024,512]{2,1,0:T(8,128)(2,1)} %shard_map.305), channel_id=1, source_target_pairs={{0,8},{4,20},{8,0},{12,28},{16,24},{20,4},{24,16},{28,12},{1,9},{5... | collective-permute-start | bytes 6291464 | tf_op jit(solution)/shard_map/ppermute | solution.py:832
  241.8 38.6 %collective-permute-start.30 = (bf16[512,2048]{1,0:T(8,128)(2,1)}, bf16[512,2048]{1,0:T(8,128)(2,1)}, u32[]{:S(2)}, u32[]{:S(2)}) collective-permute-start(bf16[512,2048]{1,0:T(8,128)(2,1)} %get-tuple-element.130), channel_id=1, source_target_pairs={{0,4},{4,0},{1,5},{5,1},{2,6},{6,2},{3,7},{7,3},{8,12},{12,8},{9,1... | collective-permute-start | bytes 6291464 | tf_op jit(solution)/shard_map/ppermute | solution.py:823
  279.6 28.2 %collective-permute-start.32 = (bf16[4,512,512]{2,1,0:T(8,128)(2,1)}, bf16[4,512,512]{2,1,0:T(8,128)(2,1)}, u32[]{:S(2)}, u32[]{:S(2)}) collective-permute-start(bf16[4,512,512]{2,1,0:T(8,128)(2,1)} %get-tuple-element.134.others), channel_id=1, source_target_pairs={{0,4},{4,0},{1,5},{5,1},{2,6},{6,2},{3,7},{7,3},{8,12},{12,8},{9,1... | collective-permute-start | bytes 6291464 | tf_op jit(solution)/shard_map/ppermute | solution.py:823
  287.9 27.8 %collective-permute-start.31 = (bf16[2,1024,512]{2,1,0:T(8,128)(2,1)}, bf16[2,1024,512]{2,1,0:T(8,128)(2,1)}, u32[]{:S(2)}, u32[]{:S(2)}) collective-permute-start(bf16[2,1024,512]{2,1,0:T(8,128)(2,1)} %shard_map.310), channel_id=1, source_target_pairs={{0,8},{4,20},{8,0},{12,28},{16,24},{20,4},{24,16},{28,12},{1,9},{5... | collective-permute-start | bytes 6291464 | tf_op jit(solution)/shard_map/ppermute | solution.py:832
  315.0 38.0 %collective-permute-start.33 = (bf16[2,1024,512]{2,1,0:T(8,128)(2,1)}, bf16[2,1024,512]{2,1,0:T(8,128)(2,1)}, u32[]{:S(2)}, u32[]{:S(2)}) collective-permute-start(bf16[2,1024,512]{2,1,0:T(8,128)(2,1)} %shard_map.313), channel_id=1, source_target_pairs={{0,8},{4,20},{8,0},{12,28},{16,24},{20,4},{24,16},{28,12},{1,9},{5... | collective-permute-start | bytes 6291464 | tf_op jit(solution)/shard_map/ppermute | solution.py:832
  321.4 25.6 %collective-permute-start.34 = (bf16[1,1024,512]{2,1,0:T(8,128)(2,1)}, bf16[1,1024,512]{2,1,0:T(8,128)(2,1)}, u32[]{:S(2)}, u32[]{:S(2)}) collective-permute-start(bf16[1,1024,512]{2,1,0:T(8,128)(2,1)} %shard_map.314), channel_id=1, source_target_pairs={{0,16},{4,12},{8,24},{12,4},{16,0},{20,28},{24,8},{28,20},{1,17},{... | collective-permute-start | bytes 3145736 | tf_op jit(solution)/shard_map/ppermute | solution.py:832
  325.8 36.7 %collective-permute-start.39 = (bf16[256,512]{1,0:T(8,128)(2,1)}, bf16[256,512]{1,0:T(8,128)(2,1)S(1)}, u32[]{:S(2)}, u32[]{:S(2)}) collective-permute-start(bf16[256,512]{1,0:T(8,128)(2,1)} %get-tuple-element.154), channel_id=1, source_target_pairs={{0,1},{1,2},{2,3},{3,0},{4,5},{5,6},{6,7},{7,4},{8,9},{9,10},{10,1... | collective-permute-start | bytes 786440 | tf_op jit(solution)/shard_map/ppermute | solution.py:820
  328.1 36.5 %collective-permute-start.40 = (bf16[256,512]{1,0:T(8,128)(2,1)}, bf16[256,512]{1,0:T(8,128)(2,1)S(1)}, u32[]{:S(2)}, u32[]{:S(2)}) collective-permute-start(bf16[256,512]{1,0:T(8,128)(2,1)} %get-tuple-element.155), channel_id=1, source_target_pairs={{0,2},{1,3},{2,0},{3,1},{4,6},{5,7},{6,4},{7,5},{8,10},{9,11},{10,... | collective-permute-start | bytes 786440 | tf_op jit(solution)/shard_map/ppermute | solution.py:820
  330.2 34.4 %collective-permute-start.41 = (bf16[256,512]{1,0:T(8,128)(2,1)}, bf16[256,512]{1,0:T(8,128)(2,1)}, u32[]{:S(2)}, u32[]{:S(2)}) collective-permute-start(bf16[256,512]{1,0:T(8,128)(2,1)} %get-tuple-element.156), channel_id=1, source_target_pairs={{0,3},{1,0},{2,1},{3,2},{4,7},{5,4},{6,5},{7,6},{8,11},{9,8},{10,9... | collective-permute-start | bytes 786440 | tf_op jit(solution)/shard_map/ppermute | solution.py:820
  358.8 29.1 %collective-permute-start.35 = (bf16[1,1024,512]{2,1,0:T(8,128)(2,1)}, bf16[1,1024,512]{2,1,0:T(8,128)(2,1)}, u32[]{:S(2)}, u32[]{:S(2)}) collective-permute-start(bf16[1,1024,512]{2,1,0:T(8,128)(2,1)} %shard_map.317), channel_id=1, source_target_pairs={{0,16},{4,12},{8,24},{12,4},{16,0},{20,28},{24,8},{28,20},{1,17},{... | collective-permute-start | bytes 3145736 | tf_op jit(solution)/shard_map/ppermute | solution.py:832
  362.5 21.1 %collective-permute-start.43 = (bf16[256,512]{1,0:T(8,128)(2,1)}, bf16[256,512]{1,0:T(8,128)(2,1)S(1)}, u32[]{:S(2)}, u32[]{:S(2)}) collective-permute-start(bf16[256,512]{1,0:T(8,128)(2,1)} %get-tuple-element.158), channel_id=1, source_target_pairs={{0,2},{1,3},{2,0},{3,1},{4,6},{5,7},{6,4},{7,5},{8,10},{9,11},{10,... | collective-permute-start | bytes 786440 | tf_op jit(solution)/shard_map/ppermute | solution.py:820
  364.6 22.2 %collective-permute-start.44 = (bf16[256,512]{1,0:T(8,128)(2,1)}, bf16[256,512]{1,0:T(8,128)(2,1)S(1)}, u32[]{:S(2)}, u32[]{:S(2)}) collective-permute-start(bf16[256,512]{1,0:T(8,128)(2,1)} %get-tuple-element.159), channel_id=1, source_target_pairs={{0,3},{1,0},{2,1},{3,2},{4,7},{5,4},{6,5},{7,6},{8,11},{9,8},{10,9... | collective-permute-start | bytes 786440 | tf_op jit(solution)/shard_map/ppermute | solution.py:820
  394.0 24.9 %collective-permute-start.45 = (bf16[1,2,256,512]{3,2,0,1:T(8,128)(2,1)S(1)}, bf16[1,2,256,512]{3,2,0,1:T(8,128)(2,1)S(1)}, u32[]{:S(2)}, u32[]{:S(2)}) collective-permute-start(bf16[1,2,256,512]{3,2,0,1:T(8,128)(2,1)S(1)} %pad_maximum_fusion.4), channel_id=1, source_target_pairs={{0,8},{4,20},{8,0},{12,28},{16,24},{20,4},{24,16},{28,12},{1,9},{5... | collective-permute-start | bytes 1572872 | tf_op jit(solution)/shard_map/ppermute | solution.py:832
  394.3 21.6 %collective-permute-start.37 = (bf16[256,512]{1,0:T(8,128)(2,1)}, bf16[256,512]{1,0:T(8,128)(2,1)S(1)}, u32[]{:S(2)}, u32[]{:S(2)}) collective-permute-start(bf16[256,512]{1,0:T(8,128)(2,1)} %get-tuple-element.152), channel_id=1, source_target_pairs={{0,2},{1,3},{2,0},{3,1},{4,6},{5,7},{6,4},{7,5},{8,10},{9,11},{10,... | collective-permute-start | bytes 786440 | tf_op jit(solution)/shard_map/ppermute | solution.py:820
  394.3 23.5 %collective-permute-start.38 = (bf16[256,512]{1,0:T(8,128)(2,1)}, bf16[256,512]{1,0:T(8,128)(2,1)S(1)}, u32[]{:S(2)}, u32[]{:S(2)}) collective-permute-start(bf16[256,512]{1,0:T(8,128)(2,1)} %get-tuple-element.153), channel_id=1, source_target_pairs={{0,3},{1,0},{2,1},{3,2},{4,7},{5,4},{6,5},{7,6},{8,11},{9,8},{10,9... | collective-permute-start | bytes 786440 | tf_op jit(solution)/shard_map/ppermute | solution.py:820
  420.4 24.4 %collective-permute-start.56 = (bf16[2,2,256,512]{3,2,0,1:T(8,128)(2,1)S(1)}, bf16[2,2,256,512]{3,2,0,1:T(8,128)(2,1)}, u32[]{:S(2)}, u32[]{:S(2)}) collective-permute-start(bf16[2,2,256,512]{3,2,0,1:T(8,128)(2,1)S(1)} %pad_maximum_fusion.3), channel_id=1, source_target_pairs={{0,16},{4,12},{8,24},{12,4},{16,0},{20,28},{24,8},{28,20},{1,17},{... | collective-permute-start | bytes 3145736 | tf_op jit(solution)/shard_map/ppermute | solution.py:832
  425.5 18.2 %collective-permute-start.47 = (bf16[2,256,512]{2,1,0:T(8,128)(2,1)S(1)}, bf16[2,256,512]{2,1,0:T(8,128)(2,1)}, u32[]{:S(2)}, u32[]{:S(2)}) collective-permute-start(bf16[2,256,512]{2,1,0:T(8,128)(2,1)S(1)} %constant_dynamic-update-slice_fusion.refs_0_), channel_id=1, source_target_pairs={{0,16},{4,12},{8,24},{12,4},{16,0},{20,28},{24,8},{28,20},{1,17},{... | collective-permute-start | bytes 1572872 | tf_op jit(solution)/shard_map/ppermute | solution.py:832
  (50 other events, 569.1 us)

commit v4 on v3

--- a/solution.py
+++ b/solution.py
@@ -336,7 +336,7 @@
     )(where, context, x, w_out, rest_out, bias, gain, shift)
 
 
-def inner_kernel(dims, where, x, own, a, b, c, d, bias, act, turned, slope, rolled, weight):
+def inner_kernel(dims, where, x, own, a, b, c, d, bias, act, early, late, slope, rolled, weight):
     group, half = dims
     unit = pl.program_id(0)
 
@@ -349,7 +349,9 @@
     below = 0.5 + 0.5 * lax.erf(total * (0.5**0.5))
     value = (total * below).astype(BF16)
     act[...] = value
-    turned[...] = value.T
+    half_seq = early.shape[1]
+    early[...] = value[:half_seq].T
+    late[...] = value[half_seq:].T
     density = jnp.exp(-0.5 * total * total) * ((2.0 * jnp.pi) ** -0.5)
     slope[...] = (below + total * density).astype(BF16)
 
@@ -369,12 +371,14 @@
         [fixed((seq, width)), columns_at(rows)] + part_specs(parts) + [columns_at(1)],
         [
             columns_at(seq),
-            spec((block, seq), lambda u, w: (block_of(w, u, chips), 0)),
+            spec((block, seq // 2), lambda u, w: (block_of(w, u, chips), 0)),
+            spec((block, seq // 2), lambda u, w: (block_of(w, u, chips), 0)),
             columns_at(seq),
         ],
         [
             struct((seq, columns), BF16),
-            struct((columns, seq), BF16),
+            struct((columns, seq // 2), BF16),
+            struct((columns, seq // 2), BF16),
             struct((seq, columns), BF16),
         ],
         [pltpu.VMEM((seq, width), BF16), pltpu.VMEM((width, block), BF16)],
@@ -681,9 +685,8 @@
     )(where, mine, others, w_qkv, *parts, first)
 
 
-def widen_kernel(dims, where, *refs):
-    parts, outs = refs[:4], refs[4:]
-    phases, by_rows = dims
+def widen_rows_kernel(phases, where, a, b, c, d, out):
+    parts = (a, b, c, d)
     chips = 1 << phases
     half = chips // 2
     for side in range(2):
@@ -691,29 +694,61 @@
         for order in range(chips):
             value = parts[2 * side + order // half][order % half].astype(F32)
             rows, columns = value.shape
-            chip = where[2 + side * chips + order]
-            if by_rows:
-                outs[0][
-                    pl.ds(pl.multiple_of(chip * rows, 8), rows),
-                    pl.ds(pl.multiple_of(core * columns, 128), columns),
-                ] = value
-                continue
-            start = (2 * chip + core) * columns
-            base = 0
-            for out in outs:
-                size = out.shape[1]
-                inside = (start >= base) & (start < base + size)
-
-                @pl.when(inside)
-                def _(out=out, start=start, base=base, value=value):
-                    out[:, pl.ds(pl.multiple_of(start - base, 128), columns)] = value
-
-                base += size
-
-
-def widen(where, parts, phases, by_rows, shapes):
+            out[
+                pl.ds(pl.multiple_of(where[2 + side * chips + order] * rows, 8), rows),
+                pl.ds(pl.multiple_of(core * columns, 128), columns),
+            ] = value
+
+
+def widen_rows(where, parts, phases, shape):
     return call(
-        partial(widen_kernel, (phases, by_rows)),
+        partial(widen_rows_kernel, phases),
+        (1,),
+        [fixed(part.shape) for part in parts],
+        fixed(shape),
+        struct(shape, F32),
+        micros=4,
+    )(where, *parts)
+
+
+def widen_kernel(dims, where, *refs):
+    parts, outs, extra = refs[:4], refs[4:-1], refs[-1]
+    phases, kinds = dims
+    chips = 1 << phases
+    half = chips // 2
+    summed = jnp.zeros(extra.shape, F32)
+    for side in range(2):
+        core = where[1] if side == 0 else 1 - where[1]
+        for order in range(chips):
+            start = 2 * where[2 + side * chips + order] + core
+            given = parts[2 * side + order // half].at[order % half]
+            at, row = 0, 0
+            for count in kinds:
+                rows = outs[at].shape[0]
+                value = given[row : row + rows, :].astype(F32)
+                row += rows
+                columns = value.shape[1]
+                base = 0
+                for out in outs[at : at + count]:
+                    size = out.shape[1]
+                    first = start * columns - base
+
+                    @pl.when((first >= 0) & (first < size))
+                    def _(out=out, first=first, value=value, columns=columns):
+                        out[:, pl.ds(pl.multiple_of(first, 128), columns)] = value
+
+                    base += size
+                at += count
+            summed = summed + given[row:, :].astype(F32)
+    extra[...] = summed
+
+
+def widen(where, parts, phases, kinds):
+    shapes = [shape for given in kinds for shape in given]
+    rows = sum(given[0][0] for given in kinds)
+    shapes.append((parts[0].shape[1] - rows, parts[0].shape[2]))
+    return call(
+        partial(widen_kernel, (phases, [len(given) for given in kinds])),
         (1,),
         [fixed(part.shape) for part in parts],
         [fixed(shape) for shape in shapes],
@@ -723,17 +758,23 @@
 
 
 def grads_kernel(dims, where, *refs):
-    orders, adds, last, group = dims
+    orders, adds, last, group, cuts, extra = dims
     units = len(orders)
     step = pl.program_id(0)
     at = 0
-    outs = refs[units * (4 + adds) :]
+    outs = refs[units * (2 + 2 * cuts + adds) + extra :]
     for u in range(units):
-        left, left_other, right, right_other = refs[at : at + 4]
-        value = dot(left[0], right[0]) + dot(left_other[0], right_other[0])
-        for add in refs[at + 4 : at + 4 + adds]:
+        right, right_other = refs[at : at + 2]
+        at += 2
+        value = 0.0
+        for given in (right, right_other):
+            size = given.shape[1] // cuts
+            for i in range(cuts):
+                value = value + dot(refs[at][0], given[0, i * size : (i + 1) * size, :])
+                at += 1
+        for add in refs[at : at + adds]:
             value = value + add[0].astype(F32)
-        at += 4 + adds
+        at += adds
         value = value.astype(BF16)
         if not last:
             outs[0][u] = value
@@ -742,34 +783,41 @@
 
             @pl.when(step == s)
             def _(s=s, value=value):
-                outs[s][...] = value
-
-
-def grads(where, left, right, maps, shape, units, received, group):
+                outs[s][: value.shape[0], :] = value
+                if extra:
+                    outs[s][value.shape[0] :, :] = refs[-group - 1][s]
+
+
+def grads(where, left, right, maps, shape, units, received, group, extra=None):
     rows, columns = shape
-    seq = left[0].shape[2]
+    cuts = len(left[0])
+    seq = left[0][0].shape[2]
     left_map, right_map, other_map = maps
     last = units == [0]
     ins, args = [], []
     for order in units:
         lefts = spec((1, rows, seq), partial(left_map, order))
-        rights = spec((1, seq, columns), partial(right_map, order))
-        others = spec((1, seq, columns), partial(other_map, order))
-        ins += [lefts, lefts, rights, others]
-        args += [left[0], left[1], right[0], right[1]]
+        ins.append(spec((1, seq * cuts, columns), partial(right_map, order)))
+        ins.append(spec((1, seq * cuts, columns), partial(other_map, order)))
+        ins += [lefts] * (2 * cuts)
+        args += [right[0], right[1], *left[0], *left[1]]
         for phase, value in enumerate(received):
             index = order >> (phase + 1)
             ins.append(spec((1, rows, columns), lambda s, w, index=index: (index, s, 0)))
             args.append(value)
     count = len(units)
+    more = 0 if extra is None else extra.shape[1]
+    if more:
+        ins.append(fixed(extra.shape))
+        args.append(extra)
     if last:
-        outs = [fixed((rows, columns))] * group
-        out_shape = [struct((rows, columns), BF16)] * group
+        outs = [fixed((rows + more, columns))] * group
+        out_shape = [struct((rows + more, columns), BF16)] * group
     else:
         outs = [spec((count, rows, columns), lambda s, w: (0, s, 0))]
         out_shape = [struct((count, group * rows, columns), BF16)]
     return call(
-        partial(grads_kernel, (units, len(received), last, group)),
+        partial(grads_kernel, (units, len(received), last, group, cuts, int(more > 0))),
         (group,),
         ins,
         outs,
@@ -877,17 +925,19 @@
             self.parts = (self.value, self.rest, self.side, sibling(after(self.rest, gates)))
 
     got_one = [from_shard(piece_one, s) for s in range(1, group)]
-    got_in = [from_shard(piece_in, s) for s in range(1, group)]
 
     vectors = (b_qv, b_out, gain_one, shift_one, b_in, b_down, gain_two, shift_two)
     sizes = [v.shape[0] for v in vectors]
     packed = jnp.concatenate(after(vectors, piece_one))
+    first_parts = Gather(jnp.stack(got_one)[None])
+    first_parts.step()
+    packed = after(packed, first_parts.first)
     got_packed = [from_shard(packed, s) for s in range(1, group)]
-
-    parts_one = gather(jnp.stack(got_one)[None], got_packed)
-    parts_in = Gather(jnp.stack(got_in)[None])
-    parts_in.step()
-    got_down = [from_shard(after(piece_down, got_in), s) for s in range(1, group)]
+    first_parts.finish()
+    parts_one = first_parts.parts
+    piece_in = after(piece_in, parts_one[3])
+    got_in = [from_shard(piece_in, s) for s in range(1, group)]
+    piece_down = after(piece_down, parts_one[3])
 
     relative = jnp.stack([packed] + got_packed)
     ordered = jnp.concatenate([relative, relative], axis=0)
@@ -905,11 +955,13 @@
     column, row = kind[:, None], kind[None, :]
 
     flat_in = tokens[0]
-    projected, rest_out = qkv(where, after(flat_in, parts_in.rest), w_qkv, parts_one, bias_qkv, group)
-    parts_in.finish()
+    projected, rest_out = qkv(where, flat_in, w_qkv, parts_one, bias_qkv, group)
+    parts_in = Gather(after(jnp.stack(got_in)[None], projected))
+    got_down = [from_shard(piece_down, s) for s in range(1, group)]
     count = model_width // (4 * HEAD_DIM)
     context, turned, logs_a = attention(where, projected, flat_in, column, row, 0, count)
-    parts_down = Gather(jnp.stack(got_down)[None])
+    parts_in.step(logs_a)
+    parts_down = Gather(after(jnp.stack(got_down)[None], logs_a))
     context, turned, logs_b = attention(
         where,
         projected,
@@ -920,11 +972,11 @@
         count,
         (context, turned),
     )
-    first_left = (turned, sibling(turned))
+    first_left = ([turned], [sibling(turned)])
     parts_down.step(logs_b)
     hidden, normed, normed_turned = out_norm(
         where,
-        after(context, parts_down.value),
+        context,
         flat_in,
         w_out,
         rest_out,
@@ -933,13 +985,13 @@
         norm_sone,
         group,
     )
+    parts_in.finish(hidden)
     parts_in = parts_in.parts
-    in_left = (normed_turned[None], sibling(normed_turned)[None])
-    act, act_turned, slope = inner(where, normed, w_in, parts_in, bias_in, group)
+    in_left = ([normed_turned[None]], [sibling(normed_turned)[None]])
+    where_down = where
+    act, *act_turned, slope = inner(where, normed, w_in, parts_in, bias_in, group)
     parts_down.finish(act)
     parts_down = parts_down.parts
-    down_left = (act_turned[None], sibling(act_turned)[None])
-    where_down = where
     if part_down % 128:
         merged = jnp.zeros((group - 1, ff_rows, model_width), BF16)
         for unit in range(reps):
@@ -947,10 +999,9 @@
             at = block_of(where, unit, chips) * part_down
             merged = lax.dynamic_update_slice_in_dim(merged, piece, at, axis=1)
         fourth = ff_rows // 4
-        parts_down = [
-            merged[:, b * fourth : (b + 1) * fourth][None] for b in (0, 2, 1, 3)
-        ]
+        parts_down = [merged[:, b * fourth : (b + 1) * fourth][None] for b in (0, 2, 1, 3)]
         where_down = jnp.stack([own, 0, 0, 1, 0, 1]).astype(jnp.int32)
+    down_left = ([v[None] for v in act_turned], [sibling(v)[None] for v in act_turned])
     output_rows, grad_second, grad_branch, branch_other, sums_two = outer(
         where_down,
         act,
@@ -981,9 +1032,9 @@
                 sent = self.send(*gates)
             return sent
 
-        def finish(self, *gates):
+        def finish(self, *gates, extra=None):
             received = after(self.received, gates)
-            parts = grads(*self.fixed, [0], received, group)
+            parts = grads(*self.fixed, [0], received, group, extra)
             self.own = parts[0]
             self.given = [to_shard(parts[s], s) for s in range(1, group)]
             return parts[0]
@@ -992,7 +1043,7 @@
             total = self.own.astype(F32)
             for value in self.given:
                 total = total + value.astype(F32)
-            return total.astype(BF16)
+            return total
 
     half = model_width // 2
     part_rows = ff_rows // chips
@@ -1021,23 +1072,24 @@
     )
     in_other = sibling(inner_other)
     sent = down.send_rest(grad_first, first_left)
-    logs = (logs_a, logs_b)
-    others, sums_others = attention_back(
-        where, projected, after(grad_context, sent), logs, grad_attn, column, row, False, part
-    )
     in_maps = (
         lambda o, s, w: (0, natural(w, s, group), 0),
         lambda o, s, w: (0, 0, 2 * w[2 + o] + w[1]),
         lambda o, s, w: (0, 0, w[2 + o]),
     )
-    in_right = after((grad_inner[None], in_other[None]), down.received, others)
+    in_right = after((grad_inner[None], in_other[None]), sent)
     inward = Scatter(in_left, in_right, in_maps, (rows, part_in))
     sent = inward.send()
-    done = down.finish(sent)
-    other_proj = sibling(others)
+    logs = (logs_a, logs_b)
+    others, sums_others = attention_back(
+        where, projected, after(grad_context, sent), logs, grad_attn, column, row, False, part
+    )
+    done = down.finish(others)
+    other_proj = sibling(after(others, done))
     mine, sums_mine = attention_back(
         where, projected, after(grad_context, done), logs, grad_attn, column, row, True, part
     )
+    sent = inward.send_rest(mine)
     each = model_width // part
 
     def plane(order, w):
@@ -1051,16 +1103,10 @@
         compact,
         compact,
     )
-    first = Scatter(first_left, (mine, other_proj), first_maps, (rows, part))
+    first_right = after((mine, other_proj), sent, down.given)
+    first = Scatter(first_left, first_right, first_maps, (rows, part))
     sent = first.send()
-    sent = inward.send_rest(sent)
-    share_down = down.total()[None]
-    grad_input = input_back(
-        where, after(mine, sent), others, grad_first, w_qkv, parts_one, group
-    )
-    done = inward.finish(grad_input)
-    sent = first.send_rest(done)
-    share_in = inward.total()[None]
+    gather_down = Gather(down.total().astype(BF16)[None, None])
     def blocks(core_parity):
         value = jnp.where(core == core_parity, sums_mine, sums_others)
         return value.reshape(3, -1, 1, part)
@@ -1077,37 +1123,32 @@
         sums_two[1],
     )
     small = jnp.concatenate([v.reshape(group, -1) for v in small], axis=1)
-    done = first.finish(sent, share_in)
-    shares = jnp.stack([share_down.reshape(share_in.shape), share_in], axis=1)
-    shares = after(shares, done)
-    gathered = Gather(shares)
-    share_one = after(first.total()[None], gathered.first)
-    gathered.step(share_one)
-    gathered.finish()
-    final_parts = gather(share_one)
-    small = after(small, done)
-    small = small + sibling(small)
-    for phase in range(phases):
-        small = small + swap(small, phase)
+    grad_input = input_back(
+        where, after(mine, sent), others, grad_first, w_qkv, parts_one, group
+    )
+    done = inward.finish(grad_input)
+    sent = first.send_rest(done)
     small = jnp.concatenate([small, small], axis=0)
     small = lax.dynamic_slice_in_dim(small, own, group, axis=0)
-    small = after(small, final_parts)
-    total = small[0]
-    for s in range(1, group):
-        total = total + to_shard(small[s], s)
-    down_parts = [
-        value[:, 0].reshape(-1, *share_down.shape[1:]) for value in gathered.parts
-    ]
-    in_parts = [value[:, 1] for value in gathered.parts]
-    (grad_wdown,) = widen(where, down_parts, phases, True, [(ff_rows, model_width)])
-    (grad_win,) = widen(where, in_parts, phases, False, [(rows, ff_width)])
-    grad_wqkv, grad_wout = widen(
+    extra = -(-small.shape[1] // (16 * part)) * 16
+    padded = jnp.pad(small, ((0, 0), (0, extra * part - small.shape[1])))
+    padded = padded.reshape(group, extra, part).astype(BF16)
+    done = first.finish(sent, extra=padded)
+    gather_down = Gather(after(down.total().astype(BF16)[None], done))
+    gather_down.step()
+    gather_down.finish()
+    grad_wdown = widen_rows(where, gather_down.parts, phases, (ff_rows, model_width))
+    shares = jnp.concatenate([inward.total(), first.total()], axis=0).astype(BF16)
+    final = Gather(shares[None])
+    final.step(grad_wdown)
+    final.finish()
+    grad_win, grad_wqkv, grad_wout, total = widen(
         where,
-        final_parts,
+        final.parts,
         phases,
-        False,
-        [(rows, qkv_width), (rows, model_width)],
-    )
+        [[(rows, ff_width)], [(rows, qkv_width), (rows, model_width)]],
+    )
+    total = total.reshape(-1)
 
     vecs, start = [], 0
     for size in sizes:

time: 477 us -> 466 us (0.977)
  starting transfers between devices: 63.4 us -> 54.2 us
  local copies, waits for them, and re-layouts: 22.9 us -> 17.2 us
    ppermute x12 -> x9, waiting for transfers between devices: 42.8 us -> 28.5 us  [to_shard(): lax.ppermute(value, 'shard', [(i, (i + step) % group) for i in range(grou...]
    ppermute x18 -> x16, waiting for transfers between devices: 56.2 us -> 68.5 us  [swap(): return lax.ppermute(value, REP, pairs)]
    squeeze x4 -> x0, local copies, waits for them, and re-layouts: 6.6 us -> none  [local(): value[:, 0].reshape(-1, *share_down.shape[1:])]
    ppermute x12 -> x9, starting transfers between devices: 14.1 us -> 9.04 us  [to_shard(): lax.ppermute(value, 'shard', [(i, (i + step) % group) for i in range(grou...]
    ppermute x18 -> x16, starting transfers between devices: 17.3 us -> 15.4 us  [swap(): return lax.ppermute(value, REP, pairs)]
    pallas_call x12 -> x11, Pallas kernels: 70.5 us -> 69.2 us  [the longest x9 57.7 us: grads(): call(partial(grads_kernel, (units, len(received), last, group, cuts, int(...]
    unnamed x68 -> x73, local copies, waits for them, and re-layouts: 8.96 us -> 9.78 us
  transfers between devices with their start and end apart: 59 -> 54, of which waited for: 25 -> 28; matrix products, arithmetic and copies ran while one was open for 6% -> 5% of each run, Pallas kernels for 40% -> 42%
where the time goes in v4:
time: 466 us; the launch traced here: 457 us
  Pallas kernels  217 us (47%)
  waiting for transfers between devices  152 us (33%)
  starting transfers between devices  54.2 us (12%)
  local copies, waits for them, and re-layouts  17.2 us (4%)
  other arithmetic  14.7 us (3%)
    ppermute x16, waiting for transfers between devices, swap(): return lax.ppermute(value, REP, pairs)  68.5 us
    pallas_call x9, Pallas kernels, grads(): call(partial(grads_kernel, (units, len(received), last, group, cuts, int(...  57.7 us
    ppermute x12, waiting for transfers between devices, from_shard(): lax.ppermute(value, 'shard', [(i, (i - step) % group) for i in range(grou...  48.2 us
    ppermute x9, waiting for transfers between devices, to_shard(): lax.ppermute(value, 'shard', [(i, (i + step) % group) for i in range(grou...  28.5 us
    pallas_call x2, Pallas kernels, attention_back(): call(partial(attend_back_kernel, (mine, per)), (each // 2,), [pairs(0), p...  26.3 us
    pallas_call x2, Pallas kernels, attention(): call(partial(attend_kernel, first), (count,), [spec((seq, block), lambda...  21.9 us
    pallas_call x1, Pallas kernels, inner_back(): call(partial(inner_back_kernel, (group, half)), (2 * chips,), [columns_at...  18.8 us
    ppermute x17, starting transfers between devices, sibling(): return lax.ppermute(value, 'core', [(0, 1), (1, 0)])  17 us
  transfers between devices with their start and end apart: 54, of which 28 were waited for; matrix products, arithmetic and copies ran while one was open for 5% of the time, Pallas kernels for 42%

profile of v4, /device:TPU:9, one launch (start us, length us, event | category | flops | bytes accessed | tf_op | source)
XLA Modules:
  0.0 456.8 jit_solution(11850383090418710124)
XLA Ops:
  8.9 11.8 %collective-permute-done.1 = bf16[256,512]{1,0:T(8,128)(2,1)S(1)} collective-permute-done((bf16[256,512]{1,0:T(8,128)(2,1)S(1)}, bf16[256,512]{1,0:T(8,128)(2,1)S(1)}, u32[]{:S(2)}, u32[]{:S(2)}) %collective-permute-start.1) | collective-permute-done | bytes 262176 | tf_op jit(solution)/shard_map/ppermute | solution.py:865
  27.9 9.9 %collective-permute-done.3 = bf16[1,3,256,512]{3,2,1,0:T(8,128)(2,1)S(1)} collective-permute-done((bf16[1,3,256,512]{3,2,1,0:T(8,128)(2,1)S(1)}, bf16[1,3,256,512]{3,2,1,0:T(8,128)(2,1)S(1)}, u32[]{:S(2)}, u32[]{:S(2)}) %collective-permute-start.3) | collective-permute-done | bytes 786464 | tf_op jit(solution)/shard_map/ppermute | solution.py:880
  39.2 18.4 %collective-permute-done.4.b = bf16[2,3,256,512]{3,2,1,0:T(8,128)(2,1)S(1)} collective-permute-done((bf16[2,3,256,512]{3,2,1,0:T(8,128)(2,1)S(1)}, bf16[2,3,256,512]{3,2,1,0:T(8,128)(2,1)S(1)}, u32[]{:S(2)}, u32[]{:S(2)}) %collective-permute-start.4) | collective-permute-done | bytes 1572896 | tf_op jit(solution)/shard_map/ppermute | solution.py:880
  73.2 12.1 %shard_map.299 = (bf16[512,4096]{1,0:T(8,128)(2,1)}, bf16[768,1024]{1,0:T(8,128)(2,1)}) custom-call(s32[10]{0:T(128)} %pad_add_fusion.where, bf16[512,1024]{1,0:T(8,128)(2,1)} %bitcast.105, bf16[256,3072]{1,0:T(8,128)(2,1)} %own.13, bf16[2,3,256,512]{3,2,1,0:T(8,128)(2,1)} %copy-done, bf16[2,3,256,512]{3,2,1,0:T(8,128)(2,1)} %copy-done.2, ...), custom_call_target="tpu_custom_call" | custom-call | bytes 44280000 | tf_op jit(solution)/shard_map/pallas_call | solution.py:150
  85.3 7.3 %collective-permute-done.12 = bf16[256,512]{1,0:T(8,128)(2,1)} collective-permute-done((bf16[256,512]{1,0:T(8,128)(2,1)S(1)}, bf16[256,512]{1,0:T(8,128)(2,1)}, u32[]{:S(2)}, u32[]{:S(2)}) %collective-permute-start.12) | collective-permute-done | bytes 262176 | tf_op jit(solution)/shard_map/ppermute | solution.py:865
  100.3 10.9 %shard_map.300 = (bf16[512,1024]{1,0:T(8,128)(2,1)}, bf16[2,1024,512]{2,1,0:T(8,128)(2,1)}, f32[512,128]{1,0:T(8,128)}) custom-call(s32[10]{0:T(128)} %pad_add_fusion.where, bf16[512,4096]{1,0:T(8,128)(2,1)} %get-tuple-element.108.q.k.v, bf16[512,4096]{1,0:T(8,128)(2,1)} %get-tuple-element.108.q.k.v, bf16[512,4096]{1,0:T(8,128)(2,1)} %get-tuple-element.108.q.k.v, ...), custom_call_target="tpu_custom_call" | custom-call | bytes 40590000 | tf_op jit(solution)/shard_map/pallas_call | solution.py:200
  117.3 7.1 %collective-permute-done.17 = bf16[128,1024]{1,0:T(8,128)(2,1)S(1)} collective-permute-done((bf16[128,1024]{1,0:T(8,128)(2,1)S(1)}, bf16[128,1024]{1,0:T(8,128)(2,1)S(1)}, u32[]{:S(2)}, u32[]{:S(2)}) %collective-permute-start.17) | collective-permute-done | bytes 262176 | tf_op jit(solution)/shard_map/ppermute | solution.py:865
  135.7 11.0 %shard_map.301 = (bf16[512,1024]{1,0:T(8,128)(2,1)}, bf16[2,1024,512]{2,1,0:T(8,128)(2,1)}, f32[512,128]{1,0:T(8,128)}) custom-call(s32[10]{0:T(128)} %pad_add_fusion.where, bf16[512,4096]{1,0:T(8,128)(2,1)} %get-tuple-element.108.q.k.v, bf16[512,4096]{1,0:T(8,128)(2,1)} %get-tuple-element.108.q.k.v, ...), custom_call_target="tpu_custom_call", output_to_operand_aliasing={{0}: (7, {}), {1}: (8, {})} | custom-call | bytes 40590000 | tf_op jit(solution)/shard_map/pallas_call | solution.py:200
  146.7 6.0 %shard_map.302 = (f32[512,1024]{1,0:T(8,128)}, bf16[512,1024]{1,0:T(8,128)(2,1)}, bf16[1024,512]{1,0:T(8,128)(2,1)}) custom-call(s32[10]{0:T(128)} %pad_add_fusion.where, bf16[512,1024]{1,0:T(8,128)(2,1)} %get-tuple-element.111.context, bf16[512,1024]{1,0:T(8,128)(2,1)} %bitcast.108, bf16[256,1024]{1,0:T(8,128)(2,1)} %own_out.1, ...), custom_call_target="tpu_custom_call" | custom-call | bytes 22140000 | tf_op jit(solution)/shard_map/pallas_call | solution.py:316
  163.1 15.8 %shard_map.303 = (bf16[512,4096]{1,0:T(8,128)(2,1)}, bf16[4096,256]{1,0:T(8,128)(2,1)}, bf16[4096,256]{1,0:T(8,128)(2,1)}, bf16[512,4096]{1,0:T(8,128)(2,1)}) custom-call(s32[10]{0:T(128)} %pad_add_fusion.where, bf16[512,1024]{1,0:T(8,128)(2,1)} %get-tuple-element.113.x, bf16[256,4096]{1,0:T(8,128)(2,1)} %own.12, ...), custom_call_target="tpu_custom_call" | custom-call | bytes 59040000 | tf_op jit(solution)/shard_map/pallas_call | solution.py:368
  184.0 16.3 %shard_map.304 = (bf16[512,1024]{1,0:T(8,128)(2,1)}, f32[512,1024]{1,0:T(8,128)}, bf16[512,1024]{1,0:T(8,128)(2,1)}, bf16[512,512]{1,0:T(8,128)(2,1)}, f32[8,1024]{1,0:T(8,128)}) custom-call(s32[10]{0:T(128)} %pad_add_fusion.where, bf16[512,4096]{1,0:T(8,128)(2,1)} %get-tuple-element.120.act, bf16[1024,1024]{1,0:T(8,128)(2,1)} %own.11, ...), custom_call_target="tpu_custom_call" | custom-call | bytes 221400000 | tf_op jit(solution)/shard_map/pallas_call | solution.py:461
  203.2 7.5 %shard_map.305 = bf16[2,1024,512]{2,1,0:T(8,128)(2,1)} custom-call(s32[10]{0:T(128)} %pad_add_fusion.where, bf16[1,512,1024]{2,1,0:T(8,128)(2,1)} %bitcast.101, bf16[1,512,512]{2,1,0:T(8,128)(2,1)} %bitcast.113, bf16[1,4096,256]{2,1,0:T(8,128)(2,1)} %bitcast.93, bf16[1,4096,256]{2,1,0:T(8,128)(2,1)} %bitcast.97, ...), custom_call_target="tpu_custom_call" | custom-call | bytes 22140000 | tf_op jit(solution)/shard_map/pallas_call | solution.py:819
  212.6 16.9 %shard_map.306 = (bf16[512,4096]{1,0:T(8,128)(2,1)}, bf16[512,2048]{1,0:T(8,128)(2,1)}, f32[1,4096]{1,0:T(1,128)}) custom-call(s32[10]{0:T(128)} %pad_add_fusion.where, bf16[512,1024]{1,0:T(8,128)(2,1)} %get-tuple-element.131.low, bf16[1024,1024]{1,0:T(8,128)(2,1)} %own.11, bf16[2,3,128,1024]{3,2,1,0:T(8,128)(2,1)} %pad_maximum_fusion.2.a, ...), custom_call_target="tpu_custom_call" | custom-call | bytes 51660000 | tf_op jit(solution)/shard_map/pallas_call | solution.py:525
  229.5 18.8 %shard_map.307 = (f32[512,1024]{1,0:T(8,128)}, bf16[512,1024]{1,0:T(8,128)(2,1)}, bf16[512,1024]{1,0:T(8,128)(2,1)}, f32[8,1024]{1,0:T(8,128)}) custom-call(s32[10]{0:T(128)} %pad_add_fusion.where, bf16[512,4096]{1,0:T(8,128)(2,1)} %get-tuple-element.135.grad_inner, bf16[256,4096]{1,0:T(8,128)(2,1)} %own.12, bf16[2,3,256,512]{3,2,1,0:T(8,128)(2,1)} %pad_maximum_fusion.1.a, ...), custom_call_target="tpu_custom_call" | custom-call | bytes 70110000 | tf_op jit(solution)/shard_map/pallas_call | solution.py:609
  248.3 5.8 %shard_map.308 = bf16[1,1024,512]{2,1,0:T(8,128)(2,1)} custom-call(s32[10]{0:T(128)} %pad_add_fusion.where, bf16[1,512,1024]{2,1,0:T(8,128)(2,1)} %bitcast.103, bf16[1,512,512]{2,1,0:T(8,128)(2,1)} %bitcast.115, bf16[1,4096,256]{2,1,0:T(8,128)(2,1)} %bitcast.95, bf16[1,4096,256]{2,1,0:T(8,128)(2,1)} %bitcast.99, ...), custom_call_target="tpu_custom_call" | custom-call | bytes 22140000 | tf_op jit(solution)/shard_map/pallas_call | solution.py:819
  254.4 7.1 %shard_map.309 = bf16[2,1024,512]{2,1,0:T(8,128)(2,1)} custom-call(s32[10]{0:T(128)} %pad_add_fusion.where, bf16[1,512,4096]{2,1,0:T(8,128)(2,1)} %bitcast.89, bf16[1,512,2048]{2,1,0:T(8,128)(2,1)} %bitcast.28.refs_1_.refs_5_, bf16[1,1024,512]{2,1,0:T(8,128)(2,1)} %bitcast.109, bf16[1,1024,512]{2,1,0:T(8,128)(2,1)} %bitcast.26.refs_3_.refs_7_, ...), custom_call_target="tpu_custom_call" | custom-call | bytes 22140000 | tf_op jit(solution)/shard_map/pallas_call | solution.py:819
  262.5 13.4 %shard_map.310 = (bf16[4,512,512]{2,1,0:T(8,128)(2,1)}, f32[3,1,512]{2,1,0:T(1,128)}) custom-call(s32[10]{0:T(128)} %pad_add_fusion.where, bf16[512,4096]{1,0:T(8,128)(2,1)} %get-tuple-element.108.q.k.v, bf16[512,4096]{1,0:T(8,128)(2,1)} %get-tuple-element.108.q.k.v, bf16[512,4096]{1,0:T(8,128)(2,1)} %get-tuple-element.108.q.k.v, ...), custom_call_target="tpu_custom_call" | custom-call | bytes 47970000 | tf_op jit(solution)/shard_map/pallas_call | solution.py:273
  275.9 6.2 %shard_map.311 = (bf16[256,512]{1,0:T(8,128)(2,1)}, bf16[256,512]{1,0:T(8,128)(2,1)}, bf16[256,512]{1,0:T(8,128)(2,1)}, bf16[256,512]{1,0:T(8,128)(2,1)}) custom-call(s32[10]{0:T(128)} %pad_add_fusion.where, bf16[1,512,1024]{2,1,0:T(8,128)(2,1)} %bitcast.104, bf16[1,512,512]{2,1,0:T(8,128)(2,1)} %bitcast.116, bf16[1,4096,256]{2,1,0:T(8,128)(2,1)} %bitcast.96, ...), custom_call_target="tpu_custom_call" | custom-call | bytes 22140000 | tf_op jit(solution)/shard_map/pallas_call | solution.py:819
  290.1 13.0 %shard_map.312 = (bf16[4,512,512]{2,1,0:T(8,128)(2,1)}, f32[3,1,512]{2,1,0:T(1,128)}) custom-call(s32[10]{0:T(128)} %pad_add_fusion.where, bf16[512,4096]{1,0:T(8,128)(2,1)} %get-tuple-element.108.q.k.v, bf16[512,4096]{1,0:T(8,128)(2,1)} %get-tuple-element.108.q.k.v, bf16[512,4096]{1,0:T(8,128)(2,1)} %get-tuple-element.108.q.k.v, ...), custom_call_target="tpu_custom_call" | custom-call | bytes 47970000 | tf_op jit(solution)/shard_map/pallas_call | solution.py:273
  303.1 5.7 %shard_map.313 = bf16[1,1024,512]{2,1,0:T(8,128)(2,1)} custom-call(s32[10]{0:T(128)} %pad_add_fusion.where, bf16[1,512,4096]{2,1,0:T(8,128)(2,1)} %bitcast.91, bf16[1,512,2048]{2,1,0:T(8,128)(2,1)} %bitcast.28.refs_1_.refs_5_, bf16[1,1024,512]{2,1,0:T(8,128)(2,1)} %bitcast.111, bf16[1,1024,512]{2,1,0:T(8,128)(2,1)} %bitcast.26.refs_3_.refs_7_, ...), custom_call_target="tpu_custom_call" | custom-call | bytes 22140000 | tf_op jit(solution)/shard_map/pallas_call | solution.py:819
  312.6 7.2 %shard_map.314 = bf16[2,1024,512]{2,1,0:T(8,128)(2,1)} custom-call(s32[10]{0:T(128)} %pad_add_fusion.where, bf16[4,512,512]{2,1,0:T(8,128)(2,1)} %get-tuple-element.159.refs_0_.refs_4_.mine, bf16[4,512,512]{2,1,0:T(8,128)(2,1)} %collective-permute-done.32.refs_1_.refs_5_, bf16[2,1024,512]{2,1,0:T(8,128)(2,1)} %get-tuple-element.139.refs_2_.refs_6_, ...), custom_call_target="tpu_custom_call" | custom-call | bytes 22140000 | tf_op jit(solution)/shard_map/pallas_call | solution.py:819
  325.2 13.4 %shard_map.315 = f32[512,1024]{1,0:T(8,128)} custom-call(s32[10]{0:T(128)} %pad_add_fusion.where, bf16[4,512,512]{2,1,0:T(8,128)(2,1)} %get-tuple-element.159.refs_0_.refs_4_.mine, bf16[4,512,512]{2,1,0:T(8,128)(2,1)} %get-tuple-element.152.others, bf16[256,3072]{1,0:T(8,128)(2,1)} %own.13, bf16[2,3,256,512]{3,2,1,0:T(8,128)(2,1)} %copy-done, ...), custom_call_target="tpu_custom_call" | custom-call | bytes 44280000 | tf_op jit(solution)/shard_map/pallas_call | solution.py:671
  338.6 7.2 %collective-permute-done.37.refs_5_ = bf16[1,1024,512]{2,1,0:T(8,128)(2,1)} collective-permute-done((bf16[1,1024,512]{2,1,0:T(8,128)(2,1)}, bf16[1,1024,512]{2,1,0:T(8,128)(2,1)}, u32[]{:S(2)}, u32[]{:S(2)}) %collective-permute-start.37) | collective-permute-done | bytes 1048608 | tf_op jit(solution)/shard_map/ppermute | solution.py:880
  345.7 6.2 %shard_map.316 = (bf16[256,512]{1,0:T(8,128)(2,1)}, bf16[256,512]{1,0:T(8,128)(2,1)}, bf16[256,512]{1,0:T(8,128)(2,1)}, bf16[256,512]{1,0:T(8,128)(2,1)}) custom-call(s32[10]{0:T(128)} %pad_add_fusion.where, bf16[1,512,4096]{2,1,0:T(8,128)(2,1)} %bitcast.92, bf16[1,512,2048]{2,1,0:T(8,128)(2,1)} %bitcast.28.refs_1_.refs_5_, bf16[1,1024,512]{2,1,0:T(8,128)(2,1)} %bitcast.112, ...), custom_call_target="tpu_custom_call" | custom-call | bytes 22140000 | tf_op jit(solution)/shard_map/pallas_call | solution.py:819
  356.6 5.8 %shard_map.317 = bf16[1,1024,512]{2,1,0:T(8,128)(2,1)} custom-call(s32[10]{0:T(128)} %pad_add_fusion.where, bf16[4,512,512]{2,1,0:T(8,128)(2,1)} %get-tuple-element.159.refs_0_.refs_4_.mine, bf16[4,512,512]{2,1,0:T(8,128)(2,1)} %collective-permute-done.32.refs_1_.refs_5_, bf16[2,1024,512]{2,1,0:T(8,128)(2,1)} %get-tuple-element.139.refs_2_.refs_6_, ...), custom_call_target="tpu_custom_call" | custom-call | bytes 22140000 | tf_op jit(solution)/shard_map/pallas_call | solution.py:819
  366.6 10.1 %collective-permute-done.42.refs_5_ = bf16[1,1024,512]{2,1,0:T(8,128)(2,1)} collective-permute-done((bf16[1,1024,512]{2,1,0:T(8,128)(2,1)}, bf16[1,1024,512]{2,1,0:T(8,128)(2,1)}, u32[]{:S(2)}, u32[]{:S(2)}) %collective-permute-start.42) | collective-permute-done | bytes 1048608 | tf_op jit(solution)/shard_map/ppermute | solution.py:880
  376.6 6.2 %shard_map.318 = (bf16[272,512]{1,0:T(8,128)(2,1)}, bf16[272,512]{1,0:T(8,128)(2,1)}, bf16[272,512]{1,0:T(8,128)(2,1)}, bf16[272,512]{1,0:T(8,128)(2,1)}) custom-call(s32[10]{0:T(128)} %pad_add_fusion.where, bf16[4,512,512]{2,1,0:T(8,128)(2,1)} %get-tuple-element.159.refs_0_.refs_4_.mine, bf16[4,512,512]{2,1,0:T(8,128)(2,1)} %collective-permute-done.32.refs_1_.refs_5_, ...), custom_call_target="tpu_custom_call" | custom-call | bytes 22140000 | tf_op jit(solution)/shard_map/pallas_call | solution.py:819
  385.8 12.7 %collective-permute-done.40 = bf16[256,512]{1,0:T(8,128)(2,1)} collective-permute-done((bf16[256,512]{1,0:T(8,128)(2,1)}, bf16[256,512]{1,0:T(8,128)(2,1)}, u32[]{:S(2)}, u32[]{:S(2)}) %collective-permute-start.40) | collective-permute-done | bytes 262176 | tf_op jit(solution)/shard_map/ppermute | solution.py:868
  401.0 8.6 %collective-permute-done.44 = bf16[272,512]{1,0:T(8,128)(2,1)S(1)} collective-permute-done((bf16[272,512]{1,0:T(8,128)(2,1)}, bf16[272,512]{1,0:T(8,128)(2,1)S(1)}, u32[]{:S(2)}, u32[]{:S(2)}) %collective-permute-start.44) | collective-permute-done | bytes 278560 | tf_op jit(solution)/shard_map/ppermute | solution.py:868
  413.4 6.5 %collective-permute-done.46 = bf16[1,528,512]{2,1,0:T(8,128)(2,1)S(1)} collective-permute-done((bf16[1,528,512]{2,1,0:T(8,128)(2,1)S(1)}, bf16[1,528,512]{2,1,0:T(8,128)(2,1)S(1)}, u32[]{:S(2)}, u32[]{:S(2)}) %collective-permute-start.46) | collective-permute-done | bytes 540704 | tf_op jit(solution)/shard_map/ppermute | solution.py:880
  429.3 11.4 %collective-permute-done.51.refs_1_ = bf16[2,528,512]{2,1,0:T(8,128)(2,1)S(1)} collective-permute-done((bf16[2,528,512]{2,1,0:T(8,128)(2,1)}, bf16[2,528,512]{2,1,0:T(8,128)(2,1)S(1)}, u32[]{:S(2)}, u32[]{:S(2)}) %collective-permute-start.51) | collective-permute-done | bytes 1081376 | tf_op jit(solution)/shard_map/ppermute | solution.py:880
  446.4 7.0 %shard_map.320 = (f32[256,4096]{1,0:T(8,128)}, f32[256,3072]{1,0:T(8,128)}, f32[256,1024]{1,0:T(8,128)}, f32[16,512]{1,0:T(8,128)}) custom-call(s32[10]{0:T(128)} %pad_add_fusion.where, bf16[2,528,512]{2,1,0:T(8,128)(2,1)} %pad_maximum_fusion.3.refs_0_, bf16[2,528,512]{2,1,0:T(8,128)(2,1)} %copy-done.4, ...), custom_call_target="tpu_custom_call" | custom-call | bytes 14760000 | tf_op jit(solution)/shard_map/pallas_call | solution.py:750
  (225 shorter events, 131.8 us)
Async XLA Ops:
  1.8 19.0 %collective-permute-start.1 = (bf16[256,512]{1,0:T(8,128)(2,1)S(1)}, bf16[256,512]{1,0:T(8,128)(2,1)S(1)}, u32[]{:S(2)}, u32[]{:S(2)}) collective-permute-start(bf16[256,512]{1,0:T(8,128)(2,1)S(1)} %fusion.1), channel_id=1, source_target_pairs={{0,2},{1,3},{2,0},{3,1},{4,6},{5,7},{6,4},{7,5},{8,10},{9,11},{10,... | collective-permute-start | bytes 786440 | tf_op jit(solution)/shard_map/ppermute | solution.py:865
  4.3 22.1 %collective-permute-start.2 = (bf16[256,512]{1,0:T(8,128)(2,1)S(1)}, bf16[256,512]{1,0:T(8,128)(2,1)S(1)}, u32[]{:S(2)}, u32[]{:S(2)}) collective-permute-start(bf16[256,512]{1,0:T(8,128)(2,1)S(1)} %fusion.1), channel_id=1, source_target_pairs={{0,1},{1,2},{2,3},{3,0},{4,5},{5,6},{6,7},{7,4},{8,9},{9,10},{10,1... | collective-permute-start | bytes 786440 | tf_op jit(solution)/shard_map/ppermute | solution.py:865
  37.9 19.6 %collective-permute-start.4 = (bf16[2,3,256,512]{3,2,1,0:T(8,128)(2,1)S(1)}, bf16[2,3,256,512]{3,2,1,0:T(8,128)(2,1)S(1)}, u32[]{:S(2)}, u32[]{:S(2)}) collective-permute-start(bf16[2,3,256,512]{3,2,1,0:T(8,128)(2,1)S(1)} %pad_maximum_fusion.a), channel_id=1, source_target_pairs={{0,16},{4,12},{8,24},{12,4},{16,0},{20,28},{24,8},{28,20},{1,17},{... | collective-permute-start | bytes 4718600 | tf_op jit(solution)/shard_map/ppermute | solution.py:880
  70.4 22.2 %collective-permute-start.12 = (bf16[256,512]{1,0:T(8,128)(2,1)S(1)}, bf16[256,512]{1,0:T(8,128)(2,1)}, u32[]{:S(2)}, u32[]{:S(2)}) collective-permute-start(bf16[256,512]{1,0:T(8,128)(2,1)S(1)} %constant_dynamic-slice_fusion.1), channel_id=1, source_target_pairs={{0,1},{1,2},{2,3},{3,0},{4,5},{5,6},{6,7},{7,4},{8,9},{9,10},{10,1... | collective-permute-start | bytes 786440 | tf_op jit(solution)/shard_map/ppermute | solution.py:865
  72.6 23.1 %collective-permute-start.10 = (bf16[256,512]{1,0:T(8,128)(2,1)S(1)}, bf16[256,512]{1,0:T(8,128)(2,1)}, u32[]{:S(2)}, u32[]{:S(2)}) collective-permute-start(bf16[256,512]{1,0:T(8,128)(2,1)S(1)} %constant_dynamic-slice_fusion.1), channel_id=1, source_target_pairs={{0,3},{1,0},{2,1},{3,2},{4,7},{5,4},{6,5},{7,6},{8,11},{9,8},{10,9... | collective-permute-start | bytes 786440 | tf_op jit(solution)/shard_map/ppermute | solution.py:865
  113.6 45.8 %collective-permute-start.14 = (bf16[2,3,256,512]{3,2,1,0:T(8,128)(2,1)}, bf16[2,3,256,512]{3,2,1,0:T(8,128)(2,1)}, u32[]{:S(2)}, u32[]{:S(2)}) collective-permute-start(bf16[2,3,256,512]{3,2,1,0:T(8,128)(2,1)} %pad_maximum_fusion.1.a), channel_id=1, source_target_pairs={{0,16},{4,12},{8,24},{12,4},{16,0},{20,28},{24,8},{28,20},{1,17},{... | collective-permute-start | bytes 4718600 | tf_op jit(solution)/shard_map/ppermute | solution.py:880
  116.3 17.1 %collective-permute-start.19 = (bf16[128,1024]{1,0:T(8,128)(2,1)S(1)}, bf16[128,1024]{1,0:T(8,128)(2,1)S(1)}, u32[]{:S(2)}, u32[]{:S(2)}) collective-permute-start(bf16[128,1024]{1,0:T(8,128)(2,1)S(1)} %constant_dynamic-slice_fusion), channel_id=1, source_target_pairs={{0,1},{1,2},{2,3},{3,0},{4,5},{5,6},{6,7},{7,4},{8,9},{9,10},{10,1... | collective-permute-start | bytes 786440 | tf_op jit(solution)/shard_map/ppermute | solution.py:865
  133.5 23.5 %collective-permute-start.20 = (bf16[1,3,128,1024]{3,2,1,0:T(8,128)(2,1)S(1)}, bf16[1,3,128,1024]{3,2,1,0:T(8,128)(2,1)}, u32[]{:S(2)}, u32[]{:S(2)}) collective-permute-start(bf16[1,3,128,1024]{3,2,1,0:T(8,128)(2,1)S(1)} %maximum_bitcast_fusion.2), channel_id=1, source_target_pairs={{0,8},{4,20},{8,0},{12,28},{16,24},{20,4},{24,16},{28,12},{1,9},{5... | collective-permute-start | bytes 2359304 | tf_op jit(solution)/shard_map/ppermute | solution.py:880
  159.4 19.9 %collective-permute-start.21 = (bf16[2,3,128,1024]{3,2,1,0:T(8,128)(2,1)}, bf16[2,3,128,1024]{3,2,1,0:T(8,128)(2,1)}, u32[]{:S(2)}, u32[]{:S(2)}) collective-permute-start(bf16[2,3,128,1024]{3,2,1,0:T(8,128)(2,1)} %pad_maximum_fusion.2.a), channel_id=1, source_target_pairs={{0,16},{4,12},{8,24},{12,4},{16,0},{20,28},{24,8},{28,20},{1,17},{... | collective-permute-start | bytes 4718600 | tf_op jit(solution)/shard_map/ppermute | solution.py:880
  161.3 21.6 %collective-permute-start.22 = (bf16[2,3,128,1024]{3,2,1,0:T(8,128)(2,1)}, bf16[2,3,128,1024]{3,2,1,0:T(8,128)(2,1)}, u32[]{:S(2)}, u32[]{:S(2)}) collective-permute-start(bf16[2,3,128,1024]{3,2,1,0:T(8,128)(2,1)} %pad_maximum_fusion.2.a), channel_id=1, source_target_pairs={{0,4},{4,0},{1,5},{5,1},{2,6},{6,2},{3,7},{7,3},{8,12},{12,8},{9,1... | collective-permute-start | bytes 4718600 | tf_op jit(solution)/shard_map/ppermute | solution.py:871
  180.6 21.8 %collective-permute-start.25 = (bf16[4096,256]{1,0:T(8,128)(2,1)}, bf16[4096,256]{1,0:T(8,128)(2,1)}, u32[]{:S(2)}, u32[]{:S(2)}) collective-permute-start(bf16[4096,256]{1,0:T(8,128)(2,1)} %get-tuple-element.129), channel_id=1, source_target_pairs={{0,4},{4,0},{1,5},{5,1},{2,6},{6,2},{3,7},{7,3},{8,12},{12,8},{9,1... | collective-permute-start | bytes 6291464 | tf_op jit(solution)/shard_map/ppermute | solution.py:871
  180.6 21.8 %collective-permute-start.26 = (bf16[4096,256]{1,0:T(8,128)(2,1)}, bf16[4096,256]{1,0:T(8,128)(2,1)}, u32[]{:S(2)}, u32[]{:S(2)}) collective-permute-start(bf16[4096,256]{1,0:T(8,128)(2,1)} %get-tuple-element.130), channel_id=1, source_target_pairs={{0,4},{4,0},{1,5},{5,1},{2,6},{6,2},{3,7},{7,3},{8,12},{12,8},{9,1... | collective-permute-start | bytes 6291464 | tf_op jit(solution)/shard_map/ppermute | solution.py:871
  200.7 47.6 %collective-permute-start.29 = (bf16[2,1024,512]{2,1,0:T(8,128)(2,1)}, bf16[2,1024,512]{2,1,0:T(8,128)(2,1)}, u32[]{:S(2)}, u32[]{:S(2)}) collective-permute-start(bf16[2,1024,512]{2,1,0:T(8,128)(2,1)} %get-tuple-element.139.refs_2_.refs_6_), channel_id=1, source_target_pairs={{0,4},{4,0},{1,5},{5,1},{2,6},{6,2},{3,7},{7,3},{8,12},{12,8},{9,1... | collective-permute-start | bytes 6291464 | tf_op jit(solution)/shard_map/ppermute | solution.py:871
  210.7 37.6 %collective-permute-start.28 = (bf16[2,1024,512]{2,1,0:T(8,128)(2,1)}, bf16[2,1024,512]{2,1,0:T(8,128)(2,1)}, u32[]{:S(2)}, u32[]{:S(2)}) collective-permute-start(bf16[2,1024,512]{2,1,0:T(8,128)(2,1)} %shard_map.305), channel_id=1, source_target_pairs={{0,8},{4,20},{8,0},{12,28},{16,24},{20,4},{24,16},{28,12},{1,9},{5... | collective-permute-start | bytes 6291464 | tf_op jit(solution)/shard_map/ppermute | solution.py:880
  210.9 18.6 %collective-permute-start.27 = (bf16[1024,512]{1,0:T(8,128)(2,1)}, bf16[1024,512]{1,0:T(8,128)(2,1)}, u32[]{:S(2)}, u32[]{:S(2)}) collective-permute-start(bf16[1024,512]{1,0:T(8,128)(2,1)} %get-tuple-element.134), channel_id=1, source_target_pairs={{0,4},{4,0},{1,5},{5,1},{2,6},{6,2},{3,7},{7,3},{8,12},{12,8},{9,1... | collective-permute-start | bytes 3145736 | tf_op jit(solution)/shard_map/ppermute | solution.py:871
  229.5 24.9 %collective-permute-start.31 = (bf16[512,2048]{1,0:T(8,128)(2,1)}, bf16[512,2048]{1,0:T(8,128)(2,1)}, u32[]{:S(2)}, u32[]{:S(2)}) collective-permute-start(bf16[512,2048]{1,0:T(8,128)(2,1)} %get-tuple-element.141), channel_id=1, source_target_pairs={{0,4},{4,0},{1,5},{5,1},{2,6},{6,2},{3,7},{7,3},{8,12},{12,8},{9,1... | collective-permute-start | bytes 6291464 | tf_op jit(solution)/shard_map/ppermute | solution.py:871
  254.1 21.8 %collective-permute-start.30 = (bf16[1,1024,512]{2,1,0:T(8,128)(2,1)}, bf16[1,1024,512]{2,1,0:T(8,128)(2,1)}, u32[]{:S(2)}, u32[]{:S(2)}) collective-permute-start(bf16[1,1024,512]{2,1,0:T(8,128)(2,1)} %shard_map.308), channel_id=1, source_target_pairs={{0,16},{4,12},{8,24},{12,4},{16,0},{20,28},{24,8},{28,20},{1,17},{... | collective-permute-start | bytes 3145736 | tf_op jit(solution)/shard_map/ppermute | solution.py:880
  261.5 41.5 %collective-permute-start.33 = (bf16[2,1024,512]{2,1,0:T(8,128)(2,1)}, bf16[2,1024,512]{2,1,0:T(8,128)(2,1)}, u32[]{:S(2)}, u32[]{:S(2)}) collective-permute-start(bf16[2,1024,512]{2,1,0:T(8,128)(2,1)} %shard_map.309), channel_id=1, source_target_pairs={{0,8},{4,20},{8,0},{12,28},{16,24},{20,4},{24,16},{28,12},{1,9},{5... | collective-permute-start | bytes 6291464 | tf_op jit(solution)/shard_map/ppermute | solution.py:880
  282.2 30.4 %collective-permute-start.32 = (bf16[4,512,512]{2,1,0:T(8,128)(2,1)}, bf16[4,512,512]{2,1,0:T(8,128)(2,1)}, u32[]{:S(2)}, u32[]{:S(2)}) collective-permute-start(bf16[4,512,512]{2,1,0:T(8,128)(2,1)} %get-tuple-element.152.others), channel_id=1, source_target_pairs={{0,4},{4,0},{1,5},{5,1},{2,6},{6,2},{3,7},{7,3},{8,12},{12,8},{9,1... | collective-permute-start | bytes 6291464 | tf_op jit(solution)/shard_map/ppermute | solution.py:871
  282.7 26.1 %collective-permute-start.34 = (bf16[256,512]{1,0:T(8,128)(2,1)}, bf16[256,512]{1,0:T(8,128)(2,1)S(1)}, u32[]{:S(2)}, u32[]{:S(2)}) collective-permute-start(bf16[256,512]{1,0:T(8,128)(2,1)} %get-tuple-element.154), channel_id=1, source_target_pairs={{0,1},{1,2},{2,3},{3,0},{4,5},{5,6},{6,7},{7,4},{8,9},{9,10},{10,1... | collective-permute-start | bytes 786440 | tf_op jit(solution)/shard_map/ppermute | solution.py:868
  286.0 22.8 %collective-permute-start.35 = (bf16[256,512]{1,0:T(8,128)(2,1)}, bf16[256,512]{1,0:T(8,128)(2,1)S(1)}, u32[]{:S(2)}, u32[]{:S(2)}) collective-permute-start(bf16[256,512]{1,0:T(8,128)(2,1)} %get-tuple-element.155), channel_id=1, source_target_pairs={{0,2},{1,3},{2,0},{3,1},{4,6},{5,7},{6,4},{7,5},{8,10},{9,11},{10,... | collective-permute-start | bytes 786440 | tf_op jit(solution)/shard_map/ppermute | solution.py:868
  290.1 22.5 %collective-permute-start.36 = (bf16[256,512]{1,0:T(8,128)(2,1)}, bf16[256,512]{1,0:T(8,128)(2,1)S(1)}, u32[]{:S(2)}, u32[]{:S(2)}) collective-permute-start(bf16[256,512]{1,0:T(8,128)(2,1)} %get-tuple-element.156), channel_id=1, source_target_pairs={{0,3},{1,0},{2,1},{3,2},{4,7},{5,4},{6,5},{7,6},{8,11},{9,8},{10,9... | collective-permute-start | bytes 786440 | tf_op jit(solution)/shard_map/ppermute | solution.py:868
  319.8 36.8 %collective-permute-start.41 = (bf16[2,1024,512]{2,1,0:T(8,128)(2,1)}, bf16[2,1024,512]{2,1,0:T(8,128)(2,1)}, u32[]{:S(2)}, u32[]{:S(2)}) collective-permute-start(bf16[2,1024,512]{2,1,0:T(8,128)(2,1)} %shard_map.314), channel_id=1, source_target_pairs={{0,8},{4,20},{8,0},{12,28},{16,24},{20,4},{24,16},{28,12},{1,9},{5... | collective-permute-start | bytes 6291464 | tf_op jit(solution)/shard_map/ppermute | solution.py:880
  320.7 25.0 %collective-permute-start.37 = (bf16[1,1024,512]{2,1,0:T(8,128)(2,1)}, bf16[1,1024,512]{2,1,0:T(8,128)(2,1)}, u32[]{:S(2)}, u32[]{:S(2)}) collective-permute-start(bf16[1,1024,512]{2,1,0:T(8,128)(2,1)} %shard_map.313), channel_id=1, source_target_pairs={{0,16},{4,12},{8,24},{12,4},{16,0},{20,28},{24,8},{28,20},{1,17},{... | collective-permute-start | bytes 3145736 | tf_op jit(solution)/shard_map/ppermute | solution.py:880
  363.9 19.9 %collective-permute-start.38 = (bf16[256,512]{1,0:T(8,128)(2,1)}, bf16[256,512]{1,0:T(8,128)(2,1)}, u32[]{:S(2)}, u32[]{:S(2)}) collective-permute-start(bf16[256,512]{1,0:T(8,128)(2,1)} %get-tuple-element.163), channel_id=1, source_target_pairs={{0,1},{1,2},{2,3},{3,0},{4,5},{5,6},{6,7},{7,4},{8,9},{9,10},{10,1... | collective-permute-start | bytes 786440 | tf_op jit(solution)/shard_map/ppermute | solution.py:868
  363.9 21.7 %collective-permute-start.39 = (bf16[256,512]{1,0:T(8,128)(2,1)}, bf16[256,512]{1,0:T(8,128)(2,1)}, u32[]{:S(2)}, u32[]{:S(2)}) collective-permute-start(bf16[256,512]{1,0:T(8,128)(2,1)} %get-tuple-element.164), channel_id=1, source_target_pairs={{0,2},{1,3},{2,0},{3,1},{4,6},{5,7},{6,4},{7,5},{8,10},{9,11},{10,... | collective-permute-start | bytes 786440 | tf_op jit(solution)/shard_map/ppermute | solution.py:868
  363.9 34.6 %collective-permute-start.40 = (bf16[256,512]{1,0:T(8,128)(2,1)}, bf16[256,512]{1,0:T(8,128)(2,1)}, u32[]{:S(2)}, u32[]{:S(2)}) collective-permute-start(bf16[256,512]{1,0:T(8,128)(2,1)} %get-tuple-element.165), channel_id=1, source_target_pairs={{0,3},{1,0},{2,1},{3,2},{4,7},{5,4},{6,5},{7,6},{8,11},{9,8},{10,9... | collective-permute-start | bytes 786440 | tf_op jit(solution)/shard_map/ppermute | solution.py:868
  382.9 16.9 %collective-permute-start.47 = (bf16[1,256,512]{2,1,0:T(8,128)(2,1)S(1)}, bf16[1,256,512]{2,1,0:T(8,128)(2,1)S(1)}, u32[]{:S(2)}, u32[]{:S(2)}) collective-permute-start(bf16[1,256,512]{2,1,0:T(8,128)(2,1)S(1)} %fusion.3), channel_id=1, source_target_pairs={{0,8},{4,20},{8,0},{12,28},{16,24},{20,4},{24,16},{28,12},{1,9},{5... | collective-permute-start | bytes 786440 | tf_op jit(solution)/shard_map/ppermute | solution.py:880
  383.8 17.2 %collective-permute-start.43 = (bf16[272,512]{1,0:T(8,128)(2,1)}, bf16[272,512]{1,0:T(8,128)(2,1)S(1)}, u32[]{:S(2)}, u32[]{:S(2)}) collective-permute-start(bf16[272,512]{1,0:T(8,128)(2,1)} %get-tuple-element.175), channel_id=1, source_target_pairs={{0,1},{1,2},{2,3},{3,0},{4,5},{5,6},{6,7},{7,4},{8,9},{9,10},{10,1... | collective-permute-start | bytes 835592 | tf_op jit(solution)/shard_map/ppermute | solution.py:868
  383.8 25.7 %collective-permute-start.44 = (bf16[272,512]{1,0:T(8,128)(2,1)}, bf16[272,512]{1,0:T(8,128)(2,1)S(1)}, u32[]{:S(2)}, u32[]{:S(2)}) collective-permute-start(bf16[272,512]{1,0:T(8,128)(2,1)} %get-tuple-element.176), channel_id=1, source_target_pairs={{0,2},{1,3},{2,0},{3,1},{4,6},{5,7},{6,4},{7,5},{8,10},{9,11},{10,... | collective-permute-start | bytes 835592 | tf_op jit(solution)/shard_map/ppermute | solution.py:868
  385.7 25.4 %collective-permute-start.45 = (bf16[272,512]{1,0:T(8,128)(2,1)}, bf16[272,512]{1,0:T(8,128)(2,1)S(1)}, u32[]{:S(2)}, u32[]{:S(2)}) collective-permute-start(bf16[272,512]{1,0:T(8,128)(2,1)} %get-tuple-element.177), channel_id=1, source_target_pairs={{0,3},{1,0},{2,1},{3,2},{4,7},{5,4},{6,5},{7,6},{8,11},{9,8},{10,9... | collective-permute-start | bytes 835592 | tf_op jit(solution)/shard_map/ppermute | solution.py:868
  426.9 17.0 %collective-permute-start.52 = (bf16[2,528,512]{2,1,0:T(8,128)(2,1)}, bf16[2,528,512]{2,1,0:T(8,128)(2,1)}, u32[]{:S(2)}, u32[]{:S(2)}) collective-permute-start(bf16[2,528,512]{2,1,0:T(8,128)(2,1)} %pad_maximum_fusion.3.refs_0_), channel_id=1, source_target_pairs={{0,4},{4,0},{1,5},{5,1},{2,6},{6,2},{3,7},{7,3},{8,12},{12,8},{9,1... | collective-permute-start | bytes 3244040 | tf_op jit(solution)/shard_map/ppermute | solution.py:871
  (47 other events, 732.5 us)

commit v5 on v4

--- a/solution.py
+++ b/solution.py
@@ -71,26 +71,54 @@
     return 2 * where[2 + unit] + jnp.where(unit < chips, where[1], 1 - where[1])
 
 
-def part_specs(parts, first=0):
-    half, steps, rows, columns = parts[0].shape
-
-    def given(index):
-        return spec(
-            (1, steps, rows, columns),
-            lambda u, w: (jnp.clip(u - first - index * half, 0, half - 1), 0, 0, 0),
-        )
-
-    return [given(index) for index in range(4)]
-
-
-def load_weight(unit, half, own, parts, weight):
-    rows = own.shape[0]
-    weight[:rows, :] = own[...]
+ANYWHERE = pl.BlockSpec(memory_space=pl.ANY)
+
+
+def stream(unit, parts, buffer, sems):
+    half = parts[0].shape[0]
+
+    def start(number, slot):
+        for index, part in enumerate(parts):
+
+            @pl.when(number // half == index)
+            def _(part=part):
+                source = part.at[lax.rem(number, half)]
+                pltpu.make_async_copy(source, buffer.at[slot], sems.at[slot]).start()
+
+    slot = lax.rem(unit, 2)
+
+    @pl.when(unit == 0)
+    def _():
+        start(unit, slot)
+
+    @pl.when(unit + 1 < half * len(parts))
+    def _():
+        start(unit + 1, 1 - slot)
+
+    pltpu.make_async_copy(parts[0].at[0], buffer.at[slot], sems.at[slot]).wait()
+    return buffer[slot].reshape(-1, buffer.shape[3])
+
+
+def stream_scratch(parts):
+    return [pltpu.VMEM((2, *parts[0].shape[1:]), BF16), pltpu.SemaphoreType.DMA((2,))]
+
+
+def stream_whole(step, parts, buffer, sems):
     for index, part in enumerate(parts):
 
-        @pl.when(unit // half == index)
-        def _(part=part):
-            weight[rows:, :] = part[0].reshape(-1, part.shape[3])
+        @pl.when(step == index)
+        def _(index=index, part=part):
+            slot = index % 2
+            pltpu.make_async_copy(part, buffer.at[slot], sems.at[slot]).start()
+
+        @pl.when(step == index + 1)
+        def _(index=index, part=part):
+            slot = index % 2
+            pltpu.make_async_copy(part, buffer.at[slot], sems.at[slot]).wait()
+
+
+def whole_scratch(parts):
+    return [pltpu.VMEM((2, *parts[0].shape), BF16), pltpu.SemaphoreType.DMA((2,))]
 
 
 def normalise(hidden):
@@ -118,7 +146,7 @@
         rolled[:, s * rows : (s + 1) * rows] = x[:, pl.ds(start, rows)]
 
 
-def qkv_kernel(dims, where, x, own, a, b, c, d, bias, out, rest_out, rolled, weight):
+def qkv_kernel(dims, where, x, own, a, b, c, d, bias, out, rest_out, rolled, *scratch):
     group, half, qkv_width = dims
     unit = pl.program_id(0)
     rows, columns = own.shape
@@ -127,17 +155,18 @@
     def _():
         roll_into(rolled, x, where, rows, group)
 
-    load_weight(unit, half, own, (a, b, c, d), weight)
+    rest = stream(unit, (a, b, c, d), *scratch)
     start = block_of(where, unit, 2 * half) * columns
 
     @pl.when(start < qkv_width)
     def _():
-        out[...] = (dot(rolled[...], weight[...]) + bias[...]).astype(BF16)
+        total = dot(rolled[:, :rows], own[...]) + dot(rolled[:, rows:], rest)
+        out[...] = (total + bias[...]).astype(BF16)
 
     @pl.when(start >= qkv_width)
     def _():
         place = pl.ds(pl.multiple_of(start - qkv_width, 128), columns)
-        rest_out[:, place] = weight[rows:, :]
+        rest_out[:, place] = rest
 
 
 def qkv(where, x, w_qkv, parts, bias, group):
@@ -154,14 +183,14 @@
             fixed((seq, width)),
             spec((rows, block), lambda u, w: (0, jnp.minimum(block_of(w, u, chips), top))),
         ]
-        + part_specs(parts)
+        + [ANYWHERE] * 4
         + [spec((1, block), lambda u, w: (0, block_of(w, u, chips)))],
         [
             spec((seq, block), lambda u, w: (0, block_of(w, u, chips))),
             fixed((width - rows, total - qkv_width)),
         ],
         [struct((seq, total), BF16), struct((width - rows, total - qkv_width), BF16)],
-        [pltpu.VMEM((seq, width), BF16), pltpu.VMEM((width, block), BF16)],
+        [pltpu.VMEM((seq, width), BF16)] + stream_scratch(parts),
         micros=12,
     )(where, x, w_qkv, *parts, bias)
 
@@ -336,7 +365,7 @@
     )(where, context, x, w_out, rest_out, bias, gain, shift)
 
 
-def inner_kernel(dims, where, x, own, a, b, c, d, bias, act, early, late, slope, rolled, weight):
+def inner_kernel(dims, where, x, own, a, b, c, d, bias, act, early, late, slope, rolled, *scratch):
     group, half = dims
     unit = pl.program_id(0)
 
@@ -344,8 +373,9 @@
     def _():
         roll_into(rolled, x, where, own.shape[0], group)
 
-    load_weight(unit, half, own, (a, b, c, d), weight)
-    total = dot(rolled[...], weight[...]) + bias[...]
+    rest = stream(unit, (a, b, c, d), *scratch)
+    rows = own.shape[0]
+    total = dot(rolled[:, :rows], own[...]) + dot(rolled[:, rows:], rest) + bias[...]
     below = 0.5 + 0.5 * lax.erf(total * (0.5**0.5))
     value = (total * below).astype(BF16)
     act[...] = value
@@ -368,7 +398,7 @@
     return call(
         partial(inner_kernel, (group, half)),
         (2 * chips,),
-        [fixed((seq, width)), columns_at(rows)] + part_specs(parts) + [columns_at(1)],
+        [fixed((seq, width)), columns_at(rows)] + [ANYWHERE] * 4 + [columns_at(1)],
         [
             columns_at(seq),
             spec((block, seq // 2), lambda u, w: (block_of(w, u, chips), 0)),
@@ -381,7 +411,7 @@
             struct((columns, seq // 2), BF16),
             struct((seq, columns), BF16),
         ],
-        [pltpu.VMEM((seq, width), BF16), pltpu.VMEM((width, block), BF16)],
+        [pltpu.VMEM((seq, width), BF16)] + stream_scratch(parts),
         micros=16,
     )(where, x, w_in, *parts, bias)
 
@@ -409,37 +439,52 @@
     sums,
     total,
     picked,
+    kept,
+    given_rows,
+    kept_sems,
+    *scratch,
 ):
     group, half = dims
     step = pl.program_id(0)
     ff_rows = own.shape[0]
     rows = a.shape[2]
+    late = [
+        pltpu.make_async_copy(hidden, kept, kept_sems.at[0]),
+        pltpu.make_async_copy(cotangent, given_rows, kept_sems.at[1]),
+    ]
+    stream_whole(step, (a, b, c, d), *scratch)
+
+    @pl.when(step == 1)
+    def _():
+        for copy in late:
+            copy.start()
 
     @pl.when(step == 0)
     def _():
         start = pl.multiple_of(where[0] * ff_rows, 128)
         total[...] = dot(act[:, pl.ds(start, ff_rows)], own[...])
 
-    for index, part in enumerate((a, b, c, d)):
-
-        @pl.when(step == index + 1)
-        def _(index=index, part=part):
-            at = 0
-            for i in range(half):
-                block = block_of(where, index * half + i, 2 * half)
-                for s in range(1, group):
-                    start = natural(where, s, group) * ff_rows + block * rows
-                    picked[:, at : at + rows] = act[:, pl.ds(pl.multiple_of(start, rows), rows)]
-                    at += rows
-            total[...] += dot(picked[...], part[...].reshape(-1, part.shape[3]))
+    @pl.when(step > 0)
+    def _():
+        at = 0
+        for i in range(half):
+            block = block_of(where, (step - 1) * half + i, 2 * half)
+            for s in range(1, group):
+                start = natural(where, s, group) * ff_rows + block * rows
+                picked[:, at : at + rows] = act[:, pl.ds(pl.multiple_of(start, rows), rows)]
+                at += rows
+        rest = scratch[0][lax.rem(step - 1, 2)].reshape(-1, a.shape[3])
+        total[...] += dot(picked[...], rest)
 
     @pl.when(step == 4)
     def _():
-        unit_one, _ = normalise(hidden[...])
+        for copy in late:
+            copy.wait()
+        unit_one, _ = normalise(kept[...])
         second = unit_one * gain_one[...] + shift_one[...] + total[...] + bias[...]
         unit, inverse = normalise(second)
         out[...] = (unit * gain_two[...] + shift_two[...]).astype(BF16)
-        given = cotangent[...].astype(F32)
+        given = given_rows[...].astype(F32)
         back = normalise_back(given, unit, inverse, gain_two[...])
         grad[...] = back
         rounded = back.astype(BF16)
@@ -462,8 +507,7 @@
         partial(outer_kernel, (group, half)),
         (5,),
         [fixed(act.shape), fixed((rows, width))]
-        + [fixed(parts[0].shape)] * 4
-        + [full, full]
+        + [ANYWHERE] * 6
         + [vector] * 5,
         [full, full, full, fixed((seq, width // 2)), fixed((8, width))],
         [
@@ -473,12 +517,21 @@
             struct((seq, width // 2), BF16),
             struct((8, width), F32),
         ],
-        [pltpu.VMEM((seq, width), F32), pltpu.VMEM((seq, half * steps * size), BF16)],
+        [
+            pltpu.VMEM((seq, width), F32),
+            pltpu.VMEM((seq, half * steps * size), BF16),
+            pltpu.VMEM((seq, width), F32),
+            pltpu.VMEM((seq, width), BF16),
+            pltpu.SemaphoreType.DMA((2,)),
+        ]
+        + whole_scratch(parts),
         micros=60,
     )(where, act, w_down, *parts, hidden, cotangent, *vectors)
 
 
-def slope_kernel(dims, where, low, own, a, b, c, d, slope, grad, grad_other, sums):
+def slope_kernel(
+    dims, where, low, own, a, b, c, d, given, grad, grad_other, sums, slope, slope_sem, *scratch
+):
     group, half, width = dims
     step = pl.program_id(0)
     ff_rows = own.shape[0]
@@ -499,22 +552,27 @@
                 there = pl.multiple_of((block // 2) * width + inside, piece)
                 grad_other[:, pl.ds(there, piece)] = value[:, at : at + piece]
 
+    slopes = pltpu.make_async_copy(given, slope, slope_sem)
+    stream_whole(step, (a, b, c, d), *scratch)
+
     @pl.when(step == 0)
     def _():
-        finish(dot_t(low[...], own[...]), where[0] * ff_rows, ff_rows)
-
-    for index, part in enumerate((a, b, c, d)):
-
-        @pl.when(step == index + 1)
-        def _(index=index, part=part):
-            back = dot_t(low[...], part[...].reshape(-1, part.shape[3]))
-            at = 0
-            for i in range(half):
-                block = block_of(where, index * half + i, 2 * half)
-                for s in range(1, group):
-                    start = natural(where, s, group) * ff_rows + block * rows
-                    finish(back[:, at : at + rows], start, rows)
-                    at += rows
+        slopes.start()
+        back = dot_t(low[...], own[...])
+        slopes.wait()
+        finish(back, where[0] * ff_rows, ff_rows)
+
+    @pl.when(step > 0)
+    def _():
+        rest = scratch[0][lax.rem(step - 1, 2)].reshape(-1, a.shape[3])
+        back = dot_t(low[...], rest)
+        at = 0
+        for i in range(half):
+            block = block_of(where, (step - 1) * half + i, 2 * half)
+            for s in range(1, group):
+                start = natural(where, s, group) * ff_rows + block * rows
+                finish(back[:, at : at + rows], start, rows)
+                at += rows
 
 
 def slope_back(where, low, w_down, parts, slope, part, group):
@@ -526,14 +584,14 @@
         partial(slope_kernel, (group, half, part)),
         (5,),
         [fixed((seq, width)), fixed((rows, width))]
-        + [fixed(parts[0].shape)] * 4
-        + [fixed((seq, columns))],
+        + [ANYWHERE] * 5,
         [fixed((seq, columns)), fixed((seq, columns // 2)), fixed((1, columns))],
         [
             struct((seq, columns), BF16),
             struct((seq, columns // 2), BF16),
             struct((1, columns), F32),
         ],
+        [pltpu.VMEM((seq, columns), BF16), pltpu.SemaphoreType.DMA(())] + whole_scratch(parts),
         micros=14,
     )(where, low, w_down, *parts, slope)
 
@@ -557,7 +615,7 @@
     grad_context,
     sums,
     total,
-    weight,
+    *scratch,
 ):
     group, half = dims
     unit = pl.program_id(0)
@@ -566,16 +624,13 @@
     def place(s):
         return pl.ds(pl.multiple_of(natural(where, s, group) * rows, 128), rows)
 
-    load_weight(unit, half, own, (a, b, c, d), weight)
-    value = dot_t(grad_inner[...], weight[...])
-
     @pl.when(unit == 0)
     def _():
-        total[...] = value
-
-    @pl.when(unit > 0)
-    def _():
-        total[...] += value
+        total[...] = jnp.zeros_like(total)
+
+    rest = stream(unit, (a, b, c, d), *scratch)
+    total[:, :rows] += dot_t(grad_inner[...], own[...])
+    total[:, rows:] += dot_t(grad_inner[...], rest)
 
     @pl.when(unit == 4 * half - 1)
     def _():
@@ -610,7 +665,7 @@
         partial(inner_back_kernel, (group, half)),
         (2 * chips,),
         [columns_at(seq), columns_at(rows)]
-        + part_specs(parts)
+        + [ANYWHERE] * 4
         + [full, full, fixed((1, width)), fixed((rows, width)), fixed((width - rows, width))],
         [full, full, full, fixed((8, width))],
         [
@@ -619,12 +674,12 @@
             struct((seq, width), BF16),
             struct((8, width), F32),
         ],
-        [pltpu.VMEM((seq, width), F32), pltpu.VMEM((width, block), BF16)],
+        [pltpu.VMEM((seq, width), F32)] + stream_scratch(parts),
         micros=19,
     )(where, grad_inner, w_in, *parts, grad_two, hidden, gain, w_out, rest_out)
 
 
-def input_back_kernel(dims, where, mine, others, own, a, b, c, d, first, out, total, weight):
+def input_back_kernel(dims, where, mine, others, own, a, b, c, d, first, out, total, *scratch):
     group, half, qkv_width = dims
     unit = pl.program_id(0)
     rows, columns = own.shape
@@ -633,21 +688,16 @@
     def _():
         total[...] = jnp.zeros_like(total)
 
+    rest = stream(unit, (a, b, c, d), *scratch)
     block = block_of(where, unit, 2 * half)
     inside = block * columns < qkv_width
     same = lax.rem(block, 2) == where[1]
 
     @pl.when(inside)
     def _():
-        load_weight(unit, half, own, (a, b, c, d), weight)
-
-    @pl.when(inside & same)
-    def _():
-        total[...] += dot_t(mine[0], weight[...])
-
-    @pl.when(inside & ~same)
-    def _():
-        total[...] += dot_t(others[0], weight[...])
+        grad = jnp.where(same, mine[0], others[0])
+        total[:, :rows] += dot_t(grad, own[...])
+        total[:, rows:] += dot_t(grad, rest)
 
     @pl.when(unit == 4 * half - 1)
     def _():
@@ -676,79 +726,66 @@
             spec((1, seq, block), plane),
             spec((rows, block), lambda u, w: (0, jnp.minimum(block_of(w, u, chips), top))),
         ]
-        + part_specs(parts)
+        + [ANYWHERE] * 4
         + [fixed((seq, width))],
         fixed((seq, width)),
         struct((seq, width), F32),
-        [pltpu.VMEM((seq, width), F32), pltpu.VMEM((width, block), BF16)],
+        [pltpu.VMEM((seq, width), F32)] + stream_scratch(parts),
         micros=12,
     )(where, mine, others, w_qkv, *parts, first)
 
 
-def widen_rows_kernel(phases, where, a, b, c, d, out):
-    parts = (a, b, c, d)
+def widen_kernel(dims, where, *refs):
+    parts, outs = refs[:4], refs[4:]
+    phases, kinds, more = dims
     chips = 1 << phases
     half = chips // 2
+    if more:
+        outs, extra = outs[:-1], outs[-1]
+        extra[...] = jnp.zeros_like(extra)
     for side in range(2):
         core = where[1] if side == 0 else 1 - where[1]
         for order in range(chips):
-            value = parts[2 * side + order // half][order % half].astype(F32)
-            rows, columns = value.shape
-            out[
-                pl.ds(pl.multiple_of(where[2 + side * chips + order] * rows, 8), rows),
-                pl.ds(pl.multiple_of(core * columns, 128), columns),
-            ] = value
-
-
-def widen_rows(where, parts, phases, shape):
-    return call(
-        partial(widen_rows_kernel, phases),
-        (1,),
-        [fixed(part.shape) for part in parts],
-        fixed(shape),
-        struct(shape, F32),
-        micros=4,
-    )(where, *parts)
-
-
-def widen_kernel(dims, where, *refs):
-    parts, outs, extra = refs[:4], refs[4:-1], refs[-1]
-    phases, kinds = dims
-    chips = 1 << phases
-    half = chips // 2
-    summed = jnp.zeros(extra.shape, F32)
-    for side in range(2):
-        core = where[1] if side == 0 else 1 - where[1]
-        for order in range(chips):
-            start = 2 * where[2 + side * chips + order] + core
+            chip = where[2 + side * chips + order]
             given = parts[2 * side + order // half].at[order % half]
             at, row = 0, 0
-            for count in kinds:
-                rows = outs[at].shape[0]
-                value = given[row : row + rows, :].astype(F32)
+            for by_rows, rows, count in kinds:
+                targets, at = outs[at : at + count], at + count
+                columns = given.shape[1]
+                step = min(rows, 128)
+
+                @pl.loop(0, rows // step)
+                def _(index, row=row, rows=rows, step=step, targets=targets, by_rows=by_rows):
+                    inside = pl.multiple_of(index * step, step)
+                    value = given[pl.ds(row + inside, step), :].astype(F32)
+                    if by_rows:
+                        down = pl.ds(pl.multiple_of(chip * rows + inside, step), step)
+                        across = pl.ds(pl.multiple_of(core * columns, 128), columns)
+                        targets[0][down, across] = value
+                        return
+                    base = 0
+                    for out in targets:
+                        first = (2 * chip + core) * columns - base
+
+                        @pl.when((first >= 0) & (first < out.shape[1]))
+                        def _(out=out, first=first):
+                            across = pl.ds(pl.multiple_of(first, 128), columns)
+                            out[pl.ds(inside, step), across] = value
+
+                        base += out.shape[1]
+
                 row += rows
-                columns = value.shape[1]
-                base = 0
-                for out in outs[at : at + count]:
-                    size = out.shape[1]
-                    first = start * columns - base
-
-                    @pl.when((first >= 0) & (first < size))
-                    def _(out=out, first=first, value=value, columns=columns):
-                        out[:, pl.ds(pl.multiple_of(first, 128), columns)] = value
-
-                    base += size
-                at += count
-            summed = summed + given[row:, :].astype(F32)
-    extra[...] = summed
-
-
-def widen(where, parts, phases, kinds):
-    shapes = [shape for given in kinds for shape in given]
-    rows = sum(given[0][0] for given in kinds)
-    shapes.append((parts[0].shape[1] - rows, parts[0].shape[2]))
+            if more:
+                extra[...] += given[row:, :].astype(F32)
+
+
+def widen(where, parts, phases, kinds, more=0):
+    shapes = [shape for *_, given in kinds for shape in given]
+    if more:
+        shapes.append((more, parts[0].shape[2]))
+    short = [(by_rows, rows, len(given)) for by_rows, rows, given in kinds]
     return call(
-        partial(widen_kernel, (phases, [len(given) for given in kinds])),
+        partial(widen_kernel, (phases, short, more)),
         (1,),
         [fixed(part.shape) for part in parts],
         [fixed(shape) for shape in shapes],
@@ -1106,7 +1143,6 @@
     first_right = after((mine, other_proj), sent, down.given)
     first = Scatter(first_left, first_right, first_maps, (rows, part))
     sent = first.send()
-    gather_down = Gather(down.total().astype(BF16)[None, None])
     def blocks(core_parity):
         value = jnp.where(core == core_parity, sums_mine, sums_others)
         return value.reshape(3, -1, 1, part)
@@ -1137,7 +1173,9 @@
     gather_down = Gather(after(down.total().astype(BF16)[None], done))
     gather_down.step()
     gather_down.finish()
-    grad_wdown = widen_rows(where, gather_down.parts, phases, (ff_rows, model_width))
+    (grad_wdown,) = widen(
+        where, gather_down.parts, phases, [(True, part_rows, [(ff_rows, model_width)])]
+    )
     shares = jnp.concatenate([inward.total(), first.total()], axis=0).astype(BF16)
     final = Gather(shares[None])
     final.step(grad_wdown)
@@ -1146,7 +1184,11 @@
         where,
         final.parts,
         phases,
-        [[(rows, ff_width)], [(rows, qkv_width), (rows, model_width)]],
+        [
+            (False, rows, [(rows, ff_width)]),
+            (False, rows, [(rows, qkv_width), (rows, model_width)]),
+        ],
+        extra,
     )
     total = total.reshape(-1)
 

time: 466 us -> 463 us (level)
  transfers between devices with their start and end apart: 54 -> 54, of which waited for: 28 -> 27; matrix products, arithmetic and copies ran while one was open for 5% -> 5% of each run, Pallas kernels for 42% -> 42%
where the time goes in v5:
time: 463 us; the launch traced here: 454 us
  Pallas kernels  214 us (46%)
  waiting for transfers between devices  152 us (33%)
  starting transfers between devices  54 us (12%)
  local copies, waits for them, and re-layouts  17.2 us (4%)
  other arithmetic  14.7 us (3%)
    ppermute x16, waiting for transfers between devices, swap(): return lax.ppermute(value, REP, pairs)  68.4 us
    pallas_call x9, Pallas kernels, grads(): call(partial(grads_kernel, (units, len(received), last, group, cuts, int(...  57.7 us
    ppermute x12, waiting for transfers between devices, from_shard(): lax.ppermute(value, 'shard', [(i, (i - step) % group) for i in range(grou...  47.5 us
    ppermute x9, waiting for transfers between devices, to_shard(): lax.ppermute(value, 'shard', [(i, (i + step) % group) for i in range(grou...  29 us
    pallas_call x2, Pallas kernels, attention_back(): call(partial(attend_back_kernel, (mine, per)), (each // 2,), [pairs(0), p...  26.2 us
    pallas_call x2, Pallas kernels, attention(): call(partial(attend_kernel, first), (count,), [spec((seq, block), lambda...  21.7 us
    pallas_call x1, Pallas kernels, inner_back(): call(partial(inner_back_kernel, (group, half)), (2 * chips,), [columns_at...  18 us
    ppermute x17, starting transfers between devices, sibling(): return lax.ppermute(value, 'core', [(0, 1), (1, 0)])  17.1 us
  transfers between devices with their start and end apart: 54, of which 27 were waited for; matrix products, arithmetic and copies ran while one was open for 5% of the time, Pallas kernels for 42%

profile of v5, /device:TPU:9, one launch (start us, length us, event | category | flops | bytes accessed | tf_op | source)
XLA Modules:
  0.0 454.2 jit_solution(368790035880168157)
XLA Ops:
  8.9 11.8 %collective-permute-done.1 = bf16[256,512]{1,0:T(8,128)(2,1)S(1)} collective-permute-done((bf16[256,512]{1,0:T(8,128)(2,1)S(1)}, bf16[256,512]{1,0:T(8,128)(2,1)S(1)}, u32[]{:S(2)}, u32[]{:S(2)}) %collective-permute-start.1) | collective-permute-done | bytes 262176 | tf_op jit(solution)/shard_map/ppermute | solution.py:902
  27.9 9.9 %collective-permute-done.3 = bf16[1,3,256,512]{3,2,1,0:T(8,128)(2,1)S(1)} collective-permute-done((bf16[1,3,256,512]{3,2,1,0:T(8,128)(2,1)S(1)}, bf16[1,3,256,512]{3,2,1,0:T(8,128)(2,1)S(1)}, u32[]{:S(2)}, u32[]{:S(2)}) %collective-permute-start.3) | collective-permute-done | bytes 786464 | tf_op jit(solution)/shard_map/ppermute | solution.py:917
  39.2 18.4 %collective-permute-done.4.b = bf16[2,3,256,512]{3,2,1,0:T(8,128)(2,1)S(1)} collective-permute-done((bf16[2,3,256,512]{3,2,1,0:T(8,128)(2,1)S(1)}, bf16[2,3,256,512]{3,2,1,0:T(8,128)(2,1)S(1)}, u32[]{:S(2)}, u32[]{:S(2)}) %collective-permute-start.4) | collective-permute-done | bytes 1572896 | tf_op jit(solution)/shard_map/ppermute | solution.py:917
  73.2 12.6 %shard_map.299 = (bf16[512,4096]{1,0:T(8,128)(2,1)}, bf16[768,1024]{1,0:T(8,128)(2,1)}) custom-call(s32[10]{0:T(128)} %pad_add_fusion.where, bf16[512,1024]{1,0:T(8,128)(2,1)} %bitcast.105, bf16[256,3072]{1,0:T(8,128)(2,1)} %own.13, bf16[2,3,256,512]{3,2,1,0:T(8,128)(2,1)} %copy-done, bf16[2,3,256,512]{3,2,1,0:T(8,128)(2,1)} %copy-done.2, ...), custom_call_target="tpu_custom_call" | custom-call | bytes 44280000 | tf_op jit(solution)/shard_map/pallas_call | solution.py:179
  85.8 6.8 %collective-permute-done.12 = bf16[256,512]{1,0:T(8,128)(2,1)} collective-permute-done((bf16[256,512]{1,0:T(8,128)(2,1)S(1)}, bf16[256,512]{1,0:T(8,128)(2,1)}, u32[]{:S(2)}, u32[]{:S(2)}) %collective-permute-start.12) | collective-permute-done | bytes 262176 | tf_op jit(solution)/shard_map/ppermute | solution.py:902
  100.3 10.8 %shard_map.300 = (bf16[512,1024]{1,0:T(8,128)(2,1)}, bf16[2,1024,512]{2,1,0:T(8,128)(2,1)}, f32[512,128]{1,0:T(8,128)}) custom-call(s32[10]{0:T(128)} %pad_add_fusion.where, bf16[512,4096]{1,0:T(8,128)(2,1)} %get-tuple-element.108.q.k.v, bf16[512,4096]{1,0:T(8,128)(2,1)} %get-tuple-element.108.q.k.v, bf16[512,4096]{1,0:T(8,128)(2,1)} %get-tuple-element.108.q.k.v, ...), custom_call_target="tpu_custom_call" | custom-call | bytes 40590000 | tf_op jit(solution)/shard_map/pallas_call | solution.py:229
  117.4 7.0 %collective-permute-done.17 = bf16[128,1024]{1,0:T(8,128)(2,1)S(1)} collective-permute-done((bf16[128,1024]{1,0:T(8,128)(2,1)S(1)}, bf16[128,1024]{1,0:T(8,128)(2,1)S(1)}, u32[]{:S(2)}, u32[]{:S(2)}) %collective-permute-start.17) | collective-permute-done | bytes 262176 | tf_op jit(solution)/shard_map/ppermute | solution.py:902
  135.7 10.9 %shard_map.301 = (bf16[512,1024]{1,0:T(8,128)(2,1)}, bf16[2,1024,512]{2,1,0:T(8,128)(2,1)}, f32[512,128]{1,0:T(8,128)}) custom-call(s32[10]{0:T(128)} %pad_add_fusion.where, bf16[512,4096]{1,0:T(8,128)(2,1)} %get-tuple-element.108.q.k.v, bf16[512,4096]{1,0:T(8,128)(2,1)} %get-tuple-element.108.q.k.v, ...), custom_call_target="tpu_custom_call", output_to_operand_aliasing={{0}: (7, {}), {1}: (8, {})} | custom-call | bytes 40590000 | tf_op jit(solution)/shard_map/pallas_call | solution.py:229
  146.5 6.0 %shard_map.302 = (f32[512,1024]{1,0:T(8,128)}, bf16[512,1024]{1,0:T(8,128)(2,1)}, bf16[1024,512]{1,0:T(8,128)(2,1)}) custom-call(s32[10]{0:T(128)} %pad_add_fusion.where, bf16[512,1024]{1,0:T(8,128)(2,1)} %get-tuple-element.111.context, bf16[512,1024]{1,0:T(8,128)(2,1)} %bitcast.108, bf16[256,1024]{1,0:T(8,128)(2,1)} %own_out.1, ...), custom_call_target="tpu_custom_call" | custom-call | bytes 22140000 | tf_op jit(solution)/shard_map/pallas_call | solution.py:345
  163.0 15.5 %shard_map.303 = (bf16[512,4096]{1,0:T(8,128)(2,1)}, bf16[4096,256]{1,0:T(8,128)(2,1)}, bf16[4096,256]{1,0:T(8,128)(2,1)}, bf16[512,4096]{1,0:T(8,128)(2,1)}) custom-call(s32[10]{0:T(128)} %pad_add_fusion.where, bf16[512,1024]{1,0:T(8,128)(2,1)} %get-tuple-element.113.x, bf16[256,4096]{1,0:T(8,128)(2,1)} %own.12, ...), custom_call_target="tpu_custom_call" | custom-call | bytes 59040000 | tf_op jit(solution)/shard_map/pallas_call | solution.py:398
  183.9 15.3 %shard_map.304 = (bf16[512,1024]{1,0:T(8,128)(2,1)}, f32[512,1024]{1,0:T(8,128)}, bf16[512,1024]{1,0:T(8,128)(2,1)}, bf16[512,512]{1,0:T(8,128)(2,1)}, f32[8,1024]{1,0:T(8,128)}) custom-call(s32[10]{0:T(128)} %pad_add_fusion.where, bf16[512,4096]{1,0:T(8,128)(2,1)} %get-tuple-element.120.act, bf16[1024,1024]{1,0:T(8,128)(2,1)} %own.11, ...), custom_call_target="tpu_custom_call" | custom-call | bytes 221400000 | tf_op jit(solution)/shard_map/pallas_call | solution.py:506
  202.2 7.5 %shard_map.305 = bf16[2,1024,512]{2,1,0:T(8,128)(2,1)} custom-call(s32[10]{0:T(128)} %pad_add_fusion.where, bf16[1,512,1024]{2,1,0:T(8,128)(2,1)} %bitcast.101, bf16[1,512,512]{2,1,0:T(8,128)(2,1)} %bitcast.113, bf16[1,4096,256]{2,1,0:T(8,128)(2,1)} %bitcast.93, bf16[1,4096,256]{2,1,0:T(8,128)(2,1)} %bitcast.97, ...), custom_call_target="tpu_custom_call" | custom-call | bytes 22140000 | tf_op jit(solution)/shard_map/pallas_call | solution.py:856
  211.5 15.4 %shard_map.306 = (bf16[512,4096]{1,0:T(8,128)(2,1)}, bf16[512,2048]{1,0:T(8,128)(2,1)}, f32[1,4096]{1,0:T(1,128)}) custom-call(s32[10]{0:T(128)} %pad_add_fusion.where, bf16[512,1024]{1,0:T(8,128)(2,1)} %get-tuple-element.131.low, bf16[1024,1024]{1,0:T(8,128)(2,1)} %own.11, bf16[2,3,128,1024]{3,2,1,0:T(8,128)(2,1)} %pad_maximum_fusion.2.a, ...), custom_call_target="tpu_custom_call" | custom-call | bytes 51660000 | tf_op jit(solution)/shard_map/pallas_call | solution.py:583
  227.0 18.0 %shard_map.307 = (f32[512,1024]{1,0:T(8,128)}, bf16[512,1024]{1,0:T(8,128)(2,1)}, bf16[512,1024]{1,0:T(8,128)(2,1)}, f32[8,1024]{1,0:T(8,128)}) custom-call(s32[10]{0:T(128)} %pad_add_fusion.where, bf16[512,4096]{1,0:T(8,128)(2,1)} %get-tuple-element.135.grad_inner, bf16[256,4096]{1,0:T(8,128)(2,1)} %own.12, bf16[2,3,256,512]{3,2,1,0:T(8,128)(2,1)} %pad_maximum_fusion.1.a, ...), custom_call_target="tpu_custom_call" | custom-call | bytes 70110000 | tf_op jit(solution)/shard_map/pallas_call | solution.py:664
  245.1 5.8 %shard_map.308 = bf16[1,1024,512]{2,1,0:T(8,128)(2,1)} custom-call(s32[10]{0:T(128)} %pad_add_fusion.where, bf16[1,512,1024]{2,1,0:T(8,128)(2,1)} %bitcast.103, bf16[1,512,512]{2,1,0:T(8,128)(2,1)} %bitcast.115, bf16[1,4096,256]{2,1,0:T(8,128)(2,1)} %bitcast.95, bf16[1,4096,256]{2,1,0:T(8,128)(2,1)} %bitcast.99, ...), custom_call_target="tpu_custom_call" | custom-call | bytes 22140000 | tf_op jit(solution)/shard_map/pallas_call | solution.py:856
  251.2 7.1 %shard_map.309 = bf16[2,1024,512]{2,1,0:T(8,128)(2,1)} custom-call(s32[10]{0:T(128)} %pad_add_fusion.where, bf16[1,512,4096]{2,1,0:T(8,128)(2,1)} %bitcast.89, bf16[1,512,2048]{2,1,0:T(8,128)(2,1)} %bitcast.28.refs_1_.refs_5_, bf16[1,1024,512]{2,1,0:T(8,128)(2,1)} %bitcast.109, bf16[1,1024,512]{2,1,0:T(8,128)(2,1)} %bitcast.26.refs_3_.refs_7_, ...), custom_call_target="tpu_custom_call" | custom-call | bytes 22140000 | tf_op jit(solution)/shard_map/pallas_call | solution.py:856
  259.4 13.0 %shard_map.310 = (bf16[4,512,512]{2,1,0:T(8,128)(2,1)}, f32[3,1,512]{2,1,0:T(1,128)}) custom-call(s32[10]{0:T(128)} %pad_add_fusion.where, bf16[512,4096]{1,0:T(8,128)(2,1)} %get-tuple-element.108.q.k.v, bf16[512,4096]{1,0:T(8,128)(2,1)} %get-tuple-element.108.q.k.v, bf16[512,4096]{1,0:T(8,128)(2,1)} %get-tuple-element.108.q.k.v, ...), custom_call_target="tpu_custom_call" | custom-call | bytes 47970000 | tf_op jit(solution)/shard_map/pallas_call | solution.py:302
  272.3 6.2 %shard_map.311 = (bf16[256,512]{1,0:T(8,128)(2,1)}, bf16[256,512]{1,0:T(8,128)(2,1)}, bf16[256,512]{1,0:T(8,128)(2,1)}, bf16[256,512]{1,0:T(8,128)(2,1)}) custom-call(s32[10]{0:T(128)} %pad_add_fusion.where, bf16[1,512,1024]{2,1,0:T(8,128)(2,1)} %bitcast.104, bf16[1,512,512]{2,1,0:T(8,128)(2,1)} %bitcast.116, bf16[1,4096,256]{2,1,0:T(8,128)(2,1)} %bitcast.96, ...), custom_call_target="tpu_custom_call" | custom-call | bytes 22140000 | tf_op jit(solution)/shard_map/pallas_call | solution.py:856
  286.5 13.2 %shard_map.312 = (bf16[4,512,512]{2,1,0:T(8,128)(2,1)}, f32[3,1,512]{2,1,0:T(1,128)}) custom-call(s32[10]{0:T(128)} %pad_add_fusion.where, bf16[512,4096]{1,0:T(8,128)(2,1)} %get-tuple-element.108.q.k.v, bf16[512,4096]{1,0:T(8,128)(2,1)} %get-tuple-element.108.q.k.v, bf16[512,4096]{1,0:T(8,128)(2,1)} %get-tuple-element.108.q.k.v, ...), custom_call_target="tpu_custom_call" | custom-call | bytes 47970000 | tf_op jit(solution)/shard_map/pallas_call | solution.py:302
  299.7 5.7 %shard_map.313 = bf16[1,1024,512]{2,1,0:T(8,128)(2,1)} custom-call(s32[10]{0:T(128)} %pad_add_fusion.where, bf16[1,512,4096]{2,1,0:T(8,128)(2,1)} %bitcast.91, bf16[1,512,2048]{2,1,0:T(8,128)(2,1)} %bitcast.28.refs_1_.refs_5_, bf16[1,1024,512]{2,1,0:T(8,128)(2,1)} %bitcast.111, bf16[1,1024,512]{2,1,0:T(8,128)(2,1)} %bitcast.26.refs_3_.refs_7_, ...), custom_call_target="tpu_custom_call" | custom-call | bytes 22140000 | tf_op jit(solution)/shard_map/pallas_call | solution.py:856
  309.0 7.2 %shard_map.314 = bf16[2,1024,512]{2,1,0:T(8,128)(2,1)} custom-call(s32[10]{0:T(128)} %pad_add_fusion.where, bf16[4,512,512]{2,1,0:T(8,128)(2,1)} %get-tuple-element.159.refs_0_.refs_4_.mine, bf16[4,512,512]{2,1,0:T(8,128)(2,1)} %collective-permute-done.32.refs_1_.refs_5_, bf16[2,1024,512]{2,1,0:T(8,128)(2,1)} %get-tuple-element.139.refs_2_.refs_6_, ...), custom_call_target="tpu_custom_call" | custom-call | bytes 22140000 | tf_op jit(solution)/shard_map/pallas_call | solution.py:856
  321.6 13.8 %shard_map.315 = f32[512,1024]{1,0:T(8,128)} custom-call(s32[10]{0:T(128)} %pad_add_fusion.where, bf16[4,512,512]{2,1,0:T(8,128)(2,1)} %get-tuple-element.159.refs_0_.refs_4_.mine, bf16[4,512,512]{2,1,0:T(8,128)(2,1)} %get-tuple-element.152.others, bf16[256,3072]{1,0:T(8,128)(2,1)} %own.13, bf16[2,3,256,512]{3,2,1,0:T(8,128)(2,1)} %copy-done, ...), custom_call_target="tpu_custom_call" | custom-call | bytes 44280000 | tf_op jit(solution)/shard_map/pallas_call | solution.py:721
  335.4 6.7 %collective-permute-done.37.refs_5_ = bf16[1,1024,512]{2,1,0:T(8,128)(2,1)} collective-permute-done((bf16[1,1024,512]{2,1,0:T(8,128)(2,1)}, bf16[1,1024,512]{2,1,0:T(8,128)(2,1)}, u32[]{:S(2)}, u32[]{:S(2)}) %collective-permute-start.37) | collective-permute-done | bytes 1048608 | tf_op jit(solution)/shard_map/ppermute | solution.py:917
  342.1 6.2 %shard_map.316 = (bf16[256,512]{1,0:T(8,128)(2,1)}, bf16[256,512]{1,0:T(8,128)(2,1)}, bf16[256,512]{1,0:T(8,128)(2,1)}, bf16[256,512]{1,0:T(8,128)(2,1)}) custom-call(s32[10]{0:T(128)} %pad_add_fusion.where, bf16[1,512,4096]{2,1,0:T(8,128)(2,1)} %bitcast.92, bf16[1,512,2048]{2,1,0:T(8,128)(2,1)} %bitcast.28.refs_1_.refs_5_, bf16[1,1024,512]{2,1,0:T(8,128)(2,1)} %bitcast.112, ...), custom_call_target="tpu_custom_call" | custom-call | bytes 22140000 | tf_op jit(solution)/shard_map/pallas_call | solution.py:856
  352.9 5.8 %shard_map.317 = bf16[1,1024,512]{2,1,0:T(8,128)(2,1)} custom-call(s32[10]{0:T(128)} %pad_add_fusion.where, bf16[4,512,512]{2,1,0:T(8,128)(2,1)} %get-tuple-element.159.refs_0_.refs_4_.mine, bf16[4,512,512]{2,1,0:T(8,128)(2,1)} %collective-permute-done.32.refs_1_.refs_5_, bf16[2,1024,512]{2,1,0:T(8,128)(2,1)} %get-tuple-element.139.refs_2_.refs_6_, ...), custom_call_target="tpu_custom_call" | custom-call | bytes 22140000 | tf_op jit(solution)/shard_map/pallas_call | solution.py:856
  363.0 10.0 %collective-permute-done.42.refs_5_ = bf16[1,1024,512]{2,1,0:T(8,128)(2,1)} collective-permute-done((bf16[1,1024,512]{2,1,0:T(8,128)(2,1)}, bf16[1,1024,512]{2,1,0:T(8,128)(2,1)}, u32[]{:S(2)}, u32[]{:S(2)}) %collective-permute-start.42) | collective-permute-done | bytes 1048608 | tf_op jit(solution)/shard_map/ppermute | solution.py:917
  373.0 6.2 %shard_map.318 = (bf16[272,512]{1,0:T(8,128)(2,1)}, bf16[272,512]{1,0:T(8,128)(2,1)}, bf16[272,512]{1,0:T(8,128)(2,1)}, bf16[272,512]{1,0:T(8,128)(2,1)}) custom-call(s32[10]{0:T(128)} %pad_add_fusion.where, bf16[4,512,512]{2,1,0:T(8,128)(2,1)} %get-tuple-element.159.refs_0_.refs_4_.mine, bf16[4,512,512]{2,1,0:T(8,128)(2,1)} %collective-permute-done.32.refs_1_.refs_5_, ...), custom_call_target="tpu_custom_call" | custom-call | bytes 22140000 | tf_op jit(solution)/shard_map/pallas_call | solution.py:856
  382.2 13.1 %collective-permute-done.40 = bf16[256,512]{1,0:T(8,128)(2,1)} collective-permute-done((bf16[256,512]{1,0:T(8,128)(2,1)}, bf16[256,512]{1,0:T(8,128)(2,1)}, u32[]{:S(2)}, u32[]{:S(2)}) %collective-permute-start.40) | collective-permute-done | bytes 262176 | tf_op jit(solution)/shard_map/ppermute | solution.py:905
  397.6 8.5 %collective-permute-done.44 = bf16[272,512]{1,0:T(8,128)(2,1)S(1)} collective-permute-done((bf16[272,512]{1,0:T(8,128)(2,1)}, bf16[272,512]{1,0:T(8,128)(2,1)S(1)}, u32[]{:S(2)}, u32[]{:S(2)}) %collective-permute-start.44) | collective-permute-done | bytes 278560 | tf_op jit(solution)/shard_map/ppermute | solution.py:905
  410.0 6.6 %collective-permute-done.46 = bf16[1,528,512]{2,1,0:T(8,128)(2,1)S(1)} collective-permute-done((bf16[1,528,512]{2,1,0:T(8,128)(2,1)S(1)}, bf16[1,528,512]{2,1,0:T(8,128)(2,1)S(1)}, u32[]{:S(2)}, u32[]{:S(2)}) %collective-permute-start.46) | collective-permute-done | bytes 540704 | tf_op jit(solution)/shard_map/ppermute | solution.py:917
  426.0 11.5 %collective-permute-done.51.refs_1_ = bf16[2,528,512]{2,1,0:T(8,128)(2,1)S(1)} collective-permute-done((bf16[2,528,512]{2,1,0:T(8,128)(2,1)}, bf16[2,528,512]{2,1,0:T(8,128)(2,1)S(1)}, u32[]{:S(2)}, u32[]{:S(2)}) %collective-permute-start.51) | collective-permute-done | bytes 1081376 | tf_op jit(solution)/shard_map/ppermute | solution.py:917
  443.2 7.3 %shard_map.320 = (f32[256,4096]{1,0:T(8,128)}, f32[256,3072]{1,0:T(8,128)}, f32[256,1024]{1,0:T(8,128)}, f32[16,512]{1,0:T(8,128)}) custom-call(s32[10]{0:T(128)} %pad_add_fusion.where, bf16[2,528,512]{2,1,0:T(8,128)(2,1)} %pad_maximum_fusion.3.refs_0_, bf16[2,528,512]{2,1,0:T(8,128)(2,1)} %copy-done.4, ...), custom_call_target="tpu_custom_call" | custom-call | bytes 14760000 | tf_op jit(solution)/shard_map/pallas_call | solution.py:787
  (225 shorter events, 132.0 us)
Async XLA Ops:
  1.8 19.0 %collective-permute-start.1 = (bf16[256,512]{1,0:T(8,128)(2,1)S(1)}, bf16[256,512]{1,0:T(8,128)(2,1)S(1)}, u32[]{:S(2)}, u32[]{:S(2)}) collective-permute-start(bf16[256,512]{1,0:T(8,128)(2,1)S(1)} %fusion.1), channel_id=1, source_target_pairs={{0,2},{1,3},{2,0},{3,1},{4,6},{5,7},{6,4},{7,5},{8,10},{9,11},{10,... | collective-permute-start | bytes 786440 | tf_op jit(solution)/shard_map/ppermute | solution.py:902
  4.3 22.1 %collective-permute-start.2 = (bf16[256,512]{1,0:T(8,128)(2,1)S(1)}, bf16[256,512]{1,0:T(8,128)(2,1)S(1)}, u32[]{:S(2)}, u32[]{:S(2)}) collective-permute-start(bf16[256,512]{1,0:T(8,128)(2,1)S(1)} %fusion.1), channel_id=1, source_target_pairs={{0,1},{1,2},{2,3},{3,0},{4,5},{5,6},{6,7},{7,4},{8,9},{9,10},{10,1... | collective-permute-start | bytes 786440 | tf_op jit(solution)/shard_map/ppermute | solution.py:902
  37.9 19.6 %collective-permute-start.4 = (bf16[2,3,256,512]{3,2,1,0:T(8,128)(2,1)S(1)}, bf16[2,3,256,512]{3,2,1,0:T(8,128)(2,1)S(1)}, u32[]{:S(2)}, u32[]{:S(2)}) collective-permute-start(bf16[2,3,256,512]{3,2,1,0:T(8,128)(2,1)S(1)} %pad_maximum_fusion.a), channel_id=1, source_target_pairs={{0,16},{4,12},{8,24},{12,4},{16,0},{20,28},{24,8},{28,20},{1,17},{... | collective-permute-start | bytes 4718600 | tf_op jit(solution)/shard_map/ppermute | solution.py:917
  70.4 22.2 %collective-permute-start.12 = (bf16[256,512]{1,0:T(8,128)(2,1)S(1)}, bf16[256,512]{1,0:T(8,128)(2,1)}, u32[]{:S(2)}, u32[]{:S(2)}) collective-permute-start(bf16[256,512]{1,0:T(8,128)(2,1)S(1)} %constant_dynamic-slice_fusion.1), channel_id=1, source_target_pairs={{0,1},{1,2},{2,3},{3,0},{4,5},{5,6},{6,7},{7,4},{8,9},{9,10},{10,1... | collective-permute-start | bytes 786440 | tf_op jit(solution)/shard_map/ppermute | solution.py:902
  72.6 23.1 %collective-permute-start.10 = (bf16[256,512]{1,0:T(8,128)(2,1)S(1)}, bf16[256,512]{1,0:T(8,128)(2,1)}, u32[]{:S(2)}, u32[]{:S(2)}) collective-permute-start(bf16[256,512]{1,0:T(8,128)(2,1)S(1)} %constant_dynamic-slice_fusion.1), channel_id=1, source_target_pairs={{0,3},{1,0},{2,1},{3,2},{4,7},{5,4},{6,5},{7,6},{8,11},{9,8},{10,9... | collective-permute-start | bytes 786440 | tf_op jit(solution)/shard_map/ppermute | solution.py:902
  113.6 45.6 %collective-permute-start.14 = (bf16[2,3,256,512]{3,2,1,0:T(8,128)(2,1)}, bf16[2,3,256,512]{3,2,1,0:T(8,128)(2,1)}, u32[]{:S(2)}, u32[]{:S(2)}) collective-permute-start(bf16[2,3,256,512]{3,2,1,0:T(8,128)(2,1)} %pad_maximum_fusion.1.a), channel_id=1, source_target_pairs={{0,16},{4,12},{8,24},{12,4},{16,0},{20,28},{24,8},{28,20},{1,17},{... | collective-permute-start | bytes 4718600 | tf_op jit(solution)/shard_map/ppermute | solution.py:917
  116.3 17.1 %collective-permute-start.19 = (bf16[128,1024]{1,0:T(8,128)(2,1)S(1)}, bf16[128,1024]{1,0:T(8,128)(2,1)S(1)}, u32[]{:S(2)}, u32[]{:S(2)}) collective-permute-start(bf16[128,1024]{1,0:T(8,128)(2,1)S(1)} %constant_dynamic-slice_fusion), channel_id=1, source_target_pairs={{0,1},{1,2},{2,3},{3,0},{4,5},{5,6},{6,7},{7,4},{8,9},{9,10},{10,1... | collective-permute-start | bytes 786440 | tf_op jit(solution)/shard_map/ppermute | solution.py:902
  133.5 23.3 %collective-permute-start.20 = (bf16[1,3,128,1024]{3,2,1,0:T(8,128)(2,1)S(1)}, bf16[1,3,128,1024]{3,2,1,0:T(8,128)(2,1)}, u32[]{:S(2)}, u32[]{:S(2)}) collective-permute-start(bf16[1,3,128,1024]{3,2,1,0:T(8,128)(2,1)S(1)} %maximum_bitcast_fusion.2), channel_id=1, source_target_pairs={{0,8},{4,20},{8,0},{12,28},{16,24},{20,4},{24,16},{28,12},{1,9},{5... | collective-permute-start | bytes 2359304 | tf_op jit(solution)/shard_map/ppermute | solution.py:917
  159.2 19.9 %collective-permute-start.21 = (bf16[2,3,128,1024]{3,2,1,0:T(8,128)(2,1)}, bf16[2,3,128,1024]{3,2,1,0:T(8,128)(2,1)}, u32[]{:S(2)}, u32[]{:S(2)}) collective-permute-start(bf16[2,3,128,1024]{3,2,1,0:T(8,128)(2,1)} %pad_maximum_fusion.2.a), channel_id=1, source_target_pairs={{0,16},{4,12},{8,24},{12,4},{16,0},{20,28},{24,8},{28,20},{1,17},{... | collective-permute-start | bytes 4718600 | tf_op jit(solution)/shard_map/ppermute | solution.py:917
  161.2 21.6 %collective-permute-start.22 = (bf16[2,3,128,1024]{3,2,1,0:T(8,128)(2,1)}, bf16[2,3,128,1024]{3,2,1,0:T(8,128)(2,1)}, u32[]{:S(2)}, u32[]{:S(2)}) collective-permute-start(bf16[2,3,128,1024]{3,2,1,0:T(8,128)(2,1)} %pad_maximum_fusion.2.a), channel_id=1, source_target_pairs={{0,4},{4,0},{1,5},{5,1},{2,6},{6,2},{3,7},{7,3},{8,12},{12,8},{9,1... | collective-permute-start | bytes 4718600 | tf_op jit(solution)/shard_map/ppermute | solution.py:908
  180.5 20.9 %collective-permute-start.25 = (bf16[4096,256]{1,0:T(8,128)(2,1)}, bf16[4096,256]{1,0:T(8,128)(2,1)}, u32[]{:S(2)}, u32[]{:S(2)}) collective-permute-start(bf16[4096,256]{1,0:T(8,128)(2,1)} %get-tuple-element.129), channel_id=1, source_target_pairs={{0,4},{4,0},{1,5},{5,1},{2,6},{6,2},{3,7},{7,3},{8,12},{12,8},{9,1... | collective-permute-start | bytes 6291464 | tf_op jit(solution)/shard_map/ppermute | solution.py:908
  180.5 20.9 %collective-permute-start.26 = (bf16[4096,256]{1,0:T(8,128)(2,1)}, bf16[4096,256]{1,0:T(8,128)(2,1)}, u32[]{:S(2)}, u32[]{:S(2)}) collective-permute-start(bf16[4096,256]{1,0:T(8,128)(2,1)} %get-tuple-element.130), channel_id=1, source_target_pairs={{0,4},{4,0},{1,5},{5,1},{2,6},{6,2},{3,7},{7,3},{8,12},{12,8},{9,1... | collective-permute-start | bytes 6291464 | tf_op jit(solution)/shard_map/ppermute | solution.py:908
  199.6 45.4 %collective-permute-start.29 = (bf16[2,1024,512]{2,1,0:T(8,128)(2,1)}, bf16[2,1024,512]{2,1,0:T(8,128)(2,1)}, u32[]{:S(2)}, u32[]{:S(2)}) collective-permute-start(bf16[2,1024,512]{2,1,0:T(8,128)(2,1)} %get-tuple-element.139.refs_2_.refs_6_), channel_id=1, source_target_pairs={{0,4},{4,0},{1,5},{5,1},{2,6},{6,2},{3,7},{7,3},{8,12},{12,8},{9,1... | collective-permute-start | bytes 6291464 | tf_op jit(solution)/shard_map/ppermute | solution.py:908
  209.6 35.4 %collective-permute-start.28 = (bf16[2,1024,512]{2,1,0:T(8,128)(2,1)}, bf16[2,1024,512]{2,1,0:T(8,128)(2,1)}, u32[]{:S(2)}, u32[]{:S(2)}) collective-permute-start(bf16[2,1024,512]{2,1,0:T(8,128)(2,1)} %shard_map.305), channel_id=1, source_target_pairs={{0,8},{4,20},{8,0},{12,28},{16,24},{20,4},{24,16},{28,12},{1,9},{5... | collective-permute-start | bytes 6291464 | tf_op jit(solution)/shard_map/ppermute | solution.py:917
  209.9 17.1 %collective-permute-start.27 = (bf16[1024,512]{1,0:T(8,128)(2,1)}, bf16[1024,512]{1,0:T(8,128)(2,1)}, u32[]{:S(2)}, u32[]{:S(2)}) collective-permute-start(bf16[1024,512]{1,0:T(8,128)(2,1)} %get-tuple-element.134), channel_id=1, source_target_pairs={{0,4},{4,0},{1,5},{5,1},{2,6},{6,2},{3,7},{7,3},{8,12},{12,8},{9,1... | collective-permute-start | bytes 3145736 | tf_op jit(solution)/shard_map/ppermute | solution.py:908
  226.9 24.3 %collective-permute-start.31 = (bf16[512,2048]{1,0:T(8,128)(2,1)}, bf16[512,2048]{1,0:T(8,128)(2,1)}, u32[]{:S(2)}, u32[]{:S(2)}) collective-permute-start(bf16[512,2048]{1,0:T(8,128)(2,1)} %get-tuple-element.141), channel_id=1, source_target_pairs={{0,4},{4,0},{1,5},{5,1},{2,6},{6,2},{3,7},{7,3},{8,12},{12,8},{9,1... | collective-permute-start | bytes 6291464 | tf_op jit(solution)/shard_map/ppermute | solution.py:908
  250.9 21.5 %collective-permute-start.30 = (bf16[1,1024,512]{2,1,0:T(8,128)(2,1)}, bf16[1,1024,512]{2,1,0:T(8,128)(2,1)}, u32[]{:S(2)}, u32[]{:S(2)}) collective-permute-start(bf16[1,1024,512]{2,1,0:T(8,128)(2,1)} %shard_map.308), channel_id=1, source_target_pairs={{0,16},{4,12},{8,24},{12,4},{16,0},{20,28},{24,8},{28,20},{1,17},{... | collective-permute-start | bytes 3145736 | tf_op jit(solution)/shard_map/ppermute | solution.py:917
  258.4 41.3 %collective-permute-start.33 = (bf16[2,1024,512]{2,1,0:T(8,128)(2,1)}, bf16[2,1024,512]{2,1,0:T(8,128)(2,1)}, u32[]{:S(2)}, u32[]{:S(2)}) collective-permute-start(bf16[2,1024,512]{2,1,0:T(8,128)(2,1)} %shard_map.309), channel_id=1, source_target_pairs={{0,8},{4,20},{8,0},{12,28},{16,24},{20,4},{24,16},{28,12},{1,9},{5... | collective-permute-start | bytes 6291464 | tf_op jit(solution)/shard_map/ppermute | solution.py:917
  278.6 30.4 %collective-permute-start.32 = (bf16[4,512,512]{2,1,0:T(8,128)(2,1)}, bf16[4,512,512]{2,1,0:T(8,128)(2,1)}, u32[]{:S(2)}, u32[]{:S(2)}) collective-permute-start(bf16[4,512,512]{2,1,0:T(8,128)(2,1)} %get-tuple-element.152.others), channel_id=1, source_target_pairs={{0,4},{4,0},{1,5},{5,1},{2,6},{6,2},{3,7},{7,3},{8,12},{12,8},{9,1... | collective-permute-start | bytes 6291464 | tf_op jit(solution)/shard_map/ppermute | solution.py:908
  279.1 26.2 %collective-permute-start.34 = (bf16[256,512]{1,0:T(8,128)(2,1)}, bf16[256,512]{1,0:T(8,128)(2,1)S(1)}, u32[]{:S(2)}, u32[]{:S(2)}) collective-permute-start(bf16[256,512]{1,0:T(8,128)(2,1)} %get-tuple-element.154), channel_id=1, source_target_pairs={{0,1},{1,2},{2,3},{3,0},{4,5},{5,6},{6,7},{7,4},{8,9},{9,10},{10,1... | collective-permute-start | bytes 786440 | tf_op jit(solution)/shard_map/ppermute | solution.py:905
  282.4 23.0 %collective-permute-start.35 = (bf16[256,512]{1,0:T(8,128)(2,1)}, bf16[256,512]{1,0:T(8,128)(2,1)S(1)}, u32[]{:S(2)}, u32[]{:S(2)}) collective-permute-start(bf16[256,512]{1,0:T(8,128)(2,1)} %get-tuple-element.155), channel_id=1, source_target_pairs={{0,2},{1,3},{2,0},{3,1},{4,6},{5,7},{6,4},{7,5},{8,10},{9,11},{10,... | collective-permute-start | bytes 786440 | tf_op jit(solution)/shard_map/ppermute | solution.py:905
  286.5 22.5 %collective-permute-start.36 = (bf16[256,512]{1,0:T(8,128)(2,1)}, bf16[256,512]{1,0:T(8,128)(2,1)S(1)}, u32[]{:S(2)}, u32[]{:S(2)}) collective-permute-start(bf16[256,512]{1,0:T(8,128)(2,1)} %get-tuple-element.156), channel_id=1, source_target_pairs={{0,3},{1,0},{2,1},{3,2},{4,7},{5,4},{6,5},{7,6},{8,11},{9,8},{10,9... | collective-permute-start | bytes 786440 | tf_op jit(solution)/shard_map/ppermute | solution.py:905
  316.1 36.8 %collective-permute-start.41 = (bf16[2,1024,512]{2,1,0:T(8,128)(2,1)}, bf16[2,1024,512]{2,1,0:T(8,128)(2,1)}, u32[]{:S(2)}, u32[]{:S(2)}) collective-permute-start(bf16[2,1024,512]{2,1,0:T(8,128)(2,1)} %shard_map.314), channel_id=1, source_target_pairs={{0,8},{4,20},{8,0},{12,28},{16,24},{20,4},{24,16},{28,12},{1,9},{5... | collective-permute-start | bytes 6291464 | tf_op jit(solution)/shard_map/ppermute | solution.py:917
  317.1 25.0 %collective-permute-start.37 = (bf16[1,1024,512]{2,1,0:T(8,128)(2,1)}, bf16[1,1024,512]{2,1,0:T(8,128)(2,1)}, u32[]{:S(2)}, u32[]{:S(2)}) collective-permute-start(bf16[1,1024,512]{2,1,0:T(8,128)(2,1)} %shard_map.313), channel_id=1, source_target_pairs={{0,16},{4,12},{8,24},{12,4},{16,0},{20,28},{24,8},{28,20},{1,17},{... | collective-permute-start | bytes 3145736 | tf_op jit(solution)/shard_map/ppermute | solution.py:917
  360.4 19.8 %collective-permute-start.38 = (bf16[256,512]{1,0:T(8,128)(2,1)}, bf16[256,512]{1,0:T(8,128)(2,1)}, u32[]{:S(2)}, u32[]{:S(2)}) collective-permute-start(bf16[256,512]{1,0:T(8,128)(2,1)} %get-tuple-element.163), channel_id=1, source_target_pairs={{0,1},{1,2},{2,3},{3,0},{4,5},{5,6},{6,7},{7,4},{8,9},{9,10},{10,1... | collective-permute-start | bytes 786440 | tf_op jit(solution)/shard_map/ppermute | solution.py:905
  360.4 21.8 %collective-permute-start.39 = (bf16[256,512]{1,0:T(8,128)(2,1)}, bf16[256,512]{1,0:T(8,128)(2,1)}, u32[]{:S(2)}, u32[]{:S(2)}) collective-permute-start(bf16[256,512]{1,0:T(8,128)(2,1)} %get-tuple-element.164), channel_id=1, source_target_pairs={{0,2},{1,3},{2,0},{3,1},{4,6},{5,7},{6,4},{7,5},{8,10},{9,11},{10,... | collective-permute-start | bytes 786440 | tf_op jit(solution)/shard_map/ppermute | solution.py:905
  360.4 34.9 %collective-permute-start.40 = (bf16[256,512]{1,0:T(8,128)(2,1)}, bf16[256,512]{1,0:T(8,128)(2,1)}, u32[]{:S(2)}, u32[]{:S(2)}) collective-permute-start(bf16[256,512]{1,0:T(8,128)(2,1)} %get-tuple-element.165), channel_id=1, source_target_pairs={{0,3},{1,0},{2,1},{3,2},{4,7},{5,4},{6,5},{7,6},{8,11},{9,8},{10,9... | collective-permute-start | bytes 786440 | tf_op jit(solution)/shard_map/ppermute | solution.py:905
  379.3 17.3 %collective-permute-start.47 = (bf16[1,256,512]{2,1,0:T(8,128)(2,1)S(1)}, bf16[1,256,512]{2,1,0:T(8,128)(2,1)S(1)}, u32[]{:S(2)}, u32[]{:S(2)}) collective-permute-start(bf16[1,256,512]{2,1,0:T(8,128)(2,1)S(1)} %fusion.3), channel_id=1, source_target_pairs={{0,8},{4,20},{8,0},{12,28},{16,24},{20,4},{24,16},{28,12},{1,9},{5... | collective-permute-start | bytes 786440 | tf_op jit(solution)/shard_map/ppermute | solution.py:917
  380.2 17.4 %collective-permute-start.43 = (bf16[272,512]{1,0:T(8,128)(2,1)}, bf16[272,512]{1,0:T(8,128)(2,1)S(1)}, u32[]{:S(2)}, u32[]{:S(2)}) collective-permute-start(bf16[272,512]{1,0:T(8,128)(2,1)} %get-tuple-element.175), channel_id=1, source_target_pairs={{0,1},{1,2},{2,3},{3,0},{4,5},{5,6},{6,7},{7,4},{8,9},{9,10},{10,1... | collective-permute-start | bytes 835592 | tf_op jit(solution)/shard_map/ppermute | solution.py:905
  380.2 25.9 %collective-permute-start.44 = (bf16[272,512]{1,0:T(8,128)(2,1)}, bf16[272,512]{1,0:T(8,128)(2,1)S(1)}, u32[]{:S(2)}, u32[]{:S(2)}) collective-permute-start(bf16[272,512]{1,0:T(8,128)(2,1)} %get-tuple-element.176), channel_id=1, source_target_pairs={{0,2},{1,3},{2,0},{3,1},{4,6},{5,7},{6,4},{7,5},{8,10},{9,11},{10,... | collective-permute-start | bytes 835592 | tf_op jit(solution)/shard_map/ppermute | solution.py:905
  382.2 25.7 %collective-permute-start.45 = (bf16[272,512]{1,0:T(8,128)(2,1)}, bf16[272,512]{1,0:T(8,128)(2,1)S(1)}, u32[]{:S(2)}, u32[]{:S(2)}) collective-permute-start(bf16[272,512]{1,0:T(8,128)(2,1)} %get-tuple-element.177), channel_id=1, source_target_pairs={{0,3},{1,0},{2,1},{3,2},{4,7},{5,4},{6,5},{7,6},{8,11},{9,8},{10,9... | collective-permute-start | bytes 835592 | tf_op jit(solution)/shard_map/ppermute | solution.py:905
  423.6 17.1 %collective-permute-start.52 = (bf16[2,528,512]{2,1,0:T(8,128)(2,1)}, bf16[2,528,512]{2,1,0:T(8,128)(2,1)}, u32[]{:S(2)}, u32[]{:S(2)}) collective-permute-start(bf16[2,528,512]{2,1,0:T(8,128)(2,1)} %pad_maximum_fusion.3.refs_0_), channel_id=1, source_target_pairs={{0,4},{4,0},{1,5},{5,1},{2,6},{6,2},{3,7},{7,3},{8,12},{12,8},{9,1... | collective-permute-start | bytes 3244040 | tf_op jit(solution)/shard_map/ppermute | solution.py:908
  (47 other events, 733.0 us)

commit v6 on v5

--- a/solution.py
+++ b/solution.py
@@ -968,9 +968,9 @@
     packed = jnp.concatenate(after(vectors, piece_one))
     first_parts = Gather(jnp.stack(got_one)[None])
     first_parts.step()
-    packed = after(packed, first_parts.first)
+    packed = after(packed, got_one)
     got_packed = [from_shard(packed, s) for s in range(1, group)]
-    first_parts.finish()
+    first_parts.finish(got_packed)
     parts_one = first_parts.parts
     piece_in = after(piece_in, parts_one[3])
     got_in = [from_shard(piece_in, s) for s in range(1, group)]

time: 463 us -> 456 us (0.985)
    ppermute x16, waiting for transfers between devices: 68.4 us -> 60.5 us  [swap(): return lax.ppermute(value, REP, pairs)]
  transfers between devices with their start and end apart: 54 -> 54, of which waited for: 27 -> 29; matrix products, arithmetic and copies ran while one was open for 5% -> 5% of each run, Pallas kernels for 42% -> 42%
where the time goes in v6:
time: 456 us; the launch traced here: 448 us
  Pallas kernels  214 us (47%)
  waiting for transfers between devices  149 us (33%)
  starting transfers between devices  50.9 us (11%)
  local copies, waits for them, and re-layouts  17.2 us (4%)
  other arithmetic  14.7 us (3%)
    ppermute x16, waiting for transfers between devices, swap(): return lax.ppermute(value, REP, pairs)  60.5 us
    pallas_call x9, Pallas kernels, grads(): call(partial(grads_kernel, (units, len(received), last, group, cuts, int(...  57.7 us
    ppermute x12, waiting for transfers between devices, from_shard(): lax.ppermute(value, 'shard', [(i, (i - step) % group) for i in range(grou...  51.2 us
    ppermute x9, waiting for transfers between devices, to_shard(): lax.ppermute(value, 'shard', [(i, (i + step) % group) for i in range(grou...  29 us
    pallas_call x2, Pallas kernels, attention_back(): call(partial(attend_back_kernel, (mine, per)), (each // 2,), [pairs(0), p...  26.2 us
    pallas_call x2, Pallas kernels, attention(): call(partial(attend_kernel, first), (count,), [spec((seq, block), lambda...  21.7 us
    pallas_call x1, Pallas kernels, inner_back(): call(partial(inner_back_kernel, (group, half)), (2 * chips,), [columns_at...  18 us
    pallas_call x1, Pallas kernels, inner(): call(partial(inner_kernel, (group, half)), (2 * chips,), [fixed((seq, wid...  15.5 us
  transfers between devices with their start and end apart: 54, of which 29 were waited for; matrix products, arithmetic and copies ran while one was open for 5% of the time, Pallas kernels for 42%

profile of v6, /device:TPU:9, one launch (start us, length us, event | category | flops | bytes accessed | tf_op | source)
XLA Modules:
  0.0 448.1 jit_solution(11205862168273486863)
XLA Ops:
  8.9 11.8 %collective-permute-done.1 = bf16[256,512]{1,0:T(8,128)(2,1)S(1)} collective-permute-done((bf16[256,512]{1,0:T(8,128)(2,1)S(1)}, bf16[256,512]{1,0:T(8,128)(2,1)S(1)}, u32[]{:S(2)}, u32[]{:S(2)}) %collective-permute-start.1) | collective-permute-done | bytes 262176 | tf_op jit(solution)/shard_map/ppermute | solution.py:902
  27.9 9.9 %collective-permute-done.3 = bf16[1,3,256,512]{3,2,1,0:T(8,128)(2,1)S(1)} collective-permute-done((bf16[1,3,256,512]{3,2,1,0:T(8,128)(2,1)S(1)}, bf16[1,3,256,512]{3,2,1,0:T(8,128)(2,1)S(1)}, u32[]{:S(2)}, u32[]{:S(2)}) %collective-permute-start.3) | collective-permute-done | bytes 786464 | tf_op jit(solution)/shard_map/ppermute | solution.py:917
  47.0 10.5 %collective-permute-done.4.b = bf16[2,3,256,512]{3,2,1,0:T(8,128)(2,1)S(1)} collective-permute-done((bf16[2,3,256,512]{3,2,1,0:T(8,128)(2,1)S(1)}, bf16[2,3,256,512]{3,2,1,0:T(8,128)(2,1)S(1)}, u32[]{:S(2)}, u32[]{:S(2)}) %collective-permute-start.4) | collective-permute-done | bytes 1572896 | tf_op jit(solution)/shard_map/ppermute | solution.py:917
  67.7 12.6 %shard_map.299 = (bf16[512,4096]{1,0:T(8,128)(2,1)}, bf16[768,1024]{1,0:T(8,128)(2,1)}) custom-call(s32[10]{0:T(128)} %pad_add_fusion.where, bf16[512,1024]{1,0:T(8,128)(2,1)} %bitcast.105, bf16[256,3072]{1,0:T(8,128)(2,1)} %own.13, bf16[2,3,256,512]{3,2,1,0:T(8,128)(2,1)} %copy-done, bf16[2,3,256,512]{3,2,1,0:T(8,128)(2,1)} %copy-done.2, ...), custom_call_target="tpu_custom_call" | custom-call | bytes 44280000 | tf_op jit(solution)/shard_map/pallas_call | solution.py:179
  80.3 5.9 %collective-permute-done.12 = bf16[256,512]{1,0:T(8,128)(2,1)} collective-permute-done((bf16[256,512]{1,0:T(8,128)(2,1)S(1)}, bf16[256,512]{1,0:T(8,128)(2,1)}, u32[]{:S(2)}, u32[]{:S(2)}) %collective-permute-start.12) | collective-permute-done | bytes 262176 | tf_op jit(solution)/shard_map/ppermute | solution.py:902
  94.2 10.8 %shard_map.300 = (bf16[512,1024]{1,0:T(8,128)(2,1)}, bf16[2,1024,512]{2,1,0:T(8,128)(2,1)}, f32[512,128]{1,0:T(8,128)}) custom-call(s32[10]{0:T(128)} %pad_add_fusion.where, bf16[512,4096]{1,0:T(8,128)(2,1)} %get-tuple-element.110.q.k.v, bf16[512,4096]{1,0:T(8,128)(2,1)} %get-tuple-element.110.q.k.v, bf16[512,4096]{1,0:T(8,128)(2,1)} %get-tuple-element.110.q.k.v, ...), custom_call_target="tpu_custom_call" | custom-call | bytes 40590000 | tf_op jit(solution)/shard_map/pallas_call | solution.py:229
  111.3 6.3 %collective-permute-done.17 = bf16[128,1024]{1,0:T(8,128)(2,1)S(1)} collective-permute-done((bf16[128,1024]{1,0:T(8,128)(2,1)S(1)}, bf16[128,1024]{1,0:T(8,128)(2,1)S(1)}, u32[]{:S(2)}, u32[]{:S(2)}) %collective-permute-start.17) | collective-permute-done | bytes 262176 | tf_op jit(solution)/shard_map/ppermute | solution.py:902
  117.6 7.4 %collective-permute-done.18 = bf16[128,1024]{1,0:T(8,128)(2,1)S(1)} collective-permute-done((bf16[128,1024]{1,0:T(8,128)(2,1)S(1)}, bf16[128,1024]{1,0:T(8,128)(2,1)S(1)}, u32[]{:S(2)}, u32[]{:S(2)}) %collective-permute-start.18) | collective-permute-done | bytes 262176 | tf_op jit(solution)/shard_map/ppermute | solution.py:902
  132.9 10.9 %shard_map.301 = (bf16[512,1024]{1,0:T(8,128)(2,1)}, bf16[2,1024,512]{2,1,0:T(8,128)(2,1)}, f32[512,128]{1,0:T(8,128)}) custom-call(s32[10]{0:T(128)} %pad_add_fusion.where, bf16[512,4096]{1,0:T(8,128)(2,1)} %get-tuple-element.110.q.k.v, bf16[512,4096]{1,0:T(8,128)(2,1)} %get-tuple-element.110.q.k.v, ...), custom_call_target="tpu_custom_call", output_to_operand_aliasing={{0}: (7, {}), {1}: (8, {})} | custom-call | bytes 40590000 | tf_op jit(solution)/shard_map/pallas_call | solution.py:229
  143.8 6.0 %shard_map.302 = (f32[512,1024]{1,0:T(8,128)}, bf16[512,1024]{1,0:T(8,128)(2,1)}, bf16[1024,512]{1,0:T(8,128)(2,1)}) custom-call(s32[10]{0:T(128)} %pad_add_fusion.where, bf16[512,1024]{1,0:T(8,128)(2,1)} %get-tuple-element.113.context, bf16[512,1024]{1,0:T(8,128)(2,1)} %bitcast.108, bf16[256,1024]{1,0:T(8,128)(2,1)} %own_out.1, ...), custom_call_target="tpu_custom_call" | custom-call | bytes 22140000 | tf_op jit(solution)/shard_map/pallas_call | solution.py:345
  157.0 15.5 %shard_map.303 = (bf16[512,4096]{1,0:T(8,128)(2,1)}, bf16[4096,256]{1,0:T(8,128)(2,1)}, bf16[4096,256]{1,0:T(8,128)(2,1)}, bf16[512,4096]{1,0:T(8,128)(2,1)}) custom-call(s32[10]{0:T(128)} %pad_add_fusion.where, bf16[512,1024]{1,0:T(8,128)(2,1)} %get-tuple-element.115.x, bf16[256,4096]{1,0:T(8,128)(2,1)} %own.12, ...), custom_call_target="tpu_custom_call" | custom-call | bytes 59040000 | tf_op jit(solution)/shard_map/pallas_call | solution.py:398
  177.9 15.3 %shard_map.304 = (bf16[512,1024]{1,0:T(8,128)(2,1)}, f32[512,1024]{1,0:T(8,128)}, bf16[512,1024]{1,0:T(8,128)(2,1)}, bf16[512,512]{1,0:T(8,128)(2,1)}, f32[8,1024]{1,0:T(8,128)}) custom-call(s32[10]{0:T(128)} %pad_add_fusion.where, bf16[512,4096]{1,0:T(8,128)(2,1)} %get-tuple-element.122.act, bf16[1024,1024]{1,0:T(8,128)(2,1)} %own.11, ...), custom_call_target="tpu_custom_call" | custom-call | bytes 221400000 | tf_op jit(solution)/shard_map/pallas_call | solution.py:506
  196.2 7.5 %shard_map.305 = bf16[2,1024,512]{2,1,0:T(8,128)(2,1)} custom-call(s32[10]{0:T(128)} %pad_add_fusion.where, bf16[1,512,1024]{2,1,0:T(8,128)(2,1)} %bitcast.101, bf16[1,512,512]{2,1,0:T(8,128)(2,1)} %bitcast.113, bf16[1,4096,256]{2,1,0:T(8,128)(2,1)} %bitcast.93, bf16[1,4096,256]{2,1,0:T(8,128)(2,1)} %bitcast.97, ...), custom_call_target="tpu_custom_call" | custom-call | bytes 22140000 | tf_op jit(solution)/shard_map/pallas_call | solution.py:856
  205.5 15.4 %shard_map.306 = (bf16[512,4096]{1,0:T(8,128)(2,1)}, bf16[512,2048]{1,0:T(8,128)(2,1)}, f32[1,4096]{1,0:T(1,128)}) custom-call(s32[10]{0:T(128)} %pad_add_fusion.where, bf16[512,1024]{1,0:T(8,128)(2,1)} %get-tuple-element.133.low, bf16[1024,1024]{1,0:T(8,128)(2,1)} %own.11, bf16[2,3,128,1024]{3,2,1,0:T(8,128)(2,1)} %pad_maximum_fusion.2.a, ...), custom_call_target="tpu_custom_call" | custom-call | bytes 51660000 | tf_op jit(solution)/shard_map/pallas_call | solution.py:583
  221.0 18.0 %shard_map.307 = (f32[512,1024]{1,0:T(8,128)}, bf16[512,1024]{1,0:T(8,128)(2,1)}, bf16[512,1024]{1,0:T(8,128)(2,1)}, f32[8,1024]{1,0:T(8,128)}) custom-call(s32[10]{0:T(128)} %pad_add_fusion.where, bf16[512,4096]{1,0:T(8,128)(2,1)} %get-tuple-element.137.grad_inner, bf16[256,4096]{1,0:T(8,128)(2,1)} %own.12, bf16[2,3,256,512]{3,2,1,0:T(8,128)(2,1)} %pad_maximum_fusion.1.a, ...), custom_call_target="tpu_custom_call" | custom-call | bytes 70110000 | tf_op jit(solution)/shard_map/pallas_call | solution.py:664
  239.1 5.8 %shard_map.308 = bf16[1,1024,512]{2,1,0:T(8,128)(2,1)} custom-call(s32[10]{0:T(128)} %pad_add_fusion.where, bf16[1,512,1024]{2,1,0:T(8,128)(2,1)} %bitcast.103, bf16[1,512,512]{2,1,0:T(8,128)(2,1)} %bitcast.115, bf16[1,4096,256]{2,1,0:T(8,128)(2,1)} %bitcast.95, bf16[1,4096,256]{2,1,0:T(8,128)(2,1)} %bitcast.99, ...), custom_call_target="tpu_custom_call" | custom-call | bytes 22140000 | tf_op jit(solution)/shard_map/pallas_call | solution.py:856
  245.3 7.1 %shard_map.309 = bf16[2,1024,512]{2,1,0:T(8,128)(2,1)} custom-call(s32[10]{0:T(128)} %pad_add_fusion.where, bf16[1,512,4096]{2,1,0:T(8,128)(2,1)} %bitcast.89, bf16[1,512,2048]{2,1,0:T(8,128)(2,1)} %bitcast.28.refs_1_.refs_5_, bf16[1,1024,512]{2,1,0:T(8,128)(2,1)} %bitcast.109, bf16[1,1024,512]{2,1,0:T(8,128)(2,1)} %bitcast.26.refs_3_.refs_7_, ...), custom_call_target="tpu_custom_call" | custom-call | bytes 22140000 | tf_op jit(solution)/shard_map/pallas_call | solution.py:856
  253.4 13.0 %shard_map.310 = (bf16[4,512,512]{2,1,0:T(8,128)(2,1)}, f32[3,1,512]{2,1,0:T(1,128)}) custom-call(s32[10]{0:T(128)} %pad_add_fusion.where, bf16[512,4096]{1,0:T(8,128)(2,1)} %get-tuple-element.110.q.k.v, bf16[512,4096]{1,0:T(8,128)(2,1)} %get-tuple-element.110.q.k.v, bf16[512,4096]{1,0:T(8,128)(2,1)} %get-tuple-element.110.q.k.v, ...), custom_call_target="tpu_custom_call" | custom-call | bytes 47970000 | tf_op jit(solution)/shard_map/pallas_call | solution.py:302
  266.4 6.2 %shard_map.311 = (bf16[256,512]{1,0:T(8,128)(2,1)}, bf16[256,512]{1,0:T(8,128)(2,1)}, bf16[256,512]{1,0:T(8,128)(2,1)}, bf16[256,512]{1,0:T(8,128)(2,1)}) custom-call(s32[10]{0:T(128)} %pad_add_fusion.where, bf16[1,512,1024]{2,1,0:T(8,128)(2,1)} %bitcast.104, bf16[1,512,512]{2,1,0:T(8,128)(2,1)} %bitcast.116, bf16[1,4096,256]{2,1,0:T(8,128)(2,1)} %bitcast.96, ...), custom_call_target="tpu_custom_call" | custom-call | bytes 22140000 | tf_op jit(solution)/shard_map/pallas_call | solution.py:856
  280.4 13.2 %shard_map.312 = (bf16[4,512,512]{2,1,0:T(8,128)(2,1)}, f32[3,1,512]{2,1,0:T(1,128)}) custom-call(s32[10]{0:T(128)} %pad_add_fusion.where, bf16[512,4096]{1,0:T(8,128)(2,1)} %get-tuple-element.110.q.k.v, bf16[512,4096]{1,0:T(8,128)(2,1)} %get-tuple-element.110.q.k.v, bf16[512,4096]{1,0:T(8,128)(2,1)} %get-tuple-element.110.q.k.v, ...), custom_call_target="tpu_custom_call" | custom-call | bytes 47970000 | tf_op jit(solution)/shard_map/pallas_call | solution.py:302
  302.9 7.2 %shard_map.314 = bf16[2,1024,512]{2,1,0:T(8,128)(2,1)} custom-call(s32[10]{0:T(128)} %pad_add_fusion.where, bf16[4,512,512]{2,1,0:T(8,128)(2,1)} %get-tuple-element.161.refs_0_.refs_4_.mine, bf16[4,512,512]{2,1,0:T(8,128)(2,1)} %collective-permute-done.32.refs_1_.refs_5_, bf16[2,1024,512]{2,1,0:T(8,128)(2,1)} %get-tuple-element.141.refs_2_.refs_6_, ...), custom_call_target="tpu_custom_call" | custom-call | bytes 22140000 | tf_op jit(solution)/shard_map/pallas_call | solution.py:856
  315.5 13.8 %shard_map.315 = f32[512,1024]{1,0:T(8,128)} custom-call(s32[10]{0:T(128)} %pad_add_fusion.where, bf16[4,512,512]{2,1,0:T(8,128)(2,1)} %get-tuple-element.161.refs_0_.refs_4_.mine, bf16[4,512,512]{2,1,0:T(8,128)(2,1)} %get-tuple-element.154.others, bf16[256,3072]{1,0:T(8,128)(2,1)} %own.13, bf16[2,3,256,512]{3,2,1,0:T(8,128)(2,1)} %copy-done, ...), custom_call_target="tpu_custom_call" | custom-call | bytes 44280000 | tf_op jit(solution)/shard_map/pallas_call | solution.py:721
  329.3 6.7 %collective-permute-done.37.refs_5_ = bf16[1,1024,512]{2,1,0:T(8,128)(2,1)} collective-permute-done((bf16[1,1024,512]{2,1,0:T(8,128)(2,1)}, bf16[1,1024,512]{2,1,0:T(8,128)(2,1)}, u32[]{:S(2)}, u32[]{:S(2)}) %collective-permute-start.37) | collective-permute-done | bytes 1048608 | tf_op jit(solution)/shard_map/ppermute | solution.py:917
  336.0 6.2 %shard_map.316 = (bf16[256,512]{1,0:T(8,128)(2,1)}, bf16[256,512]{1,0:T(8,128)(2,1)}, bf16[256,512]{1,0:T(8,128)(2,1)}, bf16[256,512]{1,0:T(8,128)(2,1)}) custom-call(s32[10]{0:T(128)} %pad_add_fusion.where, bf16[1,512,4096]{2,1,0:T(8,128)(2,1)} %bitcast.92, bf16[1,512,2048]{2,1,0:T(8,128)(2,1)} %bitcast.28.refs_1_.refs_5_, bf16[1,1024,512]{2,1,0:T(8,128)(2,1)} %bitcast.112, ...), custom_call_target="tpu_custom_call" | custom-call | bytes 22140000 | tf_op jit(solution)/shard_map/pallas_call | solution.py:856
  346.8 5.8 %shard_map.317 = bf16[1,1024,512]{2,1,0:T(8,128)(2,1)} custom-call(s32[10]{0:T(128)} %pad_add_fusion.where, bf16[4,512,512]{2,1,0:T(8,128)(2,1)} %get-tuple-element.161.refs_0_.refs_4_.mine, bf16[4,512,512]{2,1,0:T(8,128)(2,1)} %collective-permute-done.32.refs_1_.refs_5_, bf16[2,1024,512]{2,1,0:T(8,128)(2,1)} %get-tuple-element.141.refs_2_.refs_6_, ...), custom_call_target="tpu_custom_call" | custom-call | bytes 22140000 | tf_op jit(solution)/shard_map/pallas_call | solution.py:856
  356.9 10.0 %collective-permute-done.42.refs_5_ = bf16[1,1024,512]{2,1,0:T(8,128)(2,1)} collective-permute-done((bf16[1,1024,512]{2,1,0:T(8,128)(2,1)}, bf16[1,1024,512]{2,1,0:T(8,128)(2,1)}, u32[]{:S(2)}, u32[]{:S(2)}) %collective-permute-start.42) | collective-permute-done | bytes 1048608 | tf_op jit(solution)/shard_map/ppermute | solution.py:917
  366.9 6.2 %shard_map.318 = (bf16[272,512]{1,0:T(8,128)(2,1)}, bf16[272,512]{1,0:T(8,128)(2,1)}, bf16[272,512]{1,0:T(8,128)(2,1)}, bf16[272,512]{1,0:T(8,128)(2,1)}) custom-call(s32[10]{0:T(128)} %pad_add_fusion.where, bf16[4,512,512]{2,1,0:T(8,128)(2,1)} %get-tuple-element.161.refs_0_.refs_4_.mine, bf16[4,512,512]{2,1,0:T(8,128)(2,1)} %collective-permute-done.32.refs_1_.refs_5_, ...), custom_call_target="tpu_custom_call" | custom-call | bytes 22140000 | tf_op jit(solution)/shard_map/pallas_call | solution.py:856
  376.1 13.1 %collective-permute-done.40 = bf16[256,512]{1,0:T(8,128)(2,1)} collective-permute-done((bf16[256,512]{1,0:T(8,128)(2,1)}, bf16[256,512]{1,0:T(8,128)(2,1)}, u32[]{:S(2)}, u32[]{:S(2)}) %collective-permute-start.40) | collective-permute-done | bytes 262176 | tf_op jit(solution)/shard_map/ppermute | solution.py:905
  391.5 8.5 %collective-permute-done.44 = bf16[272,512]{1,0:T(8,128)(2,1)S(1)} collective-permute-done((bf16[272,512]{1,0:T(8,128)(2,1)}, bf16[272,512]{1,0:T(8,128)(2,1)S(1)}, u32[]{:S(2)}, u32[]{:S(2)}) %collective-permute-start.44) | collective-permute-done | bytes 278560 | tf_op jit(solution)/shard_map/ppermute | solution.py:905
  403.9 6.6 %collective-permute-done.46 = bf16[1,528,512]{2,1,0:T(8,128)(2,1)S(1)} collective-permute-done((bf16[1,528,512]{2,1,0:T(8,128)(2,1)S(1)}, bf16[1,528,512]{2,1,0:T(8,128)(2,1)S(1)}, u32[]{:S(2)}, u32[]{:S(2)}) %collective-permute-start.46) | collective-permute-done | bytes 540704 | tf_op jit(solution)/shard_map/ppermute | solution.py:917
  419.9 11.5 %collective-permute-done.51.refs_1_ = bf16[2,528,512]{2,1,0:T(8,128)(2,1)S(1)} collective-permute-done((bf16[2,528,512]{2,1,0:T(8,128)(2,1)}, bf16[2,528,512]{2,1,0:T(8,128)(2,1)S(1)}, u32[]{:S(2)}, u32[]{:S(2)}) %collective-permute-start.51) | collective-permute-done | bytes 1081376 | tf_op jit(solution)/shard_map/ppermute | solution.py:917
  437.1 7.3 %shard_map.320 = (f32[256,4096]{1,0:T(8,128)}, f32[256,3072]{1,0:T(8,128)}, f32[256,1024]{1,0:T(8,128)}, f32[16,512]{1,0:T(8,128)}) custom-call(s32[10]{0:T(128)} %pad_add_fusion.where, bf16[2,528,512]{2,1,0:T(8,128)(2,1)} %pad_maximum_fusion.3.refs_0_, bf16[2,528,512]{2,1,0:T(8,128)(2,1)} %copy-done.4, ...), custom_call_target="tpu_custom_call" | custom-call | bytes 14760000 | tf_op jit(solution)/shard_map/pallas_call | solution.py:787
  (225 shorter events, 133.7 us)
Async XLA Ops:
  1.8 19.0 %collective-permute-start.1 = (bf16[256,512]{1,0:T(8,128)(2,1)S(1)}, bf16[256,512]{1,0:T(8,128)(2,1)S(1)}, u32[]{:S(2)}, u32[]{:S(2)}) collective-permute-start(bf16[256,512]{1,0:T(8,128)(2,1)S(1)} %fusion.1), channel_id=1, source_target_pairs={{0,2},{1,3},{2,0},{3,1},{4,6},{5,7},{6,4},{7,5},{8,10},{9,11},{10,... | collective-permute-start | bytes 786440 | tf_op jit(solution)/shard_map/ppermute | solution.py:902
  4.3 22.1 %collective-permute-start.2 = (bf16[256,512]{1,0:T(8,128)(2,1)S(1)}, bf16[256,512]{1,0:T(8,128)(2,1)S(1)}, u32[]{:S(2)}, u32[]{:S(2)}) collective-permute-start(bf16[256,512]{1,0:T(8,128)(2,1)S(1)} %fusion.1), channel_id=1, source_target_pairs={{0,1},{1,2},{2,3},{3,0},{4,5},{5,6},{6,7},{7,4},{8,9},{9,10},{10,1... | collective-permute-start | bytes 786440 | tf_op jit(solution)/shard_map/ppermute | solution.py:902
  37.9 19.6 %collective-permute-start.4 = (bf16[2,3,256,512]{3,2,1,0:T(8,128)(2,1)S(1)}, bf16[2,3,256,512]{3,2,1,0:T(8,128)(2,1)S(1)}, u32[]{:S(2)}, u32[]{:S(2)}) collective-permute-start(bf16[2,3,256,512]{3,2,1,0:T(8,128)(2,1)S(1)} %pad_maximum_fusion.a), channel_id=1, source_target_pairs={{0,16},{4,12},{8,24},{12,4},{16,0},{20,28},{24,8},{28,20},{1,17},{... | collective-permute-start | bytes 4718600 | tf_op jit(solution)/shard_map/ppermute | solution.py:917
  63.7 22.5 %collective-permute-start.12 = (bf16[256,512]{1,0:T(8,128)(2,1)S(1)}, bf16[256,512]{1,0:T(8,128)(2,1)}, u32[]{:S(2)}, u32[]{:S(2)}) collective-permute-start(bf16[256,512]{1,0:T(8,128)(2,1)S(1)} %constant_dynamic-slice_fusion.1), channel_id=1, source_target_pairs={{0,1},{1,2},{2,3},{3,0},{4,5},{5,6},{6,7},{7,4},{8,9},{9,10},{10,1... | collective-permute-start | bytes 786440 | tf_op jit(solution)/shard_map/ppermute | solution.py:902
  65.9 23.6 %collective-permute-start.10 = (bf16[256,512]{1,0:T(8,128)(2,1)S(1)}, bf16[256,512]{1,0:T(8,128)(2,1)}, u32[]{:S(2)}, u32[]{:S(2)}) collective-permute-start(bf16[256,512]{1,0:T(8,128)(2,1)S(1)} %constant_dynamic-slice_fusion.1), channel_id=1, source_target_pairs={{0,3},{1,0},{2,1},{3,2},{4,7},{5,4},{6,5},{7,6},{8,11},{9,8},{10,9... | collective-permute-start | bytes 786440 | tf_op jit(solution)/shard_map/ppermute | solution.py:902
  107.5 45.8 %collective-permute-start.14 = (bf16[2,3,256,512]{3,2,1,0:T(8,128)(2,1)}, bf16[2,3,256,512]{3,2,1,0:T(8,128)(2,1)}, u32[]{:S(2)}, u32[]{:S(2)}) collective-permute-start(bf16[2,3,256,512]{3,2,1,0:T(8,128)(2,1)} %pad_maximum_fusion.1.a), channel_id=1, source_target_pairs={{0,16},{4,12},{8,24},{12,4},{16,0},{20,28},{24,8},{28,20},{1,17},{... | collective-permute-start | bytes 4718600 | tf_op jit(solution)/shard_map/ppermute | solution.py:917
  110.1 20.6 %collective-permute-start.19 = (bf16[128,1024]{1,0:T(8,128)(2,1)S(1)}, bf16[128,1024]{1,0:T(8,128)(2,1)S(1)}, u32[]{:S(2)}, u32[]{:S(2)}) collective-permute-start(bf16[128,1024]{1,0:T(8,128)(2,1)S(1)} %constant_dynamic-slice_fusion), channel_id=1, source_target_pairs={{0,1},{1,2},{2,3},{3,0},{4,5},{5,6},{6,7},{7,4},{8,9},{9,10},{10,1... | collective-permute-start | bytes 786440 | tf_op jit(solution)/shard_map/ppermute | solution.py:902
  130.7 20.1 %collective-permute-start.20 = (bf16[1,3,128,1024]{3,2,1,0:T(8,128)(2,1)S(1)}, bf16[1,3,128,1024]{3,2,1,0:T(8,128)(2,1)}, u32[]{:S(2)}, u32[]{:S(2)}) collective-permute-start(bf16[1,3,128,1024]{3,2,1,0:T(8,128)(2,1)S(1)} %maximum_bitcast_fusion.2), channel_id=1, source_target_pairs={{0,8},{4,20},{8,0},{12,28},{16,24},{20,4},{24,16},{28,12},{1,9},{5... | collective-permute-start | bytes 2359304 | tf_op jit(solution)/shard_map/ppermute | solution.py:917
  153.3 19.9 %collective-permute-start.21 = (bf16[2,3,128,1024]{3,2,1,0:T(8,128)(2,1)}, bf16[2,3,128,1024]{3,2,1,0:T(8,128)(2,1)}, u32[]{:S(2)}, u32[]{:S(2)}) collective-permute-start(bf16[2,3,128,1024]{3,2,1,0:T(8,128)(2,1)} %pad_maximum_fusion.2.a), channel_id=1, source_target_pairs={{0,16},{4,12},{8,24},{12,4},{16,0},{20,28},{24,8},{28,20},{1,17},{... | collective-permute-start | bytes 4718600 | tf_op jit(solution)/shard_map/ppermute | solution.py:917
  155.2 21.6 %collective-permute-start.22 = (bf16[2,3,128,1024]{3,2,1,0:T(8,128)(2,1)}, bf16[2,3,128,1024]{3,2,1,0:T(8,128)(2,1)}, u32[]{:S(2)}, u32[]{:S(2)}) collective-permute-start(bf16[2,3,128,1024]{3,2,1,0:T(8,128)(2,1)} %pad_maximum_fusion.2.a), channel_id=1, source_target_pairs={{0,4},{4,0},{1,5},{5,1},{2,6},{6,2},{3,7},{7,3},{8,12},{12,8},{9,1... | collective-permute-start | bytes 4718600 | tf_op jit(solution)/shard_map/ppermute | solution.py:908
  174.5 20.9 %collective-permute-start.25 = (bf16[4096,256]{1,0:T(8,128)(2,1)}, bf16[4096,256]{1,0:T(8,128)(2,1)}, u32[]{:S(2)}, u32[]{:S(2)}) collective-permute-start(bf16[4096,256]{1,0:T(8,128)(2,1)} %get-tuple-element.131), channel_id=1, source_target_pairs={{0,4},{4,0},{1,5},{5,1},{2,6},{6,2},{3,7},{7,3},{8,12},{12,8},{9,1... | collective-permute-start | bytes 6291464 | tf_op jit(solution)/shard_map/ppermute | solution.py:908
  174.5 20.9 %collective-permute-start.26 = (bf16[4096,256]{1,0:T(8,128)(2,1)}, bf16[4096,256]{1,0:T(8,128)(2,1)}, u32[]{:S(2)}, u32[]{:S(2)}) collective-permute-start(bf16[4096,256]{1,0:T(8,128)(2,1)} %get-tuple-element.132), channel_id=1, source_target_pairs={{0,4},{4,0},{1,5},{5,1},{2,6},{6,2},{3,7},{7,3},{8,12},{12,8},{9,1... | collective-permute-start | bytes 6291464 | tf_op jit(solution)/shard_map/ppermute | solution.py:908
  193.7 45.4 %collective-permute-start.29 = (bf16[2,1024,512]{2,1,0:T(8,128)(2,1)}, bf16[2,1024,512]{2,1,0:T(8,128)(2,1)}, u32[]{:S(2)}, u32[]{:S(2)}) collective-permute-start(bf16[2,1024,512]{2,1,0:T(8,128)(2,1)} %get-tuple-element.141.refs_2_.refs_6_), channel_id=1, source_target_pairs={{0,4},{4,0},{1,5},{5,1},{2,6},{6,2},{3,7},{7,3},{8,12},{12,8},{9,1... | collective-permute-start | bytes 6291464 | tf_op jit(solution)/shard_map/ppermute | solution.py:908
  203.7 35.4 %collective-permute-start.28 = (bf16[2,1024,512]{2,1,0:T(8,128)(2,1)}, bf16[2,1024,512]{2,1,0:T(8,128)(2,1)}, u32[]{:S(2)}, u32[]{:S(2)}) collective-permute-start(bf16[2,1024,512]{2,1,0:T(8,128)(2,1)} %shard_map.305), channel_id=1, source_target_pairs={{0,8},{4,20},{8,0},{12,28},{16,24},{20,4},{24,16},{28,12},{1,9},{5... | collective-permute-start | bytes 6291464 | tf_op jit(solution)/shard_map/ppermute | solution.py:917
  203.9 17.1 %collective-permute-start.27 = (bf16[1024,512]{1,0:T(8,128)(2,1)}, bf16[1024,512]{1,0:T(8,128)(2,1)}, u32[]{:S(2)}, u32[]{:S(2)}) collective-permute-start(bf16[1024,512]{1,0:T(8,128)(2,1)} %get-tuple-element.136), channel_id=1, source_target_pairs={{0,4},{4,0},{1,5},{5,1},{2,6},{6,2},{3,7},{7,3},{8,12},{12,8},{9,1... | collective-permute-start | bytes 3145736 | tf_op jit(solution)/shard_map/ppermute | solution.py:908
  220.9 24.3 %collective-permute-start.31 = (bf16[512,2048]{1,0:T(8,128)(2,1)}, bf16[512,2048]{1,0:T(8,128)(2,1)}, u32[]{:S(2)}, u32[]{:S(2)}) collective-permute-start(bf16[512,2048]{1,0:T(8,128)(2,1)} %get-tuple-element.143), channel_id=1, source_target_pairs={{0,4},{4,0},{1,5},{5,1},{2,6},{6,2},{3,7},{7,3},{8,12},{12,8},{9,1... | collective-permute-start | bytes 6291464 | tf_op jit(solution)/shard_map/ppermute | solution.py:908
  244.9 21.5 %collective-permute-start.30 = (bf16[1,1024,512]{2,1,0:T(8,128)(2,1)}, bf16[1,1024,512]{2,1,0:T(8,128)(2,1)}, u32[]{:S(2)}, u32[]{:S(2)}) collective-permute-start(bf16[1,1024,512]{2,1,0:T(8,128)(2,1)} %shard_map.308), channel_id=1, source_target_pairs={{0,16},{4,12},{8,24},{12,4},{16,0},{20,28},{24,8},{28,20},{1,17},{... | collective-permute-start | bytes 3145736 | tf_op jit(solution)/shard_map/ppermute | solution.py:917
  252.4 41.2 %collective-permute-start.33 = (bf16[2,1024,512]{2,1,0:T(8,128)(2,1)}, bf16[2,1024,512]{2,1,0:T(8,128)(2,1)}, u32[]{:S(2)}, u32[]{:S(2)}) collective-permute-start(bf16[2,1024,512]{2,1,0:T(8,128)(2,1)} %shard_map.309), channel_id=1, source_target_pairs={{0,8},{4,20},{8,0},{12,28},{16,24},{20,4},{24,16},{28,12},{1,9},{5... | collective-permute-start | bytes 6291464 | tf_op jit(solution)/shard_map/ppermute | solution.py:917
  272.6 30.2 %collective-permute-start.32 = (bf16[4,512,512]{2,1,0:T(8,128)(2,1)}, bf16[4,512,512]{2,1,0:T(8,128)(2,1)}, u32[]{:S(2)}, u32[]{:S(2)}) collective-permute-start(bf16[4,512,512]{2,1,0:T(8,128)(2,1)} %get-tuple-element.154.others), channel_id=1, source_target_pairs={{0,4},{4,0},{1,5},{5,1},{2,6},{6,2},{3,7},{7,3},{8,12},{12,8},{9,1... | collective-permute-start | bytes 6291464 | tf_op jit(solution)/shard_map/ppermute | solution.py:908
  273.2 26.1 %collective-permute-start.34 = (bf16[256,512]{1,0:T(8,128)(2,1)}, bf16[256,512]{1,0:T(8,128)(2,1)S(1)}, u32[]{:S(2)}, u32[]{:S(2)}) collective-permute-start(bf16[256,512]{1,0:T(8,128)(2,1)} %get-tuple-element.156), channel_id=1, source_target_pairs={{0,1},{1,2},{2,3},{3,0},{4,5},{5,6},{6,7},{7,4},{8,9},{9,10},{10,1... | collective-permute-start | bytes 786440 | tf_op jit(solution)/shard_map/ppermute | solution.py:905
  276.3 23.0 %collective-permute-start.35 = (bf16[256,512]{1,0:T(8,128)(2,1)}, bf16[256,512]{1,0:T(8,128)(2,1)S(1)}, u32[]{:S(2)}, u32[]{:S(2)}) collective-permute-start(bf16[256,512]{1,0:T(8,128)(2,1)} %get-tuple-element.157), channel_id=1, source_target_pairs={{0,2},{1,3},{2,0},{3,1},{4,6},{5,7},{6,4},{7,5},{8,10},{9,11},{10,... | collective-permute-start | bytes 786440 | tf_op jit(solution)/shard_map/ppermute | solution.py:905
  280.4 22.5 %collective-permute-start.36 = (bf16[256,512]{1,0:T(8,128)(2,1)}, bf16[256,512]{1,0:T(8,128)(2,1)S(1)}, u32[]{:S(2)}, u32[]{:S(2)}) collective-permute-start(bf16[256,512]{1,0:T(8,128)(2,1)} %get-tuple-element.158), channel_id=1, source_target_pairs={{0,3},{1,0},{2,1},{3,2},{4,7},{5,4},{6,5},{7,6},{8,11},{9,8},{10,9... | collective-permute-start | bytes 786440 | tf_op jit(solution)/shard_map/ppermute | solution.py:905
  310.0 36.8 %collective-permute-start.41 = (bf16[2,1024,512]{2,1,0:T(8,128)(2,1)}, bf16[2,1024,512]{2,1,0:T(8,128)(2,1)}, u32[]{:S(2)}, u32[]{:S(2)}) collective-permute-start(bf16[2,1024,512]{2,1,0:T(8,128)(2,1)} %shard_map.314), channel_id=1, source_target_pairs={{0,8},{4,20},{8,0},{12,28},{16,24},{20,4},{24,16},{28,12},{1,9},{5... | collective-permute-start | bytes 6291464 | tf_op jit(solution)/shard_map/ppermute | solution.py:917
  311.0 25.0 %collective-permute-start.37 = (bf16[1,1024,512]{2,1,0:T(8,128)(2,1)}, bf16[1,1024,512]{2,1,0:T(8,128)(2,1)}, u32[]{:S(2)}, u32[]{:S(2)}) collective-permute-start(bf16[1,1024,512]{2,1,0:T(8,128)(2,1)} %shard_map.313), channel_id=1, source_target_pairs={{0,16},{4,12},{8,24},{12,4},{16,0},{20,28},{24,8},{28,20},{1,17},{... | collective-permute-start | bytes 3145736 | tf_op jit(solution)/shard_map/ppermute | solution.py:917
  354.3 19.8 %collective-permute-start.38 = (bf16[256,512]{1,0:T(8,128)(2,1)}, bf16[256,512]{1,0:T(8,128)(2,1)}, u32[]{:S(2)}, u32[]{:S(2)}) collective-permute-start(bf16[256,512]{1,0:T(8,128)(2,1)} %get-tuple-element.165), channel_id=1, source_target_pairs={{0,1},{1,2},{2,3},{3,0},{4,5},{5,6},{6,7},{7,4},{8,9},{9,10},{10,1... | collective-permute-start | bytes 786440 | tf_op jit(solution)/shard_map/ppermute | solution.py:905
  354.3 21.8 %collective-permute-start.39 = (bf16[256,512]{1,0:T(8,128)(2,1)}, bf16[256,512]{1,0:T(8,128)(2,1)}, u32[]{:S(2)}, u32[]{:S(2)}) collective-permute-start(bf16[256,512]{1,0:T(8,128)(2,1)} %get-tuple-element.166), channel_id=1, source_target_pairs={{0,2},{1,3},{2,0},{3,1},{4,6},{5,7},{6,4},{7,5},{8,10},{9,11},{10,... | collective-permute-start | bytes 786440 | tf_op jit(solution)/shard_map/ppermute | solution.py:905
  354.3 34.9 %collective-permute-start.40 = (bf16[256,512]{1,0:T(8,128)(2,1)}, bf16[256,512]{1,0:T(8,128)(2,1)}, u32[]{:S(2)}, u32[]{:S(2)}) collective-permute-start(bf16[256,512]{1,0:T(8,128)(2,1)} %get-tuple-element.167), channel_id=1, source_target_pairs={{0,3},{1,0},{2,1},{3,2},{4,7},{5,4},{6,5},{7,6},{8,11},{9,8},{10,9... | collective-permute-start | bytes 786440 | tf_op jit(solution)/shard_map/ppermute | solution.py:905
  373.1 17.3 %collective-permute-start.47 = (bf16[1,256,512]{2,1,0:T(8,128)(2,1)S(1)}, bf16[1,256,512]{2,1,0:T(8,128)(2,1)S(1)}, u32[]{:S(2)}, u32[]{:S(2)}) collective-permute-start(bf16[1,256,512]{2,1,0:T(8,128)(2,1)S(1)} %fusion.3), channel_id=1, source_target_pairs={{0,8},{4,20},{8,0},{12,28},{16,24},{20,4},{24,16},{28,12},{1,9},{5... | collective-permute-start | bytes 786440 | tf_op jit(solution)/shard_map/ppermute | solution.py:917
  374.1 17.4 %collective-permute-start.43 = (bf16[272,512]{1,0:T(8,128)(2,1)}, bf16[272,512]{1,0:T(8,128)(2,1)S(1)}, u32[]{:S(2)}, u32[]{:S(2)}) collective-permute-start(bf16[272,512]{1,0:T(8,128)(2,1)} %get-tuple-element.177), channel_id=1, source_target_pairs={{0,1},{1,2},{2,3},{3,0},{4,5},{5,6},{6,7},{7,4},{8,9},{9,10},{10,1... | collective-permute-start | bytes 835592 | tf_op jit(solution)/shard_map/ppermute | solution.py:905
  374.1 25.9 %collective-permute-start.44 = (bf16[272,512]{1,0:T(8,128)(2,1)}, bf16[272,512]{1,0:T(8,128)(2,1)S(1)}, u32[]{:S(2)}, u32[]{:S(2)}) collective-permute-start(bf16[272,512]{1,0:T(8,128)(2,1)} %get-tuple-element.178), channel_id=1, source_target_pairs={{0,2},{1,3},{2,0},{3,1},{4,6},{5,7},{6,4},{7,5},{8,10},{9,11},{10,... | collective-permute-start | bytes 835592 | tf_op jit(solution)/shard_map/ppermute | solution.py:905
  376.1 25.7 %collective-permute-start.45 = (bf16[272,512]{1,0:T(8,128)(2,1)}, bf16[272,512]{1,0:T(8,128)(2,1)S(1)}, u32[]{:S(2)}, u32[]{:S(2)}) collective-permute-start(bf16[272,512]{1,0:T(8,128)(2,1)} %get-tuple-element.179), channel_id=1, source_target_pairs={{0,3},{1,0},{2,1},{3,2},{4,7},{5,4},{6,5},{7,6},{8,11},{9,8},{10,9... | collective-permute-start | bytes 835592 | tf_op jit(solution)/shard_map/ppermute | solution.py:905
  417.5 17.1 %collective-permute-start.52 = (bf16[2,528,512]{2,1,0:T(8,128)(2,1)}, bf16[2,528,512]{2,1,0:T(8,128)(2,1)}, u32[]{:S(2)}, u32[]{:S(2)}) collective-permute-start(bf16[2,528,512]{2,1,0:T(8,128)(2,1)} %pad_maximum_fusion.3.refs_0_), channel_id=1, source_target_pairs={{0,4},{4,0},{1,5},{5,1},{2,6},{6,2},{3,7},{7,3},{8,12},{12,8},{9,1... | collective-permute-start | bytes 3244040 | tf_op jit(solution)/shard_map/ppermute | solution.py:908
  (47 other events, 541.6 us)

commit v7 on v6

--- a/solution.py
+++ b/solution.py
@@ -998,7 +998,6 @@
     count = model_width // (4 * HEAD_DIM)
     context, turned, logs_a = attention(where, projected, flat_in, column, row, 0, count)
     parts_in.step(logs_a)
-    parts_down = Gather(after(jnp.stack(got_down)[None], logs_a))
     context, turned, logs_b = attention(
         where,
         projected,
@@ -1010,6 +1009,7 @@
         (context, turned),
     )
     first_left = ([turned], [sibling(turned)])
+    parts_down = Gather(after(jnp.stack(got_down)[None], logs_b))
     parts_down.step(logs_b)
     hidden, normed, normed_turned = out_norm(
         where,
@@ -1026,6 +1026,7 @@
     parts_in = parts_in.parts
     in_left = ([normed_turned[None]], [sibling(normed_turned)[None]])
     where_down = where
+    normed = after(normed, parts_down.first)
     act, *act_turned, slope = inner(where, normed, w_in, parts_in, bias_in, group)
     parts_down.finish(act)
     parts_down = parts_down.parts

time: 456 us -> 448 us (0.982)
  waiting for transfers between devices: 149 us -> 138 us
    ppermute x12, waiting for transfers between devices: 51.2 us -> 40.3 us  [from_shard(): lax.ppermute(value, 'shard', [(i, (i - step) % group) for i in range(grou...]
    unnamed x73 -> x77, local copies, waits for them, and re-layouts: 9.77 us -> 9.81 us
  transfers between devices with their start and end apart: 54 -> 54, of which waited for: 29 -> 29; matrix products, arithmetic and copies ran while one was open for 5% -> 5% of each run, Pallas kernels for 42% -> 43%
where the time goes in v7:
time: 448 us; the launch traced here: 440 us
  Pallas kernels  214 us (48%)
  waiting for transfers between devices  138 us (31%)
  starting transfers between devices  53.1 us (12%)
  local copies, waits for them, and re-layouts  17.2 us (4%)
  other arithmetic  15.8 us (4%)
    ppermute x16, waiting for transfers between devices, swap(): return lax.ppermute(value, REP, pairs)  62.2 us
    pallas_call x9, Pallas kernels, grads(): call(partial(grads_kernel, (units, len(received), last, group, cuts, int(...  57.8 us
    ppermute x12, waiting for transfers between devices, from_shard(): lax.ppermute(value, 'shard', [(i, (i - step) % group) for i in range(grou...  40.3 us
    ppermute x9, waiting for transfers between devices, to_shard(): lax.ppermute(value, 'shard', [(i, (i + step) % group) for i in range(grou...  26.6 us
    pallas_call x2, Pallas kernels, attention_back(): call(partial(attend_back_kernel, (mine, per)), (each // 2,), [pairs(0), p...  26.2 us
    pallas_call x2, Pallas kernels, attention(): call(partial(attend_kernel, first), (count,), [spec((seq, block), lambda...  21.7 us
    pallas_call x1, Pallas kernels, inner_back(): call(partial(inner_back_kernel, (group, half)), (2 * chips,), [columns_at...  18.1 us
    ppermute x12, starting transfers between devices, from_shard(): lax.ppermute(value, 'shard', [(i, (i - step) % group) for i in range(grou...  16.1 us
  transfers between devices with their start and end apart: 54, of which 29 were waited for; matrix products, arithmetic and copies ran while one was open for 5% of the time, Pallas kernels for 43%

profile of v7, /device:TPU:9, one launch (start us, length us, event | category | flops | bytes accessed | tf_op | source)
XLA Modules:
  0.0 440.3 jit_solution(8619986031286832044)
XLA Ops:
  8.9 11.8 %collective-permute-done.1 = bf16[256,512]{1,0:T(8,128)(2,1)S(1)} collective-permute-done((bf16[256,512]{1,0:T(8,128)(2,1)S(1)}, bf16[256,512]{1,0:T(8,128)(2,1)S(1)}, u32[]{:S(2)}, u32[]{:S(2)}) %collective-permute-start.1) | collective-permute-done | bytes 262176 | tf_op jit(solution)/shard_map/ppermute | solution.py:902
  20.8 5.6 %collective-permute-done.2 = bf16[256,512]{1,0:T(8,128)(2,1)S(1)} collective-permute-done((bf16[256,512]{1,0:T(8,128)(2,1)S(1)}, bf16[256,512]{1,0:T(8,128)(2,1)S(1)}, u32[]{:S(2)}, u32[]{:S(2)}) %collective-permute-start.2) | collective-permute-done | bytes 262176 | tf_op jit(solution)/shard_map/ppermute | solution.py:902
  27.9 9.9 %collective-permute-done.3 = bf16[1,3,256,512]{3,2,1,0:T(8,128)(2,1)S(1)} collective-permute-done((bf16[1,3,256,512]{3,2,1,0:T(8,128)(2,1)S(1)}, bf16[1,3,256,512]{3,2,1,0:T(8,128)(2,1)S(1)}, u32[]{:S(2)}, u32[]{:S(2)}) %collective-permute-start.3) | collective-permute-done | bytes 786464 | tf_op jit(solution)/shard_map/ppermute | solution.py:917
  47.0 10.5 %collective-permute-done.4.b = bf16[2,3,256,512]{3,2,1,0:T(8,128)(2,1)S(1)} collective-permute-done((bf16[2,3,256,512]{3,2,1,0:T(8,128)(2,1)S(1)}, bf16[2,3,256,512]{3,2,1,0:T(8,128)(2,1)S(1)}, u32[]{:S(2)}, u32[]{:S(2)}) %collective-permute-start.4) | collective-permute-done | bytes 1572896 | tf_op jit(solution)/shard_map/ppermute | solution.py:917
  67.7 12.6 %shard_map.299 = (bf16[512,4096]{1,0:T(8,128)(2,1)}, bf16[768,1024]{1,0:T(8,128)(2,1)}) custom-call(s32[10]{0:T(128)} %pad_add_fusion.where, bf16[512,1024]{1,0:T(8,128)(2,1)} %bitcast.105, bf16[256,3072]{1,0:T(8,128)(2,1)} %own.13, bf16[2,3,256,512]{3,2,1,0:T(8,128)(2,1)} %copy-done, bf16[2,3,256,512]{3,2,1,0:T(8,128)(2,1)} %copy-done.2, ...), custom_call_target="tpu_custom_call" | custom-call | bytes 44280000 | tf_op jit(solution)/shard_map/pallas_call | solution.py:179
  81.6 5.6 %collective-permute-done.16 = bf16[256,512]{1,0:T(8,128)(2,1)} collective-permute-done((bf16[256,512]{1,0:T(8,128)(2,1)S(1)}, bf16[256,512]{1,0:T(8,128)(2,1)}, u32[]{:S(2)}, u32[]{:S(2)}) %collective-permute-start.16) | collective-permute-done | bytes 262176 | tf_op jit(solution)/shard_map/ppermute | solution.py:902
  91.9 10.8 %shard_map.300 = (bf16[512,1024]{1,0:T(8,128)(2,1)}, bf16[2,1024,512]{2,1,0:T(8,128)(2,1)}, f32[512,128]{1,0:T(8,128)}) custom-call(s32[10]{0:T(128)} %pad_add_fusion.where, bf16[512,4096]{1,0:T(8,128)(2,1)} %get-tuple-element.111.q.k.v, bf16[512,4096]{1,0:T(8,128)(2,1)} %get-tuple-element.111.q.k.v, bf16[512,4096]{1,0:T(8,128)(2,1)} %get-tuple-element.111.q.k.v, ...), custom_call_target="tpu_custom_call" | custom-call | bytes 40590000 | tf_op jit(solution)/shard_map/pallas_call | solution.py:229
  112.0 10.9 %shard_map.301 = (bf16[512,1024]{1,0:T(8,128)(2,1)}, bf16[2,1024,512]{2,1,0:T(8,128)(2,1)}, f32[512,128]{1,0:T(8,128)}) custom-call(s32[10]{0:T(128)} %pad_add_fusion.where, bf16[512,4096]{1,0:T(8,128)(2,1)} %get-tuple-element.111.q.k.v, bf16[512,4096]{1,0:T(8,128)(2,1)} %get-tuple-element.111.q.k.v, ...), custom_call_target="tpu_custom_call", output_to_operand_aliasing={{0}: (7, {}), {1}: (8, {})} | custom-call | bytes 40590000 | tf_op jit(solution)/shard_map/pallas_call | solution.py:229
  122.9 6.3 %collective-permute-done.12 = bf16[128,1024]{1,0:T(8,128)(2,1)S(1)} collective-permute-done((bf16[128,1024]{1,0:T(8,128)(2,1)S(1)}, bf16[128,1024]{1,0:T(8,128)(2,1)S(1)}, u32[]{:S(2)}, u32[]{:S(2)}) %collective-permute-start.12) | collective-permute-done | bytes 262176 | tf_op jit(solution)/shard_map/ppermute | solution.py:902
  136.9 6.0 %shard_map.302 = (f32[512,1024]{1,0:T(8,128)}, bf16[512,1024]{1,0:T(8,128)(2,1)}, bf16[1024,512]{1,0:T(8,128)(2,1)}) custom-call(s32[10]{0:T(128)} %pad_add_fusion.where, bf16[512,1024]{1,0:T(8,128)(2,1)} %get-tuple-element.114.context, bf16[512,1024]{1,0:T(8,128)(2,1)} %bitcast.108, bf16[256,1024]{1,0:T(8,128)(2,1)} %own_out.1, ...), custom_call_target="tpu_custom_call" | custom-call | bytes 22140000 | tf_op jit(solution)/shard_map/pallas_call | solution.py:345
  153.2 15.5 %shard_map.303 = (bf16[512,4096]{1,0:T(8,128)(2,1)}, bf16[4096,256]{1,0:T(8,128)(2,1)}, bf16[4096,256]{1,0:T(8,128)(2,1)}, bf16[512,4096]{1,0:T(8,128)(2,1)}) custom-call(s32[10]{0:T(128)} %pad_add_fusion.where, bf16[512,1024]{1,0:T(8,128)(2,1)} %get-tuple-element.120.x, bf16[256,4096]{1,0:T(8,128)(2,1)} %own.12, ...), custom_call_target="tpu_custom_call" | custom-call | bytes 59040000 | tf_op jit(solution)/shard_map/pallas_call | solution.py:398
  174.0 15.3 %shard_map.304 = (bf16[512,1024]{1,0:T(8,128)(2,1)}, f32[512,1024]{1,0:T(8,128)}, bf16[512,1024]{1,0:T(8,128)(2,1)}, bf16[512,512]{1,0:T(8,128)(2,1)}, f32[8,1024]{1,0:T(8,128)}) custom-call(s32[10]{0:T(128)} %pad_add_fusion.where, bf16[512,4096]{1,0:T(8,128)(2,1)} %get-tuple-element.127.act, bf16[1024,1024]{1,0:T(8,128)(2,1)} %own.11, ...), custom_call_target="tpu_custom_call" | custom-call | bytes 221400000 | tf_op jit(solution)/shard_map/pallas_call | solution.py:506
  192.3 7.5 %shard_map.305 = bf16[2,1024,512]{2,1,0:T(8,128)(2,1)} custom-call(s32[10]{0:T(128)} %pad_add_fusion.where, bf16[1,512,1024]{2,1,0:T(8,128)(2,1)} %bitcast.101, bf16[1,512,512]{2,1,0:T(8,128)(2,1)} %bitcast.113, bf16[1,4096,256]{2,1,0:T(8,128)(2,1)} %bitcast.93, bf16[1,4096,256]{2,1,0:T(8,128)(2,1)} %bitcast.97, ...), custom_call_target="tpu_custom_call" | custom-call | bytes 22140000 | tf_op jit(solution)/shard_map/pallas_call | solution.py:856
  200.7 15.4 %shard_map.306 = (bf16[512,4096]{1,0:T(8,128)(2,1)}, bf16[512,2048]{1,0:T(8,128)(2,1)}, f32[1,4096]{1,0:T(1,128)}) custom-call(s32[10]{0:T(128)} %pad_add_fusion.where, bf16[512,1024]{1,0:T(8,128)(2,1)} %get-tuple-element.135.low, bf16[1024,1024]{1,0:T(8,128)(2,1)} %own.11, bf16[2,3,128,1024]{3,2,1,0:T(8,128)(2,1)} %pad_maximum_fusion.2.a, ...), custom_call_target="tpu_custom_call" | custom-call | bytes 51660000 | tf_op jit(solution)/shard_map/pallas_call | solution.py:583
  216.1 18.1 %shard_map.307 = (f32[512,1024]{1,0:T(8,128)}, bf16[512,1024]{1,0:T(8,128)(2,1)}, bf16[512,1024]{1,0:T(8,128)(2,1)}, f32[8,1024]{1,0:T(8,128)}) custom-call(s32[10]{0:T(128)} %pad_add_fusion.where, bf16[512,4096]{1,0:T(8,128)(2,1)} %get-tuple-element.139.grad_inner, bf16[256,4096]{1,0:T(8,128)(2,1)} %own.12, bf16[2,3,256,512]{3,2,1,0:T(8,128)(2,1)} %pad_maximum_fusion.1.a, ...), custom_call_target="tpu_custom_call" | custom-call | bytes 70110000 | tf_op jit(solution)/shard_map/pallas_call | solution.py:664
  234.2 5.8 %shard_map.308 = bf16[1,1024,512]{2,1,0:T(8,128)(2,1)} custom-call(s32[10]{0:T(128)} %pad_add_fusion.where, bf16[1,512,1024]{2,1,0:T(8,128)(2,1)} %bitcast.103, bf16[1,512,512]{2,1,0:T(8,128)(2,1)} %bitcast.115, bf16[1,4096,256]{2,1,0:T(8,128)(2,1)} %bitcast.95, bf16[1,4096,256]{2,1,0:T(8,128)(2,1)} %bitcast.99, ...), custom_call_target="tpu_custom_call" | custom-call | bytes 22140000 | tf_op jit(solution)/shard_map/pallas_call | solution.py:856
  241.3 7.1 %shard_map.309 = bf16[2,1024,512]{2,1,0:T(8,128)(2,1)} custom-call(s32[10]{0:T(128)} %pad_add_fusion.where, bf16[1,512,4096]{2,1,0:T(8,128)(2,1)} %bitcast.89, bf16[1,512,2048]{2,1,0:T(8,128)(2,1)} %bitcast.28.refs_1_.refs_5_, bf16[1,1024,512]{2,1,0:T(8,128)(2,1)} %bitcast.109, bf16[1,1024,512]{2,1,0:T(8,128)(2,1)} %bitcast.26.refs_3_.refs_7_, ...), custom_call_target="tpu_custom_call" | custom-call | bytes 22140000 | tf_op jit(solution)/shard_map/pallas_call | solution.py:856
  248.7 13.0 %shard_map.310 = (bf16[4,512,512]{2,1,0:T(8,128)(2,1)}, f32[3,1,512]{2,1,0:T(1,128)}) custom-call(s32[10]{0:T(128)} %pad_add_fusion.where, bf16[512,4096]{1,0:T(8,128)(2,1)} %get-tuple-element.111.q.k.v, bf16[512,4096]{1,0:T(8,128)(2,1)} %get-tuple-element.111.q.k.v, bf16[512,4096]{1,0:T(8,128)(2,1)} %get-tuple-element.111.q.k.v, ...), custom_call_target="tpu_custom_call" | custom-call | bytes 47970000 | tf_op jit(solution)/shard_map/pallas_call | solution.py:302
  261.7 6.3 %shard_map.311 = (bf16[256,512]{1,0:T(8,128)(2,1)}, bf16[256,512]{1,0:T(8,128)(2,1)}, bf16[256,512]{1,0:T(8,128)(2,1)}, bf16[256,512]{1,0:T(8,128)(2,1)}) custom-call(s32[10]{0:T(128)} %pad_add_fusion.where, bf16[1,512,1024]{2,1,0:T(8,128)(2,1)} %bitcast.104, bf16[1,512,512]{2,1,0:T(8,128)(2,1)} %bitcast.116, bf16[1,4096,256]{2,1,0:T(8,128)(2,1)} %bitcast.96, ...), custom_call_target="tpu_custom_call" | custom-call | bytes 22140000 | tf_op jit(solution)/shard_map/pallas_call | solution.py:856
  270.4 13.2 %shard_map.312 = (bf16[4,512,512]{2,1,0:T(8,128)(2,1)}, f32[3,1,512]{2,1,0:T(1,128)}) custom-call(s32[10]{0:T(128)} %pad_add_fusion.where, bf16[512,4096]{1,0:T(8,128)(2,1)} %get-tuple-element.111.q.k.v, bf16[512,4096]{1,0:T(8,128)(2,1)} %get-tuple-element.111.q.k.v, bf16[512,4096]{1,0:T(8,128)(2,1)} %get-tuple-element.111.q.k.v, ...), custom_call_target="tpu_custom_call" | custom-call | bytes 47970000 | tf_op jit(solution)/shard_map/pallas_call | solution.py:302
  283.6 5.7 %shard_map.313 = bf16[1,1024,512]{2,1,0:T(8,128)(2,1)} custom-call(s32[10]{0:T(128)} %pad_add_fusion.where, bf16[1,512,4096]{2,1,0:T(8,128)(2,1)} %bitcast.91, bf16[1,512,2048]{2,1,0:T(8,128)(2,1)} %bitcast.28.refs_1_.refs_5_, bf16[1,1024,512]{2,1,0:T(8,128)(2,1)} %bitcast.111, bf16[1,1024,512]{2,1,0:T(8,128)(2,1)} %bitcast.26.refs_3_.refs_7_, ...), custom_call_target="tpu_custom_call" | custom-call | bytes 22140000 | tf_op jit(solution)/shard_map/pallas_call | solution.py:856
  292.8 7.2 %shard_map.314 = bf16[2,1024,512]{2,1,0:T(8,128)(2,1)} custom-call(s32[10]{0:T(128)} %pad_add_fusion.where, bf16[4,512,512]{2,1,0:T(8,128)(2,1)} %get-tuple-element.163.refs_0_.refs_4_.mine, bf16[4,512,512]{2,1,0:T(8,128)(2,1)} %collective-permute-done.32.refs_1_.refs_5_, bf16[2,1024,512]{2,1,0:T(8,128)(2,1)} %get-tuple-element.143.refs_2_.refs_6_, ...), custom_call_target="tpu_custom_call" | custom-call | bytes 22140000 | tf_op jit(solution)/shard_map/pallas_call | solution.py:856
  304.8 13.8 %shard_map.315 = f32[512,1024]{1,0:T(8,128)} custom-call(s32[10]{0:T(128)} %pad_add_fusion.where, bf16[4,512,512]{2,1,0:T(8,128)(2,1)} %get-tuple-element.163.refs_0_.refs_4_.mine, bf16[4,512,512]{2,1,0:T(8,128)(2,1)} %get-tuple-element.156.others, bf16[256,3072]{1,0:T(8,128)(2,1)} %own.13, bf16[2,3,256,512]{3,2,1,0:T(8,128)(2,1)} %copy-done, ...), custom_call_target="tpu_custom_call" | custom-call | bytes 44280000 | tf_op jit(solution)/shard_map/pallas_call | solution.py:721
  318.7 8.2 %collective-permute-done.37.refs_5_ = bf16[1,1024,512]{2,1,0:T(8,128)(2,1)} collective-permute-done((bf16[1,1024,512]{2,1,0:T(8,128)(2,1)}, bf16[1,1024,512]{2,1,0:T(8,128)(2,1)}, u32[]{:S(2)}, u32[]{:S(2)}) %collective-permute-start.37) | collective-permute-done | bytes 1048608 | tf_op jit(solution)/shard_map/ppermute | solution.py:917
  326.8 6.2 %shard_map.316 = (bf16[256,512]{1,0:T(8,128)(2,1)}, bf16[256,512]{1,0:T(8,128)(2,1)}, bf16[256,512]{1,0:T(8,128)(2,1)}, bf16[256,512]{1,0:T(8,128)(2,1)}) custom-call(s32[10]{0:T(128)} %pad_add_fusion.where, bf16[1,512,4096]{2,1,0:T(8,128)(2,1)} %bitcast.92, bf16[1,512,2048]{2,1,0:T(8,128)(2,1)} %bitcast.28.refs_1_.refs_5_, bf16[1,1024,512]{2,1,0:T(8,128)(2,1)} %bitcast.112, ...), custom_call_target="tpu_custom_call" | custom-call | bytes 22140000 | tf_op jit(solution)/shard_map/pallas_call | solution.py:856
  336.8 5.8 %shard_map.317 = bf16[1,1024,512]{2,1,0:T(8,128)(2,1)} custom-call(s32[10]{0:T(128)} %pad_add_fusion.where, bf16[4,512,512]{2,1,0:T(8,128)(2,1)} %get-tuple-element.163.refs_0_.refs_4_.mine, bf16[4,512,512]{2,1,0:T(8,128)(2,1)} %collective-permute-done.32.refs_1_.refs_5_, bf16[2,1024,512]{2,1,0:T(8,128)(2,1)} %get-tuple-element.143.refs_2_.refs_6_, ...), custom_call_target="tpu_custom_call" | custom-call | bytes 22140000 | tf_op jit(solution)/shard_map/pallas_call | solution.py:856
  348.8 8.0 %collective-permute-done.42.refs_5_ = bf16[1,1024,512]{2,1,0:T(8,128)(2,1)} collective-permute-done((bf16[1,1024,512]{2,1,0:T(8,128)(2,1)}, bf16[1,1024,512]{2,1,0:T(8,128)(2,1)}, u32[]{:S(2)}, u32[]{:S(2)}) %collective-permute-start.42) | collective-permute-done | bytes 1048608 | tf_op jit(solution)/shard_map/ppermute | solution.py:917
  356.9 6.2 %shard_map.318 = (bf16[272,512]{1,0:T(8,128)(2,1)}, bf16[272,512]{1,0:T(8,128)(2,1)}, bf16[272,512]{1,0:T(8,128)(2,1)}, bf16[272,512]{1,0:T(8,128)(2,1)}) custom-call(s32[10]{0:T(128)} %pad_add_fusion.where, bf16[4,512,512]{2,1,0:T(8,128)(2,1)} %get-tuple-element.163.refs_0_.refs_4_.mine, bf16[4,512,512]{2,1,0:T(8,128)(2,1)} %collective-permute-done.32.refs_1_.refs_5_, ...), custom_call_target="tpu_custom_call" | custom-call | bytes 22140000 | tf_op jit(solution)/shard_map/pallas_call | solution.py:856
  368.3 13.4 %collective-permute-done.40 = bf16[256,512]{1,0:T(8,128)(2,1)} collective-permute-done((bf16[256,512]{1,0:T(8,128)(2,1)}, bf16[256,512]{1,0:T(8,128)(2,1)}, u32[]{:S(2)}, u32[]{:S(2)}) %collective-permute-start.40) | collective-permute-done | bytes 262176 | tf_op jit(solution)/shard_map/ppermute | solution.py:905
  396.0 6.7 %collective-permute-done.46 = bf16[1,528,512]{2,1,0:T(8,128)(2,1)S(1)} collective-permute-done((bf16[1,528,512]{2,1,0:T(8,128)(2,1)S(1)}, bf16[1,528,512]{2,1,0:T(8,128)(2,1)S(1)}, u32[]{:S(2)}, u32[]{:S(2)}) %collective-permute-start.46) | collective-permute-done | bytes 540704 | tf_op jit(solution)/shard_map/ppermute | solution.py:917
  411.9 11.7 %collective-permute-done.51.refs_1_ = bf16[2,528,512]{2,1,0:T(8,128)(2,1)S(1)} collective-permute-done((bf16[2,528,512]{2,1,0:T(8,128)(2,1)}, bf16[2,528,512]{2,1,0:T(8,128)(2,1)S(1)}, u32[]{:S(2)}, u32[]{:S(2)}) %collective-permute-start.51) | collective-permute-done | bytes 1081376 | tf_op jit(solution)/shard_map/ppermute | solution.py:917
  429.3 7.3 %shard_map.320 = (f32[256,4096]{1,0:T(8,128)}, f32[256,3072]{1,0:T(8,128)}, f32[256,1024]{1,0:T(8,128)}, f32[16,512]{1,0:T(8,128)}) custom-call(s32[10]{0:T(128)} %pad_add_fusion.where, bf16[2,528,512]{2,1,0:T(8,128)(2,1)} %pad_maximum_fusion.3.refs_0_, bf16[2,528,512]{2,1,0:T(8,128)(2,1)} %copy-done.4, ...), custom_call_target="tpu_custom_call" | custom-call | bytes 14760000 | tf_op jit(solution)/shard_map/pallas_call | solution.py:787
  (229 shorter events, 130.5 us)
Async XLA Ops:
  1.8 19.0 %collective-permute-start.1 = (bf16[256,512]{1,0:T(8,128)(2,1)S(1)}, bf16[256,512]{1,0:T(8,128)(2,1)S(1)}, u32[]{:S(2)}, u32[]{:S(2)}) collective-permute-start(bf16[256,512]{1,0:T(8,128)(2,1)S(1)} %fusion.1), channel_id=1, source_target_pairs={{0,2},{1,3},{2,0},{3,1},{4,6},{5,7},{6,4},{7,5},{8,10},{9,11},{10,... | collective-permute-start | bytes 786440 | tf_op jit(solution)/shard_map/ppermute | solution.py:902
  4.3 22.1 %collective-permute-start.2 = (bf16[256,512]{1,0:T(8,128)(2,1)S(1)}, bf16[256,512]{1,0:T(8,128)(2,1)S(1)}, u32[]{:S(2)}, u32[]{:S(2)}) collective-permute-start(bf16[256,512]{1,0:T(8,128)(2,1)S(1)} %fusion.1), channel_id=1, source_target_pairs={{0,1},{1,2},{2,3},{3,0},{4,5},{5,6},{6,7},{7,4},{8,9},{9,10},{10,1... | collective-permute-start | bytes 786440 | tf_op jit(solution)/shard_map/ppermute | solution.py:902
  37.9 19.6 %collective-permute-start.4 = (bf16[2,3,256,512]{3,2,1,0:T(8,128)(2,1)S(1)}, bf16[2,3,256,512]{3,2,1,0:T(8,128)(2,1)S(1)}, u32[]{:S(2)}, u32[]{:S(2)}) collective-permute-start(bf16[2,3,256,512]{3,2,1,0:T(8,128)(2,1)S(1)} %pad_maximum_fusion.a), channel_id=1, source_target_pairs={{0,16},{4,12},{8,24},{12,4},{16,0},{20,28},{24,8},{28,20},{1,17},{... | collective-permute-start | bytes 4718600 | tf_op jit(solution)/shard_map/ppermute | solution.py:917
  63.7 16.6 %collective-permute-start.14 = (bf16[256,512]{1,0:T(8,128)(2,1)S(1)}, bf16[256,512]{1,0:T(8,128)(2,1)}, u32[]{:S(2)}, u32[]{:S(2)}) collective-permute-start(bf16[256,512]{1,0:T(8,128)(2,1)S(1)} %constant_dynamic-slice_fusion), channel_id=1, source_target_pairs={{0,3},{1,0},{2,1},{3,2},{4,7},{5,4},{6,5},{7,6},{8,11},{9,8},{10,9... | collective-permute-start | bytes 786440 | tf_op jit(solution)/shard_map/ppermute | solution.py:902
  64.6 17.0 %collective-permute-start.15 = (bf16[256,512]{1,0:T(8,128)(2,1)S(1)}, bf16[256,512]{1,0:T(8,128)(2,1)}, u32[]{:S(2)}, u32[]{:S(2)}) collective-permute-start(bf16[256,512]{1,0:T(8,128)(2,1)S(1)} %constant_dynamic-slice_fusion), channel_id=1, source_target_pairs={{0,2},{1,3},{2,0},{3,1},{4,6},{5,7},{6,4},{7,5},{8,10},{9,11},{10,... | collective-permute-start | bytes 786440 | tf_op jit(solution)/shard_map/ppermute | solution.py:902
  67.1 20.1 %collective-permute-start.16 = (bf16[256,512]{1,0:T(8,128)(2,1)S(1)}, bf16[256,512]{1,0:T(8,128)(2,1)}, u32[]{:S(2)}, u32[]{:S(2)}) collective-permute-start(bf16[256,512]{1,0:T(8,128)(2,1)S(1)} %constant_dynamic-slice_fusion), channel_id=1, source_target_pairs={{0,1},{1,2},{2,3},{3,0},{4,5},{5,6},{6,7},{7,4},{8,9},{9,10},{10,1... | collective-permute-start | bytes 786440 | tf_op jit(solution)/shard_map/ppermute | solution.py:902
  105.2 43.3 %collective-permute-start.18 = (bf16[2,3,256,512]{3,2,1,0:T(8,128)(2,1)}, bf16[2,3,256,512]{3,2,1,0:T(8,128)(2,1)}, u32[]{:S(2)}, u32[]{:S(2)}) collective-permute-start(bf16[2,3,256,512]{3,2,1,0:T(8,128)(2,1)} %pad_maximum_fusion.1.a), channel_id=1, source_target_pairs={{0,16},{4,12},{8,24},{12,4},{16,0},{20,28},{24,8},{28,20},{1,17},{... | collective-permute-start | bytes 4718600 | tf_op jit(solution)/shard_map/ppermute | solution.py:917
  107.4 21.7 %collective-permute-start.12 = (bf16[128,1024]{1,0:T(8,128)(2,1)S(1)}, bf16[128,1024]{1,0:T(8,128)(2,1)S(1)}, u32[]{:S(2)}, u32[]{:S(2)}) collective-permute-start(bf16[128,1024]{1,0:T(8,128)(2,1)S(1)} %constant_dynamic-slice_fusion.1), channel_id=1, source_target_pairs={{0,1},{1,2},{2,3},{3,0},{4,5},{5,6},{6,7},{7,4},{8,9},{9,10},{10,1... | collective-permute-start | bytes 786440 | tf_op jit(solution)/shard_map/ppermute | solution.py:902
  111.8 21.7 %collective-permute-start.10 = (bf16[128,1024]{1,0:T(8,128)(2,1)S(1)}, bf16[128,1024]{1,0:T(8,128)(2,1)}, u32[]{:S(2)}, u32[]{:S(2)}) collective-permute-start(bf16[128,1024]{1,0:T(8,128)(2,1)S(1)} %constant_dynamic-slice_fusion.1), channel_id=1, source_target_pairs={{0,3},{1,0},{2,1},{3,2},{4,7},{5,4},{6,5},{7,6},{8,11},{9,8},{10,9... | collective-permute-start | bytes 786440 | tf_op jit(solution)/shard_map/ppermute | solution.py:902
  149.8 19.9 %collective-permute-start.21 = (bf16[2,3,128,1024]{3,2,1,0:T(8,128)(2,1)}, bf16[2,3,128,1024]{3,2,1,0:T(8,128)(2,1)}, u32[]{:S(2)}, u32[]{:S(2)}) collective-permute-start(bf16[2,3,128,1024]{3,2,1,0:T(8,128)(2,1)} %pad_maximum_fusion.2.a), channel_id=1, source_target_pairs={{0,16},{4,12},{8,24},{12,4},{16,0},{20,28},{24,8},{28,20},{1,17},{... | collective-permute-start | bytes 4718600 | tf_op jit(solution)/shard_map/ppermute | solution.py:917
  150.8 22.1 %collective-permute-start.22 = (bf16[2,3,128,1024]{3,2,1,0:T(8,128)(2,1)}, bf16[2,3,128,1024]{3,2,1,0:T(8,128)(2,1)}, u32[]{:S(2)}, u32[]{:S(2)}) collective-permute-start(bf16[2,3,128,1024]{3,2,1,0:T(8,128)(2,1)} %pad_maximum_fusion.2.a), channel_id=1, source_target_pairs={{0,4},{4,0},{1,5},{5,1},{2,6},{6,2},{3,7},{7,3},{8,12},{12,8},{9,1... | collective-permute-start | bytes 4718600 | tf_op jit(solution)/shard_map/ppermute | solution.py:908
  170.6 20.9 %collective-permute-start.25 = (bf16[4096,256]{1,0:T(8,128)(2,1)}, bf16[4096,256]{1,0:T(8,128)(2,1)}, u32[]{:S(2)}, u32[]{:S(2)}) collective-permute-start(bf16[4096,256]{1,0:T(8,128)(2,1)} %get-tuple-element.133), channel_id=1, source_target_pairs={{0,4},{4,0},{1,5},{5,1},{2,6},{6,2},{3,7},{7,3},{8,12},{12,8},{9,1... | collective-permute-start | bytes 6291464 | tf_op jit(solution)/shard_map/ppermute | solution.py:908
  170.6 20.9 %collective-permute-start.26 = (bf16[4096,256]{1,0:T(8,128)(2,1)}, bf16[4096,256]{1,0:T(8,128)(2,1)}, u32[]{:S(2)}, u32[]{:S(2)}) collective-permute-start(bf16[4096,256]{1,0:T(8,128)(2,1)} %get-tuple-element.134), channel_id=1, source_target_pairs={{0,4},{4,0},{1,5},{5,1},{2,6},{6,2},{3,7},{7,3},{8,12},{12,8},{9,1... | collective-permute-start | bytes 6291464 | tf_op jit(solution)/shard_map/ppermute | solution.py:908
  189.7 44.5 %collective-permute-start.29 = (bf16[2,1024,512]{2,1,0:T(8,128)(2,1)}, bf16[2,1024,512]{2,1,0:T(8,128)(2,1)}, u32[]{:S(2)}, u32[]{:S(2)}) collective-permute-start(bf16[2,1024,512]{2,1,0:T(8,128)(2,1)} %get-tuple-element.143.refs_2_.refs_6_), channel_id=1, source_target_pairs={{0,4},{4,0},{1,5},{5,1},{2,6},{6,2},{3,7},{7,3},{8,12},{12,8},{9,1... | collective-permute-start | bytes 6291464 | tf_op jit(solution)/shard_map/ppermute | solution.py:908
  199.8 34.5 %collective-permute-start.28 = (bf16[2,1024,512]{2,1,0:T(8,128)(2,1)}, bf16[2,1024,512]{2,1,0:T(8,128)(2,1)}, u32[]{:S(2)}, u32[]{:S(2)}) collective-permute-start(bf16[2,1024,512]{2,1,0:T(8,128)(2,1)} %shard_map.305), channel_id=1, source_target_pairs={{0,8},{4,20},{8,0},{12,28},{16,24},{20,4},{24,16},{28,12},{1,9},{5... | collective-permute-start | bytes 6291464 | tf_op jit(solution)/shard_map/ppermute | solution.py:917
  216.1 25.2 %collective-permute-start.31 = (bf16[512,2048]{1,0:T(8,128)(2,1)}, bf16[512,2048]{1,0:T(8,128)(2,1)}, u32[]{:S(2)}, u32[]{:S(2)}) collective-permute-start(bf16[512,2048]{1,0:T(8,128)(2,1)} %get-tuple-element.145), channel_id=1, source_target_pairs={{0,4},{4,0},{1,5},{5,1},{2,6},{6,2},{3,7},{7,3},{8,12},{12,8},{9,1... | collective-permute-start | bytes 6291464 | tf_op jit(solution)/shard_map/ppermute | solution.py:908
  240.1 21.6 %collective-permute-start.30 = (bf16[1,1024,512]{2,1,0:T(8,128)(2,1)}, bf16[1,1024,512]{2,1,0:T(8,128)(2,1)}, u32[]{:S(2)}, u32[]{:S(2)}) collective-permute-start(bf16[1,1024,512]{2,1,0:T(8,128)(2,1)} %shard_map.308), channel_id=1, source_target_pairs={{0,16},{4,12},{8,24},{12,4},{16,0},{20,28},{24,8},{28,20},{1,17},{... | collective-permute-start | bytes 3145736 | tf_op jit(solution)/shard_map/ppermute | solution.py:917
  248.4 35.2 %collective-permute-start.33 = (bf16[2,1024,512]{2,1,0:T(8,128)(2,1)}, bf16[2,1024,512]{2,1,0:T(8,128)(2,1)}, u32[]{:S(2)}, u32[]{:S(2)}) collective-permute-start(bf16[2,1024,512]{2,1,0:T(8,128)(2,1)} %shard_map.309), channel_id=1, source_target_pairs={{0,8},{4,20},{8,0},{12,28},{16,24},{20,4},{24,16},{28,12},{1,9},{5... | collective-permute-start | bytes 6291464 | tf_op jit(solution)/shard_map/ppermute | solution.py:917
  267.9 24.9 %collective-permute-start.32 = (bf16[4,512,512]{2,1,0:T(8,128)(2,1)}, bf16[4,512,512]{2,1,0:T(8,128)(2,1)}, u32[]{:S(2)}, u32[]{:S(2)}) collective-permute-start(bf16[4,512,512]{2,1,0:T(8,128)(2,1)} %get-tuple-element.156.others), channel_id=1, source_target_pairs={{0,4},{4,0},{1,5},{5,1},{2,6},{6,2},{3,7},{7,3},{8,12},{12,8},{9,1... | collective-permute-start | bytes 6291464 | tf_op jit(solution)/shard_map/ppermute | solution.py:908
  268.9 20.4 %collective-permute-start.34 = (bf16[256,512]{1,0:T(8,128)(2,1)}, bf16[256,512]{1,0:T(8,128)(2,1)S(1)}, u32[]{:S(2)}, u32[]{:S(2)}) collective-permute-start(bf16[256,512]{1,0:T(8,128)(2,1)} %get-tuple-element.158), channel_id=1, source_target_pairs={{0,1},{1,2},{2,3},{3,0},{4,5},{5,6},{6,7},{7,4},{8,9},{9,10},{10,1... | collective-permute-start | bytes 786440 | tf_op jit(solution)/shard_map/ppermute | solution.py:905
  268.9 23.0 %collective-permute-start.35 = (bf16[256,512]{1,0:T(8,128)(2,1)}, bf16[256,512]{1,0:T(8,128)(2,1)S(1)}, u32[]{:S(2)}, u32[]{:S(2)}) collective-permute-start(bf16[256,512]{1,0:T(8,128)(2,1)} %get-tuple-element.159), channel_id=1, source_target_pairs={{0,2},{1,3},{2,0},{3,1},{4,6},{5,7},{6,4},{7,5},{8,10},{9,11},{10,... | collective-permute-start | bytes 786440 | tf_op jit(solution)/shard_map/ppermute | solution.py:905
  269.0 23.9 %collective-permute-start.36 = (bf16[256,512]{1,0:T(8,128)(2,1)}, bf16[256,512]{1,0:T(8,128)(2,1)S(1)}, u32[]{:S(2)}, u32[]{:S(2)}) collective-permute-start(bf16[256,512]{1,0:T(8,128)(2,1)} %get-tuple-element.160), channel_id=1, source_target_pairs={{0,3},{1,0},{2,1},{3,2},{4,7},{5,4},{6,5},{7,6},{8,11},{9,8},{10,9... | collective-permute-start | bytes 786440 | tf_op jit(solution)/shard_map/ppermute | solution.py:905
  300.0 36.8 %collective-permute-start.41 = (bf16[2,1024,512]{2,1,0:T(8,128)(2,1)}, bf16[2,1024,512]{2,1,0:T(8,128)(2,1)}, u32[]{:S(2)}, u32[]{:S(2)}) collective-permute-start(bf16[2,1024,512]{2,1,0:T(8,128)(2,1)} %shard_map.314), channel_id=1, source_target_pairs={{0,8},{4,20},{8,0},{12,28},{16,24},{20,4},{24,16},{28,12},{1,9},{5... | collective-permute-start | bytes 6291464 | tf_op jit(solution)/shard_map/ppermute | solution.py:917
  301.3 25.5 %collective-permute-start.37 = (bf16[1,1024,512]{2,1,0:T(8,128)(2,1)}, bf16[1,1024,512]{2,1,0:T(8,128)(2,1)}, u32[]{:S(2)}, u32[]{:S(2)}) collective-permute-start(bf16[1,1024,512]{2,1,0:T(8,128)(2,1)} %shard_map.313), channel_id=1, source_target_pairs={{0,16},{4,12},{8,24},{12,4},{16,0},{20,28},{24,8},{28,20},{1,17},{... | collective-permute-start | bytes 3145736 | tf_op jit(solution)/shard_map/ppermute | solution.py:917
  344.1 20.4 %collective-permute-start.38 = (bf16[256,512]{1,0:T(8,128)(2,1)}, bf16[256,512]{1,0:T(8,128)(2,1)}, u32[]{:S(2)}, u32[]{:S(2)}) collective-permute-start(bf16[256,512]{1,0:T(8,128)(2,1)} %get-tuple-element.167), channel_id=1, source_target_pairs={{0,1},{1,2},{2,3},{3,0},{4,5},{5,6},{6,7},{7,4},{8,9},{9,10},{10,1... | collective-permute-start | bytes 786440 | tf_op jit(solution)/shard_map/ppermute | solution.py:905
  344.1 22.8 %collective-permute-start.39 = (bf16[256,512]{1,0:T(8,128)(2,1)}, bf16[256,512]{1,0:T(8,128)(2,1)}, u32[]{:S(2)}, u32[]{:S(2)}) collective-permute-start(bf16[256,512]{1,0:T(8,128)(2,1)} %get-tuple-element.168), channel_id=1, source_target_pairs={{0,2},{1,3},{2,0},{3,1},{4,6},{5,7},{6,4},{7,5},{8,10},{9,11},{10,... | collective-permute-start | bytes 786440 | tf_op jit(solution)/shard_map/ppermute | solution.py:905
  346.2 35.6 %collective-permute-start.40 = (bf16[256,512]{1,0:T(8,128)(2,1)}, bf16[256,512]{1,0:T(8,128)(2,1)}, u32[]{:S(2)}, u32[]{:S(2)}) collective-permute-start(bf16[256,512]{1,0:T(8,128)(2,1)} %get-tuple-element.169), channel_id=1, source_target_pairs={{0,3},{1,0},{2,1},{3,2},{4,7},{5,4},{6,5},{7,6},{8,11},{9,8},{10,9... | collective-permute-start | bytes 786440 | tf_op jit(solution)/shard_map/ppermute | solution.py:905
  363.1 19.9 %collective-permute-start.47 = (bf16[1,256,512]{2,1,0:T(8,128)(2,1)S(1)}, bf16[1,256,512]{2,1,0:T(8,128)(2,1)S(1)}, u32[]{:S(2)}, u32[]{:S(2)}) collective-permute-start(bf16[1,256,512]{2,1,0:T(8,128)(2,1)S(1)} %fusion.3), channel_id=1, source_target_pairs={{0,8},{4,20},{8,0},{12,28},{16,24},{20,4},{24,16},{28,12},{1,9},{5... | collective-permute-start | bytes 786440 | tf_op jit(solution)/shard_map/ppermute | solution.py:917
  364.4 19.9 %collective-permute-start.43 = (bf16[272,512]{1,0:T(8,128)(2,1)}, bf16[272,512]{1,0:T(8,128)(2,1)S(1)}, u32[]{:S(2)}, u32[]{:S(2)}) collective-permute-start(bf16[272,512]{1,0:T(8,128)(2,1)} %get-tuple-element.179), channel_id=1, source_target_pairs={{0,1},{1,2},{2,3},{3,0},{4,5},{5,6},{6,7},{7,4},{8,9},{9,10},{10,1... | collective-permute-start | bytes 835592 | tf_op jit(solution)/shard_map/ppermute | solution.py:905
  364.4 25.1 %collective-permute-start.44 = (bf16[272,512]{1,0:T(8,128)(2,1)}, bf16[272,512]{1,0:T(8,128)(2,1)S(1)}, u32[]{:S(2)}, u32[]{:S(2)}) collective-permute-start(bf16[272,512]{1,0:T(8,128)(2,1)} %get-tuple-element.180), channel_id=1, source_target_pairs={{0,2},{1,3},{2,0},{3,1},{4,6},{5,7},{6,4},{7,5},{8,10},{9,11},{10,... | collective-permute-start | bytes 835592 | tf_op jit(solution)/shard_map/ppermute | solution.py:905
  366.9 27.1 %collective-permute-start.45 = (bf16[272,512]{1,0:T(8,128)(2,1)}, bf16[272,512]{1,0:T(8,128)(2,1)S(1)}, u32[]{:S(2)}, u32[]{:S(2)}) collective-permute-start(bf16[272,512]{1,0:T(8,128)(2,1)} %get-tuple-element.181), channel_id=1, source_target_pairs={{0,3},{1,0},{2,1},{3,2},{4,7},{5,4},{6,5},{7,6},{8,11},{9,8},{10,9... | collective-permute-start | bytes 835592 | tf_op jit(solution)/shard_map/ppermute | solution.py:905
  410.0 16.8 %collective-permute-start.52 = (bf16[2,528,512]{2,1,0:T(8,128)(2,1)}, bf16[2,528,512]{2,1,0:T(8,128)(2,1)}, u32[]{:S(2)}, u32[]{:S(2)}) collective-permute-start(bf16[2,528,512]{2,1,0:T(8,128)(2,1)} %pad_maximum_fusion.3.refs_0_), channel_id=1, source_target_pairs={{0,4},{4,0},{1,5},{5,1},{2,6},{6,2},{3,7},{7,3},{8,12},{12,8},{9,1... | collective-permute-start | bytes 3244040 | tf_op jit(solution)/shard_map/ppermute | solution.py:908
  (49 other events, 561.6 us)

commit v8 on v7

--- a/solution.py
+++ b/solution.py
@@ -1179,8 +1179,8 @@
     )
     shares = jnp.concatenate([inward.total(), first.total()], axis=0).astype(BF16)
     final = Gather(shares[None])
-    final.step(grad_wdown)
-    final.finish()
+    final.step(gather_down.parts[3])
+    final.finish(grad_wdown)
     grad_win, grad_wqkv, grad_wout, total = widen(
         where,
         final.parts,

time: 448 us -> 442 us (0.987)
    ppermute x16, waiting for transfers between devices: 62.2 us -> 56.2 us  [swap(): return lax.ppermute(value, REP, pairs)]
    unnamed x77 -> x75, local copies, waits for them, and re-layouts: 9.81 us -> 8.01 us
  transfers between devices with their start and end apart: 54 -> 54, of which waited for: 29 -> 30; matrix products, arithmetic and copies ran while one was open for 5% -> 5% of each run, Pallas kernels for 43% -> 45%
where the time goes in v8:
time: 442 us; the launch traced here: 434 us
  Pallas kernels  214 us (48%)
  waiting for transfers between devices  134 us (30%)
  starting transfers between devices  53.2 us (12%)
  other arithmetic  15.8 us (4%)
  local copies, waits for them, and re-layouts  15.4 us (3%)
    pallas_call x9, Pallas kernels, grads(): call(partial(grads_kernel, (units, len(received), last, group, cuts, int(...  57.6 us
    ppermute x16, waiting for transfers between devices, swap(): return lax.ppermute(value, REP, pairs)  56.2 us
    ppermute x12, waiting for transfers between devices, from_shard(): lax.ppermute(value, 'shard', [(i, (i - step) % group) for i in range(grou...  40.3 us
    ppermute x9, waiting for transfers between devices, to_shard(): lax.ppermute(value, 'shard', [(i, (i + step) % group) for i in range(grou...  26.6 us
    pallas_call x2, Pallas kernels, attention_back(): call(partial(attend_back_kernel, (mine, per)), (each // 2,), [pairs(0), p...  26.2 us
    pallas_call x2, Pallas kernels, attention(): call(partial(attend_kernel, first), (count,), [spec((seq, block), lambda...  21.7 us
    pallas_call x1, Pallas kernels, inner_back(): call(partial(inner_back_kernel, (group, half)), (2 * chips,), [columns_at...  18 us
    ppermute x12, starting transfers between devices, from_shard(): lax.ppermute(value, 'shard', [(i, (i - step) % group) for i in range(grou...  16.1 us
  transfers between devices with their start and end apart: 54, of which 30 were waited for; matrix products, arithmetic and copies ran while one was open for 5% of the time, Pallas kernels for 45%

profile of v8, /device:TPU:9, one launch (start us, length us, event | category | flops | bytes accessed | tf_op | source)
XLA Modules:
  0.0 434.2 jit_solution(16722933728404453967)
XLA Ops:
  8.9 11.8 %collective-permute-done.1 = bf16[256,512]{1,0:T(8,128)(2,1)S(1)} collective-permute-done((bf16[256,512]{1,0:T(8,128)(2,1)S(1)}, bf16[256,512]{1,0:T(8,128)(2,1)S(1)}, u32[]{:S(2)}, u32[]{:S(2)}) %collective-permute-start.1) | collective-permute-done | bytes 262176 | tf_op jit(solution)/shard_map/ppermute | solution.py:902
  20.8 5.6 %collective-permute-done.2 = bf16[256,512]{1,0:T(8,128)(2,1)S(1)} collective-permute-done((bf16[256,512]{1,0:T(8,128)(2,1)S(1)}, bf16[256,512]{1,0:T(8,128)(2,1)S(1)}, u32[]{:S(2)}, u32[]{:S(2)}) %collective-permute-start.2) | collective-permute-done | bytes 262176 | tf_op jit(solution)/shard_map/ppermute | solution.py:902
  27.9 9.9 %collective-permute-done.3 = bf16[1,3,256,512]{3,2,1,0:T(8,128)(2,1)S(1)} collective-permute-done((bf16[1,3,256,512]{3,2,1,0:T(8,128)(2,1)S(1)}, bf16[1,3,256,512]{3,2,1,0:T(8,128)(2,1)S(1)}, u32[]{:S(2)}, u32[]{:S(2)}) %collective-permute-start.3) | collective-permute-done | bytes 786464 | tf_op jit(solution)/shard_map/ppermute | solution.py:917
  47.0 10.5 %collective-permute-done.4.b = bf16[2,3,256,512]{3,2,1,0:T(8,128)(2,1)S(1)} collective-permute-done((bf16[2,3,256,512]{3,2,1,0:T(8,128)(2,1)S(1)}, bf16[2,3,256,512]{3,2,1,0:T(8,128)(2,1)S(1)}, u32[]{:S(2)}, u32[]{:S(2)}) %collective-permute-start.4) | collective-permute-done | bytes 1572896 | tf_op jit(solution)/shard_map/ppermute | solution.py:917
  67.7 12.6 %shard_map.299 = (bf16[512,4096]{1,0:T(8,128)(2,1)}, bf16[768,1024]{1,0:T(8,128)(2,1)}) custom-call(s32[10]{0:T(128)} %pad_add_fusion.where, bf16[512,1024]{1,0:T(8,128)(2,1)} %bitcast.105, bf16[256,3072]{1,0:T(8,128)(2,1)} %own.13, bf16[2,3,256,512]{3,2,1,0:T(8,128)(2,1)} %copy-done, bf16[2,3,256,512]{3,2,1,0:T(8,128)(2,1)} %copy-done.2, ...), custom_call_target="tpu_custom_call" | custom-call | bytes 44280000 | tf_op jit(solution)/shard_map/pallas_call | solution.py:179
  81.6 5.6 %collective-permute-done.16 = bf16[256,512]{1,0:T(8,128)(2,1)} collective-permute-done((bf16[256,512]{1,0:T(8,128)(2,1)S(1)}, bf16[256,512]{1,0:T(8,128)(2,1)}, u32[]{:S(2)}, u32[]{:S(2)}) %collective-permute-start.16) | collective-permute-done | bytes 262176 | tf_op jit(solution)/shard_map/ppermute | solution.py:902
  91.9 10.8 %shard_map.300 = (bf16[512,1024]{1,0:T(8,128)(2,1)}, bf16[2,1024,512]{2,1,0:T(8,128)(2,1)}, f32[512,128]{1,0:T(8,128)}) custom-call(s32[10]{0:T(128)} %pad_add_fusion.where, bf16[512,4096]{1,0:T(8,128)(2,1)} %get-tuple-element.112.q.k.v, bf16[512,4096]{1,0:T(8,128)(2,1)} %get-tuple-element.112.q.k.v, bf16[512,4096]{1,0:T(8,128)(2,1)} %get-tuple-element.112.q.k.v, ...), custom_call_target="tpu_custom_call" | custom-call | bytes 40590000 | tf_op jit(solution)/shard_map/pallas_call | solution.py:229
  112.0 10.8 %shard_map.301 = (bf16[512,1024]{1,0:T(8,128)(2,1)}, bf16[2,1024,512]{2,1,0:T(8,128)(2,1)}, f32[512,128]{1,0:T(8,128)}) custom-call(s32[10]{0:T(128)} %pad_add_fusion.where, bf16[512,4096]{1,0:T(8,128)(2,1)} %get-tuple-element.112.q.k.v, bf16[512,4096]{1,0:T(8,128)(2,1)} %get-tuple-element.112.q.k.v, ...), custom_call_target="tpu_custom_call", output_to_operand_aliasing={{0}: (7, {}), {1}: (8, {})} | custom-call | bytes 40590000 | tf_op jit(solution)/shard_map/pallas_call | solution.py:229
  122.8 6.3 %collective-permute-done.12 = bf16[128,1024]{1,0:T(8,128)(2,1)S(1)} collective-permute-done((bf16[128,1024]{1,0:T(8,128)(2,1)S(1)}, bf16[128,1024]{1,0:T(8,128)(2,1)S(1)}, u32[]{:S(2)}, u32[]{:S(2)}) %collective-permute-start.12) | collective-permute-done | bytes 262176 | tf_op jit(solution)/shard_map/ppermute | solution.py:902
  136.9 6.0 %shard_map.302 = (f32[512,1024]{1,0:T(8,128)}, bf16[512,1024]{1,0:T(8,128)(2,1)}, bf16[1024,512]{1,0:T(8,128)(2,1)}) custom-call(s32[10]{0:T(128)} %pad_add_fusion.where, bf16[512,1024]{1,0:T(8,128)(2,1)} %get-tuple-element.115.context, bf16[512,1024]{1,0:T(8,128)(2,1)} %bitcast.108, bf16[256,1024]{1,0:T(8,128)(2,1)} %own_out.1, ...), custom_call_target="tpu_custom_call" | custom-call | bytes 22140000 | tf_op jit(solution)/shard_map/pallas_call | solution.py:345
  153.2 15.5 %shard_map.303 = (bf16[512,4096]{1,0:T(8,128)(2,1)}, bf16[4096,256]{1,0:T(8,128)(2,1)}, bf16[4096,256]{1,0:T(8,128)(2,1)}, bf16[512,4096]{1,0:T(8,128)(2,1)}) custom-call(s32[10]{0:T(128)} %pad_add_fusion.where, bf16[512,1024]{1,0:T(8,128)(2,1)} %get-tuple-element.121.x, bf16[256,4096]{1,0:T(8,128)(2,1)} %own.12, ...), custom_call_target="tpu_custom_call" | custom-call | bytes 59040000 | tf_op jit(solution)/shard_map/pallas_call | solution.py:398
  173.9 15.3 %shard_map.304 = (bf16[512,1024]{1,0:T(8,128)(2,1)}, f32[512,1024]{1,0:T(8,128)}, bf16[512,1024]{1,0:T(8,128)(2,1)}, bf16[512,512]{1,0:T(8,128)(2,1)}, f32[8,1024]{1,0:T(8,128)}) custom-call(s32[10]{0:T(128)} %pad_add_fusion.where, bf16[512,4096]{1,0:T(8,128)(2,1)} %get-tuple-element.128.act, bf16[1024,1024]{1,0:T(8,128)(2,1)} %own.11, ...), custom_call_target="tpu_custom_call" | custom-call | bytes 221400000 | tf_op jit(solution)/shard_map/pallas_call | solution.py:506
  192.2 7.5 %shard_map.305 = bf16[2,1024,512]{2,1,0:T(8,128)(2,1)} custom-call(s32[10]{0:T(128)} %pad_add_fusion.where, bf16[1,512,1024]{2,1,0:T(8,128)(2,1)} %bitcast.101, bf16[1,512,512]{2,1,0:T(8,128)(2,1)} %bitcast.113, bf16[1,4096,256]{2,1,0:T(8,128)(2,1)} %bitcast.93, bf16[1,4096,256]{2,1,0:T(8,128)(2,1)} %bitcast.97, ...), custom_call_target="tpu_custom_call" | custom-call | bytes 22140000 | tf_op jit(solution)/shard_map/pallas_call | solution.py:856
  200.6 15.4 %shard_map.306 = (bf16[512,4096]{1,0:T(8,128)(2,1)}, bf16[512,2048]{1,0:T(8,128)(2,1)}, f32[1,4096]{1,0:T(1,128)}) custom-call(s32[10]{0:T(128)} %pad_add_fusion.where, bf16[512,1024]{1,0:T(8,128)(2,1)} %get-tuple-element.136.low, bf16[1024,1024]{1,0:T(8,128)(2,1)} %own.11, bf16[2,3,128,1024]{3,2,1,0:T(8,128)(2,1)} %pad_maximum_fusion.2.a, ...), custom_call_target="tpu_custom_call" | custom-call | bytes 51660000 | tf_op jit(solution)/shard_map/pallas_call | solution.py:583
  216.1 18.0 %shard_map.307 = (f32[512,1024]{1,0:T(8,128)}, bf16[512,1024]{1,0:T(8,128)(2,1)}, bf16[512,1024]{1,0:T(8,128)(2,1)}, f32[8,1024]{1,0:T(8,128)}) custom-call(s32[10]{0:T(128)} %pad_add_fusion.where, bf16[512,4096]{1,0:T(8,128)(2,1)} %get-tuple-element.140.grad_inner, bf16[256,4096]{1,0:T(8,128)(2,1)} %own.12, bf16[2,3,256,512]{3,2,1,0:T(8,128)(2,1)} %pad_maximum_fusion.1.a, ...), custom_call_target="tpu_custom_call" | custom-call | bytes 70110000 | tf_op jit(solution)/shard_map/pallas_call | solution.py:664
  234.2 5.8 %shard_map.308 = bf16[1,1024,512]{2,1,0:T(8,128)(2,1)} custom-call(s32[10]{0:T(128)} %pad_add_fusion.where, bf16[1,512,1024]{2,1,0:T(8,128)(2,1)} %bitcast.103, bf16[1,512,512]{2,1,0:T(8,128)(2,1)} %bitcast.115, bf16[1,4096,256]{2,1,0:T(8,128)(2,1)} %bitcast.95, bf16[1,4096,256]{2,1,0:T(8,128)(2,1)} %bitcast.99, ...), custom_call_target="tpu_custom_call" | custom-call | bytes 22140000 | tf_op jit(solution)/shard_map/pallas_call | solution.py:856
  241.2 7.1 %shard_map.309 = bf16[2,1024,512]{2,1,0:T(8,128)(2,1)} custom-call(s32[10]{0:T(128)} %pad_add_fusion.where, bf16[1,512,4096]{2,1,0:T(8,128)(2,1)} %bitcast.89, bf16[1,512,2048]{2,1,0:T(8,128)(2,1)} %bitcast.28.refs_1_.refs_5_, bf16[1,1024,512]{2,1,0:T(8,128)(2,1)} %bitcast.109, bf16[1,1024,512]{2,1,0:T(8,128)(2,1)} %bitcast.26.refs_3_.refs_7_, ...), custom_call_target="tpu_custom_call" | custom-call | bytes 22140000 | tf_op jit(solution)/shard_map/pallas_call | solution.py:856
  248.6 13.0 %shard_map.310 = (bf16[4,512,512]{2,1,0:T(8,128)(2,1)}, f32[3,1,512]{2,1,0:T(1,128)}) custom-call(s32[10]{0:T(128)} %pad_add_fusion.where, bf16[512,4096]{1,0:T(8,128)(2,1)} %get-tuple-element.112.q.k.v, bf16[512,4096]{1,0:T(8,128)(2,1)} %get-tuple-element.112.q.k.v, bf16[512,4096]{1,0:T(8,128)(2,1)} %get-tuple-element.112.q.k.v, ...), custom_call_target="tpu_custom_call" | custom-call | bytes 47970000 | tf_op jit(solution)/shard_map/pallas_call | solution.py:302
  261.5 6.2 %shard_map.311 = (bf16[256,512]{1,0:T(8,128)(2,1)}, bf16[256,512]{1,0:T(8,128)(2,1)}, bf16[256,512]{1,0:T(8,128)(2,1)}, bf16[256,512]{1,0:T(8,128)(2,1)}) custom-call(s32[10]{0:T(128)} %pad_add_fusion.where, bf16[1,512,1024]{2,1,0:T(8,128)(2,1)} %bitcast.104, bf16[1,512,512]{2,1,0:T(8,128)(2,1)} %bitcast.116, bf16[1,4096,256]{2,1,0:T(8,128)(2,1)} %bitcast.96, ...), custom_call_target="tpu_custom_call" | custom-call | bytes 22140000 | tf_op jit(solution)/shard_map/pallas_call | solution.py:856
  270.3 13.2 %shard_map.312 = (bf16[4,512,512]{2,1,0:T(8,128)(2,1)}, f32[3,1,512]{2,1,0:T(1,128)}) custom-call(s32[10]{0:T(128)} %pad_add_fusion.where, bf16[512,4096]{1,0:T(8,128)(2,1)} %get-tuple-element.112.q.k.v, bf16[512,4096]{1,0:T(8,128)(2,1)} %get-tuple-element.112.q.k.v, bf16[512,4096]{1,0:T(8,128)(2,1)} %get-tuple-element.112.q.k.v, ...), custom_call_target="tpu_custom_call" | custom-call | bytes 47970000 | tf_op jit(solution)/shard_map/pallas_call | solution.py:302
  283.5 5.7 %shard_map.313 = bf16[1,1024,512]{2,1,0:T(8,128)(2,1)} custom-call(s32[10]{0:T(128)} %pad_add_fusion.where, bf16[1,512,4096]{2,1,0:T(8,128)(2,1)} %bitcast.91, bf16[1,512,2048]{2,1,0:T(8,128)(2,1)} %bitcast.28.refs_1_.refs_5_, bf16[1,1024,512]{2,1,0:T(8,128)(2,1)} %bitcast.111, bf16[1,1024,512]{2,1,0:T(8,128)(2,1)} %bitcast.26.refs_3_.refs_7_, ...), custom_call_target="tpu_custom_call" | custom-call | bytes 22140000 | tf_op jit(solution)/shard_map/pallas_call | solution.py:856
  292.8 7.2 %shard_map.314 = bf16[2,1024,512]{2,1,0:T(8,128)(2,1)} custom-call(s32[10]{0:T(128)} %pad_add_fusion.where, bf16[4,512,512]{2,1,0:T(8,128)(2,1)} %get-tuple-element.164.refs_0_.refs_4_.mine, bf16[4,512,512]{2,1,0:T(8,128)(2,1)} %collective-permute-done.32.refs_1_.refs_5_, bf16[2,1024,512]{2,1,0:T(8,128)(2,1)} %get-tuple-element.144.refs_2_.refs_6_, ...), custom_call_target="tpu_custom_call" | custom-call | bytes 22140000 | tf_op jit(solution)/shard_map/pallas_call | solution.py:856
  304.7 13.8 %shard_map.315 = f32[512,1024]{1,0:T(8,128)} custom-call(s32[10]{0:T(128)} %pad_add_fusion.where, bf16[4,512,512]{2,1,0:T(8,128)(2,1)} %get-tuple-element.164.refs_0_.refs_4_.mine, bf16[4,512,512]{2,1,0:T(8,128)(2,1)} %get-tuple-element.157.others, bf16[256,3072]{1,0:T(8,128)(2,1)} %own.13, bf16[2,3,256,512]{3,2,1,0:T(8,128)(2,1)} %copy-done, ...), custom_call_target="tpu_custom_call" | custom-call | bytes 44280000 | tf_op jit(solution)/shard_map/pallas_call | solution.py:721
  318.6 8.1 %collective-permute-done.37.refs_5_ = bf16[1,1024,512]{2,1,0:T(8,128)(2,1)} collective-permute-done((bf16[1,1024,512]{2,1,0:T(8,128)(2,1)}, bf16[1,1024,512]{2,1,0:T(8,128)(2,1)}, u32[]{:S(2)}, u32[]{:S(2)}) %collective-permute-start.37) | collective-permute-done | bytes 1048608 | tf_op jit(solution)/shard_map/ppermute | solution.py:917
  326.7 6.1 %shard_map.316 = (bf16[256,512]{1,0:T(8,128)(2,1)}, bf16[256,512]{1,0:T(8,128)(2,1)}, bf16[256,512]{1,0:T(8,128)(2,1)}, bf16[256,512]{1,0:T(8,128)(2,1)}) custom-call(s32[10]{0:T(128)} %pad_add_fusion.where, bf16[1,512,4096]{2,1,0:T(8,128)(2,1)} %bitcast.92, bf16[1,512,2048]{2,1,0:T(8,128)(2,1)} %bitcast.28.refs_1_.refs_5_, bf16[1,1024,512]{2,1,0:T(8,128)(2,1)} %bitcast.112, ...), custom_call_target="tpu_custom_call" | custom-call | bytes 22140000 | tf_op jit(solution)/shard_map/pallas_call | solution.py:856
  336.7 5.8 %shard_map.317 = bf16[1,1024,512]{2,1,0:T(8,128)(2,1)} custom-call(s32[10]{0:T(128)} %pad_add_fusion.where, bf16[4,512,512]{2,1,0:T(8,128)(2,1)} %get-tuple-element.164.refs_0_.refs_4_.mine, bf16[4,512,512]{2,1,0:T(8,128)(2,1)} %collective-permute-done.32.refs_1_.refs_5_, bf16[2,1024,512]{2,1,0:T(8,128)(2,1)} %get-tuple-element.144.refs_2_.refs_6_, ...), custom_call_target="tpu_custom_call" | custom-call | bytes 22140000 | tf_op jit(solution)/shard_map/pallas_call | solution.py:856
  348.7 8.0 %collective-permute-done.42.refs_5_ = bf16[1,1024,512]{2,1,0:T(8,128)(2,1)} collective-permute-done((bf16[1,1024,512]{2,1,0:T(8,128)(2,1)}, bf16[1,1024,512]{2,1,0:T(8,128)(2,1)}, u32[]{:S(2)}, u32[]{:S(2)}) %collective-permute-start.42) | collective-permute-done | bytes 1048608 | tf_op jit(solution)/shard_map/ppermute | solution.py:917
  356.8 6.3 %shard_map.318 = (bf16[272,512]{1,0:T(8,128)(2,1)}, bf16[272,512]{1,0:T(8,128)(2,1)}, bf16[272,512]{1,0:T(8,128)(2,1)}, bf16[272,512]{1,0:T(8,128)(2,1)}) custom-call(s32[10]{0:T(128)} %pad_add_fusion.where, bf16[4,512,512]{2,1,0:T(8,128)(2,1)} %get-tuple-element.164.refs_0_.refs_4_.mine, bf16[4,512,512]{2,1,0:T(8,128)(2,1)} %collective-permute-done.32.refs_1_.refs_5_, ...), custom_call_target="tpu_custom_call" | custom-call | bytes 22140000 | tf_op jit(solution)/shard_map/pallas_call | solution.py:856
  368.3 13.4 %collective-permute-done.40 = bf16[256,512]{1,0:T(8,128)(2,1)} collective-permute-done((bf16[256,512]{1,0:T(8,128)(2,1)}, bf16[256,512]{1,0:T(8,128)(2,1)}, u32[]{:S(2)}, u32[]{:S(2)}) %collective-permute-start.40) | collective-permute-done | bytes 262176 | tf_op jit(solution)/shard_map/ppermute | solution.py:905
  395.8 6.8 %collective-permute-done.46 = bf16[1,528,512]{2,1,0:T(8,128)(2,1)S(1)} collective-permute-done((bf16[1,528,512]{2,1,0:T(8,128)(2,1)S(1)}, bf16[1,528,512]{2,1,0:T(8,128)(2,1)S(1)}, u32[]{:S(2)}, u32[]{:S(2)}) %collective-permute-start.46) | collective-permute-done | bytes 540704 | tf_op jit(solution)/shard_map/ppermute | solution.py:917
  412.7 5.6 %collective-permute-done.50.refs_1_ = bf16[2,528,512]{2,1,0:T(8,128)(2,1)} collective-permute-done((bf16[2,528,512]{2,1,0:T(8,128)(2,1)}, bf16[2,528,512]{2,1,0:T(8,128)(2,1)}, u32[]{:S(2)}, u32[]{:S(2)}) %collective-permute-start.50) | collective-permute-done | bytes 1081376 | tf_op jit(solution)/shard_map/ppermute | solution.py:917
  423.2 7.3 %shard_map.320 = (f32[256,4096]{1,0:T(8,128)}, f32[256,3072]{1,0:T(8,128)}, f32[256,1024]{1,0:T(8,128)}, f32[16,512]{1,0:T(8,128)}) custom-call(s32[10]{0:T(128)} %pad_add_fusion.where, bf16[2,528,512]{2,1,0:T(8,128)(2,1)} %pad_maximum_fusion.3.refs_0_, bf16[2,528,512]{2,1,0:T(8,128)(2,1)} %collective-permute-done.50.refs_1_, ...), custom_call_target="tpu_custom_call" | custom-call | bytes 14760000 | tf_op jit(solution)/shard_map/pallas_call | solution.py:787
  (227 shorter events, 130.9 us)
Async XLA Ops:
  1.8 19.0 %collective-permute-start.1 = (bf16[256,512]{1,0:T(8,128)(2,1)S(1)}, bf16[256,512]{1,0:T(8,128)(2,1)S(1)}, u32[]{:S(2)}, u32[]{:S(2)}) collective-permute-start(bf16[256,512]{1,0:T(8,128)(2,1)S(1)} %fusion.1), channel_id=1, source_target_pairs={{0,2},{1,3},{2,0},{3,1},{4,6},{5,7},{6,4},{7,5},{8,10},{9,11},{10,... | collective-permute-start | bytes 786440 | tf_op jit(solution)/shard_map/ppermute | solution.py:902
  4.3 22.1 %collective-permute-start.2 = (bf16[256,512]{1,0:T(8,128)(2,1)S(1)}, bf16[256,512]{1,0:T(8,128)(2,1)S(1)}, u32[]{:S(2)}, u32[]{:S(2)}) collective-permute-start(bf16[256,512]{1,0:T(8,128)(2,1)S(1)} %fusion.1), channel_id=1, source_target_pairs={{0,1},{1,2},{2,3},{3,0},{4,5},{5,6},{6,7},{7,4},{8,9},{9,10},{10,1... | collective-permute-start | bytes 786440 | tf_op jit(solution)/shard_map/ppermute | solution.py:902
  37.9 19.6 %collective-permute-start.4 = (bf16[2,3,256,512]{3,2,1,0:T(8,128)(2,1)S(1)}, bf16[2,3,256,512]{3,2,1,0:T(8,128)(2,1)S(1)}, u32[]{:S(2)}, u32[]{:S(2)}) collective-permute-start(bf16[2,3,256,512]{3,2,1,0:T(8,128)(2,1)S(1)} %pad_maximum_fusion.a), channel_id=1, source_target_pairs={{0,16},{4,12},{8,24},{12,4},{16,0},{20,28},{24,8},{28,20},{1,17},{... | collective-permute-start | bytes 4718600 | tf_op jit(solution)/shard_map/ppermute | solution.py:917
  63.7 16.6 %collective-permute-start.14 = (bf16[256,512]{1,0:T(8,128)(2,1)S(1)}, bf16[256,512]{1,0:T(8,128)(2,1)}, u32[]{:S(2)}, u32[]{:S(2)}) collective-permute-start(bf16[256,512]{1,0:T(8,128)(2,1)S(1)} %constant_dynamic-slice_fusion), channel_id=1, source_target_pairs={{0,3},{1,0},{2,1},{3,2},{4,7},{5,4},{6,5},{7,6},{8,11},{9,8},{10,9... | collective-permute-start | bytes 786440 | tf_op jit(solution)/shard_map/ppermute | solution.py:902
  64.6 17.0 %collective-permute-start.15 = (bf16[256,512]{1,0:T(8,128)(2,1)S(1)}, bf16[256,512]{1,0:T(8,128)(2,1)}, u32[]{:S(2)}, u32[]{:S(2)}) collective-permute-start(bf16[256,512]{1,0:T(8,128)(2,1)S(1)} %constant_dynamic-slice_fusion), channel_id=1, source_target_pairs={{0,2},{1,3},{2,0},{3,1},{4,6},{5,7},{6,4},{7,5},{8,10},{9,11},{10,... | collective-permute-start | bytes 786440 | tf_op jit(solution)/shard_map/ppermute | solution.py:902
  67.1 20.1 %collective-permute-start.16 = (bf16[256,512]{1,0:T(8,128)(2,1)S(1)}, bf16[256,512]{1,0:T(8,128)(2,1)}, u32[]{:S(2)}, u32[]{:S(2)}) collective-permute-start(bf16[256,512]{1,0:T(8,128)(2,1)S(1)} %constant_dynamic-slice_fusion), channel_id=1, source_target_pairs={{0,1},{1,2},{2,3},{3,0},{4,5},{5,6},{6,7},{7,4},{8,9},{9,10},{10,1... | collective-permute-start | bytes 786440 | tf_op jit(solution)/shard_map/ppermute | solution.py:902
  105.2 43.3 %collective-permute-start.18 = (bf16[2,3,256,512]{3,2,1,0:T(8,128)(2,1)}, bf16[2,3,256,512]{3,2,1,0:T(8,128)(2,1)}, u32[]{:S(2)}, u32[]{:S(2)}) collective-permute-start(bf16[2,3,256,512]{3,2,1,0:T(8,128)(2,1)} %pad_maximum_fusion.1.a), channel_id=1, source_target_pairs={{0,16},{4,12},{8,24},{12,4},{16,0},{20,28},{24,8},{28,20},{1,17},{... | collective-permute-start | bytes 4718600 | tf_op jit(solution)/shard_map/ppermute | solution.py:917
  107.4 21.7 %collective-permute-start.12 = (bf16[128,1024]{1,0:T(8,128)(2,1)S(1)}, bf16[128,1024]{1,0:T(8,128)(2,1)S(1)}, u32[]{:S(2)}, u32[]{:S(2)}) collective-permute-start(bf16[128,1024]{1,0:T(8,128)(2,1)S(1)} %constant_dynamic-slice_fusion.1), channel_id=1, source_target_pairs={{0,1},{1,2},{2,3},{3,0},{4,5},{5,6},{6,7},{7,4},{8,9},{9,10},{10,1... | collective-permute-start | bytes 786440 | tf_op jit(solution)/shard_map/ppermute | solution.py:902
  111.8 21.7 %collective-permute-start.10 = (bf16[128,1024]{1,0:T(8,128)(2,1)S(1)}, bf16[128,1024]{1,0:T(8,128)(2,1)}, u32[]{:S(2)}, u32[]{:S(2)}) collective-permute-start(bf16[128,1024]{1,0:T(8,128)(2,1)S(1)} %constant_dynamic-slice_fusion.1), channel_id=1, source_target_pairs={{0,3},{1,0},{2,1},{3,2},{4,7},{5,4},{6,5},{7,6},{8,11},{9,8},{10,9... | collective-permute-start | bytes 786440 | tf_op jit(solution)/shard_map/ppermute | solution.py:902
  149.8 19.9 %collective-permute-start.21 = (bf16[2,3,128,1024]{3,2,1,0:T(8,128)(2,1)}, bf16[2,3,128,1024]{3,2,1,0:T(8,128)(2,1)}, u32[]{:S(2)}, u32[]{:S(2)}) collective-permute-start(bf16[2,3,128,1024]{3,2,1,0:T(8,128)(2,1)} %pad_maximum_fusion.2.a), channel_id=1, source_target_pairs={{0,16},{4,12},{8,24},{12,4},{16,0},{20,28},{24,8},{28,20},{1,17},{... | collective-permute-start | bytes 4718600 | tf_op jit(solution)/shard_map/ppermute | solution.py:917
  150.8 22.1 %collective-permute-start.22 = (bf16[2,3,128,1024]{3,2,1,0:T(8,128)(2,1)}, bf16[2,3,128,1024]{3,2,1,0:T(8,128)(2,1)}, u32[]{:S(2)}, u32[]{:S(2)}) collective-permute-start(bf16[2,3,128,1024]{3,2,1,0:T(8,128)(2,1)} %pad_maximum_fusion.2.a), channel_id=1, source_target_pairs={{0,4},{4,0},{1,5},{5,1},{2,6},{6,2},{3,7},{7,3},{8,12},{12,8},{9,1... | collective-permute-start | bytes 4718600 | tf_op jit(solution)/shard_map/ppermute | solution.py:908
  170.6 20.9 %collective-permute-start.25 = (bf16[4096,256]{1,0:T(8,128)(2,1)}, bf16[4096,256]{1,0:T(8,128)(2,1)}, u32[]{:S(2)}, u32[]{:S(2)}) collective-permute-start(bf16[4096,256]{1,0:T(8,128)(2,1)} %get-tuple-element.134), channel_id=1, source_target_pairs={{0,4},{4,0},{1,5},{5,1},{2,6},{6,2},{3,7},{7,3},{8,12},{12,8},{9,1... | collective-permute-start | bytes 6291464 | tf_op jit(solution)/shard_map/ppermute | solution.py:908
  170.6 20.9 %collective-permute-start.26 = (bf16[4096,256]{1,0:T(8,128)(2,1)}, bf16[4096,256]{1,0:T(8,128)(2,1)}, u32[]{:S(2)}, u32[]{:S(2)}) collective-permute-start(bf16[4096,256]{1,0:T(8,128)(2,1)} %get-tuple-element.135), channel_id=1, source_target_pairs={{0,4},{4,0},{1,5},{5,1},{2,6},{6,2},{3,7},{7,3},{8,12},{12,8},{9,1... | collective-permute-start | bytes 6291464 | tf_op jit(solution)/shard_map/ppermute | solution.py:908
  189.7 44.5 %collective-permute-start.29 = (bf16[2,1024,512]{2,1,0:T(8,128)(2,1)}, bf16[2,1024,512]{2,1,0:T(8,128)(2,1)}, u32[]{:S(2)}, u32[]{:S(2)}) collective-permute-start(bf16[2,1024,512]{2,1,0:T(8,128)(2,1)} %get-tuple-element.144.refs_2_.refs_6_), channel_id=1, source_target_pairs={{0,4},{4,0},{1,5},{5,1},{2,6},{6,2},{3,7},{7,3},{8,12},{12,8},{9,1... | collective-permute-start | bytes 6291464 | tf_op jit(solution)/shard_map/ppermute | solution.py:908
  199.7 34.5 %collective-permute-start.28 = (bf16[2,1024,512]{2,1,0:T(8,128)(2,1)}, bf16[2,1024,512]{2,1,0:T(8,128)(2,1)}, u32[]{:S(2)}, u32[]{:S(2)}) collective-permute-start(bf16[2,1024,512]{2,1,0:T(8,128)(2,1)} %shard_map.305), channel_id=1, source_target_pairs={{0,8},{4,20},{8,0},{12,28},{16,24},{20,4},{24,16},{28,12},{1,9},{5... | collective-permute-start | bytes 6291464 | tf_op jit(solution)/shard_map/ppermute | solution.py:917
  199.9 16.2 %collective-permute-start.27 = (bf16[1024,512]{1,0:T(8,128)(2,1)}, bf16[1024,512]{1,0:T(8,128)(2,1)}, u32[]{:S(2)}, u32[]{:S(2)}) collective-permute-start(bf16[1024,512]{1,0:T(8,128)(2,1)} %get-tuple-element.139), channel_id=1, source_target_pairs={{0,4},{4,0},{1,5},{5,1},{2,6},{6,2},{3,7},{7,3},{8,12},{12,8},{9,1... | collective-permute-start | bytes 3145736 | tf_op jit(solution)/shard_map/ppermute | solution.py:908
  216.0 25.2 %collective-permute-start.31 = (bf16[512,2048]{1,0:T(8,128)(2,1)}, bf16[512,2048]{1,0:T(8,128)(2,1)}, u32[]{:S(2)}, u32[]{:S(2)}) collective-permute-start(bf16[512,2048]{1,0:T(8,128)(2,1)} %get-tuple-element.146), channel_id=1, source_target_pairs={{0,4},{4,0},{1,5},{5,1},{2,6},{6,2},{3,7},{7,3},{8,12},{12,8},{9,1... | collective-permute-start | bytes 6291464 | tf_op jit(solution)/shard_map/ppermute | solution.py:908
  240.0 21.5 %collective-permute-start.30 = (bf16[1,1024,512]{2,1,0:T(8,128)(2,1)}, bf16[1,1024,512]{2,1,0:T(8,128)(2,1)}, u32[]{:S(2)}, u32[]{:S(2)}) collective-permute-start(bf16[1,1024,512]{2,1,0:T(8,128)(2,1)} %shard_map.308), channel_id=1, source_target_pairs={{0,16},{4,12},{8,24},{12,4},{16,0},{20,28},{24,8},{28,20},{1,17},{... | collective-permute-start | bytes 3145736 | tf_op jit(solution)/shard_map/ppermute | solution.py:917
  248.4 35.2 %collective-permute-start.33 = (bf16[2,1024,512]{2,1,0:T(8,128)(2,1)}, bf16[2,1024,512]{2,1,0:T(8,128)(2,1)}, u32[]{:S(2)}, u32[]{:S(2)}) collective-permute-start(bf16[2,1024,512]{2,1,0:T(8,128)(2,1)} %shard_map.309), channel_id=1, source_target_pairs={{0,8},{4,20},{8,0},{12,28},{16,24},{20,4},{24,16},{28,12},{1,9},{5... | collective-permute-start | bytes 6291464 | tf_op jit(solution)/shard_map/ppermute | solution.py:917
  267.8 25.0 %collective-permute-start.32 = (bf16[4,512,512]{2,1,0:T(8,128)(2,1)}, bf16[4,512,512]{2,1,0:T(8,128)(2,1)}, u32[]{:S(2)}, u32[]{:S(2)}) collective-permute-start(bf16[4,512,512]{2,1,0:T(8,128)(2,1)} %get-tuple-element.157.others), channel_id=1, source_target_pairs={{0,4},{4,0},{1,5},{5,1},{2,6},{6,2},{3,7},{7,3},{8,12},{12,8},{9,1... | collective-permute-start | bytes 6291464 | tf_op jit(solution)/shard_map/ppermute | solution.py:908
  268.8 20.4 %collective-permute-start.34 = (bf16[256,512]{1,0:T(8,128)(2,1)}, bf16[256,512]{1,0:T(8,128)(2,1)S(1)}, u32[]{:S(2)}, u32[]{:S(2)}) collective-permute-start(bf16[256,512]{1,0:T(8,128)(2,1)} %get-tuple-element.159), channel_id=1, source_target_pairs={{0,1},{1,2},{2,3},{3,0},{4,5},{5,6},{6,7},{7,4},{8,9},{9,10},{10,1... | collective-permute-start | bytes 786440 | tf_op jit(solution)/shard_map/ppermute | solution.py:905
  268.8 23.0 %collective-permute-start.35 = (bf16[256,512]{1,0:T(8,128)(2,1)}, bf16[256,512]{1,0:T(8,128)(2,1)S(1)}, u32[]{:S(2)}, u32[]{:S(2)}) collective-permute-start(bf16[256,512]{1,0:T(8,128)(2,1)} %get-tuple-element.160), channel_id=1, source_target_pairs={{0,2},{1,3},{2,0},{3,1},{4,6},{5,7},{6,4},{7,5},{8,10},{9,11},{10,... | collective-permute-start | bytes 786440 | tf_op jit(solution)/shard_map/ppermute | solution.py:905
  268.9 23.9 %collective-permute-start.36 = (bf16[256,512]{1,0:T(8,128)(2,1)}, bf16[256,512]{1,0:T(8,128)(2,1)S(1)}, u32[]{:S(2)}, u32[]{:S(2)}) collective-permute-start(bf16[256,512]{1,0:T(8,128)(2,1)} %get-tuple-element.161), channel_id=1, source_target_pairs={{0,3},{1,0},{2,1},{3,2},{4,7},{5,4},{6,5},{7,6},{8,11},{9,8},{10,9... | collective-permute-start | bytes 786440 | tf_op jit(solution)/shard_map/ppermute | solution.py:905
  299.9 36.8 %collective-permute-start.41 = (bf16[2,1024,512]{2,1,0:T(8,128)(2,1)}, bf16[2,1024,512]{2,1,0:T(8,128)(2,1)}, u32[]{:S(2)}, u32[]{:S(2)}) collective-permute-start(bf16[2,1024,512]{2,1,0:T(8,128)(2,1)} %shard_map.314), channel_id=1, source_target_pairs={{0,8},{4,20},{8,0},{12,28},{16,24},{20,4},{24,16},{28,12},{1,9},{5... | collective-permute-start | bytes 6291464 | tf_op jit(solution)/shard_map/ppermute | solution.py:917
  301.3 25.4 %collective-permute-start.37 = (bf16[1,1024,512]{2,1,0:T(8,128)(2,1)}, bf16[1,1024,512]{2,1,0:T(8,128)(2,1)}, u32[]{:S(2)}, u32[]{:S(2)}) collective-permute-start(bf16[1,1024,512]{2,1,0:T(8,128)(2,1)} %shard_map.313), channel_id=1, source_target_pairs={{0,16},{4,12},{8,24},{12,4},{16,0},{20,28},{24,8},{28,20},{1,17},{... | collective-permute-start | bytes 3145736 | tf_op jit(solution)/shard_map/ppermute | solution.py:917
  343.9 20.4 %collective-permute-start.38 = (bf16[256,512]{1,0:T(8,128)(2,1)}, bf16[256,512]{1,0:T(8,128)(2,1)}, u32[]{:S(2)}, u32[]{:S(2)}) collective-permute-start(bf16[256,512]{1,0:T(8,128)(2,1)} %get-tuple-element.168), channel_id=1, source_target_pairs={{0,1},{1,2},{2,3},{3,0},{4,5},{5,6},{6,7},{7,4},{8,9},{9,10},{10,1... | collective-permute-start | bytes 786440 | tf_op jit(solution)/shard_map/ppermute | solution.py:905
  343.9 22.9 %collective-permute-start.39 = (bf16[256,512]{1,0:T(8,128)(2,1)}, bf16[256,512]{1,0:T(8,128)(2,1)}, u32[]{:S(2)}, u32[]{:S(2)}) collective-permute-start(bf16[256,512]{1,0:T(8,128)(2,1)} %get-tuple-element.169), channel_id=1, source_target_pairs={{0,2},{1,3},{2,0},{3,1},{4,6},{5,7},{6,4},{7,5},{8,10},{9,11},{10,... | collective-permute-start | bytes 786440 | tf_op jit(solution)/shard_map/ppermute | solution.py:905
  346.1 35.5 %collective-permute-start.40 = (bf16[256,512]{1,0:T(8,128)(2,1)}, bf16[256,512]{1,0:T(8,128)(2,1)}, u32[]{:S(2)}, u32[]{:S(2)}) collective-permute-start(bf16[256,512]{1,0:T(8,128)(2,1)} %get-tuple-element.170), channel_id=1, source_target_pairs={{0,3},{1,0},{2,1},{3,2},{4,7},{5,4},{6,5},{7,6},{8,11},{9,8},{10,9... | collective-permute-start | bytes 786440 | tf_op jit(solution)/shard_map/ppermute | solution.py:905
  363.0 19.8 %collective-permute-start.47 = (bf16[1,256,512]{2,1,0:T(8,128)(2,1)S(1)}, bf16[1,256,512]{2,1,0:T(8,128)(2,1)S(1)}, u32[]{:S(2)}, u32[]{:S(2)}) collective-permute-start(bf16[1,256,512]{2,1,0:T(8,128)(2,1)S(1)} %fusion.3), channel_id=1, source_target_pairs={{0,8},{4,20},{8,0},{12,28},{16,24},{20,4},{24,16},{28,12},{1,9},{5... | collective-permute-start | bytes 786440 | tf_op jit(solution)/shard_map/ppermute | solution.py:917
  364.4 19.8 %collective-permute-start.43 = (bf16[272,512]{1,0:T(8,128)(2,1)}, bf16[272,512]{1,0:T(8,128)(2,1)S(1)}, u32[]{:S(2)}, u32[]{:S(2)}) collective-permute-start(bf16[272,512]{1,0:T(8,128)(2,1)} %get-tuple-element.180), channel_id=1, source_target_pairs={{0,1},{1,2},{2,3},{3,0},{4,5},{5,6},{6,7},{7,4},{8,9},{9,10},{10,1... | collective-permute-start | bytes 835592 | tf_op jit(solution)/shard_map/ppermute | solution.py:905
  364.4 25.0 %collective-permute-start.44 = (bf16[272,512]{1,0:T(8,128)(2,1)}, bf16[272,512]{1,0:T(8,128)(2,1)S(1)}, u32[]{:S(2)}, u32[]{:S(2)}) collective-permute-start(bf16[272,512]{1,0:T(8,128)(2,1)} %get-tuple-element.181), channel_id=1, source_target_pairs={{0,2},{1,3},{2,0},{3,1},{4,6},{5,7},{6,4},{7,5},{8,10},{9,11},{10,... | collective-permute-start | bytes 835592 | tf_op jit(solution)/shard_map/ppermute | solution.py:905
  366.8 27.1 %collective-permute-start.45 = (bf16[272,512]{1,0:T(8,128)(2,1)}, bf16[272,512]{1,0:T(8,128)(2,1)S(1)}, u32[]{:S(2)}, u32[]{:S(2)}) collective-permute-start(bf16[272,512]{1,0:T(8,128)(2,1)} %get-tuple-element.182), channel_id=1, source_target_pairs={{0,3},{1,0},{2,1},{3,2},{4,7},{5,4},{6,5},{7,6},{8,11},{9,8},{10,9... | collective-permute-start | bytes 835592 | tf_op jit(solution)/shard_map/ppermute | solution.py:905
  (48 other events, 559.7 us)
